TPU v7x, 128 devices: a whole 4x4x4 slice. The times are simulated.
128 devices in a mesh: dp: 16 (over x_lo, y, core), tensor: 8 (over x_hi, z).
Axes of the slice: x: 4 (x_hi: 2, x_lo: 2; x = x_hi * 2 + x_lo), y: 4, z: 4, core: 2. Of those that a mesh axis runs over, the one named last changes fastest.
Arguments:
- block_input: bfloat16 [32768, 768], P(('dp', 'tensor')), may hold values from -6 to 6
- w_value: bfloat16 [768, 768], replicated, may hold values from -0.21875 to 0.21875
- b_value: bfloat16 [768], replicated, may hold values from -2 to 2
- conv_kernel: bfloat16 [65, 768], replicated, may hold values from -0.75 to 0.75
- w_out: bfloat16 [768, 768], replicated, may hold values from -0.21875 to 0.21875
- b_out: bfloat16 [768], replicated, may hold values from -2 to 2
- gain_attn: bfloat16 [768], replicated, may hold values from 0.5 to 1.5
- shift_attn: bfloat16 [768], replicated, may hold values from -2 to 2
- w_up: bfloat16 [768, 3072], P(None, 'tensor'), may hold values from -0.21875 to 0.21875
- b_up: bfloat16 [3072], P('tensor'), may hold values from -2 to 2
- w_down: bfloat16 [3072, 768], P('tensor'), may hold values from -0.109375 to 0.109375
- b_down: bfloat16 [768], replicated, may hold values from -2 to 2
- gain_ffn: bfloat16 [768], replicated, may hold values from 0.5 to 1.5
- shift_ffn: bfloat16 [768], replicated, may hold values from -2 to 2
- query_codes: int32 [32768, 384], P(('dp', 'tensor')), may hold values from 0 to 255
- key_codes: int32 [32768, 384], P(('dp', 'tensor')), may hold values from 0 to 255
- key_live: int32 [32768], P(('dp', 'tensor')), may hold values 0 or 1
- seq_lengths: int32 [128, 4], P(('dp', 'tensor')), may hold values from 1 to 128, 256 in all within a row
- out_grad: bfloat16 [32768, 768], P(('dp', 'tensor')), may hold values from -6 to 6
Outputs:
- block_output: bfloat16 [32768, 768], P(('dp', 'tensor'))
- input_grad: float32 [32768, 768], P(('dp', 'tensor'))
- grad_w_value: float32 [768, 768], replicated
- grad_b_value: float32 [768], replicated
- grad_conv_kernel: float32 [65, 768], replicated
- grad_w_out: float32 [768, 768], replicated
- grad_b_out: float32 [768], replicated
- grad_gain_attn: float32 [768], replicated
- grad_shift_attn: float32 [768], replicated
- grad_w_up: float32 [768, 3072], P(None, 'tensor')
- grad_b_up: float32 [3072], P('tensor')
- grad_w_down: float32 [3072, 768], P('tensor')
- grad_b_down: float32 [768], replicated
- grad_gain_ffn: float32 [768], replicated
- grad_shift_ffn: float32 [768], replicated
Inputs may be any that keep to these rules, and one draw needn't show every extreme that they name: `seq_lengths`: each item's lengths sum to 256; the longest is 128. `key_live`: 1 marks a live key, 0 a padded one. `query_codes`: column h * 32 + s holds head h's code in hash set s. `key_codes`: column h * 32 + s holds head h's code in hash set s.
All inputs are finite; a program needn't handle non-finite values. No bound on the sum of `key_live` on one device may be relied on, other than what follows from the above.
Results may differ from a plain program's by a relative error of at most 0.02.
Values may be sent and summed in bfloat16 or wider, within the bound.
No kernel may reach another device: no remote copies, remote signals or barrier semaphores. Data moves between devices by JAX's collectives and lax.ppermute only.
A program may use at most 128 MiB of HBM per device.

v0:
```python
from functools import partial

import jax
import jax.numpy as jnp
from jax import lax
from jax.sharding import PartitionSpec as P

HEADS = 12
SETS = 32
BUCKETS = 256


def dot_last(former, latter):
    return lax.dot_general(
        former, latter, (((1,), (1,)), ((), ())), preferred_element_type=jnp.float32
    )


def dot_first(former, latter):
    return lax.dot_general(
        former, latter, (((0,), (0,)), ((), ())), preferred_element_type=jnp.float32
    )


def layer_norm(residual, gain_vec, shift_vec):
    average = jnp.mean(residual, axis=-1, keepdims=True)
    centred = residual - average
    variance = jnp.mean(centred * centred, axis=-1, keepdims=True)
    return centred * lax.rsqrt(variance + 1e-05) * gain_vec + shift_vec


def head_norm(mixed, head_count, head_dim):
    grouped = mixed.reshape(mixed.shape[0], head_count, head_dim)
    scaling = lax.rsqrt(jnp.mean(grouped * grouped, axis=-1, keepdims=True) + 1e-06)
    return (grouped * scaling).reshape(mixed.shape)


def gelu_exact(pre_act):
    return jax.nn.gelu(pre_act, approximate=False)


def depth_conv(values, kernel, segment):
    taps = kernel.shape[0]
    margin = taps // 2
    length = values.shape[0]
    padded = jnp.pad(values, ((margin, margin), (0, 0)))
    seg_padded = jnp.pad(segment, (margin, margin), constant_values=-1)
    running = jnp.zeros_like(values)
    for offset in range(taps):
        joined = (seg_padded[offset : offset + length] == segment).astype(jnp.float32)[:, None]
        running = running + padded[offset : offset + length] * joined * kernel[offset][None, :]
    return running


def conv_back(grad_out, values, kernel, segment):
    taps = kernel.shape[0]
    margin = taps // 2
    length = values.shape[0]
    padded = jnp.pad(values, ((margin, margin), (0, 0)))
    grad_padded = jnp.pad(grad_out, ((margin, margin), (0, 0)))
    seg_padded = jnp.pad(segment, (margin, margin), constant_values=-1)
    value_grad = jnp.zeros_like(values)
    tap_rows = []
    for offset in range(taps):
        joined = (seg_padded[offset : offset + length] == segment).astype(jnp.float32)[:, None]
        tap_rows.append(jnp.sum(grad_out * joined * padded[offset : offset + length], axis=0))
        mirror = 2 * margin - offset
        back_joined = (seg_padded[mirror : mirror + length] == segment).astype(jnp.float32)[:, None]
        value_grad = (
            value_grad
            + grad_padded[mirror : mirror + length] * back_joined * kernel[offset][None, :]
        )
    return (value_grad, jnp.stack(tap_rows, axis=0))


def body(
    block_input,
    w_value,
    b_value,
    conv_kernel,
    w_out,
    b_out,
    gain_attn,
    shift_attn,
    w_up,
    b_up,
    w_down,
    b_down,
    gain_ffn,
    shift_ffn,
    query_codes,
    key_codes,
    key_live,
    seq_lengths,
    out_grad,
):
    length = block_input.shape[0]
    model_width = block_input.shape[1]
    head_dim = model_width // HEADS
    live_keys = key_live.astype(jnp.float32)[:, None]
    seq_ends = jnp.cumsum(seq_lengths[0], dtype=jnp.int32)
    positions = jnp.arange(length, dtype=jnp.int32)
    segment = jnp.sum(
        (seq_ends[None, :] <= positions[:, None]).astype(jnp.int32), axis=1, dtype=jnp.int32
    )
    query_heads = query_codes.reshape(length, HEADS, SETS).transpose(1, 0, 2)
    key_heads = key_codes.reshape(length, HEADS, SETS).transpose(1, 0, 2)
    joined = (segment[:, None] == segment[None, :]).astype(jnp.float32)
    bucket_ids = jnp.arange(BUCKETS, dtype=jnp.int32)

    def head_counts(pair):
        query_set, key_set = pair
        query_hot = (
            (query_set[:, :, None] == bucket_ids[None, None, :])
            .astype(jnp.bfloat16)
            .reshape(length, SETS * BUCKETS)
        )
        key_hot = (
            (key_set[:, :, None] == bucket_ids[None, None, :])
            .astype(jnp.bfloat16)
            .reshape(length, SETS * BUCKETS)
        )
        counts = dot_last(query_hot, key_hot)
        return (counts * joined / SETS).astype(jnp.bfloat16)

    collide = lax.map(head_counts, (query_heads, key_heads))
    kernel_f = conv_kernel.astype(jnp.float32)
    value_pre = jnp.dot(block_input, w_value, preferred_element_type=jnp.float32) + b_value.astype(
        jnp.float32
    )
    values = value_pre.astype(jnp.bfloat16)
    masked = values.astype(jnp.float32) * live_keys
    masked_low = masked.astype(jnp.bfloat16)
    mixed = jnp.einsum(
        "hij,jhd->ihd",
        collide,
        masked_low.reshape(length, HEADS, head_dim),
        preferred_element_type=jnp.float32,
    ).reshape(length, model_width)
    normed, norm_back = jax.vjp(partial(head_norm, head_count=HEADS, head_dim=head_dim), mixed)
    context = (normed + depth_conv(masked, kernel_f, segment)).astype(jnp.bfloat16)
    attended = jnp.dot(context, w_out, preferred_element_type=jnp.float32) + b_out.astype(
        jnp.float32
    )
    first, first_back = jax.vjp(
        layer_norm,
        block_input.astype(jnp.float32) + attended,
        gain_attn.astype(jnp.float32),
        shift_attn.astype(jnp.float32),
    )
    first_low = first.astype(jnp.bfloat16)
    gathered = lax.all_gather(first_low, "tensor", axis=0, tiled=True)
    upper = jnp.dot(gathered, w_up, preferred_element_type=jnp.float32) + b_up.astype(jnp.float32)
    active_f, gelu_back = jax.vjp(gelu_exact, upper)
    active = active_f.astype(jnp.bfloat16)
    branch = lax.psum_scatter(
        jnp.dot(active, w_down, preferred_element_type=jnp.float32).astype(jnp.bfloat16),
        "tensor",
        scatter_dimension=0,
        tiled=True,
    ).astype(jnp.float32) + b_down.astype(jnp.float32)
    block_output, second_back = jax.vjp(
        layer_norm, first + branch, gain_ffn.astype(jnp.float32), shift_ffn.astype(jnp.float32)
    )
    grad_second, grad_gain_ffn, grad_shift_ffn = second_back(out_grad.astype(jnp.float32))
    branch_grad = grad_second.astype(jnp.bfloat16)
    grad_b_down = jnp.sum(branch_grad.astype(jnp.float32), axis=0)
    grad_rows_all = lax.all_gather(branch_grad, "tensor", axis=0, tiled=True)
    active_grad = dot_last(grad_rows_all, w_down)
    grad_w_down = dot_first(active, grad_rows_all)
    upper_grad = gelu_back(active_grad)[0].astype(jnp.bfloat16)
    grad_w_up = dot_first(gathered, upper_grad)
    grad_b_up = jnp.sum(upper_grad.astype(jnp.float32), axis=0)
    first_grad_ffn = lax.psum_scatter(
        dot_last(upper_grad, w_up).astype(jnp.bfloat16), "tensor", scatter_dimension=0, tiled=True
    ).astype(jnp.float32)
    first_grad = grad_second + first_grad_ffn
    resid_grad, grad_gain_attn, grad_shift_attn = first_back(first_grad)
    attended_grad = resid_grad.astype(jnp.bfloat16)
    grad_b_out = jnp.sum(attended_grad.astype(jnp.float32), axis=0)
    grad_w_out = dot_first(context, attended_grad)
    context_grad = dot_last(attended_grad, w_out)
    mixed_grad = norm_back(context_grad)[0].astype(jnp.bfloat16)
    conv_value_grad, grad_kernel = conv_back(context_grad, masked, kernel_f, segment)
    masked_att = jnp.einsum(
        "hij,ihd->jhd",
        collide,
        mixed_grad.reshape(length, HEADS, head_dim),
        preferred_element_type=jnp.float32,
    ).reshape(length, model_width)
    value_grad = ((masked_att + conv_value_grad) * live_keys).astype(jnp.bfloat16)
    grad_b_value = jnp.sum(value_grad.astype(jnp.float32), axis=0)
    grad_w_value = dot_first(block_input, value_grad)
    input_grad = resid_grad + dot_last(value_grad, w_value)
    grad_w_up, grad_w_down, grad_b_up = (
        lax.psum(grad_w_up.astype(jnp.bfloat16), "dp").astype(jnp.float32),
        lax.psum(grad_w_down.astype(jnp.bfloat16), "dp").astype(jnp.float32),
        lax.psum(grad_b_up.astype(jnp.bfloat16), "dp").astype(jnp.float32),
    )
    (
        grad_w_value,
        grad_b_value,
        grad_kernel,
        grad_w_out,
        grad_b_out,
        grad_gain_attn,
        grad_shift_attn,
        grad_b_down,
        grad_gain_ffn,
        grad_shift_ffn,
    ) = lax.psum(
        (
            grad_w_value,
            grad_b_value,
            grad_kernel,
            grad_w_out,
            grad_b_out,
            grad_gain_attn,
            grad_shift_attn,
            grad_b_down,
            grad_gain_ffn,
            grad_shift_ffn,
        ),
        ("dp", "tensor"),
    )
    return (
        block_output.astype(jnp.bfloat16),
        input_grad,
        grad_w_value,
        grad_b_value,
        grad_kernel,
        grad_w_out,
        grad_b_out,
        grad_gain_attn,
        grad_shift_attn,
        grad_w_up,
        grad_b_up,
        grad_w_down,
        grad_b_down,
        grad_gain_ffn,
        grad_shift_ffn,
    )


def solution(mesh):
    return jax.shard_map(
        body,
        mesh=mesh,
        in_specs=(
            P(("dp", "tensor"), None),
            P(),
            P(),
            P(),
            P(),
            P(),
            P(),
            P(),
            P(None, "tensor"),
            P("tensor"),
            P("tensor", None),
            P(),
            P(),
            P(),
            P(("dp", "tensor"), None),
            P(("dp", "tensor"), None),
            P(("dp", "tensor")),
            P(("dp", "tensor"), None),
            P(("dp", "tensor"), None),
        ),
        out_specs=(
            P(("dp", "tensor"), None),
            P(("dp", "tensor"), None),
            P(),
            P(),
            P(),
            P(),
            P(),
            P(),
            P(),
            P(None, "tensor"),
            P("tensor"),
            P("tensor", None),
            P(),
            P(),
            P(),
        ),
        check_vma=False,
    )
```

profile of v0, /device:TPU:1, one launch (start us, length us, event | category | flops | bytes accessed | tf_op | source)
XLA Modules:
  0.0 701.2 jit_solution(10940862884612107198)
XLA Ops:
  17.3 43.1 %while.12 = (s32[]{:T(128)}, bf16[12,256,256]{2,1,0:T(8,128)(2,1)}, s32[12,256,32]{1,2,0:T(8,128)S(1)}, s32[12,256,32]{1,2,0:T(8,128)S(1)}, s32[256]{0:T(256)S(1)}, /*index=5*/s32[]{:T(128)}) while((s32[]{:T(128)}, bf16[12,256,256]{2,1,0:T(8,128)(2,1)}, s32[12,256,32]{1,2,0:T(8,128)S(1)}, s32[12,256,32]{1,2,0:T(8,128)S(1)}, ...), condition=%wide.region_3.4_spmd.clone.clone, body=%wide.region_2.3_spmd.clone.clone.sunk | while | flops 1078198272 | bytes 330313 | solution.py:126
  17.4 3.6 fusion.266
  21.0 3.6 fusion.266
  24.6 3.6 fusion.266
  28.1 3.6 fusion.266
  31.7 3.6 fusion.266
  35.3 3.6 fusion.266
  38.9 3.6 fusion.266
  42.5 3.6 fusion.266
  46.1 3.6 fusion.266
  49.7 3.6 fusion.266
  53.2 3.6 fusion.266
  56.8 3.6 fusion.266
  61.2 2.0 multiply_reduce_fusion.70
  66.3 11.6 %add_convert_fusion.2 = bf16[256,768]{1,0:T(8,128)(2,1)S(1)} fusion(f32[256,768]{1,0:T(8,128)S(1)} %copy.51, f32[256,768]{1,0:T(8,128)S(1)} %get-tuple-element.368, f32[768]{0:T(1024)} %get-tuple-element.198, f32[256]{0:T(256)} %get-tuple-element.366, f32[768]{0:T(1024)} %get-tuple-element.199, f32[256]{0:T(256)} %get-tuple-element.365, ...), kind=kLoop, calls=%fused_computation.456 | loop fusion | flops 38338560 | bytes 2231296 | tf_op jit(solution)/shard_map/convert_element_type | solution.py:141
  78.7 1.9 fusion.236
  85.1 64.2 %all-gather.3.cloned.1.call-done = bf16[2048,768]{1,0:T(8,128)(2,1)} async-done(((bf16[256,768]{1,0:T(8,128)(2,1)}), bf16[2048,768]{1,0:T(8,128)(2,1)}) %all-gather.3.cloned.1.call-update) | async-done | bytes 3145744 | tf_op jit(solution)/shard_map/all_gather | solution.py:152
  149.4 11.6 %multiply_convert_fusion = (bf16[2048,384]{1,0:T(8,128)(2,1)S(1)}, f32[2048,384]{1,0:T(8,128)}, f32[2048,384]{1,0:T(8,128)}) fusion(f32[384]{0:T(512)} %convert_element_type.529, bf16[2048,768]{1,0:T(8,128)(2,1)} %all-gather.3.cloned.1.call-done, bf16[768,384]{1,0:T(8,128)(2,1)} %param.29), kind=kOutput, calls=%fused_computation.148 | convolution fusion | flops 1259864064 | bytes 11601408 | tf_op jit(solution)/shard_map/dot_general | solution.py:153
  162.2 3.4 convolution_convert_fusion.1
  169.5 72.7 %reduce-scatter.3.cloned.1.call-done = bf16[256,768]{1,0:T(8,128)(2,1)} async-done(((bf16[2048,768]{1,0:T(8,128)(2,1)}), bf16[256,768]{1,0:T(8,128)(2,1)}) %reduce-scatter.3.cloned.1.call-update) | async-done | bytes 393232 | tf_op jit(solution)/shard_map/reduce_scatter | solution.py:156
  243.9 1.9 fusion.26
  249.4 62.5 %all-gather.5.cloned.1.call-done = bf16[2048,768]{1,0:T(8,128)(2,1)} async-done(((bf16[256,768]{1,0:T(8,128)(2,1)}), bf16[2048,768]{1,0:T(8,128)(2,1)}) %all-gather.5.cloned.1.call-update) | async-done | bytes 3145744 | tf_op jit(solution)/shard_map/all_gather | solution.py:168
  311.9 7.3 %fusion.230 = (bf16[384]{0:T(512)(128)(2,1)}, bf16[2048,384]{1,0:T(8,128)(2,1)S(1)}) fusion(f32[2048,384]{1,0:T(8,128)} %get-tuple-element.299, f32[2048,384]{1,0:T(8,128)} %get-tuple-element.373, bf16[2048,768]{1,0:T(8,128)(2,1)} %all-gather.5.cloned.1.call-done, bf16[384,768]{1,0:T(8,128)(2,1)} %param.31), kind=kOutput, calls=%fused_computation.674 | convolution fusion | flops 1219755648 | bytes 11600640 | tf_op jit(solution)/shard_map/dot_general | solution.py:14
  320.3 3.5 convolution_convert_fusion
  323.9 4.7 convolution_convert_fusion.2
  328.7 2.6 convolution_convert_fusion.3
  331.4 69.1 %reduce-scatter.5.cloned.1.call-done = bf16[256,768]{1,0:T(8,128)(2,1)} async-done(((bf16[2048,768]{1,0:T(8,128)(2,1)}), bf16[256,768]{1,0:T(8,128)(2,1)}) %reduce-scatter.5.cloned.1.call-update) | async-done | bytes 393232 | tf_op jit(solution)/shard_map/reduce_scatter | solution.py:174
  400.5 2.4 multiply_reduce_fusion
  403.5 1.8 fusion.231
  407.4 1.9 fusion.237
  410.7 11.4 %multiply_reduce_fusion.46 = (f32[768]{0:T(1024)}, f32[768]{0:T(1024)}, f32[768]{0:T(1024)}, f32[768]{0:T(1024)}, f32[768]{0:T(1024)}, /*index=5*/f32[768]{0:T(1024)}, f32[768]{0:T(1024)}, f32[768]{0:T(1024)}, f32[768]{0:T(1024)}) fusion(f32[256,768]{1,0:T(8,128)S(1)} %get-tuple-element.374, f32[256,768]{1,0:T(8,128)S(1)} %get-tuple-element.368, ...), kind=kLoop, calls=%fused_computation.426 | loop fusion | flops 5301504 | bytes 1609728 | tf_op jit(solution)/shard_map/reduce_sum | solution.py:66
  422.1 2.9 multiply_reduce_fusion.37
  425.1 2.1 multiply_reduce_fusion.19
  427.3 2.1 multiply_reduce_fusion.10
  429.5 2.9 multiply_reduce_fusion.1
  432.5 2.1 multiply_reduce_fusion.28
  434.7 2.2 multiply_reduce_fusion.55
  460.1 5.8 stack.263
  466.0 11.7 %convert_reduce_fusion.3 = (f32[768]{0:T(1024)S(1)}, bf16[256,768]{1,0:T(8,128)(2,1)S(1)}) fusion(f32[256]{0:T(256)} %copy-done.110, f32[256,768]{1,0:T(8,128)S(1)} %copy.53, f32[768]{0:T(1024)} %get-tuple-element.198, f32[256]{0:T(256)} %get-tuple-element.303, f32[768]{0:T(1024)} %get-tuple-element.199, f32[256]{0:T(256)} %get-tuple-element.321, ...), kind=kLoop, calls=%fused_computation.446 | loop fusion | flops 38927616 | bytes 2235392 | tf_op jit(solution)/shard_map/reduce_sum | solution.py:192
  477.7 1.9 convolution_bitcast_fusion
  480.3 28.6 %psum.99 = bf16[384]{0:T(512)(128)(2,1)S(1)} all-reduce(bf16[384]{0:T(512)(128)(2,1)S(1)} %copy-done.120), channel_id=1, replica_groups=mesh['dp'=16,'tensor'=8] {'dp'}, use_global_device_ids=true, to_apply=%region_94.95 | all-reduce | flops 384 | bytes 1536 | tf_op jit(solution)/shard_map/psum | solution.py:198
  509.4 14.3 %all-reduce.11.cloned.1.call-done = (bf16[768,384]{1,0:T(8,128)(2,1)}, bf16[384,768]{1,0:T(8,128)(2,1)}) async-done(((bf16[768,384]{1,0:T(8,128)(2,1)}, bf16[384,768]{1,0:T(8,128)(2,1)}), (bf16[768,384]{1,0:T(8,128)(2,1)}, bf16[384,768]{1,0:T(8,128)(2,1)})) %all-reduce.11.cloned.1.call-update) | async-done | bytes 1179664 | tf_op jit(solution)/shard_map/psum | solution.py:196
  523.7 2.2 convert_element_type.548
  525.9 2.2 convert_element_type.551
  528.0 68.4 %all-reduce.3 = (f32[768]{0:T(1024)}, f32[768]{0:T(1024)}, f32[768]{0:T(1024)}, f32[768]{0:T(1024)}, f32[768]{0:T(1024)}, /*index=5*/f32[768]{0:T(1024)}, f32[768]{0:T(1024)}) all-reduce(f32[768]{0:T(1024)S(1)} %get-tuple-element.290, f32[768]{0:T(1024)S(1)} %copy-done.37, ...), channel_id=1, replica_groups=mesh['dp'=16,'tensor'=8] {'dp','tensor'}, use_global_device_ids=true, to_apply=%region_18.19 | all-reduce | flops 5376 | bytes 43008 | tf_op jit(solution)/shard_map/psum | solution.py:211
  597.9 89.3 %all-reduce.9.cloned.1.call-done = (f32[768,768]{0,1:T(8,128)}, f32[65,768]{1,0:T(8,128)}, f32[768,768]{1,0:T(8,128)}) async-done(((f32[768,768]{0,1:T(8,128)}, f32[65,768]{1,0:T(8,128)}, f32[768,768]{1,0:T(8,128)}), (f32[768,768]{0,1:T(8,128)}, f32[65,768]{1,0:T(8,128)}, f32[768,768]{1,0:T(8,128)})) %all-reduce.9.cloned.1.call-update) | async-done | bytes 4918288 | tf_op jit(solution)/shard_map/psum | solution.py:211
  687.1 3.1 copy.54
  690.9 3.2 copy.70
  (389 shorter events, 60.3 us)
Async XLA Ops:
  7.2 53.3 %copy-start = (bf16[768,768]{1,0:T(8,128)(2,1)S(1)}, bf16[768,768]{1,0:T(8,128)(2,1)}, u32[]{:S(2)}) copy-start(bf16[768,768]{1,0:T(8,128)(2,1)} %param.22) | copy-start | bytes 3538948
  7.2 142.2 %all-gather.3.cloned.1.call-start = ((), (), s32[]{:S(2)}) async-start(), calls=%async_computation.2 | async-start | bytes 3538944 | tf_op jit(solution)/shard_map/all_gather | solution.py:152
  17.3 43.1 %copy-start.119 = (s32[256]{0:T(256)S(1)}, s32[256]{0:T(256)}, u32[]{:S(2)}) copy-start(s32[256]{0:T(256)} %param.37) | copy-start | bytes 3076
  17.3 43.1 %copy-start.116 = (bf16[768]{0:T(1024)(128)(2,1)S(1)}, bf16[768]{0:T(1024)(128)(2,1)}, u32[]{:S(2)}) copy-start(bf16[768]{0:T(1024)(128)(2,1)} %param.23) | copy-start | bytes 4612
  17.3 43.1 %copy-start.6 = (bf16[256,768]{1,0:T(8,128)(2,1)S(1)}, bf16[256,768]{1,0:T(8,128)(2,1)}, u32[]{:S(2)}) copy-start(bf16[256,768]{1,0:T(8,128)(2,1)} %param.21) | copy-start | bytes 1179652
  83.6 158.7 %reduce-scatter.3.cloned.1.call-start = ((), (), s32[]{:S(2)}) async-start(), calls=%async_computation.3 | async-start | bytes 3538944 | tf_op jit(solution)/shard_map/reduce_scatter | solution.py:156
  165.6 146.2 %all-gather.5.cloned.1.call-start = ((), (), s32[]{:S(2)}) async-start(), calls=%async_computation.4 | async-start | bytes 3538944 | tf_op jit(solution)/shard_map/all_gather | solution.py:168
  249.3 151.2 %reduce-scatter.5.cloned.1.call-start = ((), (), s32[]{:S(2)}) async-start(), calls=%async_computation.5 | async-start | bytes 3538944 | tf_op jit(solution)/shard_map/reduce_scatter | solution.py:174
  323.9 199.8 %all-reduce.11.cloned.1.call-start = ((), (), s32[]{:S(2)}) async-start(), calls=%async_computation.7 | async-start | bytes 2359296 | tf_op jit(solution)/shard_map/psum | solution.py:196
  331.4 355.8 %all-reduce.9.cloned.1.call-start = ((), (), s32[]{:S(2)}) async-start(), calls=%async_computation.6 | async-start | bytes 9879552 | tf_op jit(solution)/shard_map/psum | solution.py:211
  437.2 20.9 %copy-start.66 = (f32[768]{0:T(1024)S(1)}, f32[768]{0:T(1024)}, u32[]{:S(2)}) copy-start(f32[768]{0:T(1024)} %get-tuple-element.138) | copy-start | bytes 9220
  437.2 21.0 %copy-start.65 = (f32[768]{0:T(1024)S(1)}, f32[768]{0:T(1024)}, u32[]{:S(2)}) copy-start(f32[768]{0:T(1024)} %get-tuple-element.137) | copy-start | bytes 9220
  437.2 21.0 %copy-start.64 = (f32[768]{0:T(1024)S(1)}, f32[768]{0:T(1024)}, u32[]{:S(2)}) copy-start(f32[768]{0:T(1024)} %get-tuple-element.136) | copy-start | bytes 9220
  437.2 21.0 %copy-start.63 = (f32[768]{0:T(1024)S(1)}, f32[768]{0:T(1024)}, u32[]{:S(2)}) copy-start(f32[768]{0:T(1024)} %get-tuple-element.135) | copy-start | bytes 9220
  437.2 21.0 %copy-start.62 = (f32[768]{0:T(1024)S(1)}, f32[768]{0:T(1024)}, u32[]{:S(2)}) copy-start(f32[768]{0:T(1024)} %get-tuple-element.134) | copy-start | bytes 9220
  437.2 21.0 %copy-start.61 = (f32[768]{0:T(1024)S(1)}, f32[768]{0:T(1024)}, u32[]{:S(2)}) copy-start(f32[768]{0:T(1024)} %get-tuple-element.133) | copy-start | bytes 9220
  437.3 21.0 %copy-start.60 = (f32[768]{0:T(1024)S(1)}, f32[768]{0:T(1024)}, u32[]{:S(2)}) copy-start(f32[768]{0:T(1024)} %get-tuple-element.132) | copy-start | bytes 9220
  437.3 21.0 %copy-start.59 = (f32[768]{0:T(1024)S(1)}, f32[768]{0:T(1024)}, u32[]{:S(2)}) copy-start(f32[768]{0:T(1024)} %get-tuple-element.131) | copy-start | bytes 9220
  437.3 21.0 %copy-start.58 = (f32[768]{0:T(1024)S(1)}, f32[768]{0:T(1024)}, u32[]{:S(2)}) copy-start(f32[768]{0:T(1024)} %get-tuple-element.130) | copy-start | bytes 9220
  437.3 21.1 %copy-start.57 = (f32[768]{0:T(1024)S(1)}, f32[768]{0:T(1024)}, u32[]{:S(2)}) copy-start(f32[768]{0:T(1024)} %get-tuple-element.129) | copy-start | bytes 9220
  437.3 21.1 %copy-start.56 = (f32[768]{0:T(1024)S(1)}, f32[768]{0:T(1024)}, u32[]{:S(2)}) copy-start(f32[768]{0:T(1024)} %get-tuple-element.128) | copy-start | bytes 9220
  437.3 21.1 %copy-start.55 = (f32[768]{0:T(1024)S(1)}, f32[768]{0:T(1024)}, u32[]{:S(2)}) copy-start(f32[768]{0:T(1024)} %get-tuple-element.163) | copy-start | bytes 9220
  437.3 21.1 %copy-start.54 = (f32[768]{0:T(1024)S(1)}, f32[768]{0:T(1024)}, u32[]{:S(2)}) copy-start(f32[768]{0:T(1024)} %get-tuple-element.162) | copy-start | bytes 9220
  437.3 21.1 %copy-start.53 = (f32[768]{0:T(1024)S(1)}, f32[768]{0:T(1024)}, u32[]{:S(2)}) copy-start(f32[768]{0:T(1024)} %get-tuple-element.161) | copy-start | bytes 9220
  437.3 21.1 %copy-start.52 = (f32[768]{0:T(1024)S(1)}, f32[768]{0:T(1024)}, u32[]{:S(2)}) copy-start(f32[768]{0:T(1024)} %get-tuple-element.160) | copy-start | bytes 9220
  437.3 21.1 %copy-start.51 = (f32[768]{0:T(1024)S(1)}, f32[768]{0:T(1024)}, u32[]{:S(2)}) copy-start(f32[768]{0:T(1024)} %get-tuple-element.159) | copy-start | bytes 9220
  437.4 21.1 %copy-start.50 = (f32[768]{0:T(1024)S(1)}, f32[768]{0:T(1024)}, u32[]{:S(2)}) copy-start(f32[768]{0:T(1024)} %get-tuple-element.158) | copy-start | bytes 9220
  437.4 21.2 %copy-start.49 = (f32[768]{0:T(1024)S(1)}, f32[768]{0:T(1024)}, u32[]{:S(2)}) copy-start(f32[768]{0:T(1024)} %get-tuple-element.157) | copy-start | bytes 9220
  437.4 21.2 %copy-start.48 = (f32[768]{0:T(1024)S(1)}, f32[768]{0:T(1024)}, u32[]{:S(2)}) copy-start(f32[768]{0:T(1024)} %get-tuple-element.156) | copy-start | bytes 9220
  437.4 21.2 %copy-start.47 = (f32[768]{0:T(1024)S(1)}, f32[768]{0:T(1024)}, u32[]{:S(2)}) copy-start(f32[768]{0:T(1024)} %get-tuple-element.155) | copy-start | bytes 9220
  437.4 21.2 %copy-start.46 = (f32[768]{0:T(1024)S(1)}, f32[768]{0:T(1024)}, u32[]{:S(2)}) copy-start(f32[768]{0:T(1024)} %get-tuple-element.190) | copy-start | bytes 9220
  437.4 21.2 %copy-start.45 = (f32[768]{0:T(1024)S(1)}, f32[768]{0:T(1024)}, u32[]{:S(2)}) copy-start(f32[768]{0:T(1024)} %get-tuple-element.189) | copy-start | bytes 9220
  437.4 21.2 %copy-start.44 = (f32[768]{0:T(1024)S(1)}, f32[768]{0:T(1024)}, u32[]{:S(2)}) copy-start(f32[768]{0:T(1024)} %get-tuple-element.188) | copy-start | bytes 9220
  437.4 21.2 %copy-start.43 = (f32[768]{0:T(1024)S(1)}, f32[768]{0:T(1024)}, u32[]{:S(2)}) copy-start(f32[768]{0:T(1024)} %get-tuple-element.187) | copy-start | bytes 9220
  437.4 21.2 %copy-start.42 = (f32[768]{0:T(1024)S(1)}, f32[768]{0:T(1024)}, u32[]{:S(2)}) copy-start(f32[768]{0:T(1024)} %get-tuple-element.186) | copy-start | bytes 9220
  437.4 21.2 %copy-start.41 = (f32[768]{0:T(1024)S(1)}, f32[768]{0:T(1024)}, u32[]{:S(2)}) copy-start(f32[768]{0:T(1024)} %get-tuple-element.185) | copy-start | bytes 9220
  437.5 21.3 %copy-start.40 = (f32[768]{0:T(1024)S(1)}, f32[768]{0:T(1024)}, u32[]{:S(2)}) copy-start(f32[768]{0:T(1024)} %get-tuple-element.184) | copy-start | bytes 9220
  437.5 21.3 %copy-start.39 = (f32[768]{0:T(1024)S(1)}, f32[768]{0:T(1024)}, u32[]{:S(2)}) copy-start(f32[768]{0:T(1024)} %get-tuple-element.183) | copy-start | bytes 9220
  437.5 21.3 %copy-start.38 = (f32[768]{0:T(1024)S(1)}, f32[768]{0:T(1024)}, u32[]{:S(2)}) copy-start(f32[768]{0:T(1024)} %get-tuple-element.182) | copy-start | bytes 9220
  438.8 38.8 %copy-start.7 = (bf16[256,768]{1,0:T(8,128)(2,1)S(1)}, bf16[256,768]{1,0:T(8,128)(2,1)}, u32[]{:S(2)}) copy-start(bf16[256,768]{1,0:T(8,128)(2,1)} %param.21) | copy-start | bytes 1179652
  479.6 48.4 %copy-start.32 = (f32[768]{0:T(1024)S(1)}, f32[768]{0:T(1024)}, u32[]{:S(2)}) copy-start(f32[768]{0:T(1024)} %get-tuple-element.193) | copy-start | bytes 9220
  479.6 48.4 %copy-start.33 = (f32[768]{0:T(1024)S(1)}, f32[768]{0:T(1024)}, u32[]{:S(2)}) copy-start(f32[768]{0:T(1024)} %get-tuple-element.196) | copy-start | bytes 9220
  479.6 48.4 %copy-start.34 = (f32[768]{0:T(1024)S(1)}, f32[768]{0:T(1024)}, u32[]{:S(2)}) copy-start(f32[768]{0:T(1024)} %get-tuple-element.286) | copy-start | bytes 9220
  479.6 48.4 %copy-start.35 = (f32[768]{0:T(1024)S(1)}, f32[768]{0:T(1024)}, u32[]{:S(2)}) copy-start(f32[768]{0:T(1024)} %get-tuple-element.126) | copy-start | bytes 9220
  479.6 48.4 %copy-start.36 = (f32[768]{0:T(1024)S(1)}, f32[768]{0:T(1024)}, u32[]{:S(2)}) copy-start(f32[768]{0:T(1024)} %get-tuple-element.195) | copy-start | bytes 9220
  479.6 48.4 %copy-start.37 = (f32[768]{0:T(1024)S(1)}, f32[768]{0:T(1024)}, u32[]{:S(2)}) copy-start(f32[768]{0:T(1024)} %get-tuple-element.288) | copy-start | bytes 9220
  479.6 116.9 %copy-start.3 = (f32[256,768]{1,0:T(8,128)S(1)}, f32[256,768]{1,0:T(8,128)}, u32[]{:S(2)}) copy-start(f32[256,768]{1,0:T(8,128)} %copy-done.2) | copy-start | bytes 2359300
  479.6 116.9 %copy-start.115 = (f32[256]{0:T(256)S(1)}, f32[256]{0:T(256)}, u32[]{:S(2)}) copy-start(f32[256]{0:T(256)} %copy-done.114) | copy-start | bytes 3076
  (82 other events, 863.3 us)
Sparse Core Ops, SparseCore 0:
  83.7 65.6 all-gather.2
  165.7 76.4 reduce-scatter.2
  249.4 62.3 all-gather.4
  324.0 76.4 reduce-scatter.4
  403.5 120.2 all-reduce.10
  529.7 157.4 all-reduce.8
where the time goes:
time: 710 us; the launch traced here: 701 us
  waiting for transfers between devices  372 us (52%)
  blocking collectives  97 us (14%)
  matrix products  88.4 us (12%)
  other arithmetic  78.7 us (11%)
  local copies, waits for them, and re-layouts  48.2 us (7%)
  between operations  16.2 us (2%)
    psum x1, waiting for transfers between devices, body(): lax.psum((grad_w_value, grad_b_value, grad_kernel, grad_w_out, grad_b_out...  89.3 us
    reduce_scatter x1, waiting for transfers between devices, body(): lax.psum_scatter(jnp.dot(active, w_down, preferred_element_type=jnp.float...  72.7 us
    reduce_scatter x1, waiting for transfers between devices, body(): lax.psum_scatter(dot_last(upper_grad, w_up).astype(jnp.bfloat16), 'tensor...  69.1 us
    psum x1, blocking collectives, body(): lax.psum((grad_w_value, grad_b_value, grad_kernel, grad_w_out, grad_b_out...  68.4 us
    all_gather x1, waiting for transfers between devices, body(): gathered = lax.all_gather(first_low, 'tensor', axis=0, tiled=True)  64.2 us
    all_gather x1, waiting for transfers between devices, body(): grad_rows_all = lax.all_gather(branch_grad, 'tensor', axis=0, tiled=True)  62.5 us
    dot_general x16, matrix products, dot_last(): lax.dot_general(former, latter, (((1,), (1,)), ((), ())), preferred_eleme...  56.4 us
    psum x1, blocking collectives, body(): lax.psum(grad_b_up.astype(jnp.bfloat16), 'dp').astype(jnp.float32)  28.6 us
  transfers between devices with their start and end apart: 6, of which 6 were waited for; matrix products, arithmetic and copies ran while one was open for 14% of the time, Pallas kernels for 0%

commit v1 on v0

v1 whole, which is shorter than its diff:
```python
import math

import jax
import jax.numpy as jnp
from jax import lax
from jax.experimental import pallas as pl
from jax.experimental.pallas import tpu as pltpu
from jax.sharding import PartitionSpec as P

HEADS = 12
SETS = 32
ROWS = 256
WIDTH = 768
HEAD_DIM = 64
COLS = WIDTH // 128
TAPS = 65
MARGIN = 32
DFT_LEN = 384
FREQ = 256
LIVE_FREQ = DFT_LEN // 2 + 1
PIECE = 24
UNITS = 3 * COLS + 1
TALL = 848
TALL_TILES = TALL // 8
PACK = 640
ALL = ("dp", "tensor")

bf16 = jnp.bfloat16
f32 = jnp.float32
i32 = jnp.int32

VMEM = pl.BlockSpec(memory_space=pltpu.VMEM)
SMEM = pl.BlockSpec(memory_space=pltpu.SMEM)


def shape(dims, dtype):
    return jax.ShapeDtypeStruct(dims, dtype)


def params(mib):
    return pltpu.CompilerParams(vmem_limit_bytes=mib << 20)


def dot(a, b):
    return lax.dot_general(a, b, (((1,), (0,)), ((), ())), preferred_element_type=f32)


def dot_last(a, b):
    return lax.dot_general(a, b, (((1,), (1,)), ((), ())), preferred_element_type=f32)


def dot_first(a, b):
    return lax.dot_general(a, b, (((0,), (0,)), ((), ())), preferred_element_type=f32)


def lanes(dims):
    return lax.broadcasted_iota(i32, dims, len(dims) - 1)


def norm_rows(r):
    mean = jnp.mean(r, axis=-1, keepdims=True)
    centred = r - mean
    inv = lax.rsqrt(jnp.mean(centred * centred, axis=-1, keepdims=True) + 1e-05)
    return centred * inv, inv


def norm_back(g, n, inv, gain):
    e = g * gain
    return (
        e - jnp.mean(e, axis=-1, keepdims=True) - n * jnp.mean(e * n, axis=-1, keepdims=True)
    ) * inv


def prep_kernel(place, up_ref, down_ref, bias_ref, out_ref, tall, cols, piece):
    rep = place[0] % 8

    @pl.when(pl.program_id(0) == 0)
    def _():
        @pl.when(place[0] < 8)
        def _():
            tall[...] = up_ref[...].astype(f32).T
            cols[...] = jnp.broadcast_to(bias_ref[...].astype(f32), (8, 384)).T

        @pl.when(place[0] >= 8)
        def _():
            tall[...] = down_ref[...].astype(f32)
            cols[...] = jnp.zeros(cols.shape, f32)

        for c in range(2):
            start = pl.multiple_of(192 * c + PIECE * rep, 8)
            rows = tall[pl.ds(start, PIECE), :]
            for ct in range(COLS):
                part = rows[:, ct * 128 : ct * 128 + 128].reshape(3, 8, 128)
                piece[c, 3 * ct : 3 * ct + 3] = part.astype(bf16)
            bias = jnp.zeros((8, 128), f32)
            for rt in range(3):
                col = cols[pl.ds(pl.multiple_of(start + 8 * rt, 8), 8), :][:, 0:1]
                bias = jnp.where(lanes((8, 128)) == rt, jnp.broadcast_to(col, (8, 128)), bias)
            piece[c, UNITS - 1] = bias.astype(bf16)

    for s in range(16):
        out_ref[s] = piece[s // 8]


def prep(place, w_up, w_down, b_up):
    whole = lambda *dims: pl.BlockSpec(dims, lambda i: (0,) * len(dims))
    return pl.pallas_call(
        prep_kernel,
        grid=(8,),
        out_shape=shape((128, UNITS, 8, 128), bf16),
        in_specs=[SMEM, whole(768, 384), whole(384, 768), whole(1, 384)],
        out_specs=pl.BlockSpec((16, UNITS, 8, 128), lambda i: (i, 0, 0, 0)),
        scratch_shapes=[
            pltpu.VMEM((384, 768), f32),
            pltpu.VMEM((384, 8), f32),
            pltpu.VMEM((2, UNITS, 8, 128), bf16),
        ],
        compiler_params=params(32),
        name="prep",
    )(place, w_up, w_down, b_up)


def segment_ends(len_ref):
    e0 = len_ref[0, 0]
    e1 = e0 + len_ref[0, 1]
    return e0, e1, e1 + len_ref[0, 2]


def segment_of(p, ends):
    return sum((p >= e).astype(i32) for e in ends)


def turn(product):
    r = product.astype(f32) * (1.0 / DFT_LEN)
    m = product - DFT_LEN * jnp.round(r).astype(i32)
    x = m.astype(f32) * (2.0 * math.pi / DFT_LEN)
    z = x * x
    c = 1.0
    s = 1.0
    for k in range(8, 0, -1):
        c = 1.0 - z * c * (1.0 / ((2 * k - 1) * (2 * k)))
        s = 1.0 - z * s * (1.0 / ((2 * k) * (2 * k + 1)))
    return c, x * s


def attend_kernel(
    len_ref, x_ref, wv_ref, bv_ref, taps_ref, wo_ref, bo_ref, ga_ref, sa_ref, q_ref, k_ref, live_ref,
    n_ref, inv_ref, low_ref, ctx_ref, col_ref, nrm_ref, scl_ref, wave_ref, wavet_ref, ks_ref, vs_ref,
    tapt_ref, live_out, qw, kb, jn, tapbuf, mix, mskd,
):
    ends = segment_ends(len_ref)
    square = (ROWS, ROWS)
    rows_i = lax.broadcasted_iota(i32, square, 0)
    lanes_i = lax.broadcasted_iota(i32, square, 1)
    jn[...] = jnp.where(segment_of(rows_i, ends) == segment_of(lanes_i, ends), 1.0 / SETS, 0.0)
    d = lax.broadcasted_iota(i32, (384, 128), 0) - 4 * lax.broadcasted_iota(i32, (384, 128), 1)
    w_lo = jnp.where(d == 0, 1.0, jnp.where(d == 1, 256.0, 0.0)).astype(bf16)
    w_hi = jnp.where(d == 2, 1.0, jnp.where(d == 3, 256.0, 0.0)).astype(bf16)
    q_codes = q_ref[...].astype(f32).astype(bf16)
    k_codes = k_ref[...].astype(f32).astype(bf16)
    qw[...] = dot(q_codes, w_lo).astype(i32) | (dot(q_codes, w_hi).astype(i32) << 16)
    kw = dot(k_codes, w_lo).T.astype(i32) | (dot(k_codes, w_hi).T.astype(i32) << 16)
    for r in range(96):
        for j in range(2):
            kb[r, j] = jnp.broadcast_to(kw[r : r + 1, j * 128 : j * 128 + 128], (8, 128))
    low7 = jnp.int32(0x7F7F7F7F)
    ones = jnp.int32(0x01010101)
    byte2 = jnp.int32(0x00FF00FF)
    tile_rows = 32
    groups = tile_rows // 8

    def tile(rt, carry):
        rs = pl.ds(pl.multiple_of(rt * tile_rows, tile_rows), tile_rows)
        qt = qw[rs, :]
        for h in range(HEADS):
            acc = [[jnp.zeros((8, 128), i32) for _ in range(2)] for _ in range(groups)]
            for g in range(8):
                c = h * 8 + g
                qc = [
                    jnp.broadcast_to(qt[t * 8 : t * 8 + 8, c : c + 1], (8, 128))
                    for t in range(groups)
                ]
                for j in range(2):
                    kk = kb[c, j]
                    for t in range(groups):
                        x = qc[t] ^ kk
                        y = ((x & low7) + low7) | x
                        acc[t][j] = acc[t][j] + (lax.shift_right_logical(y, 7) & ones)
            for j in range(2):
                parts = []
                for t in range(groups):
                    z = acc[t][j]
                    z = (z & byte2) + (lax.shift_right_logical(z, 8) & byte2)
                    z = (z & jnp.int32(0xFFFF)) + lax.shift_right_logical(z, 16)
                    parts.append((SETS - z).astype(f32))
                m = jnp.concatenate(parts, axis=0) * jn[rs, j * 128 : j * 128 + 128]
                col_ref[h, rs, j * 128 : j * 128 + 128] = m.astype(bf16)
        return carry

    lax.fori_loop(0, ROWS // tile_rows, tile, 0)

    dims = (FREQ, ROWS)
    f = lax.broadcasted_iota(i32, dims, 0)
    p = lax.broadcasted_iota(i32, dims, 1)
    c, s = turn(f * (p + MARGIN * segment_of(p, ends)))
    ok = f < LIVE_FREQ
    wave_ref[0:FREQ] = jnp.where(ok, c, 0.0).astype(bf16)
    wave_ref[FREQ:] = jnp.where(ok, s, 0.0).astype(bf16)
    p = lax.broadcasted_iota(i32, dims, 0)
    f = lax.broadcasted_iota(i32, dims, 1)
    c, s = turn(f * (p + MARGIN * segment_of(p, ends)))
    ok = f < LIVE_FREQ
    wavet_ref[:, 0:FREQ] = jnp.where(ok, c, 0.0).astype(bf16)
    wavet_ref[:, FREQ:] = jnp.where(ok, s, 0.0).astype(bf16)
    dims = (FREQ, 128)
    f = lax.broadcasted_iota(i32, dims, 0)
    c, s = turn(f * (lax.broadcasted_iota(i32, dims, 1) - MARGIN))
    tap_c = c.astype(bf16)
    tap_s = s.astype(bf16)
    dims = (128, FREQ)
    f = lax.broadcasted_iota(i32, dims, 1)
    c, s = turn(f * (lax.broadcasted_iota(i32, dims, 0) - MARGIN))
    tapt_ref[:, 0:FREQ] = c.astype(bf16)
    tapt_ref[:, FREQ:] = s.astype(bf16)
    tapbuf[...] = jnp.zeros(tapbuf.shape, f32)
    tapbuf[0:TAPS] = taps_ref[...].astype(f32)
    kernel = tapbuf[...].astype(bf16)
    f = lax.broadcasted_iota(i32, (FREQ, 1), 0)
    weight = jnp.where((f == 0) | (f == DFT_LEN // 2), 1.0 / DFT_LEN, 2.0 / DFT_LEN)
    weight = jnp.where(f < LIVE_FREQ, weight, 0.0)
    k_cos = dot(tap_c, kernel) * weight
    k_sin = dot(tap_s, kernel) * weight
    ks_ref[0:FREQ] = k_cos
    ks_ref[FREQ:] = k_sin

    live = jnp.broadcast_to(live_ref[...].astype(f32), (8, ROWS)).T[:, 0:1]
    live_out[...] = jnp.broadcast_to(live, (ROWS, 128))
    values = (dot(x_ref[...], wv_ref[...]) + bv_ref[...].astype(f32)).astype(bf16).astype(f32)
    mskd[...] = (values * live).astype(bf16)
    masked = mskd[...]
    spec = dot(wave_ref[...], masked)
    vs_ref[...] = spec.astype(bf16)
    v_cos = spec[0:FREQ]
    v_sin = spec[FREQ:]
    first_head = lanes((ROWS, 128)) < HEAD_DIM
    y_cos = (k_cos * v_cos + k_sin * v_sin).astype(bf16)
    y_sin = (k_cos * v_sin - k_sin * v_cos).astype(bf16)
    conv = dot(wavet_ref[:, 0:FREQ], y_cos) + dot(wavet_ref[:, FREQ:], y_sin)
    for b in range(COLS):
        cs = slice(b * 128, b * 128 + 128)
        block = masked[:, cs]
        m = jnp.where(first_head, dot(col_ref[2 * b], block), dot(col_ref[2 * b + 1], block))
        sq = m * m
        one = jnp.sum(jnp.where(first_head, sq, 0.0), axis=1, keepdims=True)
        two = jnp.sum(jnp.where(first_head, 0.0, sq), axis=1, keepdims=True)
        scale = lax.rsqrt(jnp.where(first_head, one, two) * (1.0 / HEAD_DIM) + 1e-06)
        scl_ref[:, cs] = scale
        nrm = m * scale
        nrm_ref[:, cs] = nrm.astype(bf16)
        mix[:, cs] = nrm
    context = (mix[...] + conv).astype(bf16)
    ctx_ref[...] = context
    attended = dot(context, wo_ref[...]) + bo_ref[...].astype(f32)
    n, inv = norm_rows(x_ref[...].astype(f32) + attended)
    n_ref[...] = n
    inv_ref[...] = jnp.broadcast_to(inv, (ROWS, 128))
    low_ref[...] = (n * ga_ref[...].astype(f32) + sa_ref[...].astype(f32)).astype(bf16)


def attend(seq_lengths, x, wv, bv, taps, wo, bo, ga, sa, q, k, live):
    wide = (ROWS, WIDTH)
    return pl.pallas_call(
        attend_kernel,
        out_shape=(
            shape(wide, f32), shape((ROWS, 128), f32), shape(wide, bf16), shape(wide, bf16),
            shape((HEADS, ROWS, ROWS), bf16), shape(wide, bf16), shape(wide, f32),
            shape((2 * FREQ, ROWS), bf16), shape((ROWS, 2 * FREQ), bf16),
            shape((2 * FREQ, WIDTH), f32), shape((2 * FREQ, WIDTH), bf16),
            shape((128, 2 * FREQ), bf16), shape((ROWS, 128), f32),
        ),
        in_specs=[SMEM] + [VMEM] * 11,
        out_specs=(VMEM,) * 13,
        scratch_shapes=[
            pltpu.VMEM((ROWS, 128), i32),
            pltpu.VMEM((96, 2, 8, 128), i32),
            pltpu.VMEM((ROWS, ROWS), f32),
            pltpu.VMEM((128, WIDTH), f32),
            pltpu.VMEM(wide, f32),
            pltpu.VMEM(wide, bf16),
        ],
        compiler_params=params(48),
        name="attend",
    )(seq_lengths, x, wv, bv, taps, wo, bo, ga, sa, q, k, live)


def untile(ref, first):
    part = ref[:, first : first + 3].astype(f32)
    return part.reshape(-1, 128).astype(bf16)


def load_up(ref, out):
    for ct in range(COLS):
        out[:, ct * 128 : ct * 128 + 128] = untile(ref, 3 * ct)
    tile = ref[:, UNITS - 1].astype(f32)
    lane = lanes(tile.shape)
    parts = [jnp.where(lane == rt, tile, 0.0)[:, None] for rt in range(3)]
    out[:, WIDTH:] = jnp.concatenate(parts, axis=1).reshape(-1, 128).astype(bf16)


def load_down(ref, out):
    for ct in range(COLS):
        out[:, ct * 128 : ct * 128 + 128] = untile(ref, 3 * ct)


def ffn_kernel(own, sib, up, down, act, slope, part_own, part_sib, rows, wu, wd, acc):
    step = pl.program_id(0)

    @pl.when(step == 0)
    def _():
        rows[0:ROWS, 0:WIDTH] = own[...]
        rows[ROWS:, 0:WIDTH] = sib[...]
        rows[:, WIDTH:] = jnp.where(lanes((2 * ROWS, 128)) < 3, 1.0, 0.0).astype(bf16)
        acc[...] = jnp.zeros(acc.shape, f32)

    load_up(up, wu)
    load_down(down, wd)

    def block(i, carry):
        hs = pl.ds(pl.multiple_of(i * 256, 256), 256)
        upper = dot_last(rows[...], wu[hs, :])
        cdf = 0.5 * (1.0 + lax.erf(upper * math.sqrt(0.5)))
        a = (upper * cdf).astype(bf16)
        act[i] = a
        density = jnp.exp(-0.5 * upper * upper) * (1.0 / math.sqrt(2.0 * math.pi))
        slope[i] = (cdf + upper * density).astype(bf16)
        acc[...] += dot(a, wd[hs, :])
        return carry

    lax.fori_loop(0, 3, block, 0)

    @pl.when(step == 1)
    def _():
        part_own[...] = acc[0:ROWS]
        part_sib[...] = acc[ROWS:].astype(bf16)


def ffn(own, sib, weights):
    wide = (ROWS, WIDTH)
    whole = lambda *dims: pl.BlockSpec(dims, lambda b: (0,) * len(dims))
    piece = (32, UNITS, 8, 128)
    hidden = (3, 2 * ROWS, 256)
    return pl.pallas_call(
        ffn_kernel,
        grid=(2,),
        out_shape=(
            shape((6, 2 * ROWS, 256), bf16), shape((6, 2 * ROWS, 256), bf16),
            shape(wide, f32), shape(wide, bf16),
        ),
        in_specs=[
            whole(*wide), whole(*wide),
            pl.BlockSpec(piece, lambda b: (b, 0, 0, 0)),
            pl.BlockSpec(piece, lambda b: (2 + b, 0, 0, 0)),
        ],
        out_specs=(
            pl.BlockSpec(hidden, lambda b: (b, 0, 0)), pl.BlockSpec(hidden, lambda b: (b, 0, 0)),
            whole(*wide), whole(*wide),
        ),
        scratch_shapes=[
            pltpu.VMEM((2 * ROWS, WIDTH + 128), bf16),
            pltpu.VMEM((768, WIDTH + 128), bf16),
            pltpu.VMEM((768, WIDTH), bf16),
            pltpu.VMEM((2 * ROWS, WIDTH), f32),
        ],
        compiler_params=params(48),
        name="ffn",
    )(own, sib, weights, weights)


def middle_kernel(n1, own, got, bd, ga, sa, gf, sf, og, out, second, low, sums):
    first = n1[...] * ga[...].astype(f32) + sa[...].astype(f32)
    n, inv = norm_rows(first + own[...] + got[...].astype(f32) + bd[...].astype(f32))
    gain = gf[...].astype(f32)
    out[...] = (n * gain + sf[...].astype(f32)).astype(bf16)
    g = og[...].astype(f32)
    grad = norm_back(g, n, inv, gain)
    second[...] = grad
    grad_low = grad.astype(bf16)
    low[...] = grad_low
    sums[0:1] = jnp.sum(grad_low.astype(f32), axis=0, keepdims=True)
    sums[1:2] = jnp.sum(g * n, axis=0, keepdims=True)
    sums[2:3] = jnp.sum(g, axis=0, keepdims=True)
    sums[3:8] = jnp.zeros((5, WIDTH), f32)


def middle(*args):
    wide = (ROWS, WIDTH)
    return pl.pallas_call(
        middle_kernel,
        out_shape=(shape(wide, bf16), shape(wide, f32), shape(wide, bf16), shape((8, WIDTH), f32)),
        in_specs=[VMEM] * 9,
        out_specs=(VMEM,) * 4,
        compiler_params=params(32),
        name="middle",
    )(*args)


def ffn_back_kernel(
    own, sib, r_own, r_sib, up, down, act, slope, grads, first_own, first_sib, rows, g, wu, wd, acc,
    gu, gd,
):
    step = pl.program_id(0)

    @pl.when(step == 0)
    def _():
        g[0:ROWS] = own[...]
        g[ROWS:] = sib[...]
        rows[0:ROWS, 0:WIDTH] = r_own[...]
        rows[ROWS:, 0:WIDTH] = r_sib[...]
        rows[:, WIDTH:] = jnp.ones((2 * ROWS, 128), bf16)
        acc[...] = jnp.zeros(acc.shape, f32)

    load_up(up, wu)
    load_down(down, wd)

    def block(i, carry):
        hs = pl.ds(pl.multiple_of(i * 256, 256), 256)
        u = (dot_last(g[...], wd[hs, :]) * slope[i].astype(f32)).astype(bf16)
        gd[hs, :] = dot_first(act[i], g[...])
        gu[hs, :] = dot_first(u, rows[...])
        acc[...] += dot(u, wu[hs, 0:WIDTH])
        return carry

    lax.fori_loop(0, 3, block, 0)
    for ct in range(COLS):
        cs = slice(ct * 128, ct * 128 + 128)
        grads[0, :, 3 * ct : 3 * ct + 3] = gu[:, cs].reshape(32, 3, 8, 128).astype(bf16)
        grads[1, :, 3 * ct : 3 * ct + 3] = gd[:, cs].reshape(32, 3, 8, 128).astype(bf16)
    bias = gu[:, WIDTH:].reshape(32, 3, 8, 128)
    lane = lanes((32, 8, 128))
    tile = jnp.where(lane == 0, bias[:, 0], jnp.where(lane == 1, bias[:, 1], bias[:, 2]))
    grads[0, :, UNITS - 1] = tile.astype(bf16)
    grads[1, :, UNITS - 1] = jnp.zeros((32, 8, 128), bf16)

    @pl.when(step == 1)
    def _():
        first_own[...] = acc[0:ROWS]
        first_sib[...] = acc[ROWS:].astype(bf16)


def ffn_back(own, sib, r_own, r_sib, weights, act, slope):
    wide = (ROWS, WIDTH)
    whole = lambda *dims: pl.BlockSpec(dims, lambda b: (0,) * len(dims))
    piece = (32, UNITS, 8, 128)
    hidden = pl.BlockSpec((3, 2 * ROWS, 256), lambda b: (b, 0, 0))
    return pl.pallas_call(
        ffn_back_kernel,
        grid=(2,),
        out_shape=(shape((2, 64, UNITS, 8, 128), bf16), shape(wide, f32), shape(wide, bf16)),
        in_specs=[
            whole(*wide), whole(*wide), whole(*wide), whole(*wide),
            pl.BlockSpec(piece, lambda b: (b, 0, 0, 0)),
            pl.BlockSpec(piece, lambda b: (2 + b, 0, 0, 0)),
            hidden, hidden,
        ],
        out_specs=(
            pl.BlockSpec((2, 32, UNITS, 8, 128), lambda b: (0, b, 0, 0, 0)),
            whole(*wide), whole(*wide),
        ),
        scratch_shapes=[
            pltpu.VMEM((2 * ROWS, WIDTH + 128), bf16),
            pltpu.VMEM((2 * ROWS, WIDTH), bf16),
            pltpu.VMEM((768, WIDTH + 128), bf16),
            pltpu.VMEM((768, WIDTH), bf16),
            pltpu.VMEM((2 * ROWS, WIDTH), f32),
            pltpu.VMEM((768, WIDTH + 128), f32),
            pltpu.VMEM((768, WIDTH), f32),
        ],
        compiler_params=params(56),
        name="ffn_back",
    )(own, sib, r_own, r_sib, weights, weights, act, slope)


def back_kernel(
    place, own, got, second, n1, inv1, ga, ctx, wo, nrm, scl, wave, wavet, ks, vs, tapt, col, live, x,
    wv, sums, in_grad, keep, give, buf_a, buf_b, mg, mb,
):
    first_grad = second[...] + own[...] + got[...].astype(f32)
    n = n1[...]
    buf_a[768 + 2 : 768 + 3] = jnp.sum(first_grad * n, axis=0, keepdims=True)
    buf_a[768 + 3 : 768 + 4] = jnp.sum(first_grad, axis=0, keepdims=True)
    resid = norm_back(first_grad, n, inv1[...][:, 0:1], ga[...].astype(f32))
    ag = resid.astype(bf16)
    buf_a[768 + 1 : 768 + 2] = jnp.sum(ag.astype(f32), axis=0, keepdims=True)
    buf_a[768 + 4 : 768 + 7] = sums[0:3]
    buf_a[768 + 7 :] = jnp.zeros((TALL - 775, WIDTH), f32)
    buf_b[0:768] = dot_first(ctx[...], ag)
    cg = dot_last(ag, wo[...])
    first_head = lanes((ROWS, 128)) < HEAD_DIM
    for b in range(COLS):
        cs = slice(b * 128, b * 128 + 128)
        c = cg[:, cs]
        m = nrm[:, cs].astype(f32)
        prod = c * m
        one = jnp.sum(jnp.where(first_head, prod, 0.0), axis=1, keepdims=True)
        two = jnp.sum(jnp.where(first_head, 0.0, prod), axis=1, keepdims=True)
        mean = jnp.where(first_head, one, two) * (1.0 / HEAD_DIM)
        mg[:, cs] = (scl[:, cs] * (c - m * mean)).astype(bf16)
    for b in range(COLS):
        cs = slice(b * 128, b * 128 + 128)
        block = mg[:, cs]
        mb[:, cs] = jnp.where(
            first_head, dot_first(col[2 * b], block), dot_first(col[2 * b + 1], block)
        )
    spec = dot(wave[...], cg.astype(bf16))
    g_cos = spec[0:FREQ]
    g_sin = spec[FREQ:]
    k_cos = ks[0:FREQ]
    k_sin = ks[FREQ:]
    z_cos = (k_cos * g_cos - k_sin * g_sin).astype(bf16)
    z_sin = (k_cos * g_sin + k_sin * g_cos).astype(bf16)
    conv = dot(wavet[:, 0:FREQ], z_cos) + dot(wavet[:, FREQ:], z_sin)
    v_cos = vs[0:FREQ].astype(f32)
    v_sin = vs[FREQ:].astype(f32)
    f = lax.broadcasted_iota(i32, (FREQ, 1), 0)
    weight = jnp.where((f == 0) | (f == DFT_LEN // 2), 1.0 / DFT_LEN, 2.0 / DFT_LEN)
    weight = jnp.where(f < LIVE_FREQ, weight, 0.0)
    re = ((g_cos * v_cos + g_sin * v_sin) * weight).astype(bf16)
    im = ((g_cos * v_sin - g_sin * v_cos) * weight).astype(bf16)
    gk = dot(tapt[:, 0:FREQ], re) + dot(tapt[:, FREQ:], im)
    buf_b[768:] = jnp.zeros((TALL - 768, WIDTH), f32)
    buf_b[768 : 768 + TAPS] = gk[0:TAPS]
    vg = ((mb[...] + conv) * live[...][:, 0:1]).astype(bf16)
    buf_a[768:769] = jnp.sum(vg.astype(f32), axis=0, keepdims=True)
    buf_a[0:768] = dot_first(x[...], vg)
    in_grad[...] = resid + dot_last(vg, wv[...])

    def write(kept, given):
        for ct in range(COLS):
            cs = slice(ct * 128, ct * 128 + 128)
            ts = slice(ct * TALL_TILES, ct * TALL_TILES + TALL_TILES)
            keep[ts] = kept[:, cs].reshape(TALL_TILES, 8, 128)
            give[ts] = given[:, cs].reshape(TALL_TILES, 8, 128).astype(bf16)

    rest = PACK - COLS * TALL_TILES
    keep[PACK - rest :] = jnp.zeros((rest, 8, 128), f32)
    give[PACK - rest :] = jnp.zeros((rest, 8, 128), bf16)

    @pl.when(place[0] % 2 == 0)
    def _():
        write(buf_a, buf_b)

    @pl.when(place[0] % 2 == 1)
    def _():
        write(buf_b, buf_a)


def attend_back(*args):
    wide = (ROWS, WIDTH)
    return pl.pallas_call(
        back_kernel,
        out_shape=(shape(wide, f32), shape((PACK, 8, 128), f32), shape((PACK, 8, 128), bf16)),
        in_specs=[SMEM] + [VMEM] * 20,
        out_specs=(VMEM,) * 3,
        scratch_shapes=[
            pltpu.VMEM((TALL, WIDTH), f32),
            pltpu.VMEM((TALL, WIDTH), f32),
            pltpu.VMEM(wide, bf16),
            pltpu.VMEM(wide, f32),
        ],
        compiler_params=params(56),
        name="attend_back",
    )(*args)


def sum_ffn_kernel(got, out, acc):
    step = pl.program_id(0)

    @pl.when(step == 0)
    def _():
        acc[...] = jnp.zeros(acc.shape, f32)

    for c in range(2):
        total = acc[c]
        for t in range(8):
            total = total + got[c * 8 + t].astype(f32)
        acc[c] = total

    @pl.when(step == 7)
    def _():
        out[...] = acc[...].astype(bf16)


def sum_ffn(got):
    return pl.pallas_call(
        sum_ffn_kernel,
        grid=(8,),
        out_shape=shape((2, UNITS, 8, 128), bf16),
        in_specs=[pl.BlockSpec((16, UNITS, 8, 128), lambda i: (i, 0, 0, 0))],
        out_specs=pl.BlockSpec((2, UNITS, 8, 128), lambda i: (0, 0, 0, 0)),
        scratch_shapes=[pltpu.VMEM((2, UNITS, 8, 128), f32)],
        compiler_params=params(32),
        name="sum_ffn",
    )(got)


def sum_rest_kernel(got, out):
    per = PACK // 128
    total = [jnp.zeros((per, 8, 128), f32) for _ in range(2)]
    for i in range(8):
        for c in range(2):
            for t in range(8):
                total[c] = total[c] + got[i * 16 + c * 8 + t].astype(f32)
    low = [t.astype(bf16) for t in total]
    for i in range(8):
        for c in range(2):
            for t in range(8):
                out[i * 16 + c * 8 + t] = low[c]


def sum_rest(got):
    return pl.pallas_call(
        sum_rest_kernel,
        out_shape=shape(got.shape, bf16),
        in_specs=[VMEM],
        out_specs=VMEM,
        compiler_params=params(32),
        name="sum_rest",
    )(got)


def final_kernel(
    place, own, other, ffn_ref, bias_ref, g_wv, g_bv, g_conv, g_wo, g_bo, g_ga, g_sa, g_up, g_bup,
    g_down, g_bd, g_gf, g_sf, vecs,
):
    ct = pl.program_id(0)

    def write(a, b):
        g_wv[...] = a[0:96].astype(f32).reshape(768, 128)
        vecs[ct] = a[96].astype(f32)
        g_wo[...] = b[0:96].astype(f32).reshape(768, 128)
        g_conv[...] = b[96:105].astype(f32).reshape(72, 128)[0:TAPS]

    @pl.when(place[0] % 2 == 0)
    def _():
        write(own, other)

    @pl.when(place[0] % 2 == 1)
    def _():
        write(other, own)

    for c in range(2):
        rs = slice(192 * c, 192 * c + 192)
        g_down[rs, :] = ffn_ref[8:16, c].astype(f32).reshape(192, 128)
        g_up[:, rs] = ffn_ref[0:8, c].astype(f32).reshape(192, 128).T

    @pl.when(ct == COLS - 1)
    def _():
        for j, ref in enumerate((g_bv, g_bo, g_ga, g_sa, g_bd, g_gf, g_sf)):
            for i in range(COLS):
                ref[i * 128 : i * 128 + 128] = vecs[i, j]
        parts = []
        for c in range(2):
            tile = bias_ref[0:8, c, 0].astype(f32)
            lane = lanes(tile.shape)
            rows = [jnp.where(lane == rt, tile, 0.0)[:, None] for rt in range(3)]
            parts.append(jnp.concatenate(rows, axis=1).reshape(192, 128))
        tall = jnp.concatenate(parts, axis=0).astype(bf16)
        g_bup[...] = dot_last(jnp.ones((8, 128), bf16), tall)[0]


def final(place, own, other, gathered):
    tile = pl.BlockSpec((TALL_TILES, 8, 128), lambda i: (i, 0, 0))
    tall = pl.BlockSpec((768, 128), lambda i: (0, i))
    vec = pl.BlockSpec((WIDTH,), lambda i: (0,))
    v = shape((WIDTH,), f32)
    return pl.pallas_call(
        final_kernel,
        grid=(COLS,),
        out_shape=(
            shape((768, 768), f32), v, shape((TAPS, 768), f32), shape((768, 768), f32), v, v, v,
            shape((768, 384), f32), shape((384,), f32), shape((384, 768), f32), v, v, v,
        ),
        in_specs=[
            SMEM, tile, tile,
            pl.BlockSpec((16, 2, 3, 8, 128), lambda i: (0, 0, i, 0, 0)),
            pl.BlockSpec((16, 2, 1, 8, 128), lambda i: (0, 0, UNITS - 1, 0, 0)),
        ],
        out_specs=(
            tall, vec, pl.BlockSpec((TAPS, 128), lambda i: (0, i)), tall, vec, vec, vec,
            pl.BlockSpec((128, 384), lambda i: (i, 0)), pl.BlockSpec((384,), lambda i: (0,)),
            pl.BlockSpec((384, 128), lambda i: (0, i)), vec, vec, vec,
        ),
        scratch_shapes=[pltpu.VMEM((COLS, 8, 128), f32)],
        compiler_params=params(32),
        name="final",
    )(place, own, other, gathered, gathered)


def body(
    block_input,
    w_value,
    b_value,
    conv_kernel,
    w_out,
    b_out,
    gain_attn,
    shift_attn,
    w_up,
    b_up,
    w_down,
    b_down,
    gain_ffn,
    shift_ffn,
    query_codes,
    key_codes,
    key_live,
    seq_lengths,
    out_grad,
):
    dp = lax.axis_index("dp")
    place = jnp.stack([dp, lax.axis_index("tensor")]).astype(i32)
    pairs = [(i, i ^ 1) for i in range(lax.axis_size("dp"))]

    def swap(x):
        return lax.ppermute(x, "dp", pairs)

    def exchange(x):
        return lax.all_to_all(x, ALL, 0, 0, tiled=True)

    def row(v):
        return v.reshape(1, -1)

    weights = exchange(prep(place, w_up, w_down, row(b_up)))
    (n1, inv1, low, ctx, collide, nrm, scl, wave, wavet, ks, vs, tapt, live) = attend(
        seq_lengths, block_input, w_value, row(b_value), conv_kernel, w_out, row(b_out),
        row(gain_attn), row(shift_attn), query_codes, key_codes, row(key_live),
    )
    low_sib = swap(low)
    act, slope, part_own, part_sib = ffn(low, low_sib, weights)
    block_output, second, grad_low, sums = middle(
        n1, part_own, swap(part_sib), row(b_down), row(gain_attn), row(shift_attn), row(gain_ffn),
        row(shift_ffn), out_grad,
    )
    grads, first_own, first_sib = ffn_back(
        grad_low, swap(grad_low), low, low_sib, weights, act, slope
    )
    owned = exchange(grads.reshape(128, UNITS, 8, 128))
    input_grad, keep, give = attend_back(
        place, first_own, swap(first_sib), second, n1, inv1, row(gain_attn), ctx, w_out, nrm, scl,
        wave, wavet, ks, vs, tapt, collide, live, block_input, w_value, sums,
    )
    pair = (keep + swap(give).astype(f32)).astype(bf16).reshape(128, PACK // 128, 8, 128)
    owned = sum_ffn(owned)
    pair, owned = lax.optimization_barrier((pair, owned))
    gathered = lax.all_gather(owned, "dp", axis=0)
    back = exchange(sum_rest(exchange(pair))).reshape(PACK, 8, 128)
    (g_wv, g_bv, g_conv, g_wo, g_bo, g_ga, g_sa, g_up, g_bup, g_down, g_bd, g_gf, g_sf) = final(
        place, back, swap(back), gathered
    )
    return (
        block_output, input_grad, g_wv, g_bv, g_conv, g_wo, g_bo, g_ga, g_sa, g_up, g_bup, g_down,
        g_bd, g_gf, g_sf,
    )


def solution(mesh):
    rows = P(ALL, None)
    return jax.shard_map(
        body,
        mesh=mesh,
        in_specs=(
            rows, P(), P(), P(), P(), P(), P(), P(),
            P(None, "tensor"), P("tensor"), P("tensor", None), P(), P(), P(),
            rows, rows, P(ALL), rows, rows,
        ),
        out_specs=(
            rows, rows, P(), P(), P(), P(), P(), P(), P(),
            P(None, "tensor"), P("tensor"), P("tensor", None), P(), P(), P(),
        ),
        check_vma=False,
    )
```

time: 710 us -> 278 us (0.39); the launches traced: 701 us -> 277 us
  waiting for transfers between devices: 372 us -> 122 us
  matrix products: 88.4 us -> 0 us
  other arithmetic: 78.7 us -> 2.15 us
  blocking collectives: 97 us -> 27.5 us
  Pallas kernels: 0 us -> 64.3 us
  local copies, waits for them, and re-layouts: 48.2 us -> 16.7 us
  starting transfers between devices: 0.5 us -> 30 us
    reduce_scatter x2 -> x0, waiting for transfers between devices: 142 us -> none  [the longest x1 72.7 us: body(): lax.psum_scatter(jnp.dot(active, w_down, preferred_element_type=jnp.float...]
    all_gather x2 -> x1, waiting for transfers between devices: 127 us -> 17 us  [body(): gathered = lax.all_gather(owned, 'dp', axis=0)]
    psum x2 -> x0, waiting for transfers between devices: 104 us -> none  [the longest x1 89.3 us: body(): lax.psum((grad_w_value, grad_b_value, grad_kernel, grad_w_out, grad_b_out...]
    psum x2 -> x0, blocking collectives: 97 us -> none  [the longest x1 68.4 us: body(): lax.psum((grad_w_value, grad_b_value, grad_kernel, grad_w_out, grad_b_out...]
    all_to_all x0 -> x3, waiting for transfers between devices: none -> 95.9 us  [exchange(): return lax.all_to_all(x, ALL, 0, 0, tiled=True)]
    dot_general x26 -> x0, matrix products: 88.4 us -> none  [the longest x16 56.4 us: dot_last(): lax.dot_general(former, latter, (((1,), (1,)), ((), ())), preferred_eleme...]
    pallas_call x0 -> x9, Pallas kernels: none -> 64.3 us  [the longest x1 14.9 us: attend(): pl.pallas_call(attend_kernel, out_shape=(shape(wide, f32), shape((ROWS, 1...]
    reduce_sum x19 -> x0, other arithmetic: 49.1 us -> none  [the longest x7 25.8 us: conv_back(): jnp.sum(grad_out * joined * padded[offset:offset + length], axis=0)]
  transfers between devices with their start and end apart: 6 -> 10, of which waited for: 6 -> 9; matrix products, arithmetic and copies ran while one was open for 14% -> 1% of each run, Pallas kernels for 0% -> 9%
where the time goes in v1:
time: 278 us; the launch traced here: 277 us
  waiting for transfers between devices  122 us (44%)
  Pallas kernels  64.3 us (23%)
  starting transfers between devices  30 us (11%)
  blocking collectives  27.5 us (10%)
  local copies, waits for them, and re-layouts  16.7 us (6%)
  between operations  14.4 us (5%)
    all_to_all x3, waiting for transfers between devices, exchange(): return lax.all_to_all(x, ALL, 0, 0, tiled=True)  95.9 us
    all_to_all x1, blocking collectives, exchange(): return lax.all_to_all(x, ALL, 0, 0, tiled=True)  27.5 us
    all_to_all x3, starting transfers between devices, exchange(): return lax.all_to_all(x, ALL, 0, 0, tiled=True)  25.1 us
    all_gather x1, waiting for transfers between devices, body(): gathered = lax.all_gather(owned, 'dp', axis=0)  17 us
    unnamed x82, local copies, waits for them, and re-layouts  16 us
    pallas_call x1, Pallas kernels, attend(): pl.pallas_call(attend_kernel, out_shape=(shape(wide, f32), shape((ROWS, 1...  14.9 us
    pallas_call x1, Pallas kernels, ffn_back(): pl.pallas_call(ffn_back_kernel, grid=(2,), out_shape=(shape((2, 64, UNITS...  13.8 us
    pallas_call x1, Pallas kernels, attend_back(): pl.pallas_call(back_kernel, out_shape=(shape(wide, f32), shape((PACK, 8,...  10.7 us
  transfers between devices with their start and end apart: 10, of which 9 were waited for; matrix products, arithmetic and copies ran while one was open for 1% of the time, Pallas kernels for 9%

profile of v1, /device:TPU:1, one launch (start us, length us, event | category | flops | bytes accessed | tf_op | source)
XLA Modules:
  0.0 276.9 jit_solution(12992729672462108994)
XLA Ops:
  7.2 0.7 reshape.74.bias_ref
  7.9 1.1 copy-done.11
  9.0 1.1 copy-done.12
  10.1 1.7 prep.1
  11.9 2.2 copy-done
  14.2 11.9 %all-to-all-start = ((bf16[128,19,8,128]{3,2,1,0:T(8,128)(2,1)}), bf16[128,19,8,128]{3,2,1,0:T(8,128)(2,1)}, u32[]{:S(2)}, u32[]{:S(2)}) async-start(bf16[128,19,8,128]{3,2,1,0:T(8,128)(2,1)} %copy-done), calls=%async_computation | async-start | bytes 9961472 | tf_op jit(solution)/shard_map/all_to_all | solution.py:728
  26.3 14.9 %attend.1 = (f32[256,768]{1,0:T(8,128)S(1)}, f32[256,128]{1,0:T(8,128)S(1)}, bf16[256,768]{1,0:T(8,128)(2,1)S(1)}, bf16[256,768]{1,0:T(8,128)(2,1)S(1)}, bf16[12...) custom-call(s32[1,4]{1,0:T(1,128)S(1)} %copy-done.30, ...), custom_call_target="tpu_custom_call" | custom-call | tf_op jit(solution)/shard_map/attend/pallas_call | solution.py:272
  41.1 0.9 copy-done.8
  42.0 0.9 copy-done.9
  42.9 0.8 copy-done.13
  43.7 0.7 copy-done.14
  44.4 0.7 copy-done.19
  45.1 0.7 copy-done.20
  45.8 0.7 copy-done.21
  46.5 0.6 copy-done.22
  47.1 0.7 copy-done.23
  47.8 1.2 collective-permute-start
  49.0 1.3 collective-permute-done.sib.r_sib
  50.4 35.6 %all-to-all-done.up.down = bf16[128,19,8,128]{3,2,1,0:T(8,128)(2,1)} async-done(((bf16[128,19,8,128]{3,2,1,0:T(8,128)(2,1)}), bf16[128,19,8,128]{3,2,1,0:T(8,128)(2,1)}, u32[]{:S(2)}, u32[]{:S(2)}) %all-to-all-start) | async-done | bytes 4980768 | tf_op jit(solution)/shard_map/all_to_all | solution.py:728
  86.0 9.9 %ffn.1 = (bf16[6,512,256]{2,1,0:T(8,128)(2,1)S(1)}, bf16[6,512,256]{2,1,0:T(8,128)(2,1)S(1)}, f32[256,768]{1,0:T(8,128)S(1)}, bf16[256,768]{1,0:T(8,128)(2,1)S(1)}) custom-call(bf16[256,768]{1,0:T(8,128)(2,1)S(1)} %get-tuple-element.58.own.r_own, bf16[256,768]{1,0:T(8,128)(2,1)S(1)} %collective-permute-done.sib.r_sib, ...), custom_call_target="tpu_custom_call" | custom-call | tf_op jit(solution)/shard_map/ffn/pallas_call | solution.py:352
  95.9 1.2 copy-done.5
  97.1 0.6 collective-permute-start.1
  97.7 1.3 collective-permute-done.1.got
  99.1 1.4 middle.1
  100.4 0.9 copy-done.10
  101.3 0.4 collective-permute-start.2
  101.7 1.3 collective-permute-done.2.sib
  103.1 0.7 copy-done.32
  103.8 13.8 %ffn_back.1 = (bf16[2,64,19,8,128]{4,3,2,1,0:T(8,128)(2,1)}, f32[256,768]{1,0:T(8,128)}, bf16[256,768]{1,0:T(8,128)(2,1)}) custom-call(bf16[256,768]{1,0:T(8,128)(2,1)} %copy-done.18, bf16[256,768]{1,0:T(8,128)(2,1)} %copy-done.32, bf16[256,768]{1,0:T(8,128)(2,1)} %copy-done.6, bf16[256,768]{1,0:T(8,128)(2,1)} %copy-done.7, ...), custom_call_target="tpu_custom_call" | custom-call | tf_op jit(solution)/shard_map/ffn_back/pallas_call | solution.py:455
  117.6 7.5 %all-to-all-start.1 = ((bf16[128,19,8,128]{3,2,1,0:T(8,128)(2,1)}), bf16[128,19,8,128]{3,2,1,0:T(8,128)(2,1)}, u32[]{:S(2)}, u32[]{:S(2)}) async-start(bf16[128,19,8,128]{3,2,1,0:T(8,128)(2,1)} %bitcast.13), calls=%async_computation.1 | async-start | bytes 9961472 | tf_op jit(solution)/shard_map/all_to_all | solution.py:728
  125.2 1.2 collective-permute-start.3
  126.4 1.3 collective-permute-done.3.got
  127.7 0.8 copy-done.31
  128.5 10.7 %attend_back.1 = (f32[256,768]{1,0:T(8,128)}, f32[640,8,128]{2,1,0:T(8,128)}, bf16[640,8,128]{2,1,0:T(8,128)(2,1)}) custom-call(s32[2]{0:T(128)} %copy-done.27, f32[256,768]{1,0:T(8,128)} %get-tuple-element.65.own, bf16[256,768]{1,0:T(8,128)(2,1)} %copy-done.31, f32[256,768]{1,0:T(8,128)} %copy-done.10, f32[256,768]{1,0:T(8,128)} %copy-done.2, ...), custom_call_target="tpu_custom_call" | custom-call | tf_op jit(solution)/shard_map/attend_back/pallas_call | solution.py:559
  139.2 0.4 collective-permute-start.4
  139.6 2.9 %collective-permute-done.4 = bf16[640,8,128]{2,1,0:T(8,128)(2,1)S(1)} collective-permute-done((bf16[640,8,128]{2,1,0:T(8,128)(2,1)}, bf16[640,8,128]{2,1,0:T(8,128)(2,1)S(1)}, u32[]{:S(2)}, u32[]{:S(2)}) %collective-permute-start.4) | collective-permute-done | bytes 1310752 | tf_op jit(solution)/shard_map/ppermute | solution.py:725
  142.5 2.1 add_convert_fusion
  144.5 40.6 %all-to-all-done.1.got = bf16[128,19,8,128]{3,2,1,0:T(8,128)(2,1)} async-done(((bf16[128,19,8,128]{3,2,1,0:T(8,128)(2,1)}), bf16[128,19,8,128]{3,2,1,0:T(8,128)(2,1)}, u32[]{:S(2)}, u32[]{:S(2)}) %all-to-all-start.1) | async-done | bytes 4980768 | tf_op jit(solution)/shard_map/all_to_all | solution.py:728
  185.1 5.6 %sum_ffn.1 = bf16[2,19,8,128]{3,2,1,0:T(8,128)(2,1)} custom-call(bf16[128,19,8,128]{3,2,1,0:T(8,128)(2,1)} %all-to-all-done.1.got), custom_call_target="tpu_custom_call" | custom-call | tf_op jit(solution)/shard_map/sum_ffn/pallas_call | solution.py:594
  190.8 27.5 %all_to_all.20.got = bf16[128,5,8,128]{3,2,1,0:T(8,128)(2,1)S(1)} all-to-all(bf16[128,5,8,128]{3,2,1,0:T(8,128)(2,1)S(1)} %bitcast.12), channel_id=1, replica_groups=mesh['dp'=16,'tensor'=8] {'dp','tensor'}, dimensions={0} | all-to-all | bytes 2621440 | tf_op jit(solution)/shard_map/all_to_all | solution.py:728
  218.3 1.3 sum_rest.1
  219.6 5.7 %all-to-all-start.3 = ((bf16[128,5,8,128]{3,2,1,0:T(8,128)(2,1)}), bf16[128,5,8,128]{3,2,1,0:T(8,128)(2,1)S(1)}, u32[]{:S(2)}, u32[]{:S(2)}) async-start(bf16[128,5,8,128]{3,2,1,0:T(8,128)(2,1)} %sum_rest.1), calls=%async_computation.3 | async-start | bytes 2621440 | tf_op jit(solution)/shard_map/all_to_all | solution.py:728
  225.3 0.7 all-gather.3.cloned.1.call-update
  226.0 19.7 %all-to-all-done.3 = bf16[128,5,8,128]{3,2,1,0:T(8,128)(2,1)S(1)} async-done(((bf16[128,5,8,128]{3,2,1,0:T(8,128)(2,1)}), bf16[128,5,8,128]{3,2,1,0:T(8,128)(2,1)S(1)}, u32[]{:S(2)}, u32[]{:S(2)}) %all-to-all-start.3) | async-done | bytes 1310752 | tf_op jit(solution)/shard_map/all_to_all | solution.py:728
  245.7 1.2 collective-permute-start.5
  246.8 17.0 %all-gather.3.cloned.1.call-done = bf16[32,19,8,128]{3,2,1,0:T(8,128)(2,1)} async-done(((bf16[2,19,8,128]{3,2,1,0:T(8,128)(2,1)}), bf16[32,19,8,128]{3,2,1,0:T(8,128)(2,1)}) %all-gather.3.cloned.1.call-update) | async-done | bytes 1245200 | tf_op jit(solution)/shard_map/all_gather | solution.py:755
  263.8 1.3 copy-done.1
  265.1 5.0 %final.1 = (f32[768,768]{1,0:T(8,128)}, f32[768]{0:T(1024)}, f32[65,768]{1,0:T(8,128)}, f32[768,768]{1,0:T(8,128)}, f32[768]{0:T(1024)}, /*index=5*/f32[768]{0:T...) custom-call(s32[2]{0:T(128)S(1)} %copy-done.28, ...), custom_call_target="tpu_custom_call" | custom-call | tf_op jit(solution)/shard_map/final/pallas_call | solution.py:676
  (75 shorter events, 0.3 us)
Async XLA Ops:
  7.9 1.1 copy-start.11
  9.0 1.1 copy-start.12
  10.1 1.8 copy-start.27
  11.8 2.2 copy-start
  14.1 12.0 %copy-start.33 = (bf16[768]{0:T(1024)(128)(2,1)S(1)}, bf16[768]{0:T(1024)(128)(2,1)}, u32[]{:S(2)}) copy-start(bf16[768]{0:T(1024)(128)(2,1)} %param.25) | copy-start | bytes 4612
  14.1 12.0 %copy-start.34 = (bf16[768]{0:T(1024)(128)(2,1)S(1)}, bf16[768]{0:T(1024)(128)(2,1)}, u32[]{:S(2)}) copy-start(bf16[768]{0:T(1024)(128)(2,1)} %param.26) | copy-start | bytes 4612
  14.1 12.1 %copy-start.35 = (bf16[768]{0:T(1024)(128)(2,1)S(1)}, bf16[768]{0:T(1024)(128)(2,1)}, u32[]{:S(2)}) copy-start(bf16[768]{0:T(1024)(128)(2,1)} %param.21) | copy-start | bytes 4612
  14.1 12.1 %copy-start.36 = (bf16[768]{0:T(1024)(128)(2,1)S(1)}, bf16[768]{0:T(1024)(128)(2,1)}, u32[]{:S(2)}) copy-start(bf16[768]{0:T(1024)(128)(2,1)} %param.24) | copy-start | bytes 4612
  14.1 12.1 %copy-start.3 = (bf16[256,768]{1,0:T(8,128)(2,1)S(1)}, bf16[256,768]{1,0:T(8,128)(2,1)}, u32[]{:S(2)}) copy-start(bf16[256,768]{1,0:T(8,128)(2,1)} %x.1) | copy-start | bytes 1179652
  14.1 12.1 %copy-start.16 = (s32[256,384]{1,0:T(8,128)S(1)}, s32[256,384]{1,0:T(8,128)}, u32[]{:S(2)}) copy-start(s32[256,384]{1,0:T(8,128)} %q_ref.1) | copy-start | bytes 1179652
  14.1 12.1 %copy-start.17 = (s32[256,384]{1,0:T(8,128)S(1)}, s32[256,384]{1,0:T(8,128)}, u32[]{:S(2)}) copy-start(s32[256,384]{1,0:T(8,128)} %k_ref.1) | copy-start | bytes 1179652
  14.1 12.1 %copy-start.24 = (bf16[65,768]{1,0:T(8,128)(2,1)S(1)}, bf16[65,768]{1,0:T(8,128)(2,1)}, u32[]{:S(2)}) copy-start(bf16[65,768]{1,0:T(8,128)(2,1)} %taps_ref.1) | copy-start | bytes 299524
  14.1 12.1 %copy-start.29 = (s32[256]{0:T(256)S(1)}, s32[256]{0:T(256)}, u32[]{:S(2)}) copy-start(s32[256]{0:T(256)} %param.35) | copy-start | bytes 3076
  14.2 12.1 %copy-start.30 = (s32[1,4]{1,0:T(1,128)S(1)}, s32[1,4]{1,0:T(1,128)}, u32[]{:S(2)}) copy-start(s32[1,4]{1,0:T(1,128)} %len_ref.1) | copy-start | bytes 52
  14.2 71.9 %all-to-all-start = ((bf16[128,19,8,128]{3,2,1,0:T(8,128)(2,1)}), bf16[128,19,8,128]{3,2,1,0:T(8,128)(2,1)}, u32[]{:S(2)}, u32[]{:S(2)}) async-start(bf16[128,19,8,128]{3,2,1,0:T(8,128)(2,1)} %copy-done), calls=%async_computation | async-start | bytes 9961472 | tf_op jit(solution)/shard_map/all_to_all | solution.py:728
  26.1 72.9 %copy-start.25 = (bf16[1,768]{1,0:T(2,128)(2,1)}, bf16[1,768]{1,0:T(2,128)(2,1)S(1)}, u32[]{:S(2)}) copy-start(bf16[1,768]{1,0:T(2,128)(2,1)S(1)} %reshape.71.ga_ref.ga) | copy-start | bytes 4612
  41.1 0.9 copy-start.8
  42.0 0.9 copy-start.9
  42.9 0.8 copy-start.13
  43.7 0.8 copy-start.14
  44.4 0.7 copy-start.19
  45.1 0.7 copy-start.20
  47.8 48.1 %copy-start.6 = (bf16[256,768]{1,0:T(8,128)(2,1)}, bf16[256,768]{1,0:T(8,128)(2,1)S(1)}, u32[]{:S(2)}) copy-start(bf16[256,768]{1,0:T(8,128)(2,1)S(1)} %get-tuple-element.58.own.r_own) | copy-start | bytes 1179652
  47.8 51.3 %copy-start.2 = (f32[256,768]{1,0:T(8,128)}, f32[256,768]{1,0:T(8,128)S(1)}, u32[]{:S(2)}) copy-start(f32[256,768]{1,0:T(8,128)S(1)} %get-tuple-element.57.n1) | copy-start | bytes 2359300
  47.8 49.9 %copy-start.37 = (bf16[768]{0:T(1024)(128)(2,1)S(1)}, bf16[768]{0:T(1024)(128)(2,1)}, u32[]{:S(2)}) copy-start(bf16[768]{0:T(1024)(128)(2,1)} %param.30) | copy-start | bytes 4612
  47.8 49.9 %copy-start.38 = (bf16[768]{0:T(1024)(128)(2,1)S(1)}, bf16[768]{0:T(1024)(128)(2,1)}, u32[]{:S(2)}) copy-start(bf16[768]{0:T(1024)(128)(2,1)} %param.31) | copy-start | bytes 4612
  47.8 49.9 %copy-start.39 = (bf16[768]{0:T(1024)(128)(2,1)S(1)}, bf16[768]{0:T(1024)(128)(2,1)}, u32[]{:S(2)}) copy-start(bf16[768]{0:T(1024)(128)(2,1)} %param.32) | copy-start | bytes 4612
  47.8 51.2 %copy-start.15 = (bf16[256,768]{1,0:T(8,128)(2,1)S(1)}, bf16[256,768]{1,0:T(8,128)(2,1)}, u32[]{:S(2)}) copy-start(bf16[256,768]{1,0:T(8,128)(2,1)} %og.1) | copy-start | bytes 1179652
  47.8 2.6 collective-permute-start
  50.4 45.5 %copy-start.7 = (bf16[256,768]{1,0:T(8,128)(2,1)}, bf16[256,768]{1,0:T(8,128)(2,1)S(1)}, u32[]{:S(2)}) copy-start(bf16[256,768]{1,0:T(8,128)(2,1)S(1)} %collective-permute-done.sib.r_sib) | copy-start | bytes 1179652
  95.9 1.2 copy-start.5
  97.1 3.3 %copy-start.4 = (bf16[6,512,256]{2,1,0:T(8,128)(2,1)}, bf16[6,512,256]{2,1,0:T(8,128)(2,1)S(1)}, u32[]{:S(2)}) copy-start(bf16[6,512,256]{2,1,0:T(8,128)(2,1)S(1)} %get-tuple-element.63.act) | copy-start | bytes 4718596
  97.1 1.9 collective-permute-start.1
  100.4 0.9 copy-start.10
  101.3 1.7 copy-start.18
  101.3 16.3 %copy-start.26 = (f32[8,768]{1,0:T(8,128)}, f32[8,768]{1,0:T(8,128)S(1)}, u32[]{:S(2)}) copy-start(f32[8,768]{1,0:T(8,128)S(1)} %get-tuple-element.79.sums) | copy-start | bytes 73732
  101.3 1.7 collective-permute-start.2
  103.1 0.8 copy-start.32
  117.6 7.6 %copy-start.40 = (bf16[256,768]{1,0:T(8,128)(2,1)S(1)}, bf16[256,768]{1,0:T(8,128)(2,1)}, u32[]{:S(2)}) copy-start(bf16[256,768]{1,0:T(8,128)(2,1)} %get-tuple-element.66) | copy-start | bytes 1179652
  117.6 67.5 %all-to-all-start.1 = ((bf16[128,19,8,128]{3,2,1,0:T(8,128)(2,1)}), bf16[128,19,8,128]{3,2,1,0:T(8,128)(2,1)}, u32[]{:S(2)}, u32[]{:S(2)}) async-start(bf16[128,19,8,128]{3,2,1,0:T(8,128)(2,1)} %bitcast.13), calls=%async_computation.1 | async-start | bytes 9961472 | tf_op jit(solution)/shard_map/all_to_all | solution.py:728
  125.2 2.6 collective-permute-start.3
  127.7 0.8 copy-start.31
  139.2 3.2 %collective-permute-start.4 = (bf16[640,8,128]{2,1,0:T(8,128)(2,1)}, bf16[640,8,128]{2,1,0:T(8,128)(2,1)S(1)}, u32[]{:S(2)}, u32[]{:S(2)}) collective-permute-start(bf16[640,8,128]{2,1,0:T(8,128)(2,1)} %get-tuple-element.82), channel_id=1, source_target_pairs={{0,8},{8,0},{16,24},{24,16},{32,40},{40,32},{48,56},{56,48},{64,72... | collective-permute-start | bytes 3932168 | tf_op jit(solution)/shard_map/ppermute | solution.py:725
  219.6 44.2 %copy-start.28 = (s32[2]{0:T(128)S(1)}, s32[2]{0:T(128)}, u32[]{:S(2)}) copy-start(s32[2]{0:T(128)} %copy-done.27) | copy-start | bytes 28
  219.6 26.1 %all-to-all-start.3 = ((bf16[128,5,8,128]{3,2,1,0:T(8,128)(2,1)}), bf16[128,5,8,128]{3,2,1,0:T(8,128)(2,1)S(1)}, u32[]{:S(2)}, u32[]{:S(2)}) async-start(bf16[128,5,8,128]{3,2,1,0:T(8,128)(2,1)} %sum_rest.1), calls=%async_computation.3 | async-start | bytes 2621440 | tf_op jit(solution)/shard_map/all_to_all | solution.py:728
  225.2 38.5 %all-gather.3.cloned.1.call-start = ((), (), s32[]{:S(2)}) async-start(), calls=%async_computation.4 | async-start | bytes 1323008 | tf_op jit(solution)/shard_map/all_gather | solution.py:755
  245.7 18.1 %collective-permute-start.5 = (bf16[640,8,128]{2,1,0:T(8,128)(2,1)S(1)}, bf16[640,8,128]{2,1,0:T(8,128)(2,1)S(1)}, u32[]{:S(2)}, u32[]{:S(2)}) collective-permute-start(bf16[640,8,128]{2,1,0:T(8,128)(2,1)S(1)} %bitcast.7), channel_id=1, source_target_pairs={{0,8},{8,0},{16,24},{24,16},{32,40},{40,32},{48,56},{56,48},{64,72... | collective-permute-start | bytes 3932168 | tf_op jit(solution)/shard_map/ppermute | solution.py:725
  263.8 1.3 copy-start.1
  (3 other events, 2.0 us)
Sparse Core Ops, SparseCore 0:
  228.4 35.3 all-gather.2

commit v2 on v1

--- a/solution.py
+++ b/solution.py
@@ -18,8 +18,13 @@
 DFT_LEN = 384
 FREQ = 256
 LIVE_FREQ = DFT_LEN // 2 + 1
+CLASSES = 4
+SUB = 96
 PIECE = 24
-UNITS = 3 * COLS + 1
+PIECES = SUB // PIECE
+UNITS = 10
+HIDDEN = 768
+HALF = ROWS // 2
 TALL = 848
 TALL_TILES = TALL // 8
 PACK = 640
@@ -73,6 +78,7 @@
 
 def prep_kernel(place, up_ref, down_ref, bias_ref, out_ref, tall, cols, piece):
     rep = place[0] % 8
+    side = rep % 2
 
     @pl.when(pl.program_id(0) == 0)
     def _():
@@ -86,34 +92,36 @@
             tall[...] = down_ref[...].astype(f32)
             cols[...] = jnp.zeros(cols.shape, f32)
 
-        for c in range(2):
-            start = pl.multiple_of(192 * c + PIECE * rep, 8)
+        for q in range(CLASSES):
+            start = pl.multiple_of(SUB * q + PIECE * (rep // 2), 8)
             rows = tall[pl.ds(start, PIECE), :]
-            for ct in range(COLS):
-                part = rows[:, ct * 128 : ct * 128 + 128].reshape(3, 8, 128)
-                piece[c, 3 * ct : 3 * ct + 3] = part.astype(bf16)
+            for j in range(3):
+                left = rows[:, j * 128 : j * 128 + 128]
+                right = rows[:, 384 + j * 128 : 512 + j * 128]
+                part = jnp.where(side == 0, left, right).reshape(3, 8, 128)
+                piece[q, 3 * j : 3 * j + 3] = part.astype(bf16)
             bias = jnp.zeros((8, 128), f32)
             for rt in range(3):
                 col = cols[pl.ds(pl.multiple_of(start + 8 * rt, 8), 8), :][:, 0:1]
                 bias = jnp.where(lanes((8, 128)) == rt, jnp.broadcast_to(col, (8, 128)), bias)
-            piece[c, UNITS - 1] = bias.astype(bf16)
-
-    for s in range(16):
-        out_ref[s] = piece[s // 8]
+            piece[q, UNITS - 1] = jnp.where(side == 0, bias, 0.0).astype(bf16)
+
+    for n in range(32):
+        out_ref[n] = piece[n // 8]
 
 
 def prep(place, w_up, w_down, b_up):
     whole = lambda *dims: pl.BlockSpec(dims, lambda i: (0,) * len(dims))
     return pl.pallas_call(
         prep_kernel,
-        grid=(8,),
+        grid=(4,),
         out_shape=shape((128, UNITS, 8, 128), bf16),
         in_specs=[SMEM, whole(768, 384), whole(384, 768), whole(1, 384)],
-        out_specs=pl.BlockSpec((16, UNITS, 8, 128), lambda i: (i, 0, 0, 0)),
+        out_specs=pl.BlockSpec((32, UNITS, 8, 128), lambda i: (i, 0, 0, 0)),
         scratch_shapes=[
             pltpu.VMEM((384, 768), f32),
             pltpu.VMEM((384, 8), f32),
-            pltpu.VMEM((2, UNITS, 8, 128), bf16),
+            pltpu.VMEM((CLASSES, UNITS, 8, 128), bf16),
         ],
         compiler_params=params(32),
         name="prep",
@@ -145,7 +153,7 @@
 
 def attend_kernel(
     len_ref, x_ref, wv_ref, bv_ref, taps_ref, wo_ref, bo_ref, ga_ref, sa_ref, q_ref, k_ref, live_ref,
-    n_ref, inv_ref, low_ref, ctx_ref, col_ref, nrm_ref, scl_ref, wave_ref, wavet_ref, ks_ref, vs_ref,
+    n_ref, inv_ref, low_ref, low_a, low_b, ctx_ref, col_ref, nrm_ref, scl_ref, wave_ref, wavet_ref, ks_ref, vs_ref,
     tapt_ref, live_out, qw, kb, jn, tapbuf, mix, mskd,
 ):
     ends = segment_ends(len_ref)
@@ -264,22 +272,26 @@
     n, inv = norm_rows(x_ref[...].astype(f32) + attended)
     n_ref[...] = n
     inv_ref[...] = jnp.broadcast_to(inv, (ROWS, 128))
-    low_ref[...] = (n * ga_ref[...].astype(f32) + sa_ref[...].astype(f32)).astype(bf16)
+    low = (n * ga_ref[...].astype(f32) + sa_ref[...].astype(f32)).astype(bf16)
+    low_ref[...] = low
+    low_a[...] = low[0:HALF]
+    low_b[...] = low[HALF:]
 
 
 def attend(seq_lengths, x, wv, bv, taps, wo, bo, ga, sa, q, k, live):
     wide = (ROWS, WIDTH)
+    half = (HALF, WIDTH)
     return pl.pallas_call(
         attend_kernel,
         out_shape=(
-            shape(wide, f32), shape((ROWS, 128), f32), shape(wide, bf16), shape(wide, bf16),
-            shape((HEADS, ROWS, ROWS), bf16), shape(wide, bf16), shape(wide, f32),
+            shape(wide, f32), shape((ROWS, 128), f32), shape(wide, bf16), shape(half, bf16),
+            shape(half, bf16), shape(wide, bf16), shape((HEADS, ROWS, ROWS), bf16), shape(wide, bf16), shape(wide, f32),
             shape((2 * FREQ, ROWS), bf16), shape((ROWS, 2 * FREQ), bf16),
             shape((2 * FREQ, WIDTH), f32), shape((2 * FREQ, WIDTH), bf16),
             shape((128, 2 * FREQ), bf16), shape((ROWS, 128), f32),
         ),
         in_specs=[SMEM] + [VMEM] * 11,
-        out_specs=(VMEM,) * 13,
+        out_specs=(VMEM,) * 15,
         scratch_shapes=[
             pltpu.VMEM((ROWS, 128), i32),
             pltpu.VMEM((96, 2, 8, 128), i32),
@@ -288,97 +300,121 @@
             pltpu.VMEM(wide, f32),
             pltpu.VMEM(wide, bf16),
         ],
-        compiler_params=params(48),
+        compiler_params=params(32),
         name="attend",
     )(seq_lengths, x, wv, bv, taps, wo, bo, ga, sa, q, k, live)
 
 
-def untile(ref, first):
-    part = ref[:, first : first + 3].astype(f32)
-    return part.reshape(-1, 128).astype(bf16)
-
-
-def load_up(ref, out):
-    for ct in range(COLS):
-        out[:, ct * 128 : ct * 128 + 128] = untile(ref, 3 * ct)
-    tile = ref[:, UNITS - 1].astype(f32)
-    lane = lanes(tile.shape)
-    parts = [jnp.where(lane == rt, tile, 0.0)[:, None] for rt in range(3)]
-    out[:, WIDTH:] = jnp.concatenate(parts, axis=1).reshape(-1, 128).astype(bf16)
-
-
-def load_down(ref, out):
-    for ct in range(COLS):
-        out[:, ct * 128 : ct * 128 + 128] = untile(ref, 3 * ct)
-
-
-def ffn_kernel(own, sib, up, down, act, slope, part_own, part_sib, rows, wu, wd, acc):
-    step = pl.program_id(0)
-
-    @pl.when(step == 0)
-    def _():
-        rows[0:ROWS, 0:WIDTH] = own[...]
-        rows[ROWS:, 0:WIDTH] = sib[...]
-        rows[:, WIDTH:] = jnp.where(lanes((2 * ROWS, 128)) < 3, 1.0, 0.0).astype(bf16)
-        acc[...] = jnp.zeros(acc.shape, f32)
-
-    load_up(up, wu)
-    load_down(down, wd)
+def unpack(ref, m, out):
+    for a in range(PIECES):
+        rs = slice(a * 192, a * 192 + 192)
+        for ct in range(COLS):
+            first = 3 * (ct % 3)
+            part = ref[m, a, ct // 3, :, first : first + 3].astype(f32)
+            out[rs, ct * 128 : ct * 128 + 128] = part.reshape(192, 128).astype(bf16)
+
+
+def unpack_bias(ref, out):
+    for a in range(PIECES):
+        tile = ref[0, a, 0, :, UNITS - 1].astype(f32)
+        lane = lanes(tile.shape)
+        parts = [jnp.where(lane == rt, tile, 0.0)[:, None] for rt in range(3)]
+        column = jnp.concatenate(parts, axis=1).reshape(192, 128)
+        out[a * 192 : a * 192 + 192, WIDTH:] = column.astype(bf16)
+
+
+def ffn_rows(own, sib, rows, ones):
+    rows[0:ROWS, 0:WIDTH] = own
+    rows[ROWS:, 0:WIDTH] = sib
+    rows[:, WIDTH:] = jnp.where(lanes((2 * ROWS, 128)) < ones, 1.0, 0.0).astype(bf16)
+
+
+def ffn_blocks(rows, wu, wd, act, slope, acc):
+    acc[...] = jnp.zeros(acc.shape, f32)
 
     def block(i, carry):
         hs = pl.ds(pl.multiple_of(i * 256, 256), 256)
         upper = dot_last(rows[...], wu[hs, :])
         cdf = 0.5 * (1.0 + lax.erf(upper * math.sqrt(0.5)))
         a = (upper * cdf).astype(bf16)
-        act[i] = a
+        act[:, hs] = a
         density = jnp.exp(-0.5 * upper * upper) * (1.0 / math.sqrt(2.0 * math.pi))
-        slope[i] = (cdf + upper * density).astype(bf16)
+        slope[:, hs] = (cdf + upper * density).astype(bf16)
         acc[...] += dot(a, wd[hs, :])
         return carry
 
-    lax.fori_loop(0, 3, block, 0)
-
-    @pl.when(step == 1)
-    def _():
-        part_own[...] = acc[0:ROWS]
-        part_sib[...] = acc[ROWS:].astype(bf16)
-
-
-def ffn(own, sib, weights):
+    lax.fori_loop(0, HIDDEN // 256, block, 0)
+
+
+def ffn_far_kernel(
+    got_a, got_b, sib, w, act, slope, part_own, part_sib, rows_out, wu, wd, rows, acc,
+):
+    ffn_rows(jnp.concatenate([got_a[...], got_b[...]], axis=0), sib[...], rows, 3)
+    unpack(w, 0, wu)
+    unpack_bias(w, wu)
+    unpack(w, 1, wd)
+    rows_out[...] = rows[:, 0:WIDTH]
+    ffn_blocks(rows, wu, wd, act, slope, acc)
+    part_own[...] = acc[0:ROWS]
+    part_sib[...] = acc[ROWS:].astype(bf16)
+
+
+def ffn_near_kernel(own, sib, wu, wd, act, slope, part_own, part_sib, rows_out, rows, acc):
+    ffn_rows(own[...], sib[...], rows, 3)
+    rows_out[...] = rows[:, 0:WIDTH]
+    ffn_blocks(rows, wu, wd, act, slope, acc)
+    part_own[...] = acc[0:ROWS]
+    part_sib[...] = acc[ROWS:].astype(bf16)
+
+
+def ffn_call(kernel, weights_out, *args):
     wide = (ROWS, WIDTH)
-    whole = lambda *dims: pl.BlockSpec(dims, lambda b: (0,) * len(dims))
-    piece = (32, UNITS, 8, 128)
-    hidden = (3, 2 * ROWS, 256)
-    return pl.pallas_call(
-        ffn_kernel,
-        grid=(2,),
-        out_shape=(
-            shape((6, 2 * ROWS, 256), bf16), shape((6, 2 * ROWS, 256), bf16),
-            shape(wide, f32), shape(wide, bf16),
-        ),
-        in_specs=[
-            whole(*wide), whole(*wide),
-            pl.BlockSpec(piece, lambda b: (b, 0, 0, 0)),
-            pl.BlockSpec(piece, lambda b: (2 + b, 0, 0, 0)),
-        ],
-        out_specs=(
-            pl.BlockSpec(hidden, lambda b: (b, 0, 0)), pl.BlockSpec(hidden, lambda b: (b, 0, 0)),
-            whole(*wide), whole(*wide),
-        ),
+    tall = shape((2 * ROWS, WIDTH), bf16)
+    outs = (tall, tall, shape(wide, f32), shape(wide, bf16), tall)
+    if weights_out:
+        outs += (shape((HIDDEN, WIDTH + 128), bf16), shape((HIDDEN, WIDTH), bf16))
+    return pl.pallas_call(
+        kernel,
+        out_shape=outs,
+        in_specs=[VMEM] * len(args),
+        out_specs=(VMEM,) * len(outs),
         scratch_shapes=[
             pltpu.VMEM((2 * ROWS, WIDTH + 128), bf16),
-            pltpu.VMEM((768, WIDTH + 128), bf16),
-            pltpu.VMEM((768, WIDTH), bf16),
             pltpu.VMEM((2 * ROWS, WIDTH), f32),
         ],
-        compiler_params=params(48),
-        name="ffn",
-    )(own, sib, weights, weights)
-
-
-def middle_kernel(n1, own, got, bd, ga, sa, gf, sf, og, out, second, low, sums):
+        compiler_params=params(24),
+        name="ffn_far" if weights_out else "ffn_near",
+    )(*args)
+
+
+def combine_kernel(own, got, out_a, out_b):
+    total = (own[...] + got[...].astype(f32)).astype(bf16)
+    out_a[...] = total[0:HALF]
+    out_b[...] = total[HALF:]
+
+
+def combine(own, got):
+    half = shape((HALF, WIDTH), bf16)
+    return pl.pallas_call(
+        combine_kernel,
+        out_shape=(half, half),
+        in_specs=[VMEM] * 2,
+        out_specs=(VMEM,) * 2,
+        compiler_params=params(32),
+        name="combine",
+    )(own, got)
+
+
+def gather_rows(own, near, far_a, far_b):
+    far = jnp.concatenate([far_a[...], far_b[...]], axis=0)
+    return own[...] + near[...].astype(f32) + far.astype(f32)
+
+
+def middle_kernel(
+    n1, own, near, far_a, far_b, bd, ga, sa, gf, sf, og, out, second, low, low_a, low_b, sums,
+):
     first = n1[...] * ga[...].astype(f32) + sa[...].astype(f32)
-    n, inv = norm_rows(first + own[...] + got[...].astype(f32) + bd[...].astype(f32))
+    n, inv = norm_rows(first + gather_rows(own, near, far_a, far_b) + bd[...].astype(f32))
     gain = gf[...].astype(f32)
     out[...] = (n * gain + sf[...].astype(f32)).astype(bf16)
     g = og[...].astype(f32)
@@ -386,6 +422,8 @@
     second[...] = grad
     grad_low = grad.astype(bf16)
     low[...] = grad_low
+    low_a[...] = grad_low[0:HALF]
+    low_b[...] = grad_low[HALF:]
     sums[0:1] = jnp.sum(grad_low.astype(f32), axis=0, keepdims=True)
     sums[1:2] = jnp.sum(g * n, axis=0, keepdims=True)
     sums[2:3] = jnp.sum(g, axis=0, keepdims=True)
@@ -394,97 +432,104 @@
 
 def middle(*args):
     wide = (ROWS, WIDTH)
+    half = (HALF, WIDTH)
     return pl.pallas_call(
         middle_kernel,
-        out_shape=(shape(wide, bf16), shape(wide, f32), shape(wide, bf16), shape((8, WIDTH), f32)),
-        in_specs=[VMEM] * 9,
-        out_specs=(VMEM,) * 4,
+        out_shape=(
+            shape(wide, bf16), shape(wide, f32), shape(wide, bf16), shape(half, bf16),
+            shape(half, bf16), shape((8, WIDTH), f32),
+        ),
+        in_specs=[VMEM] * 11,
+        out_specs=(VMEM,) * 6,
         compiler_params=params(32),
         name="middle",
     )(*args)
 
 
-def ffn_back_kernel(
-    own, sib, r_own, r_sib, up, down, act, slope, grads, first_own, first_sib, rows, g, wu, wd, acc,
-    gu, gd,
-):
-    step = pl.program_id(0)
-
-    @pl.when(step == 0)
-    def _():
-        g[0:ROWS] = own[...]
-        g[ROWS:] = sib[...]
-        rows[0:ROWS, 0:WIDTH] = r_own[...]
-        rows[ROWS:, 0:WIDTH] = r_sib[...]
-        rows[:, WIDTH:] = jnp.ones((2 * ROWS, 128), bf16)
-        acc[...] = jnp.zeros(acc.shape, f32)
-
-    load_up(up, wu)
-    load_down(down, wd)
+def back_blocks(g, wu, wd, slope, u_out, bias, acc):
+    acc[...] = jnp.zeros(acc.shape, f32)
+    bias[...] = jnp.zeros(bias.shape, f32)
 
     def block(i, carry):
         hs = pl.ds(pl.multiple_of(i * 256, 256), 256)
-        u = (dot_last(g[...], wd[hs, :]) * slope[i].astype(f32)).astype(bf16)
-        gd[hs, :] = dot_first(act[i], g[...])
-        gu[hs, :] = dot_first(u, rows[...])
+        u = (dot_last(g[...], wd[hs, :]) * slope[:, hs].astype(f32)).astype(bf16)
+        u_out[:, hs] = u
+        bias[0:1, hs] = jnp.sum(u.astype(f32), axis=0, keepdims=True)
         acc[...] += dot(u, wu[hs, 0:WIDTH])
         return carry
 
-    lax.fori_loop(0, 3, block, 0)
-    for ct in range(COLS):
-        cs = slice(ct * 128, ct * 128 + 128)
-        grads[0, :, 3 * ct : 3 * ct + 3] = gu[:, cs].reshape(32, 3, 8, 128).astype(bf16)
-        grads[1, :, 3 * ct : 3 * ct + 3] = gd[:, cs].reshape(32, 3, 8, 128).astype(bf16)
-    bias = gu[:, WIDTH:].reshape(32, 3, 8, 128)
-    lane = lanes((32, 8, 128))
-    tile = jnp.where(lane == 0, bias[:, 0], jnp.where(lane == 1, bias[:, 1], bias[:, 2]))
-    grads[0, :, UNITS - 1] = tile.astype(bf16)
-    grads[1, :, UNITS - 1] = jnp.zeros((32, 8, 128), bf16)
-
-    @pl.when(step == 1)
-    def _():
-        first_own[...] = acc[0:ROWS]
-        first_sib[...] = acc[ROWS:].astype(bf16)
-
-
-def ffn_back(own, sib, r_own, r_sib, weights, act, slope):
+    lax.fori_loop(0, HIDDEN // 256, block, 0)
+
+
+def back_near_kernel(own, sib, wu, wd, slope, first_own, first_sib, g, u, bias, acc):
+    g[0:ROWS] = own[...]
+    g[ROWS:] = sib[...]
+    back_blocks(g, wu, wd, slope, u, bias, acc)
+    first_own[...] = acc[0:ROWS]
+    first_sib[...] = acc[ROWS:].astype(bf16)
+
+
+def back_far_kernel(got_a, got_b, sib, wu, wd, slope, first_own, first_sib, g, u, bias, acc):
+    g[0:HALF] = got_a[...]
+    g[HALF:ROWS] = got_b[...]
+    g[ROWS:] = sib[...]
+    back_blocks(g, wu, wd, slope, u, bias, acc)
+    first_own[...] = acc[0:ROWS]
+    first_sib[...] = acc[ROWS:].astype(bf16)
+
+
+def back_call(kernel, name, *args):
     wide = (ROWS, WIDTH)
-    whole = lambda *dims: pl.BlockSpec(dims, lambda b: (0,) * len(dims))
-    piece = (32, UNITS, 8, 128)
-    hidden = pl.BlockSpec((3, 2 * ROWS, 256), lambda b: (b, 0, 0))
-    return pl.pallas_call(
-        ffn_back_kernel,
-        grid=(2,),
-        out_shape=(shape((2, 64, UNITS, 8, 128), bf16), shape(wide, f32), shape(wide, bf16)),
-        in_specs=[
-            whole(*wide), whole(*wide), whole(*wide), whole(*wide),
-            pl.BlockSpec(piece, lambda b: (b, 0, 0, 0)),
-            pl.BlockSpec(piece, lambda b: (2 + b, 0, 0, 0)),
-            hidden, hidden,
-        ],
-        out_specs=(
-            pl.BlockSpec((2, 32, UNITS, 8, 128), lambda b: (0, b, 0, 0, 0)),
-            whole(*wide), whole(*wide),
-        ),
-        scratch_shapes=[
-            pltpu.VMEM((2 * ROWS, WIDTH + 128), bf16),
-            pltpu.VMEM((2 * ROWS, WIDTH), bf16),
-            pltpu.VMEM((768, WIDTH + 128), bf16),
-            pltpu.VMEM((768, WIDTH), bf16),
-            pltpu.VMEM((2 * ROWS, WIDTH), f32),
-            pltpu.VMEM((768, WIDTH + 128), f32),
-            pltpu.VMEM((768, WIDTH), f32),
-        ],
-        compiler_params=params(56),
-        name="ffn_back",
-    )(own, sib, r_own, r_sib, weights, weights, act, slope)
+    tall = shape((2 * ROWS, WIDTH), bf16)
+    outs = (shape(wide, f32), shape(wide, bf16), tall, tall, shape((8, HIDDEN), f32))
+    return pl.pallas_call(
+        kernel,
+        out_shape=outs,
+        in_specs=[VMEM] * len(args),
+        out_specs=(VMEM,) * len(outs),
+        scratch_shapes=[pltpu.VMEM((2 * ROWS, WIDTH), f32)],
+        compiler_params=params(24),
+        name=name,
+    )(*args)
+
+
+def pack_kernel(gu, gd, bias_n, bias_f, grads):
+    column = (bias_n[...] + bias_f[...]).T[:, 0:1]
+    for a in range(PIECES):
+        rs = slice(a * 192, a * 192 + 192)
+        for ct in range(COLS):
+            cs = slice(ct * 128, ct * 128 + 128)
+            us = slice(3 * (ct % 3), 3 * (ct % 3) + 3)
+            up = gu[rs, cs].astype(f32).reshape(8, 3, 8, 128)
+            down = gd[rs, cs].astype(f32).reshape(8, 3, 8, 128)
+            grads[0, a, ct // 3, :, us] = up.astype(bf16)
+            grads[1, a, ct // 3, :, us] = down.astype(bf16)
+        bias = jnp.broadcast_to(column[rs], (192, 128)).reshape(8, 3, 8, 128)
+        lane = lanes((8, 8, 128))
+        tile = jnp.where(lane == 0, bias[:, 0], jnp.where(lane == 1, bias[:, 1], bias[:, 2]))
+        empty = jnp.zeros((8, 8, 128), bf16)
+        grads[0, a, 0, :, UNITS - 1] = tile.astype(bf16)
+        grads[0, a, 1, :, UNITS - 1] = empty
+        grads[1, a, 0, :, UNITS - 1] = empty
+        grads[1, a, 1, :, UNITS - 1] = empty
+
+
+def pack(*args):
+    return pl.pallas_call(
+        pack_kernel,
+        out_shape=shape((2, PIECES, 2, 8, UNITS, 8, 128), bf16),
+        in_specs=[VMEM] * 4,
+        out_specs=VMEM,
+        compiler_params=params(16),
+        name="pack",
+    )(*args)
 
 
 def back_kernel(
-    place, own, got, second, n1, inv1, ga, ctx, wo, nrm, scl, wave, wavet, ks, vs, tapt, col, live, x,
+    place, own, near, far_a, far_b, second, n1, inv1, ga, ctx, wo, nrm, scl, wave, wavet, ks, vs, tapt, col, live, x,
     wv, sums, in_grad, keep, give, buf_a, buf_b, mg, mb,
 ):
-    first_grad = second[...] + own[...] + got[...].astype(f32)
+    first_grad = second[...] + gather_rows(own, near, far_a, far_b)
     n = n1[...]
     buf_a[768 + 2 : 768 + 3] = jnp.sum(first_grad * n, axis=0, keepdims=True)
     buf_a[768 + 3 : 768 + 4] = jnp.sum(first_grad, axis=0, keepdims=True)
@@ -538,11 +583,11 @@
         for ct in range(COLS):
             cs = slice(ct * 128, ct * 128 + 128)
             ts = slice(ct * TALL_TILES, ct * TALL_TILES + TALL_TILES)
-            keep[ts] = kept[:, cs].reshape(TALL_TILES, 8, 128)
+            keep[ts] = kept[:, cs].reshape(TALL_TILES, 8, 128).astype(bf16)
             give[ts] = given[:, cs].reshape(TALL_TILES, 8, 128).astype(bf16)
 
     rest = PACK - COLS * TALL_TILES
-    keep[PACK - rest :] = jnp.zeros((rest, 8, 128), f32)
+    keep[PACK - rest :] = jnp.zeros((rest, 8, 128), bf16)
     give[PACK - rest :] = jnp.zeros((rest, 8, 128), bf16)
 
     @pl.when(place[0] % 2 == 0)
@@ -558,8 +603,8 @@
     wide = (ROWS, WIDTH)
     return pl.pallas_call(
         back_kernel,
-        out_shape=(shape(wide, f32), shape((PACK, 8, 128), f32), shape((PACK, 8, 128), bf16)),
-        in_specs=[SMEM] + [VMEM] * 20,
+        out_shape=(shape(wide, f32), shape((PACK, 8, 128), bf16), shape((PACK, 8, 128), bf16)),
+        in_specs=[SMEM] + [VMEM] * 22,
         out_specs=(VMEM,) * 3,
         scratch_shapes=[
             pltpu.VMEM((TALL, WIDTH), f32),
@@ -567,7 +612,7 @@
             pltpu.VMEM(wide, bf16),
             pltpu.VMEM(wide, f32),
         ],
-        compiler_params=params(56),
+        compiler_params=params(40),
         name="attend_back",
     )(*args)
 
@@ -579,13 +624,13 @@
     def _():
         acc[...] = jnp.zeros(acc.shape, f32)
 
-    for c in range(2):
-        total = acc[c]
+    for q in range(CLASSES):
+        total = acc[q]
         for t in range(8):
-            total = total + got[c * 8 + t].astype(f32)
-        acc[c] = total
-
-    @pl.when(step == 7)
+            total = total + got[q * 8 + t].astype(f32)
+        acc[q] = total
+
+    @pl.when(step == 3)
     def _():
         out[...] = acc[...].astype(bf16)
 
@@ -593,11 +638,11 @@
 def sum_ffn(got):
     return pl.pallas_call(
         sum_ffn_kernel,
-        grid=(8,),
-        out_shape=shape((2, UNITS, 8, 128), bf16),
-        in_specs=[pl.BlockSpec((16, UNITS, 8, 128), lambda i: (i, 0, 0, 0))],
-        out_specs=pl.BlockSpec((2, UNITS, 8, 128), lambda i: (0, 0, 0, 0)),
-        scratch_shapes=[pltpu.VMEM((2, UNITS, 8, 128), f32)],
+        grid=(4,),
+        out_shape=shape((CLASSES, UNITS, 8, 128), bf16),
+        in_specs=[pl.BlockSpec((32, UNITS, 8, 128), lambda i: (i, 0, 0, 0))],
+        out_specs=pl.BlockSpec((CLASSES, UNITS, 8, 128), lambda i: (0, 0, 0, 0)),
+        scratch_shapes=[pltpu.VMEM((CLASSES, UNITS, 8, 128), f32)],
         compiler_params=params(32),
         name="sum_ffn",
     )(got)
@@ -629,8 +674,8 @@
 
 
 def final_kernel(
-    place, own, other, ffn_ref, bias_ref, g_wv, g_bv, g_conv, g_wo, g_bo, g_ga, g_sa, g_up, g_bup,
-    g_down, g_bd, g_gf, g_sf, vecs,
+    place, own, other, ffn_own, ffn_oth, bias_own, bias_oth, g_wv, g_bv, g_conv, g_wo, g_bo, g_ga, g_sa, g_up, g_bup,
+    g_down, g_bd, g_gf, g_sf, vecs, tall,
 ):
     ct = pl.program_id(0)
 
@@ -648,30 +693,62 @@
     def _():
         write(other, own)
 
-    for c in range(2):
-        rs = slice(192 * c, 192 * c + 192)
-        g_down[rs, :] = ffn_ref[8:16, c].astype(f32).reshape(192, 128)
-        g_up[:, rs] = ffn_ref[0:8, c].astype(f32).reshape(192, 128).T
+    core = place[0] % 2
+
+    def index(m, a):
+        return (m + place[0] // 8) % 2 * 4 + (place[0] // 2 % 4 + 4 - a) % 4
+
+    def spread(ref):
+        for a in range(PIECES):
+            up = ref[index(0, a)].astype(f32)
+            down = ref[index(1, a)].astype(f32)
+            for q in range(CLASSES):
+                rs = slice(SUB * q + PIECE * a, SUB * q + PIECE * a + PIECE)
+                tall[rs, :] = up[q].reshape(PIECE, 128)
+                g_down[rs, :] = down[q].reshape(PIECE, 128)
+
+    @pl.when(ct // 3 == core)
+    def _():
+        spread(ffn_own)
+
+    @pl.when(ct // 3 != core)
+    def _():
+        spread(ffn_oth)
+
+    g_up[...] = tall[...].T
 
     @pl.when(ct == COLS - 1)
     def _():
         for j, ref in enumerate((g_bv, g_bo, g_ga, g_sa, g_bd, g_gf, g_sf)):
             for i in range(COLS):
                 ref[i * 128 : i * 128 + 128] = vecs[i, j]
-        parts = []
-        for c in range(2):
-            tile = bias_ref[0:8, c, 0].astype(f32)
-            lane = lanes(tile.shape)
-            rows = [jnp.where(lane == rt, tile, 0.0)[:, None] for rt in range(3)]
-            parts.append(jnp.concatenate(rows, axis=1).reshape(192, 128))
-        tall = jnp.concatenate(parts, axis=0).astype(bf16)
-        g_bup[...] = dot_last(jnp.ones((8, 128), bf16), tall)[0]
-
-
-def final(place, own, other, gathered):
+
+        def bias(ref):
+            lane = lanes((CLASSES, 8, 128))
+            for a in range(PIECES):
+                tile = ref[index(0, a)][:, 0].astype(f32)
+                rows = [jnp.where(lane == rt, tile, 0.0)[:, None] for rt in range(3)]
+                column = jnp.concatenate(rows, axis=1)
+                for q in range(CLASSES):
+                    rs = slice(SUB * q + PIECE * a, SUB * q + PIECE * a + PIECE)
+                    tall[rs, :] = column[q].reshape(PIECE, 128)
+            g_bup[...] = dot_last(jnp.ones((8, 128), bf16), tall[...].astype(bf16))[0]
+
+        @pl.when(core == 0)
+        def _():
+            bias(bias_own)
+
+        @pl.when(core == 1)
+        def _():
+            bias(bias_oth)
+
+
+def final(place, own, other, ffn_own, ffn_oth):
     tile = pl.BlockSpec((TALL_TILES, 8, 128), lambda i: (i, 0, 0))
     tall = pl.BlockSpec((768, 128), lambda i: (0, i))
     vec = pl.BlockSpec((WIDTH,), lambda i: (0,))
+    units = pl.BlockSpec((8, CLASSES, 3, 8, 128), lambda i: (0, 0, i % 3, 0, 0))
+    last = pl.BlockSpec((8, CLASSES, 1, 8, 128), lambda i: (0, 0, UNITS - 1, 0, 0))
     v = shape((WIDTH,), f32)
     return pl.pallas_call(
         final_kernel,
@@ -682,18 +759,17 @@
         ),
         in_specs=[
             SMEM, tile, tile,
-            pl.BlockSpec((16, 2, 3, 8, 128), lambda i: (0, 0, i, 0, 0)),
-            pl.BlockSpec((16, 2, 1, 8, 128), lambda i: (0, 0, UNITS - 1, 0, 0)),
+            units, units, last, last,
         ],
         out_specs=(
             tall, vec, pl.BlockSpec((TAPS, 128), lambda i: (0, i)), tall, vec, vec, vec,
             pl.BlockSpec((128, 384), lambda i: (i, 0)), pl.BlockSpec((384,), lambda i: (0,)),
             pl.BlockSpec((384, 128), lambda i: (0, i)), vec, vec, vec,
         ),
-        scratch_shapes=[pltpu.VMEM((COLS, 8, 128), f32)],
+        scratch_shapes=[pltpu.VMEM((COLS, 8, 128), f32), pltpu.VMEM((384, 128), f32)],
         compiler_params=params(32),
         name="final",
-    )(place, own, other, gathered, gathered)
+    )(place, own, other, ffn_own, ffn_oth, ffn_own, ffn_oth)
 
 
 def body(
@@ -719,10 +795,19 @@
 ):
     dp = lax.axis_index("dp")
     place = jnp.stack([dp, lax.axis_index("tensor")]).astype(i32)
-    pairs = [(i, i ^ 1) for i in range(lax.axis_size("dp"))]
+    n_dp = lax.axis_size("dp")
+
+    def shift(i, by):
+        return i // 8 * 8 + (i // 2 + by) % 4 * 2 + i % 2
 
     def swap(x):
-        return lax.ppermute(x, "dp", pairs)
+        return lax.ppermute(x, "dp", [(i, i ^ 1) for i in range(n_dp)])
+
+    def ahead(x):
+        return lax.ppermute(x, "dp", [(i, shift(i, 1)) for i in range(n_dp)])
+
+    def behind(x):
+        return lax.ppermute(x, "dp", [(i, shift(i, -1)) for i in range(n_dp)])
 
     def exchange(x):
         return lax.all_to_all(x, ALL, 0, 0, tiled=True)
@@ -730,32 +815,63 @@
     def row(v):
         return v.reshape(1, -1)
 
+    def fetch(a, b):
+        far_a, far_b = ahead(a), behind(b)
+        return far_a, far_b, swap(jnp.concatenate([far_a, far_b], axis=0))
+
+    def send_back(own, sib):
+        a, b = combine(own, swap(sib))
+        return behind(a), ahead(b)
+
     weights = exchange(prep(place, w_up, w_down, row(b_up)))
-    (n1, inv1, low, ctx, collide, nrm, scl, wave, wavet, ks, vs, tapt, live) = attend(
+    weights = weights.reshape(2, PIECES, 2, 8, UNITS, 8, 128)
+    (n1, inv1, low, low_a, low_b, ctx, collide, nrm, scl, wave, wavet, ks, vs, tapt, live) = attend(
         seq_lengths, block_input, w_value, row(b_value), conv_kernel, w_out, row(b_out),
         row(gain_attn), row(shift_attn), query_codes, key_codes, row(key_live),
     )
     low_sib = swap(low)
-    act, slope, part_own, part_sib = ffn(low, low_sib, weights)
-    block_output, second, grad_low, sums = middle(
-        n1, part_own, swap(part_sib), row(b_down), row(gain_attn), row(shift_attn), row(gain_ffn),
-        row(shift_ffn), out_grad,
-    )
-    grads, first_own, first_sib = ffn_back(
-        grad_low, swap(grad_low), low, low_sib, weights, act, slope
-    )
+    row_a, row_b, row_sib = fetch(low_a, low_b)
+    act_f, slope_f, far_own, far_sib, rows_f, wu, wd = ffn_call(
+        ffn_far_kernel, True, row_a, row_b, row_sib, weights
+    )
+    act_n, slope_n, near_own, near_sib, rows_n = ffn_call(
+        ffn_near_kernel, False, low, low_sib, wu, wd
+    )
+    back_a, back_b = send_back(far_own, far_sib)
+    block_output, second, grad, grad_a, grad_b, sums = middle(
+        n1, near_own, swap(near_sib), back_a, back_b, row(b_down), row(gain_attn), row(shift_attn),
+        row(gain_ffn), row(shift_ffn), out_grad,
+    )
+    got_a, got_b, got_sib = fetch(grad_a, grad_b)
+    near_own, near_sib, g_n, u_n, bias_n = back_call(
+        back_near_kernel, "back_near", grad, swap(grad), wu, wd, slope_n
+    )
+    far_own, far_sib, g_f, u_f, bias_f = back_call(
+        back_far_kernel, "back_far", got_a, got_b, got_sib, wu, wd, slope_f
+    )
+    grad_down = (dot_first(act_n, g_n) + dot_first(act_f, g_f)).astype(bf16)
+    grad_up = (dot_first(u_n, rows_n) + dot_first(u_f, rows_f)).astype(bf16)
+    grads = pack(grad_up, grad_down, bias_n, bias_f)
+    back_a, back_b = send_back(far_own, far_sib)
+    grads, back_a, back_b = lax.optimization_barrier((grads, back_a, back_b))
     owned = exchange(grads.reshape(128, UNITS, 8, 128))
     input_grad, keep, give = attend_back(
-        place, first_own, swap(first_sib), second, n1, inv1, row(gain_attn), ctx, w_out, nrm, scl,
-        wave, wavet, ks, vs, tapt, collide, live, block_input, w_value, sums,
+        place, near_own, swap(near_sib), back_a, back_b, second, n1, inv1, row(gain_attn), ctx,
+        w_out, nrm, scl, wave, wavet, ks, vs, tapt, collide, live, block_input, w_value, sums,
     )
     pair = (keep + swap(give).astype(f32)).astype(bf16).reshape(128, PACK // 128, 8, 128)
     owned = sum_ffn(owned)
     pair, owned = lax.optimization_barrier((pair, owned))
-    gathered = lax.all_gather(owned, "dp", axis=0)
+    around = [owned]
+    for side in range(2):
+        for by in range(4):
+            if side or by:
+                pairs = [(i, (i // 8 + side) % 2 * 8 + shift(i % 8, by)) for i in range(n_dp)]
+                around.append(lax.ppermute(owned, "dp", pairs))
+    ffn_own = jnp.stack(around)
     back = exchange(sum_rest(exchange(pair))).reshape(PACK, 8, 128)
     (g_wv, g_bv, g_conv, g_wo, g_bo, g_ga, g_sa, g_up, g_bup, g_down, g_bd, g_gf, g_sf) = final(
-        place, back, swap(back), gathered
+        place, back, swap(back), ffn_own, swap(ffn_own)
     )
     return (
         block_output, input_grad, g_wv, g_bv, g_conv, g_wo, g_bo, g_ga, g_sa, g_up, g_bup, g_down,

time: 278 us -> 231 us (0.83)
  waiting for transfers between devices: 122 us -> 46.8 us
  local copies, waits for them, and re-layouts: 16.7 us -> 44.7 us
  starting transfers between devices: 30 us -> 57 us
  Pallas kernels: 64.3 us -> 47.5 us
  between operations: 14.4 us -> 1.25 us
  matrix products: 0 us -> 3.3 us
    all_to_all x3, waiting for transfers between devices: 95.9 us -> 2.24 us  [exchange(): return lax.all_to_all(x, ALL, 0, 0, tiled=True)]
    ppermute x6 -> x26, waiting for transfers between devices: 8.24 us -> 44.5 us  [the longest x7 17.3 us: body(): around.append(lax.ppermute(owned, 'dp', pairs))]
    unnamed x82 -> x125, local copies, waits for them, and re-layouts: 16 us -> 44 us
    ppermute x6 -> x26, starting transfers between devices: 4.88 us -> 30.9 us  [the longest x11 10.6 us: swap(): return lax.ppermute(x, 'dp', [(i, i ^ 1) for i in range(n_dp)])]
    all_gather x1 -> x0, waiting for transfers between devices: 17 us -> none  [body(): gathered = lax.all_gather(owned, 'dp', axis=0)]
    pallas_call x4 -> x9, Pallas kernels: 31 us -> 19.6 us  [the longest x2 9.19 us: ffn_call(): pl.pallas_call(kernel, out_shape=outs, in_specs=[VMEM] * len(args), out_s...]
    pallas_call x1, Pallas kernels: 10.7 us -> 6.65 us  [attend_back(): pl.pallas_call(back_kernel, out_shape=(shape(wide, f32), shape((PACK, 8,...]
    dot_general x0 -> x4, matrix products: none -> 3.3 us  [dot_first(): lax.dot_general(a, b, (((0,), (0,)), ((), ())), preferred_element_type=f32)]
  transfers between devices with their start and end apart: 10 -> 29, of which waited for: 9 -> 14; matrix products, arithmetic and copies ran while one was open for 1% -> 2% of each run, Pallas kernels for 9% -> 15%
where the time goes in v2:
time: 231 us; the launch traced here: 229 us
  starting transfers between devices  57 us (25%)
  Pallas kernels  47.5 us (21%)
  waiting for transfers between devices  46.8 us (20%)
  local copies, waits for them, and re-layouts  44.7 us (19%)
  blocking collectives  27 us (12%)
  matrix products  3.3 us (1%)
    unnamed x125, local copies, waits for them, and re-layouts  44 us
    all_to_all x1, blocking collectives, exchange(): return lax.all_to_all(x, ALL, 0, 0, tiled=True)  27 us
    all_to_all x3, starting transfers between devices, exchange(): return lax.all_to_all(x, ALL, 0, 0, tiled=True)  26.1 us
    ppermute x7, waiting for transfers between devices, body(): around.append(lax.ppermute(owned, 'dp', pairs))  17.3 us
    pallas_call x1, Pallas kernels, attend(): pl.pallas_call(attend_kernel, out_shape=(shape(wide, f32), shape((ROWS, 1...  13.1 us
    ppermute x4, waiting for transfers between devices, ahead(): return lax.ppermute(x, 'dp', [(i, shift(i, 1)) for i in range(n_dp)])  12.2 us
    ppermute x11, starting transfers between devices, swap(): return lax.ppermute(x, 'dp', [(i, i ^ 1) for i in range(n_dp)])  10.6 us
    ppermute x7, starting transfers between devices, body(): around.append(lax.ppermute(owned, 'dp', pairs))  10.6 us
  transfers between devices with their start and end apart: 29, of which 14 were waited for; matrix products, arithmetic and copies ran while one was open for 2% of the time, Pallas kernels for 15%

profile of v2, /device:TPU:1, one launch (start us, length us, event | category | flops | bytes accessed | tf_op | source)
XLA Modules:
  0.0 229.1 jit_solution(16393214271780871052)
XLA Ops:
  3.5 1.4 prep.1
  4.9 1.5 copy-done
  6.4 11.5 %all-to-all-start = ((bf16[128,10,8,128]{3,2,1,0:T(8,128)(2,1)}), bf16[128,10,8,128]{3,2,1,0:T(8,128)(2,1)S(1)}, u32[]{:S(2)}, u32[]{:S(2)}) async-start(bf16[128,10,8,128]{3,2,1,0:T(8,128)(2,1)} %copy-done), calls=%async_computation | async-start | bytes 5242880 | tf_op jit(solution)/shard_map/all_to_all | solution.py:813
  18.0 1.3 copy-done.1
  19.3 1.3 copy-done.3
  25.1 13.1 %attend.1 = (f32[256,768]{1,0:T(8,128)S(1)}, f32[256,128]{1,0:T(8,128)S(1)}, bf16[256,768]{1,0:T(8,128)(2,1)}, bf16[128,768]{1,0:T(8,128)(2,1)S(1)}, bf16[128,76...) custom-call(s32[1,4]{1,0:T(1,128)S(1)} %copy-done.49, ...), custom_call_target="tpu_custom_call" | custom-call | tf_op jit(solution)/shard_map/attend/pallas_call | solution.py:284
  45.6 1.4 collective-permute-start.1
  47.0 1.3 collective-permute-start.2
  48.2 6.2 %collective-permute-done.1.got_a = bf16[128,768]{1,0:T(8,128)(2,1)S(1)} collective-permute-done((bf16[128,768]{1,0:T(8,128)(2,1)S(1)}, bf16[128,768]{1,0:T(8,128)(2,1)S(1)}, u32[]{:S(2)}, u32[]{:S(2)}) %collective-permute-start.1) | collective-permute-done | bytes 196640 | tf_op jit(solution)/shard_map/ppermute | solution.py:807
  56.7 1.9 collective-permute-done.3.sib
  62.2 4.2 %ffn_far.1 = (bf16[512,768]{1,0:T(8,128)(2,1)S(1)}, bf16[512,768]{1,0:T(8,128)(2,1)S(1)}, f32[256,768]{1,0:T(8,128)S(1)}, bf16[256,768]{1,0:T(8,128)(2,1)S(1)}, ...) custom-call(bf16[128,768]{1,0:T(8,128)(2,1)S(1)} %copy-done.19, ...), custom_call_target="tpu_custom_call" | custom-call | tf_op jit(solution)/shard_map/ffn_far/pallas_call | solution.py:376
  66.9 5.0 %ffn_near.1 = (bf16[512,768]{1,0:T(8,128)(2,1)S(1)}, bf16[512,768]{1,0:T(8,128)(2,1)S(1)}, f32[256,768]{1,0:T(8,128)S(1)}, bf16[256,768]{1,0:T(8,128)(2,1)S(1)}, bf16[512,768]{1,0:T(8,128)(2,1)S(1)}) custom-call(bf16[256,768]{1,0:T(8,128)(2,1)} %get-tuple-element.84.own, bf16[256,768]{1,0:T(8,128)(2,1)} %collective-permute-done.sib, ...), custom_call_target="tpu_custom_call" | custom-call | tf_op jit(solution)/shard_map/ffn_near/pallas_call | solution.py:376
  72.2 1.5 collective-permute-start.6
  73.8 4.6 %collective-permute-done.6.far_a = bf16[128,768]{1,0:T(8,128)(2,1)S(1)} collective-permute-done((bf16[128,768]{1,0:T(8,128)(2,1)S(1)}, bf16[128,768]{1,0:T(8,128)(2,1)S(1)}, u32[]{:S(2)}, u32[]{:S(2)}) %collective-permute-start.6) | collective-permute-done | bytes 196640 | tf_op jit(solution)/shard_map/ppermute | solution.py:810
  78.4 2.3 %collective-permute-done.7.far_b = bf16[128,768]{1,0:T(8,128)(2,1)S(1)} collective-permute-done((bf16[128,768]{1,0:T(8,128)(2,1)S(1)}, bf16[128,768]{1,0:T(8,128)(2,1)S(1)}, u32[]{:S(2)}, u32[]{:S(2)}) %collective-permute-start.7) | collective-permute-done | bytes 196640 | tf_op jit(solution)/shard_map/ppermute | solution.py:807
  80.7 1.6 middle.1
  82.3 2.7 %collective-permute-start.11 = (bf16[128,768]{1,0:T(8,128)(2,1)S(1)}, bf16[128,768]{1,0:T(8,128)(2,1)S(1)}, u32[]{:S(2)}, u32[]{:S(2)}) collective-permute-start(bf16[128,768]{1,0:T(8,128)(2,1)S(1)} %get-tuple-element.103), channel_id=1, source_target_pairs={{0,48},{8,56},{16,0},{24,8},{32,16},{40,24},{48,32},{56,40},{64,11... | collective-permute-start | bytes 589832 | tf_op jit(solution)/shard_map/ppermute | solution.py:810
  85.0 2.1 collective-permute-start.8
  87.1 1.3 collective-permute-done.10.got_a
  88.4 2.5 %collective-permute-start.12 = (bf16[256,768]{1,0:T(8,128)(2,1)S(1)}, bf16[256,768]{1,0:T(8,128)(2,1)S(1)}, u32[]{:S(2)}, u32[]{:S(2)}) collective-permute-start(bf16[256,768]{1,0:T(8,128)(2,1)S(1)} %pad_maximum_fusion.1), channel_id=1, source_target_pairs={{0,8},{8,0},{16,24},{24,16},{32,40},{40,32},{48,56},{56,48},{64,72... | collective-permute-start | bytes 1179656 | tf_op jit(solution)/shard_map/ppermute | solution.py:804
  90.9 3.2 %back_near.1 = (f32[256,768]{1,0:T(8,128)S(1)}, bf16[256,768]{1,0:T(8,128)(2,1)S(1)}, bf16[512,768]{1,0:T(8,128)(2,1)S(1)}, bf16[512,768]{1,0:T(8,128)(2,1)S(1)}, f32[8,768]{1,0:T(8,128)S(1)}) custom-call(bf16[256,768]{1,0:T(8,128)(2,1)S(1)} %get-tuple-element.96.own, bf16[256,768]{1,0:T(8,128)(2,1)S(1)} %collective-permute-done.8.sib, ...), custom_call_target="tpu_custom_call" | custom-call | tf_op jit(solution)/shard_map/back_near/pallas_call | solution.py:485
  95.0 3.2 %back_far.1 = (f32[256,768]{1,0:T(8,128)S(1)}, bf16[256,768]{1,0:T(8,128)(2,1)S(1)}, bf16[512,768]{1,0:T(8,128)(2,1)S(1)}, bf16[512,768]{1,0:T(8,128)(2,1)S(1)}, f32[8,768]{1,0:T(8,128)S(1)}) custom-call(bf16[128,768]{1,0:T(8,128)(2,1)S(1)} %collective-permute-done.10.got_a, bf16[128,768]{1,0:T(8,128)(2,1)S(1)} %collective-permute-done.11.got_b, ...), custom_call_target="tpu_custom_call" | custom-call | tf_op jit(solution)/shard_map/back_far/pallas_call | solution.py:485
  100.9 2.9 %collective-permute-start.14 = (bf16[128,768]{1,0:T(8,128)(2,1)S(1)}, bf16[128,768]{1,0:T(8,128)(2,1)S(1)}, u32[]{:S(2)}, u32[]{:S(2)}) collective-permute-start(bf16[128,768]{1,0:T(8,128)(2,1)S(1)} %get-tuple-element.115), channel_id=1, source_target_pairs={{0,48},{8,56},{16,0},{24,8},{32,16},{40,24},{48,32},{56,40},{64,11... | collective-permute-start | bytes 589832 | tf_op jit(solution)/shard_map/ppermute | solution.py:810
  104.7 2.1 pack.1
  108.3 2.4 %collective-permute-done.15.far_b = bf16[128,768]{1,0:T(8,128)(2,1)S(1)} collective-permute-done((bf16[128,768]{1,0:T(8,128)(2,1)S(1)}, bf16[128,768]{1,0:T(8,128)(2,1)S(1)}, u32[]{:S(2)}, u32[]{:S(2)}) %collective-permute-start.15) | collective-permute-done | bytes 196640 | tf_op jit(solution)/shard_map/ppermute | solution.py:807
  111.4 8.9 %all-to-all-start.1 = ((bf16[128,10,8,128]{3,2,1,0:T(8,128)(2,1)}), bf16[128,10,8,128]{3,2,1,0:T(8,128)(2,1)S(1)}, u32[]{:S(2)}, u32[]{:S(2)}) async-start(bf16[128,10,8,128]{3,2,1,0:T(8,128)(2,1)} %bitcast.5), calls=%async_computation.1 | async-start | bytes 5242880 | tf_op jit(solution)/shard_map/all_to_all | solution.py:813
  120.3 1.4 collective-permute-start.9
  121.7 1.6 collective-permute-done.9.near
  123.2 1.3 copy-done.2
  124.5 1.3 copy-done.4
  126.8 1.4 copy-done.9
  141.0 6.6 %attend_back.1 = (f32[256,768]{1,0:T(8,128)}, bf16[640,8,128]{2,1,0:T(8,128)(2,1)S(1)}, bf16[640,8,128]{2,1,0:T(8,128)(2,1)S(1)}) custom-call(s32[2]{0:T(128)S(1)} %pad_add_fusion.place, f32[256,768]{1,0:T(8,128)S(1)} %copy-done.17, bf16[256,768]{1,0:T(8,128)(2,1)S(1)} %collective-permute-done.9.near, bf16[128,768]{1,0:T(8,128)(2,1)S(1)} %copy-done.38, ...), custom_call_target="tpu_custom_call" | custom-call | tf_op jit(solution)/shard_map/attend_back/pallas_call | solution.py:604
  148.0 2.7 %collective-permute-done.16 = bf16[640,8,128]{2,1,0:T(8,128)(2,1)S(1)} collective-permute-done((bf16[640,8,128]{2,1,0:T(8,128)(2,1)S(1)}, bf16[640,8,128]{2,1,0:T(8,128)(2,1)S(1)}, u32[]{:S(2)}, u32[]{:S(2)}) %collective-permute-start.16) | collective-permute-done | bytes 1310752 | tf_op jit(solution)/shard_map/ppermute | solution.py:804
  150.7 1.4 add_convert_fusion
  152.1 2.2 all-to-all-done.1.got
  155.6 27.0 %all_to_all.20.got = bf16[128,5,8,128]{3,2,1,0:T(8,128)(2,1)S(1)} all-to-all(bf16[128,5,8,128]{3,2,1,0:T(8,128)(2,1)S(1)} %bitcast.35), channel_id=1, replica_groups=mesh['dp'=16,'tensor'=8] {'dp','tensor'}, dimensions={0} | all-to-all | bytes 2621440 | tf_op jit(solution)/shard_map/all_to_all | solution.py:813
  182.7 1.3 sum_rest.1
  184.0 5.7 %all-to-all-start.3 = ((bf16[128,5,8,128]{3,2,1,0:T(8,128)(2,1)}), bf16[128,5,8,128]{3,2,1,0:T(8,128)(2,1)S(1)}, u32[]{:S(2)}, u32[]{:S(2)}) async-start(bf16[128,5,8,128]{3,2,1,0:T(8,128)(2,1)} %sum_rest.1), calls=%async_computation.3 | async-start | bytes 2621440 | tf_op jit(solution)/shard_map/all_to_all | solution.py:813
  189.7 3.6 %collective-permute-start.24 = (bf16[4,10,8,128]{3,2,1,0:T(8,128)(2,1)S(1)}, bf16[4,10,8,128]{3,2,1,0:T(8,128)(2,1)S(1)}, u32[]{:S(2)}, u32[]{:S(2)}) collective-permute-start(bf16[4,10,8,128]{3,2,1,0:T(8,128)(2,1)S(1)} %sum_ffn.1), channel_id=1, source_target_pairs={{0,112},{8,120},{16,64},{24,72},{32,80},{40,88},{48,96},{56,104},{... | collective-permute-start | bytes 245768 | tf_op jit(solution)/shard_map/ppermute | solution.py:870
  193.8 1.5 collective-permute-start.22
  195.6 1.5 collective-permute-start.18
  197.1 8.1 %collective-permute-done.18 = bf16[4,10,8,128]{3,2,1,0:T(8,128)(2,1)S(1)} collective-permute-done((bf16[4,10,8,128]{3,2,1,0:T(8,128)(2,1)S(1)}, bf16[4,10,8,128]{3,2,1,0:T(8,128)(2,1)S(1)}, u32[]{:S(2)}, u32[]{:S(2)}) %collective-permute-start.18) | collective-permute-done | bytes 81952 | tf_op jit(solution)/shard_map/ppermute | solution.py:870
  205.3 2.9 %collective-permute-start.19 = (bf16[4,10,8,128]{3,2,1,0:T(8,128)(2,1)S(1)}, bf16[4,10,8,128]{3,2,1,0:T(8,128)(2,1)S(1)}, u32[]{:S(2)}, u32[]{:S(2)}) collective-permute-start(bf16[4,10,8,128]{3,2,1,0:T(8,128)(2,1)S(1)} %sum_ffn.1), channel_id=1, source_target_pairs={{0,32},{8,40},{16,48},{24,56},{32,0},{40,8},{48,16},{56,24},{64,96... | collective-permute-start | bytes 245768 | tf_op jit(solution)/shard_map/ppermute | solution.py:870
  208.2 6.1 %collective-permute-done.19 = bf16[4,10,8,128]{3,2,1,0:T(8,128)(2,1)S(1)} collective-permute-done((bf16[4,10,8,128]{3,2,1,0:T(8,128)(2,1)S(1)}, bf16[4,10,8,128]{3,2,1,0:T(8,128)(2,1)S(1)}, u32[]{:S(2)}, u32[]{:S(2)}) %collective-permute-start.19) | collective-permute-done | bytes 81952 | tf_op jit(solution)/shard_map/ppermute | solution.py:870
  214.5 3.1 %collective-permute-done.20 = bf16[4,10,8,128]{3,2,1,0:T(8,128)(2,1)S(1)} collective-permute-done((bf16[4,10,8,128]{3,2,1,0:T(8,128)(2,1)S(1)}, bf16[4,10,8,128]{3,2,1,0:T(8,128)(2,1)S(1)}, u32[]{:S(2)}, u32[]{:S(2)}) %collective-permute-start.20) | collective-permute-done | bytes 81952 | tf_op jit(solution)/shard_map/ppermute | solution.py:870
  217.7 2.4 %collective-permute-start.17 = (bf16[640,8,128]{2,1,0:T(8,128)(2,1)S(1)}, bf16[640,8,128]{2,1,0:T(8,128)(2,1)S(1)}, u32[]{:S(2)}, u32[]{:S(2)}) collective-permute-start(bf16[640,8,128]{2,1,0:T(8,128)(2,1)S(1)} %bitcast.32), channel_id=1, source_target_pairs={{0,8},{8,0},{16,24},{24,16},{32,40},{40,32},{48,56},{56,48},{64,72... | collective-permute-start | bytes 3932168 | tf_op jit(solution)/shard_map/ppermute | solution.py:804
  220.3 3.4 %collective-permute-done.25.ffn_oth.bias_oth = bf16[8,4,10,8,128]{4,3,2,1,0:T(8,128)(2,1)S(1)} collective-permute-done((bf16[8,4,10,8,128]{4,3,2,1,0:T(8,128)(2,1)S(1)}, bf16[8,4,10,8,128]{4,3,2,1,0:T(8,128)(2,1)S(1)}, u32[]{:S(2)}, u32[]{:S(2)}) %collective-permute-start.25) | collective-permute-done | bytes 655392 | tf_op jit(solution)/shard_map/ppermute | solution.py:804
  223.7 5.3 %final.1 = (f32[768,768]{1,0:T(8,128)}, f32[768]{0:T(1024)}, f32[65,768]{1,0:T(8,128)}, f32[768,768]{1,0:T(8,128)}, f32[768]{0:T(1024)}, /*index=5*/f32[768]{0:T...) custom-call(s32[2]{0:T(128)S(1)} %pad_add_fusion.place, ...), custom_call_target="tpu_custom_call" | custom-call | tf_op jit(solution)/shard_map/final/pallas_call | solution.py:753
  (167 shorter events, 44.9 us)
Async XLA Ops:
  4.9 1.5 copy-start
  6.4 11.5 %copy-start.52 = (bf16[768]{0:T(1024)(128)(2,1)S(1)}, bf16[768]{0:T(1024)(128)(2,1)}, u32[]{:S(2)}) copy-start(bf16[768]{0:T(1024)(128)(2,1)} %param.25) | copy-start | bytes 4612
  6.4 11.6 %copy-start.53 = (bf16[768]{0:T(1024)(128)(2,1)S(1)}, bf16[768]{0:T(1024)(128)(2,1)}, u32[]{:S(2)}) copy-start(bf16[768]{0:T(1024)(128)(2,1)} %param.26) | copy-start | bytes 4612
  6.4 11.6 %copy-start.54 = (bf16[768]{0:T(1024)(128)(2,1)S(1)}, bf16[768]{0:T(1024)(128)(2,1)}, u32[]{:S(2)}) copy-start(bf16[768]{0:T(1024)(128)(2,1)} %param.21) | copy-start | bytes 4612
  6.4 11.6 %copy-start.55 = (bf16[768]{0:T(1024)(128)(2,1)S(1)}, bf16[768]{0:T(1024)(128)(2,1)}, u32[]{:S(2)}) copy-start(bf16[768]{0:T(1024)(128)(2,1)} %param.24) | copy-start | bytes 4612
  6.4 11.6 %copy-start.48 = (s32[256]{0:T(256)S(1)}, s32[256]{0:T(256)}, u32[]{:S(2)}) copy-start(s32[256]{0:T(256)} %param.35) | copy-start | bytes 3076
  6.4 53.0 %all-to-all-start = ((bf16[128,10,8,128]{3,2,1,0:T(8,128)(2,1)}), bf16[128,10,8,128]{3,2,1,0:T(8,128)(2,1)S(1)}, u32[]{:S(2)}, u32[]{:S(2)}) async-start(bf16[128,10,8,128]{3,2,1,0:T(8,128)(2,1)} %copy-done), calls=%async_computation | async-start | bytes 5242880 | tf_op jit(solution)/shard_map/all_to_all | solution.py:813
  18.0 1.3 copy-start.1
  19.3 1.3 copy-start.3
  45.6 11.1 %copy-start.10 = (f32[256,768]{1,0:T(8,128)}, f32[256,768]{1,0:T(8,128)S(1)}, u32[]{:S(2)}) copy-start(f32[256,768]{1,0:T(8,128)S(1)} %get-tuple-element.123.scl) | copy-start | bytes 2359300
  45.6 8.8 %collective-permute-start.1 = (bf16[128,768]{1,0:T(8,128)(2,1)S(1)}, bf16[128,768]{1,0:T(8,128)(2,1)S(1)}, u32[]{:S(2)}, u32[]{:S(2)}) collective-permute-start(bf16[128,768]{1,0:T(8,128)(2,1)S(1)} %get-tuple-element.85), channel_id=1, source_target_pairs={{0,16},{8,24},{16,32},{24,40},{32,48},{40,56},{48,0},{56,8},{64,80... | collective-permute-start | bytes 589832 | tf_op jit(solution)/shard_map/ppermute | solution.py:807
  47.0 7.4 %collective-permute-start.2 = (bf16[128,768]{1,0:T(8,128)(2,1)S(1)}, bf16[128,768]{1,0:T(8,128)(2,1)S(1)}, u32[]{:S(2)}, u32[]{:S(2)}) collective-permute-start(bf16[128,768]{1,0:T(8,128)(2,1)S(1)} %get-tuple-element.86), channel_id=1, source_target_pairs={{0,48},{8,56},{16,0},{24,8},{32,16},{40,24},{48,32},{56,40},{64,11... | collective-permute-start | bytes 589832 | tf_op jit(solution)/shard_map/ppermute | solution.py:810
  55.8 2.8 %collective-permute-start.3 = (bf16[256,768]{1,0:T(8,128)(2,1)S(1)}, bf16[256,768]{1,0:T(8,128)(2,1)S(1)}, u32[]{:S(2)}, u32[]{:S(2)}) collective-permute-start(bf16[256,768]{1,0:T(8,128)(2,1)S(1)} %pad_maximum_fusion), channel_id=1, source_target_pairs={{0,8},{8,0},{16,24},{24,16},{32,40},{40,32},{48,56},{56,48},{64,72... | collective-permute-start | bytes 1179656 | tf_op jit(solution)/shard_map/ppermute | solution.py:804
  56.7 10.2 %collective-permute-start = (bf16[256,768]{1,0:T(8,128)(2,1)}, bf16[256,768]{1,0:T(8,128)(2,1)}, u32[]{:S(2)}, u32[]{:S(2)}) collective-permute-start(bf16[256,768]{1,0:T(8,128)(2,1)} %get-tuple-element.84.own), channel_id=1, source_target_pairs={{0,8},{8,0},{16,24},{24,16},{32,40},{40,32},{48,56},{56,48},{64,72... | collective-permute-start | bytes 1179656 | tf_op jit(solution)/shard_map/ppermute | solution.py:804
  66.4 5.7 %collective-permute-start.5 = (bf16[256,768]{1,0:T(8,128)(2,1)S(1)}, bf16[256,768]{1,0:T(8,128)(2,1)S(1)}, u32[]{:S(2)}, u32[]{:S(2)}) collective-permute-start(bf16[256,768]{1,0:T(8,128)(2,1)S(1)} %get-tuple-element.92), channel_id=1, source_target_pairs={{0,8},{8,0},{16,24},{24,16},{32,40},{40,32},{48,56},{56,48},{64,72... | collective-permute-start | bytes 1179656 | tf_op jit(solution)/shard_map/ppermute | solution.py:804
  66.9 6.9 %copy-start.56 = (bf16[768]{0:T(1024)(128)(2,1)S(1)}, bf16[768]{0:T(1024)(128)(2,1)}, u32[]{:S(2)}) copy-start(bf16[768]{0:T(1024)(128)(2,1)} %param.30) | copy-start | bytes 4612
  66.9 6.9 %copy-start.57 = (bf16[768]{0:T(1024)(128)(2,1)S(1)}, bf16[768]{0:T(1024)(128)(2,1)}, u32[]{:S(2)}) copy-start(bf16[768]{0:T(1024)(128)(2,1)} %param.31) | copy-start | bytes 4612
  66.9 6.9 %copy-start.58 = (bf16[768]{0:T(1024)(128)(2,1)S(1)}, bf16[768]{0:T(1024)(128)(2,1)}, u32[]{:S(2)}) copy-start(bf16[768]{0:T(1024)(128)(2,1)} %param.32) | copy-start | bytes 4612
  66.9 13.8 %copy-start.30 = (bf16[256,768]{1,0:T(8,128)(2,1)S(1)}, bf16[256,768]{1,0:T(8,128)(2,1)}, u32[]{:S(2)}) copy-start(bf16[256,768]{1,0:T(8,128)(2,1)} %og.1) | copy-start | bytes 1179652
  71.9 1.9 collective-permute-start.4
  72.2 6.2 %collective-permute-start.6 = (bf16[128,768]{1,0:T(8,128)(2,1)S(1)}, bf16[128,768]{1,0:T(8,128)(2,1)S(1)}, u32[]{:S(2)}, u32[]{:S(2)}) collective-permute-start(bf16[128,768]{1,0:T(8,128)(2,1)S(1)} %get-tuple-element.93), channel_id=1, source_target_pairs={{0,48},{8,56},{16,0},{24,8},{32,16},{40,24},{48,32},{56,40},{64,11... | collective-permute-start | bytes 589832 | tf_op jit(solution)/shard_map/ppermute | solution.py:810
  73.7 7.0 %collective-permute-start.7 = (bf16[128,768]{1,0:T(8,128)(2,1)S(1)}, bf16[128,768]{1,0:T(8,128)(2,1)S(1)}, u32[]{:S(2)}, u32[]{:S(2)}) collective-permute-start(bf16[128,768]{1,0:T(8,128)(2,1)S(1)} %get-tuple-element.94), channel_id=1, source_target_pairs={{0,16},{8,24},{16,32},{24,40},{32,48},{40,56},{48,0},{56,8},{64,80... | collective-permute-start | bytes 589832 | tf_op jit(solution)/shard_map/ppermute | solution.py:807
  82.3 11.8 %copy-start.14 = (f32[256,768]{1,0:T(8,128)}, f32[256,768]{1,0:T(8,128)S(1)}, u32[]{:S(2)}) copy-start(f32[256,768]{1,0:T(8,128)S(1)} %get-tuple-element.119.second) | copy-start | bytes 2359300
  82.3 11.9 %copy-start.46 = (f32[8,768]{1,0:T(8,128)}, f32[8,768]{1,0:T(8,128)S(1)}, u32[]{:S(2)}) copy-start(f32[8,768]{1,0:T(8,128)S(1)} %get-tuple-element.131.sums) | copy-start | bytes 73732
  82.3 6.1 %collective-permute-start.10 = (bf16[128,768]{1,0:T(8,128)(2,1)S(1)}, bf16[128,768]{1,0:T(8,128)(2,1)S(1)}, u32[]{:S(2)}, u32[]{:S(2)}) collective-permute-start(bf16[128,768]{1,0:T(8,128)(2,1)S(1)} %get-tuple-element.102), channel_id=1, source_target_pairs={{0,16},{8,24},{16,32},{24,40},{32,48},{40,56},{48,0},{56,8},{64,80... | collective-permute-start | bytes 589832 | tf_op jit(solution)/shard_map/ppermute | solution.py:807
  82.3 6.1 %collective-permute-start.11 = (bf16[128,768]{1,0:T(8,128)(2,1)S(1)}, bf16[128,768]{1,0:T(8,128)(2,1)S(1)}, u32[]{:S(2)}, u32[]{:S(2)}) collective-permute-start(bf16[128,768]{1,0:T(8,128)(2,1)S(1)} %get-tuple-element.103), channel_id=1, source_target_pairs={{0,48},{8,56},{16,0},{24,8},{32,16},{40,24},{48,32},{56,40},{64,11... | collective-permute-start | bytes 589832 | tf_op jit(solution)/shard_map/ppermute | solution.py:810
  85.0 6.0 %collective-permute-start.8 = (bf16[256,768]{1,0:T(8,128)(2,1)S(1)}, bf16[256,768]{1,0:T(8,128)(2,1)S(1)}, u32[]{:S(2)}, u32[]{:S(2)}) collective-permute-start(bf16[256,768]{1,0:T(8,128)(2,1)S(1)} %get-tuple-element.96.own), channel_id=1, source_target_pairs={{0,8},{8,0},{16,24},{24,16},{32,40},{40,32},{48,56},{56,48},{64,72... | collective-permute-start | bytes 1179656 | tf_op jit(solution)/shard_map/ppermute | solution.py:804
  88.4 6.6 %collective-permute-start.12 = (bf16[256,768]{1,0:T(8,128)(2,1)S(1)}, bf16[256,768]{1,0:T(8,128)(2,1)S(1)}, u32[]{:S(2)}, u32[]{:S(2)}) collective-permute-start(bf16[256,768]{1,0:T(8,128)(2,1)S(1)} %pad_maximum_fusion.1), channel_id=1, source_target_pairs={{0,8},{8,0},{16,24},{24,16},{32,40},{40,32},{48,56},{56,48},{64,72... | collective-permute-start | bytes 1179656 | tf_op jit(solution)/shard_map/ppermute | solution.py:804
  95.0 3.2 %copy-start.50 = (bf16[256,768]{1,0:T(8,128)(2,1)}, bf16[256,768]{1,0:T(8,128)(2,1)S(1)}, u32[]{:S(2)}) copy-start(bf16[256,768]{1,0:T(8,128)(2,1)S(1)} %get-tuple-element.99) | copy-start | bytes 1179652
  98.2 2.6 %collective-permute-start.13 = (bf16[256,768]{1,0:T(8,128)(2,1)S(1)}, bf16[256,768]{1,0:T(8,128)(2,1)S(1)}, u32[]{:S(2)}, u32[]{:S(2)}) collective-permute-start(bf16[256,768]{1,0:T(8,128)(2,1)S(1)} %get-tuple-element.114), channel_id=1, source_target_pairs={{0,8},{8,0},{16,24},{24,16},{32,40},{40,32},{48,56},{56,48},{64,72... | collective-permute-start | bytes 1179656 | tf_op jit(solution)/shard_map/ppermute | solution.py:804
  100.9 6.7 %collective-permute-start.14 = (bf16[128,768]{1,0:T(8,128)(2,1)S(1)}, bf16[128,768]{1,0:T(8,128)(2,1)S(1)}, u32[]{:S(2)}, u32[]{:S(2)}) collective-permute-start(bf16[128,768]{1,0:T(8,128)(2,1)S(1)} %get-tuple-element.115), channel_id=1, source_target_pairs={{0,48},{8,56},{16,0},{24,8},{32,16},{40,24},{48,32},{56,40},{64,11... | collective-permute-start | bytes 589832 | tf_op jit(solution)/shard_map/ppermute | solution.py:810
  103.8 6.9 %collective-permute-start.15 = (bf16[128,768]{1,0:T(8,128)(2,1)S(1)}, bf16[128,768]{1,0:T(8,128)(2,1)S(1)}, u32[]{:S(2)}, u32[]{:S(2)}) collective-permute-start(bf16[128,768]{1,0:T(8,128)(2,1)S(1)} %get-tuple-element.116), channel_id=1, source_target_pairs={{0,16},{8,24},{16,32},{24,40},{32,48},{40,56},{48,0},{56,8},{64,80... | collective-permute-start | bytes 589832 | tf_op jit(solution)/shard_map/ppermute | solution.py:807
  111.4 42.9 %all-to-all-start.1 = ((bf16[128,10,8,128]{3,2,1,0:T(8,128)(2,1)}), bf16[128,10,8,128]{3,2,1,0:T(8,128)(2,1)S(1)}, u32[]{:S(2)}, u32[]{:S(2)}) async-start(bf16[128,10,8,128]{3,2,1,0:T(8,128)(2,1)} %bitcast.5), calls=%async_computation.1 | async-start | bytes 5242880 | tf_op jit(solution)/shard_map/all_to_all | solution.py:813
  120.3 2.9 %collective-permute-start.9 = (bf16[256,768]{1,0:T(8,128)(2,1)}, bf16[256,768]{1,0:T(8,128)(2,1)S(1)}, u32[]{:S(2)}, u32[]{:S(2)}) collective-permute-start(bf16[256,768]{1,0:T(8,128)(2,1)} %copy-done.50), channel_id=1, source_target_pairs={{0,8},{8,0},{16,24},{24,16},{32,40},{40,32},{48,56},{56,48},{64,72... | collective-permute-start | bytes 1179656 | tf_op jit(solution)/shard_map/ppermute | solution.py:804
  123.2 1.3 copy-start.2
  126.8 1.4 copy-start.9
  147.7 3.0 %collective-permute-start.16 = (bf16[640,8,128]{2,1,0:T(8,128)(2,1)S(1)}, bf16[640,8,128]{2,1,0:T(8,128)(2,1)S(1)}, u32[]{:S(2)}, u32[]{:S(2)}) collective-permute-start(bf16[640,8,128]{2,1,0:T(8,128)(2,1)S(1)} %get-tuple-element.134), channel_id=1, source_target_pairs={{0,8},{8,0},{16,24},{24,16},{32,40},{40,32},{48,56},{56,48},{64,72... | collective-permute-start | bytes 3932168 | tf_op jit(solution)/shard_map/ppermute | solution.py:804
  154.3 1.3 copy-start.51
  184.0 33.6 %all-to-all-start.3 = ((bf16[128,5,8,128]{3,2,1,0:T(8,128)(2,1)}), bf16[128,5,8,128]{3,2,1,0:T(8,128)(2,1)S(1)}, u32[]{:S(2)}, u32[]{:S(2)}) async-start(bf16[128,5,8,128]{3,2,1,0:T(8,128)(2,1)} %sum_rest.1), calls=%async_computation.3 | async-start | bytes 2621440 | tf_op jit(solution)/shard_map/all_to_all | solution.py:813
  189.7 30.5 %collective-permute-start.24 = (bf16[4,10,8,128]{3,2,1,0:T(8,128)(2,1)S(1)}, bf16[4,10,8,128]{3,2,1,0:T(8,128)(2,1)S(1)}, u32[]{:S(2)}, u32[]{:S(2)}) collective-permute-start(bf16[4,10,8,128]{3,2,1,0:T(8,128)(2,1)S(1)} %sum_ffn.1), channel_id=1, source_target_pairs={{0,112},{8,120},{16,64},{24,72},{32,80},{40,88},{48,96},{56,104},{... | collective-permute-start | bytes 245768 | tf_op jit(solution)/shard_map/ppermute | solution.py:870
  193.3 26.8 %collective-permute-start.23 = (bf16[4,10,8,128]{3,2,1,0:T(8,128)(2,1)S(1)}, bf16[4,10,8,128]{3,2,1,0:T(8,128)(2,1)S(1)}, u32[]{:S(2)}, u32[]{:S(2)}) collective-permute-start(bf16[4,10,8,128]{3,2,1,0:T(8,128)(2,1)S(1)} %sum_ffn.1), channel_id=1, source_target_pairs={{0,96},{8,104},{16,112},{24,120},{32,64},{40,72},{48,80},{56,88},{... | collective-permute-start | bytes 245768 | tf_op jit(solution)/shard_map/ppermute | solution.py:870
  193.8 26.3 %collective-permute-start.22 = (bf16[4,10,8,128]{3,2,1,0:T(8,128)(2,1)S(1)}, bf16[4,10,8,128]{3,2,1,0:T(8,128)(2,1)S(1)}, u32[]{:S(2)}, u32[]{:S(2)}) collective-permute-start(bf16[4,10,8,128]{3,2,1,0:T(8,128)(2,1)S(1)} %sum_ffn.1), channel_id=1, source_target_pairs={{0,80},{8,88},{16,96},{24,104},{32,112},{40,120},{48,64},{56,72},{... | collective-permute-start | bytes 245768 | tf_op jit(solution)/shard_map/ppermute | solution.py:870
  195.3 22.3 %collective-permute-start.21 = (bf16[4,10,8,128]{3,2,1,0:T(8,128)(2,1)S(1)}, bf16[4,10,8,128]{3,2,1,0:T(8,128)(2,1)S(1)}, u32[]{:S(2)}, u32[]{:S(2)}) collective-permute-start(bf16[4,10,8,128]{3,2,1,0:T(8,128)(2,1)S(1)} %sum_ffn.1), channel_id=1, source_target_pairs={{0,64},{8,72},{16,80},{24,88},{32,96},{40,104},{48,112},{56,120},{... | collective-permute-start | bytes 245768 | tf_op jit(solution)/shard_map/ppermute | solution.py:870
  195.6 9.7 %collective-permute-start.18 = (bf16[4,10,8,128]{3,2,1,0:T(8,128)(2,1)S(1)}, bf16[4,10,8,128]{3,2,1,0:T(8,128)(2,1)S(1)}, u32[]{:S(2)}, u32[]{:S(2)}) collective-permute-start(bf16[4,10,8,128]{3,2,1,0:T(8,128)(2,1)S(1)} %sum_ffn.1), channel_id=1, source_target_pairs={{0,16},{8,24},{16,32},{24,40},{32,48},{40,56},{48,0},{56,8},{64,80... | collective-permute-start | bytes 245768 | tf_op jit(solution)/shard_map/ppermute | solution.py:870
  205.3 9.0 %collective-permute-start.19 = (bf16[4,10,8,128]{3,2,1,0:T(8,128)(2,1)S(1)}, bf16[4,10,8,128]{3,2,1,0:T(8,128)(2,1)S(1)}, u32[]{:S(2)}, u32[]{:S(2)}) collective-permute-start(bf16[4,10,8,128]{3,2,1,0:T(8,128)(2,1)S(1)} %sum_ffn.1), channel_id=1, source_target_pairs={{0,32},{8,40},{16,48},{24,56},{32,0},{40,8},{48,16},{56,24},{64,96... | collective-permute-start | bytes 245768 | tf_op jit(solution)/shard_map/ppermute | solution.py:870
  214.3 3.3 %collective-permute-start.20 = (bf16[4,10,8,128]{3,2,1,0:T(8,128)(2,1)S(1)}, bf16[4,10,8,128]{3,2,1,0:T(8,128)(2,1)S(1)}, u32[]{:S(2)}, u32[]{:S(2)}) collective-permute-start(bf16[4,10,8,128]{3,2,1,0:T(8,128)(2,1)S(1)} %sum_ffn.1), channel_id=1, source_target_pairs={{0,48},{8,56},{16,0},{24,8},{32,16},{40,24},{48,32},{56,40},{64,11... | collective-permute-start | bytes 245768 | tf_op jit(solution)/shard_map/ppermute | solution.py:870
  217.7 6.0 %collective-permute-start.17 = (bf16[640,8,128]{2,1,0:T(8,128)(2,1)S(1)}, bf16[640,8,128]{2,1,0:T(8,128)(2,1)S(1)}, u32[]{:S(2)}, u32[]{:S(2)}) collective-permute-start(bf16[640,8,128]{2,1,0:T(8,128)(2,1)S(1)} %bitcast.32), channel_id=1, source_target_pairs={{0,8},{8,0},{16,24},{24,16},{32,40},{40,32},{48,56},{56,48},{64,72... | collective-permute-start | bytes 3932168 | tf_op jit(solution)/shard_map/ppermute | solution.py:804
  220.2 3.5 %collective-permute-start.25 = (bf16[8,4,10,8,128]{4,3,2,1,0:T(8,128)(2,1)S(1)}, bf16[8,4,10,8,128]{4,3,2,1,0:T(8,128)(2,1)S(1)}, u32[]{:S(2)}, u32[]{:S(2)}) collective-permute-start(bf16[8,4,10,8,128]{4,3,2,1,0:T(8,128)(2,1)S(1)} %bitcast_dynamic-update-slice_fusion.ffn_own.bias_own), channel_id=1, source_target_pairs={{0,8},{8,0},{16,24},{24,16},{32,40},{40,32},{48,56},{56,48},{64,72... | collective-permute-start | bytes 1966088 | tf_op jit(solution)/shard_map/ppermute | solution.py:804
  (40 other events, 36.3 us)

commit v3 on v2

--- a/solution.py
+++ b/solution.py
@@ -23,6 +23,7 @@
 PIECE = 24
 PIECES = SUB // PIECE
 UNITS = 10
+GRAD_UNITS = 9
 HIDDEN = 768
 HALF = ROWS // 2
 TALL = 848
@@ -36,6 +37,7 @@
 
 VMEM = pl.BlockSpec(memory_space=pltpu.VMEM)
 SMEM = pl.BlockSpec(memory_space=pltpu.SMEM)
+HBM = pl.BlockSpec(memory_space=pltpu.HBM)
 
 
 def shape(dims, dtype):
@@ -76,56 +78,156 @@
     ) * inv
 
 
-def prep_kernel(place, up_ref, down_ref, bias_ref, out_ref, tall, cols, piece):
+class Staged:
+    def __init__(self, ref, buf, sem, incoming):
+        pair = (ref, buf) if incoming else (buf, ref)
+        self.buf = buf
+        self.copy = pltpu.make_async_copy(*pair, sem)
+        self.incoming = incoming
+        self.pending = True
+        if incoming:
+            self.copy.start()
+
+    def ready(self):
+        if self.pending:
+            self.copy.wait()
+            self.pending = False
+
+    def leave(self):
+        if self.pending:
+            self.copy.start()
+            self.pending = False
+
+    def __getitem__(self, index):
+        if self.incoming:
+            self.ready()
+        return self.buf[index]
+
+    def __setitem__(self, index, value):
+        self.buf[index] = value
+
+
+def staged_call(kernel, name, mib, ins, outs, scratch=()):
+    spec = {"smem": SMEM, "vmem": VMEM, "hbm": HBM}
+    arrays = [a for _, a in ins]
+    kinds = [k for k, _ in ins] + [k for k, _ in outs]
+    avals = arrays + [o for _, o in outs]
+    staged = [i for i, k in enumerate(kinds) if k == "hbm"]
+    n_in = len(ins)
+
+    if not staged:
+        return pl.pallas_call(
+            kernel,
+            out_shape=tuple(o for _, o in outs),
+            in_specs=[spec[k] for k, _ in ins],
+            out_specs=tuple(spec[k] for k, _ in outs),
+            scratch_shapes=list(scratch),
+            compiler_params=params(mib),
+            name=name,
+        )(*arrays)
+
+    def run(*refs):
+        refs = list(refs)
+        sems = refs.pop()
+        split = len(refs) - len(staged)
+        bufs = refs[split:]
+        refs = refs[:split]
+        for n, i in enumerate(staged):
+            refs[i] = Staged(refs[i], bufs[n], sems.at[n], i < n_in)
+        kernel(*refs)
+        for i in staged:
+            if i < n_in:
+                refs[i].ready()
+            else:
+                refs[i].leave()
+        for i in staged:
+            if i >= n_in:
+                refs[i].copy.wait()
+
+    buffers = [pltpu.VMEM(avals[i].shape, avals[i].dtype) for i in staged]
+    arrays = [
+        pltpu.with_memory_space_constraint(a, pltpu.HBM) if k == "hbm" else a for k, a in ins
+    ]
+    return pl.pallas_call(
+        run,
+        out_shape=tuple(pltpu.HBM(o.shape, o.dtype) if k == "hbm" else o for k, o in outs),
+        in_specs=[spec[k] for k, _ in ins],
+        out_specs=tuple(spec[k] for k, _ in outs),
+        scratch_shapes=[*scratch, *buffers, pltpu.SemaphoreType.DMA((len(staged),))],
+        compiler_params=params(mib),
+        name=name,
+    )(*arrays)
+
+
+def prep_kernel(place, up_ref, down_ref, bias_ref, out_ref, up, down, tall, cols, block, sems):
     rep = place[0] % 8
     side = rep % 2
 
-    @pl.when(pl.program_id(0) == 0)
+    @pl.when(place[0] < 8)
     def _():
-        @pl.when(place[0] < 8)
-        def _():
-            tall[...] = up_ref[...].astype(f32).T
-            cols[...] = jnp.broadcast_to(bias_ref[...].astype(f32), (8, 384)).T
-
-        @pl.when(place[0] >= 8)
-        def _():
-            tall[...] = down_ref[...].astype(f32)
-            cols[...] = jnp.zeros(cols.shape, f32)
-
-        for q in range(CLASSES):
-            start = pl.multiple_of(SUB * q + PIECE * (rep // 2), 8)
-            rows = tall[pl.ds(start, PIECE), :]
+        copy = pltpu.make_async_copy(up_ref, up, sems.at[0])
+        copy.start()
+        cols[...] = jnp.broadcast_to(bias_ref[...].astype(f32), (8, 384)).T
+        copy.wait()
+        tall[...] = up[...].astype(f32).T
+
+    @pl.when(place[0] >= 8)
+    def _():
+        copy = pltpu.make_async_copy(down_ref, down, sems.at[0])
+        copy.start()
+        cols[...] = jnp.zeros(cols.shape, f32)
+        copy.wait()
+        tall[...] = down[...].astype(f32)
+
+    for q in range(CLASSES):
+        start = pl.multiple_of(SUB * q + PIECE * (rep // 2), 8)
+        rows = tall[pl.ds(start, PIECE), :]
+        piece = []
+        for j in range(3):
+            left = rows[:, j * 128 : j * 128 + 128]
+            right = rows[:, 384 + j * 128 : 512 + j * 128]
+            piece.append(jnp.where(side == 0, left, right).reshape(3, 8, 128).astype(bf16))
+        bias = jnp.zeros((8, 128), f32)
+        for rt in range(3):
+            col = cols[pl.ds(pl.multiple_of(start + 8 * rt, 8), 8), :][:, 0:1]
+            bias = jnp.where(lanes((8, 128)) == rt, jnp.broadcast_to(col, (8, 128)), bias)
+        bias = jnp.where(side == 0, bias, 0.0).astype(bf16)
+        for n in range(8):
             for j in range(3):
-                left = rows[:, j * 128 : j * 128 + 128]
-                right = rows[:, 384 + j * 128 : 512 + j * 128]
-                part = jnp.where(side == 0, left, right).reshape(3, 8, 128)
-                piece[q, 3 * j : 3 * j + 3] = part.astype(bf16)
-            bias = jnp.zeros((8, 128), f32)
-            for rt in range(3):
-                col = cols[pl.ds(pl.multiple_of(start + 8 * rt, 8), 8), :][:, 0:1]
-                bias = jnp.where(lanes((8, 128)) == rt, jnp.broadcast_to(col, (8, 128)), bias)
-            piece[q, UNITS - 1] = jnp.where(side == 0, bias, 0.0).astype(bf16)
-
-    for n in range(32):
-        out_ref[n] = piece[n // 8]
+                block[q * 8 + n, 3 * j : 3 * j + 3] = piece[j]
+            block[q * 8 + n, UNITS - 1] = bias
+    copies = [
+        pltpu.make_async_copy(block, out_ref.at[32 * i : 32 * i + 32], sems.at[1 + i])
+        for i in range(4)
+    ]
+    for copy in copies:
+        copy.start()
+    for copy in copies:
+        copy.wait()
 
 
 def prep(place, w_up, w_down, b_up):
-    whole = lambda *dims: pl.BlockSpec(dims, lambda i: (0,) * len(dims))
     return pl.pallas_call(
         prep_kernel,
-        grid=(4,),
-        out_shape=shape((128, UNITS, 8, 128), bf16),
-        in_specs=[SMEM, whole(768, 384), whole(384, 768), whole(1, 384)],
-        out_specs=pl.BlockSpec((32, UNITS, 8, 128), lambda i: (i, 0, 0, 0)),
+        out_shape=pltpu.HBM((128, UNITS, 8, 128), bf16),
+        in_specs=[SMEM, HBM, HBM, VMEM],
+        out_specs=HBM,
         scratch_shapes=[
+            pltpu.VMEM((768, 384), bf16),
+            pltpu.VMEM((384, 768), bf16),
             pltpu.VMEM((384, 768), f32),
             pltpu.VMEM((384, 8), f32),
-            pltpu.VMEM((CLASSES, UNITS, 8, 128), bf16),
+            pltpu.VMEM((32, UNITS, 8, 128), bf16),
+            pltpu.SemaphoreType.DMA((5,)),
         ],
-        compiler_params=params(32),
+        compiler_params=params(16),
         name="prep",
-    )(place, w_up, w_down, b_up)
+    )(
+        place,
+        pltpu.with_memory_space_constraint(w_up, pltpu.HBM),
+        pltpu.with_memory_space_constraint(w_down, pltpu.HBM),
+        b_up,
+    )
 
 
 def segment_ends(len_ref):
@@ -174,7 +276,7 @@
     low7 = jnp.int32(0x7F7F7F7F)
     ones = jnp.int32(0x01010101)
     byte2 = jnp.int32(0x00FF00FF)
-    tile_rows = 32
+    tile_rows = 16
     groups = tile_rows // 8
 
     def tile(rt, carry):
@@ -206,6 +308,8 @@
         return carry
 
     lax.fori_loop(0, ROWS // tile_rows, tile, 0)
+
+    col_ref.leave()
 
     dims = (FREQ, ROWS)
     f = lax.broadcasted_iota(i32, dims, 0)
@@ -254,9 +358,12 @@
     y_cos = (k_cos * v_cos + k_sin * v_sin).astype(bf16)
     y_sin = (k_cos * v_sin - k_sin * v_cos).astype(bf16)
     conv = dot(wavet_ref[:, 0:FREQ], y_cos) + dot(wavet_ref[:, FREQ:], y_sin)
-    for b in range(COLS):
-        cs = slice(b * 128, b * 128 + 128)
-        block = masked[:, cs]
+    for done in (wave_ref, wavet_ref, tapt_ref, ks_ref, live_out, vs_ref):
+        done.leave()
+
+    def heads(b, carry):
+        cs = pl.ds(pl.multiple_of(b * 128, 128), 128)
+        block = mskd[:, cs]
         m = jnp.where(first_head, dot(col_ref[2 * b], block), dot(col_ref[2 * b + 1], block))
         sq = m * m
         one = jnp.sum(jnp.where(first_head, sq, 0.0), axis=1, keepdims=True)
@@ -266,8 +373,13 @@
         nrm = m * scale
         nrm_ref[:, cs] = nrm.astype(bf16)
         mix[:, cs] = nrm
+        return carry
+
+    lax.fori_loop(0, COLS, heads, 0)
     context = (mix[...] + conv).astype(bf16)
     ctx_ref[...] = context
+    for done in (scl_ref, nrm_ref, ctx_ref):
+        done.leave()
     attended = dot(context, wo_ref[...]) + bo_ref[...].astype(f32)
     n, inv = norm_rows(x_ref[...].astype(f32) + attended)
     n_ref[...] = n
@@ -281,18 +393,23 @@
 def attend(seq_lengths, x, wv, bv, taps, wo, bo, ga, sa, q, k, live):
     wide = (ROWS, WIDTH)
     half = (HALF, WIDTH)
-    return pl.pallas_call(
-        attend_kernel,
-        out_shape=(
-            shape(wide, f32), shape((ROWS, 128), f32), shape(wide, bf16), shape(half, bf16),
-            shape(half, bf16), shape(wide, bf16), shape((HEADS, ROWS, ROWS), bf16), shape(wide, bf16), shape(wide, f32),
-            shape((2 * FREQ, ROWS), bf16), shape((ROWS, 2 * FREQ), bf16),
-            shape((2 * FREQ, WIDTH), f32), shape((2 * FREQ, WIDTH), bf16),
-            shape((128, 2 * FREQ), bf16), shape((ROWS, 128), f32),
-        ),
-        in_specs=[SMEM] + [VMEM] * 11,
-        out_specs=(VMEM,) * 15,
-        scratch_shapes=[
+    h = "hbm"
+    v = "vmem"
+    return staged_call(
+        attend_kernel, "attend", 36,
+        [
+            ("smem", seq_lengths), (h, x), (h, wv), (v, bv), (v, taps), (h, wo), (v, bo), (v, ga),
+            (v, sa), (h, q), (h, k), (v, live),
+        ],
+        [
+            (h, shape(wide, f32)), (h, shape((ROWS, 128), f32)), (v, shape(wide, bf16)),
+            (v, shape(half, bf16)), (v, shape(half, bf16)), (h, shape(wide, bf16)),
+            (h, shape((HEADS, ROWS, ROWS), bf16)), (h, shape(wide, bf16)), (h, shape(wide, f32)),
+            (h, shape((2 * FREQ, ROWS), bf16)), (h, shape((ROWS, 2 * FREQ), bf16)),
+            (h, shape((2 * FREQ, WIDTH), f32)), (h, shape((2 * FREQ, WIDTH), bf16)),
+            (h, shape((128, 2 * FREQ), bf16)), (h, shape((ROWS, 128), f32)),
+        ],
+        [
             pltpu.VMEM((ROWS, 128), i32),
             pltpu.VMEM((96, 2, 8, 128), i32),
             pltpu.VMEM((ROWS, ROWS), f32),
@@ -300,9 +417,7 @@
             pltpu.VMEM(wide, f32),
             pltpu.VMEM(wide, bf16),
         ],
-        compiler_params=params(32),
-        name="attend",
-    )(seq_lengths, x, wv, bv, taps, wo, bo, ga, sa, q, k, live)
+    )
 
 
 def unpack(ref, m, out):
@@ -321,12 +436,6 @@
         parts = [jnp.where(lane == rt, tile, 0.0)[:, None] for rt in range(3)]
         column = jnp.concatenate(parts, axis=1).reshape(192, 128)
         out[a * 192 : a * 192 + 192, WIDTH:] = column.astype(bf16)
-
-
-def ffn_rows(own, sib, rows, ones):
-    rows[0:ROWS, 0:WIDTH] = own
-    rows[ROWS:, 0:WIDTH] = sib
-    rows[:, WIDTH:] = jnp.where(lanes((2 * ROWS, 128)) < ones, 1.0, 0.0).astype(bf16)
 
 
 def ffn_blocks(rows, wu, wd, act, slope, acc):
@@ -346,10 +455,12 @@
     lax.fori_loop(0, HIDDEN // 256, block, 0)
 
 
-def ffn_far_kernel(
-    got_a, got_b, sib, w, act, slope, part_own, part_sib, rows_out, wu, wd, rows, acc,
+def ffn_near_kernel(
+    own, sib, w, act, slope, part_own, part_sib, rows_out, wu, wd, rows, acc,
 ):
-    ffn_rows(jnp.concatenate([got_a[...], got_b[...]], axis=0), sib[...], rows, 3)
+    rows[0:ROWS, 0:WIDTH] = own[...]
+    rows[ROWS:, 0:WIDTH] = sib[...]
+    rows[:, WIDTH:] = jnp.where(lanes((2 * ROWS, 128)) < 3, 1.0, 0.0).astype(bf16)
     unpack(w, 0, wu)
     unpack_bias(w, wu)
     unpack(w, 1, wd)
@@ -359,32 +470,37 @@
     part_sib[...] = acc[ROWS:].astype(bf16)
 
 
-def ffn_near_kernel(own, sib, wu, wd, act, slope, part_own, part_sib, rows_out, rows, acc):
-    ffn_rows(own[...], sib[...], rows, 3)
+def ffn_far_kernel(
+    got_a, got_b, sib_a, sib_b, wu, wd, act, slope, part_own, part_sib, rows_out, rows, acc,
+):
+    for i, ref in enumerate((got_a, got_b, sib_a, sib_b)):
+        rows[i * HALF : i * HALF + HALF, 0:WIDTH] = ref[...]
+    rows[:, WIDTH:] = jnp.where(lanes((2 * ROWS, 128)) < 3, 1.0, 0.0).astype(bf16)
     rows_out[...] = rows[:, 0:WIDTH]
     ffn_blocks(rows, wu, wd, act, slope, acc)
     part_own[...] = acc[0:ROWS]
     part_sib[...] = acc[ROWS:].astype(bf16)
 
 
-def ffn_call(kernel, weights_out, *args):
+def ffn_call(kernel, name, ins, outs):
     wide = (ROWS, WIDTH)
     tall = shape((2 * ROWS, WIDTH), bf16)
-    outs = (tall, tall, shape(wide, f32), shape(wide, bf16), tall)
-    if weights_out:
-        outs += (shape((HIDDEN, WIDTH + 128), bf16), shape((HIDDEN, WIDTH), bf16))
-    return pl.pallas_call(
-        kernel,
-        out_shape=outs,
-        in_specs=[VMEM] * len(args),
-        out_specs=(VMEM,) * len(outs),
-        scratch_shapes=[
-            pltpu.VMEM((2 * ROWS, WIDTH + 128), bf16),
-            pltpu.VMEM((2 * ROWS, WIDTH), f32),
-        ],
-        compiler_params=params(24),
-        name="ffn_far" if weights_out else "ffn_near",
-    )(*args)
+    return staged_call(
+        kernel, name, 24, ins,
+        [("vmem", o) for o in (tall, tall, shape(wide, f32), shape(wide, bf16), tall, *outs)],
+        [pltpu.VMEM((2 * ROWS, WIDTH + 128), bf16), pltpu.VMEM((2 * ROWS, WIDTH), f32)],
+    )
+
+
+def ffn_near(own, sib, weights):
+    return ffn_call(
+        ffn_near_kernel, "ffn_near", [("vmem", own), ("vmem", sib), ("hbm", weights)],
+        [shape((HIDDEN, WIDTH + 128), bf16), shape((HIDDEN, WIDTH), bf16)],
+    )
+
+
+def ffn_far(*args):
+    return ffn_call(ffn_far_kernel, "ffn_far", [("vmem", a) for a in args], [])
 
 
 def combine_kernel(own, got, out_a, out_b):
@@ -433,22 +549,18 @@
 def middle(*args):
     wide = (ROWS, WIDTH)
     half = (HALF, WIDTH)
-    return pl.pallas_call(
-        middle_kernel,
-        out_shape=(
-            shape(wide, bf16), shape(wide, f32), shape(wide, bf16), shape(half, bf16),
-            shape(half, bf16), shape((8, WIDTH), f32),
-        ),
-        in_specs=[VMEM] * 11,
-        out_specs=(VMEM,) * 6,
-        compiler_params=params(32),
-        name="middle",
-    )(*args)
+    return staged_call(
+        middle_kernel, "middle", 16, [("vmem", a) for a in args],
+        [
+            ("hbm", shape(wide, bf16)), ("hbm", shape(wide, f32)), ("vmem", shape(wide, bf16)),
+            ("vmem", shape(half, bf16)), ("vmem", shape(half, bf16)), ("hbm", shape((8, WIDTH), f32)),
+        ],
+    )
 
 
 def back_blocks(g, wu, wd, slope, u_out, bias, acc):
     acc[...] = jnp.zeros(acc.shape, f32)
-    bias[...] = jnp.zeros(bias.shape, f32)
+    bias[...] = jnp.zeros((8, HIDDEN), f32)
 
     def block(i, carry):
         hs = pl.ds(pl.multiple_of(i * 256, 256), 256)
@@ -469,10 +581,11 @@
     first_sib[...] = acc[ROWS:].astype(bf16)
 
 
-def back_far_kernel(got_a, got_b, sib, wu, wd, slope, first_own, first_sib, g, u, bias, acc):
-    g[0:HALF] = got_a[...]
-    g[HALF:ROWS] = got_b[...]
-    g[ROWS:] = sib[...]
+def back_far_kernel(
+    got_a, got_b, sib_a, sib_b, wu, wd, slope, first_own, first_sib, g, u, bias, acc,
+):
+    for i, ref in enumerate((got_a, got_b, sib_a, sib_b)):
+        g[i * HALF : i * HALF + HALF] = ref[...]
     back_blocks(g, wu, wd, slope, u, bias, acc)
     first_own[...] = acc[0:ROWS]
     first_sib[...] = acc[ROWS:].astype(bf16)
@@ -481,20 +594,17 @@
 def back_call(kernel, name, *args):
     wide = (ROWS, WIDTH)
     tall = shape((2 * ROWS, WIDTH), bf16)
-    outs = (shape(wide, f32), shape(wide, bf16), tall, tall, shape((8, HIDDEN), f32))
-    return pl.pallas_call(
-        kernel,
-        out_shape=outs,
-        in_specs=[VMEM] * len(args),
-        out_specs=(VMEM,) * len(outs),
-        scratch_shapes=[pltpu.VMEM((2 * ROWS, WIDTH), f32)],
-        compiler_params=params(24),
-        name=name,
-    )(*args)
-
-
-def pack_kernel(gu, gd, bias_n, bias_f, grads):
-    column = (bias_n[...] + bias_f[...]).T[:, 0:1]
+    return staged_call(
+        kernel, name, 20, [("vmem", a) for a in args],
+        [
+            ("hbm" if name == "back_near" else "vmem", shape(wide, f32)), ("vmem", shape(wide, bf16)),
+            ("vmem", tall), ("vmem", tall), ("hbm", shape((8, HIDDEN), f32)),
+        ],
+        [pltpu.VMEM((2 * ROWS, WIDTH), f32)],
+    )
+
+
+def pack_kernel(gu, gd, grads):
     for a in range(PIECES):
         rs = slice(a * 192, a * 192 + 192)
         for ct in range(COLS):
@@ -504,30 +614,18 @@
             down = gd[rs, cs].astype(f32).reshape(8, 3, 8, 128)
             grads[0, a, ct // 3, :, us] = up.astype(bf16)
             grads[1, a, ct // 3, :, us] = down.astype(bf16)
-        bias = jnp.broadcast_to(column[rs], (192, 128)).reshape(8, 3, 8, 128)
-        lane = lanes((8, 8, 128))
-        tile = jnp.where(lane == 0, bias[:, 0], jnp.where(lane == 1, bias[:, 1], bias[:, 2]))
-        empty = jnp.zeros((8, 8, 128), bf16)
-        grads[0, a, 0, :, UNITS - 1] = tile.astype(bf16)
-        grads[0, a, 1, :, UNITS - 1] = empty
-        grads[1, a, 0, :, UNITS - 1] = empty
-        grads[1, a, 1, :, UNITS - 1] = empty
 
 
 def pack(*args):
-    return pl.pallas_call(
-        pack_kernel,
-        out_shape=shape((2, PIECES, 2, 8, UNITS, 8, 128), bf16),
-        in_specs=[VMEM] * 4,
-        out_specs=VMEM,
-        compiler_params=params(16),
-        name="pack",
-    )(*args)
+    return staged_call(
+        pack_kernel, "pack", 12, [("vmem", a) for a in args],
+        [("hbm", shape((2, PIECES, 2, 8, GRAD_UNITS, 8, 128), bf16))],
+    )[0]
 
 
 def back_kernel(
     place, own, near, far_a, far_b, second, n1, inv1, ga, ctx, wo, nrm, scl, wave, wavet, ks, vs, tapt, col, live, x,
-    wv, sums, in_grad, keep, give, buf_a, buf_b, mg, mb,
+    wv, sums, bias_n, bias_f, in_grad, keep, give, buf_a, buf_b, mb,
 ):
     first_grad = second[...] + gather_rows(own, near, far_a, far_b)
     n = n1[...]
@@ -538,24 +636,32 @@
     buf_a[768 + 1 : 768 + 2] = jnp.sum(ag.astype(f32), axis=0, keepdims=True)
     buf_a[768 + 4 : 768 + 7] = sums[0:3]
     buf_a[768 + 7 :] = jnp.zeros((TALL - 775, WIDTH), f32)
+    mine = lax.broadcasted_iota(i32, (8, WIDTH), 0) == place[0] % CLASSES
+    bias = jnp.broadcast_to(bias_n[0:1] + bias_f[0:1], (8, WIDTH))
+    buf_a[776:784] = jnp.where(mine, bias, 0.0)
     buf_b[0:768] = dot_first(ctx[...], ag)
     cg = dot_last(ag, wo[...])
+    mb[...] = cg
     first_head = lanes((ROWS, 128)) < HEAD_DIM
-    for b in range(COLS):
-        cs = slice(b * 128, b * 128 + 128)
-        c = cg[:, cs]
+    nrm.ready()
+    scl.ready()
+    col.ready()
+
+    def heads(b, carry):
+        cs = pl.ds(pl.multiple_of(b * 128, 128), 128)
+        c = mb[:, cs]
         m = nrm[:, cs].astype(f32)
         prod = c * m
         one = jnp.sum(jnp.where(first_head, prod, 0.0), axis=1, keepdims=True)
         two = jnp.sum(jnp.where(first_head, 0.0, prod), axis=1, keepdims=True)
         mean = jnp.where(first_head, one, two) * (1.0 / HEAD_DIM)
-        mg[:, cs] = (scl[:, cs] * (c - m * mean)).astype(bf16)
-    for b in range(COLS):
-        cs = slice(b * 128, b * 128 + 128)
-        block = mg[:, cs]
+        block = (scl[:, cs] * (c - m * mean)).astype(bf16)
         mb[:, cs] = jnp.where(
             first_head, dot_first(col[2 * b], block), dot_first(col[2 * b + 1], block)
         )
+        return carry
+
+    lax.fori_loop(0, COLS, heads, 0)
     spec = dot(wave[...], cg.astype(bf16))
     g_cos = spec[0:FREQ]
     g_sin = spec[FREQ:]
@@ -601,20 +707,19 @@
 
 def attend_back(*args):
     wide = (ROWS, WIDTH)
-    return pl.pallas_call(
-        back_kernel,
-        out_shape=(shape(wide, f32), shape((PACK, 8, 128), bf16), shape((PACK, 8, 128), bf16)),
-        in_specs=[SMEM] + [VMEM] * 22,
-        out_specs=(VMEM,) * 3,
-        scratch_shapes=[
+    packed = shape((PACK, 8, 128), bf16)
+    kinds = ["smem"] + ["hbm"] * (len(args) - 1)
+    for i in (2, 3, 4, 8):
+        kinds[i] = "vmem"
+    return staged_call(
+        back_kernel, "attend_back", 40, list(zip(kinds, args, strict=True)),
+        [("hbm", shape(wide, f32)), ("vmem", packed), ("vmem", packed)],
+        [
             pltpu.VMEM((TALL, WIDTH), f32),
             pltpu.VMEM((TALL, WIDTH), f32),
-            pltpu.VMEM(wide, bf16),
             pltpu.VMEM(wide, f32),
         ],
-        compiler_params=params(40),
-        name="attend_back",
-    )(*args)
+    )
 
 
 def sum_ffn_kernel(got, out, acc):
@@ -639,10 +744,10 @@
     return pl.pallas_call(
         sum_ffn_kernel,
         grid=(4,),
-        out_shape=shape((CLASSES, UNITS, 8, 128), bf16),
-        in_specs=[pl.BlockSpec((32, UNITS, 8, 128), lambda i: (i, 0, 0, 0))],
-        out_specs=pl.BlockSpec((CLASSES, UNITS, 8, 128), lambda i: (0, 0, 0, 0)),
-        scratch_shapes=[pltpu.VMEM((CLASSES, UNITS, 8, 128), f32)],
+        out_shape=shape((CLASSES, GRAD_UNITS, 8, 128), bf16),
+        in_specs=[pl.BlockSpec((32, GRAD_UNITS, 8, 128), lambda i: (i, 0, 0, 0))],
+        out_specs=pl.BlockSpec((CLASSES, GRAD_UNITS, 8, 128), lambda i: (0, 0, 0, 0)),
+        scratch_shapes=[pltpu.VMEM((CLASSES, GRAD_UNITS, 8, 128), f32)],
         compiler_params=params(32),
         name="sum_ffn",
     )(got)
@@ -673,30 +778,12 @@
     )(got)
 
 
-def final_kernel(
-    place, own, other, ffn_own, ffn_oth, bias_own, bias_oth, g_wv, g_bv, g_conv, g_wo, g_bo, g_ga, g_sa, g_up, g_bup,
-    g_down, g_bd, g_gf, g_sf, vecs, tall,
-):
+def final_ffn_kernel(place, ffn_own, ffn_oth, g_up, g_down, tall):
     ct = pl.program_id(0)
-
-    def write(a, b):
-        g_wv[...] = a[0:96].astype(f32).reshape(768, 128)
-        vecs[ct] = a[96].astype(f32)
-        g_wo[...] = b[0:96].astype(f32).reshape(768, 128)
-        g_conv[...] = b[96:105].astype(f32).reshape(72, 128)[0:TAPS]
-
-    @pl.when(place[0] % 2 == 0)
-    def _():
-        write(own, other)
-
-    @pl.when(place[0] % 2 == 1)
-    def _():
-        write(other, own)
-
     core = place[0] % 2
 
     def index(m, a):
-        return (m + place[0] // 8) % 2 * 4 + (place[0] // 2 % 4 + 4 - a) % 4
+        return (place[0] // 2 % 4 + 4 - a) % 4 * 2 + (m + place[0] // 8) % 2
 
     def spread(ref):
         for a in range(PIECES):
@@ -717,59 +804,87 @@
 
     g_up[...] = tall[...].T
 
+
+def final_ffn(place, ffn_own, ffn_oth):
+    units = pl.BlockSpec((8, CLASSES, 3, 8, 128), lambda i: (0, 0, i % 3, 0, 0))
+    return pl.pallas_call(
+        final_ffn_kernel,
+        grid=(COLS,),
+        out_shape=(shape((768, 384), f32), shape((384, 768), f32)),
+        in_specs=[SMEM, units, units],
+        out_specs=(
+            pl.BlockSpec((128, 384), lambda i: (i, 0)),
+            pl.BlockSpec((384, 128), lambda i: (0, i)),
+        ),
+        scratch_shapes=[pltpu.VMEM((384, 128), f32)],
+        compiler_params=params(16),
+        name="final_ffn",
+    )(place, ffn_own, ffn_oth)
+
+
+def final_kernel(
+    place, own, other, g_wv, g_bv, g_conv, g_wo, g_bo, g_ga, g_sa, g_bup, g_bd, g_gf, g_sf, vecs,
+    bias, line,
+):
+    ct = pl.program_id(0)
+
+    def write(a, b):
+        g_wv[...] = a[0:96].astype(f32).reshape(768, 128)
+        vecs[ct] = a[96].astype(f32)
+        bias[ct] = a[97].astype(f32)
+        g_wo[...] = b[0:96].astype(f32).reshape(768, 128)
+        g_conv[...] = b[96:105].astype(f32).reshape(72, 128)[0:TAPS]
+
+    @pl.when(place[0] % 2 == 0)
+    def _():
+        write(own, other)
+
+    @pl.when(place[0] % 2 == 1)
+    def _():
+        write(other, own)
+
     @pl.when(ct == COLS - 1)
     def _():
         for j, ref in enumerate((g_bv, g_bo, g_ga, g_sa, g_bd, g_gf, g_sf)):
             for i in range(COLS):
                 ref[i * 128 : i * 128 + 128] = vecs[i, j]
-
-        def bias(ref):
-            lane = lanes((CLASSES, 8, 128))
-            for a in range(PIECES):
-                tile = ref[index(0, a)][:, 0].astype(f32)
-                rows = [jnp.where(lane == rt, tile, 0.0)[:, None] for rt in range(3)]
-                column = jnp.concatenate(rows, axis=1)
-                for q in range(CLASSES):
-                    rs = slice(SUB * q + PIECE * a, SUB * q + PIECE * a + PIECE)
-                    tall[rs, :] = column[q].reshape(PIECE, 128)
-            g_bup[...] = dot_last(jnp.ones((8, 128), bf16), tall[...].astype(bf16))[0]
-
-        @pl.when(core == 0)
-        def _():
-            bias(bias_own)
-
-        @pl.when(core == 1)
-        def _():
-            bias(bias_oth)
-
-
-def final(place, own, other, ffn_own, ffn_oth):
+        n = lanes((128, 128))
+        a = (n >= PIECE).astype(i32) + (n >= 2 * PIECE).astype(i32) + (n >= 3 * PIECE).astype(i32)
+        at = (8 * a + place[1]) * PIECE + n - PIECE * a
+        total = jnp.zeros((8, 128), f32)
+        for i in range(COLS):
+            pick = lax.broadcasted_iota(i32, (128, 128), 0) + 128 * i == at
+            total = total + dot(bias[i].astype(bf16), jnp.where(pick, 1.0, 0.0).astype(bf16))
+        for q in range(CLASSES):
+            line[0:1, SUB * q : SUB * q + SUB] = total[q : q + 1, 0:SUB]
+        g_bup[...] = line[...][0]
+
+
+def final(place, own, other):
     tile = pl.BlockSpec((TALL_TILES, 8, 128), lambda i: (i, 0, 0))
     tall = pl.BlockSpec((768, 128), lambda i: (0, i))
     vec = pl.BlockSpec((WIDTH,), lambda i: (0,))
-    units = pl.BlockSpec((8, CLASSES, 3, 8, 128), lambda i: (0, 0, i % 3, 0, 0))
-    last = pl.BlockSpec((8, CLASSES, 1, 8, 128), lambda i: (0, 0, UNITS - 1, 0, 0))
     v = shape((WIDTH,), f32)
     return pl.pallas_call(
         final_kernel,
         grid=(COLS,),
         out_shape=(
             shape((768, 768), f32), v, shape((TAPS, 768), f32), shape((768, 768), f32), v, v, v,
-            shape((768, 384), f32), shape((384,), f32), shape((384, 768), f32), v, v, v,
+            shape((384,), f32), v, v, v,
         ),
-        in_specs=[
-            SMEM, tile, tile,
-            units, units, last, last,
-        ],
+        in_specs=[SMEM, tile, tile],
         out_specs=(
             tall, vec, pl.BlockSpec((TAPS, 128), lambda i: (0, i)), tall, vec, vec, vec,
-            pl.BlockSpec((128, 384), lambda i: (i, 0)), pl.BlockSpec((384,), lambda i: (0,)),
-            pl.BlockSpec((384, 128), lambda i: (0, i)), vec, vec, vec,
+            pl.BlockSpec((384,), lambda i: (0,)), vec, vec, vec,
         ),
-        scratch_shapes=[pltpu.VMEM((COLS, 8, 128), f32), pltpu.VMEM((384, 128), f32)],
-        compiler_params=params(32),
+        scratch_shapes=[
+            pltpu.VMEM((COLS, 8, 128), f32),
+            pltpu.VMEM((COLS, 8, 128), f32),
+            pltpu.VMEM((1, 384), f32),
+        ],
+        compiler_params=params(16),
         name="final",
-    )(place, own, other, ffn_own, ffn_oth, ffn_own, ffn_oth)
+    )(place, own, other)
 
 
 def body(
@@ -815,14 +930,6 @@
     def row(v):
         return v.reshape(1, -1)
 
-    def fetch(a, b):
-        far_a, far_b = ahead(a), behind(b)
-        return far_a, far_b, swap(jnp.concatenate([far_a, far_b], axis=0))
-
-    def send_back(own, sib):
-        a, b = combine(own, swap(sib))
-        return behind(a), ahead(b)
-
     weights = exchange(prep(place, w_up, w_down, row(b_up)))
     weights = weights.reshape(2, PIECES, 2, 8, UNITS, 8, 128)
     (n1, inv1, low, low_a, low_b, ctx, collide, nrm, scl, wave, wavet, ks, vs, tapt, live) = attend(
@@ -830,48 +937,52 @@
         row(gain_attn), row(shift_attn), query_codes, key_codes, row(key_live),
     )
     low_sib = swap(low)
-    row_a, row_b, row_sib = fetch(low_a, low_b)
-    act_f, slope_f, far_own, far_sib, rows_f, wu, wd = ffn_call(
-        ffn_far_kernel, True, row_a, row_b, row_sib, weights
-    )
-    act_n, slope_n, near_own, near_sib, rows_n = ffn_call(
-        ffn_near_kernel, False, low, low_sib, wu, wd
-    )
-    back_a, back_b = send_back(far_own, far_sib)
+    row_a, row_b = ahead(low_a), behind(low_b)
+    act_n, slope_n, near_own, near_sib, rows_n, wu, wd = ffn_near(low, low_sib, weights)
+    act_f, slope_f, far_own, far_sib, rows_f = ffn_far(
+        row_a, row_b, swap(row_a), swap(row_b), wu, wd
+    )
+    sent_a, sent_b = combine(far_own, swap(far_sib))
     block_output, second, grad, grad_a, grad_b, sums = middle(
-        n1, near_own, swap(near_sib), back_a, back_b, row(b_down), row(gain_attn), row(shift_attn),
-        row(gain_ffn), row(shift_ffn), out_grad,
-    )
-    got_a, got_b, got_sib = fetch(grad_a, grad_b)
+        n1, near_own, swap(near_sib), behind(sent_a), ahead(sent_b), row(b_down), row(gain_attn),
+        row(shift_attn), row(gain_ffn), row(shift_ffn), out_grad,
+    )
+    got_a, got_b = ahead(grad_a), behind(grad_b)
     near_own, near_sib, g_n, u_n, bias_n = back_call(
         back_near_kernel, "back_near", grad, swap(grad), wu, wd, slope_n
     )
+    got_a, got_b, near_sib = lax.optimization_barrier((got_a, got_b, near_sib))
     far_own, far_sib, g_f, u_f, bias_f = back_call(
-        back_far_kernel, "back_far", got_a, got_b, got_sib, wu, wd, slope_f
-    )
+        back_far_kernel, "back_far", got_a, got_b, swap(got_a), swap(got_b), wu, wd, slope_f
+    )
+    sent_a, sent_b = combine(far_own, swap(far_sib))
+    u_f, sent_a, sent_b = lax.optimization_barrier((u_f, sent_a, sent_b))
     grad_down = (dot_first(act_n, g_n) + dot_first(act_f, g_f)).astype(bf16)
     grad_up = (dot_first(u_n, rows_n) + dot_first(u_f, rows_f)).astype(bf16)
-    grads = pack(grad_up, grad_down, bias_n, bias_f)
-    back_a, back_b = send_back(far_own, far_sib)
+    grads = pack(grad_up, grad_down)
+    back_a, back_b = behind(sent_a), ahead(sent_b)
     grads, back_a, back_b = lax.optimization_barrier((grads, back_a, back_b))
-    owned = exchange(grads.reshape(128, UNITS, 8, 128))
+    owned = exchange(grads.reshape(128, GRAD_UNITS, 8, 128))
     input_grad, keep, give = attend_back(
-        place, near_own, swap(near_sib), back_a, back_b, second, n1, inv1, row(gain_attn), ctx,
-        w_out, nrm, scl, wave, wavet, ks, vs, tapt, collide, live, block_input, w_value, sums,
-    )
-    pair = (keep + swap(give).astype(f32)).astype(bf16).reshape(128, PACK // 128, 8, 128)
+        place, near_own, swap(near_sib), back_a, back_b, second, n1, inv1,
+        row(gain_attn), ctx, w_out, nrm, scl, wave, wavet, ks, vs, tapt, collide, live, block_input,
+        w_value, sums, bias_n, bias_f,
+    )
+    pair = (keep.astype(f32) + swap(give).astype(f32)).astype(bf16)
+    pair = pair.reshape(128, PACK // 128, 8, 128)
     owned = sum_ffn(owned)
     pair, owned = lax.optimization_barrier((pair, owned))
-    around = [owned]
-    for side in range(2):
-        for by in range(4):
-            if side or by:
-                pairs = [(i, (i // 8 + side) % 2 * 8 + shift(i % 8, by)) for i in range(n_dp)]
-                around.append(lax.ppermute(owned, "dp", pairs))
-    ffn_own = jnp.stack(around)
-    back = exchange(sum_rest(exchange(pair))).reshape(PACK, 8, 128)
-    (g_wv, g_bv, g_conv, g_wo, g_bo, g_ga, g_sa, g_up, g_bup, g_down, g_bd, g_gf, g_sf) = final(
-        place, back, swap(back), ffn_own, swap(ffn_own)
+    two = jnp.stack([owned, lax.ppermute(owned, "dp", [(i, (i + 8) % 16) for i in range(n_dp)])])
+    summed = sum_rest(exchange(pair))
+    summed, two = lax.optimization_barrier((summed, two))
+    opposite = lax.ppermute(two, "dp", [(i, shift(i, 2)) for i in range(n_dp)])
+    ffn_own = jnp.stack([two, ahead(two), opposite, behind(two)])
+    back = exchange(summed).reshape(PACK, 8, 128)
+    back, ffn_own = lax.optimization_barrier((back, ffn_own))
+    ffn_own = ffn_own.reshape(8, CLASSES, GRAD_UNITS, 8, 128)
+    g_up, g_down = final_ffn(place, ffn_own, swap(ffn_own))
+    g_wv, g_bv, g_conv, g_wo, g_bo, g_ga, g_sa, g_bup, g_bd, g_gf, g_sf = final(
+        place, back, swap(back)
     )
     return (
         block_output, input_grad, g_wv, g_bv, g_conv, g_wo, g_bo, g_ga, g_sa, g_up, g_bup, g_down,

time: 231 us -> 211 us (0.913)
  local copies, waits for them, and re-layouts: 44.7 us -> 0.8 us
  waiting for transfers between devices: 46.8 us -> 82.7 us
  blocking collectives: 27 us -> 0 us
  Pallas kernels: 47.5 us -> 65.3 us
    unnamed x125 -> x24, local copies, waits for them, and re-layouts: 44 us -> 0.08 us
    all_to_all x1 -> x0, blocking collectives: 27 us -> none  [exchange(): return lax.all_to_all(x, ALL, 0, 0, tiled=True)]
    pallas_call x10 -> x11, Pallas kernels: 40.7 us -> 59.8 us  [the longest x7 48.5 us: staged_call(): pl.pallas_call(run, out_shape=tuple((pltpu.HBM(o.shape, o.dtype) if k ==...]
    ppermute x4 -> x5, waiting for transfers between devices: 5.46 us -> 20.9 us  [behind(): return lax.ppermute(x, 'dp', [(i, shift(i, -1)) for i in range(n_dp)])]
    all_to_all x3 -> x4, waiting for transfers between devices: 2.24 us -> 14 us  [exchange(): return lax.all_to_all(x, ALL, 0, 0, tiled=True)]
    ppermute x4 -> x5, waiting for transfers between devices: 12.2 us -> 21.4 us  [ahead(): return lax.ppermute(x, 'dp', [(i, shift(i, 1)) for i in range(n_dp)])]
    ppermute x7 -> x2, starting transfers between devices: 10.6 us -> 1.99 us  [the longest x1 1.46 us: body(): lax.ppermute(owned, 'dp', [(i, (i + 8) % 16) for i in range(n_dp)])]
    all_to_all x3 -> x4, starting transfers between devices: 26.1 us -> 32.3 us  [exchange(): return lax.all_to_all(x, ALL, 0, 0, tiled=True)]
  transfers between devices with their start and end apart: 29 -> 29, of which waited for: 14 -> 18; matrix products, arithmetic and copies ran while one was open for 2% -> 2% of each run, Pallas kernels for 15% -> 22%
where the time goes in v3:
time: 211 us; the launch traced here: 210 us
  waiting for transfers between devices  82.7 us (39%)
  Pallas kernels  65.3 us (31%)
  starting transfers between devices  55.3 us (26%)
  matrix products  3.28 us (2%)
    pallas_call x7, Pallas kernels, staged_call(): pl.pallas_call(run, out_shape=tuple((pltpu.HBM(o.shape, o.dtype) if k ==...  48.5 us
    all_to_all x4, starting transfers between devices, exchange(): return lax.all_to_all(x, ALL, 0, 0, tiled=True)  32.3 us
    ppermute x5, waiting for transfers between devices, ahead(): return lax.ppermute(x, 'dp', [(i, shift(i, 1)) for i in range(n_dp)])  21.4 us
    ppermute x5, waiting for transfers between devices, behind(): return lax.ppermute(x, 'dp', [(i, shift(i, -1)) for i in range(n_dp)])  20.9 us
    ppermute x1, waiting for transfers between devices, body(): lax.ppermute(owned, 'dp', [(i, (i + 8) % 16) for i in range(n_dp)])  15.6 us
    all_to_all x4, waiting for transfers between devices, exchange(): return lax.all_to_all(x, ALL, 0, 0, tiled=True)  14 us
    ppermute x5, starting transfers between devices, behind(): return lax.ppermute(x, 'dp', [(i, shift(i, -1)) for i in range(n_dp)])  10.8 us
    ppermute x13, waiting for transfers between devices, swap(): return lax.ppermute(x, 'dp', [(i, i ^ 1) for i in range(n_dp)])  9.32 us
  transfers between devices with their start and end apart: 29, of which 18 were waited for; matrix products, arithmetic and copies ran while one was open for 2% of the time, Pallas kernels for 22%

profile of v3, /device:TPU:1, one launch (start us, length us, event | category | flops | bytes accessed | tf_op | source)
XLA Modules:
  0.0 210.2 jit_solution(7871618350920358884)
XLA Ops:
  1.4 3.5 %prep.1 = bf16[128,10,8,128]{3,2,1,0:T(8,128)(2,1)} custom-call(s32[2]{0:T(128)S(1)} %pad_add_fusion.place.refs_0_, bf16[768,384]{1,0:T(8,128)(2,1)} %up_ref.1, bf16[384,768]{1,0:T(8,128)(2,1)} %down_ref.1, bf16[1,384]{1,0:T(2,128)(2,1)S(1)} %reshape.80.bias_ref), custom_call_target="tpu_custom_call" | custom-call | tf_op jit(solution)/shard_map/prep/pallas_call | solution.py:210
  5.0 11.9 %all-to-all-start = ((bf16[128,10,8,128]{3,2,1,0:T(8,128)(2,1)}), bf16[128,10,8,128]{3,2,1,0:T(8,128)(2,1)}, u32[]{:S(2)}, u32[]{:S(2)}) async-start(bf16[128,10,8,128]{3,2,1,0:T(8,128)(2,1)} %prep.1), calls=%async_computation | async-start | bytes 5242880 | tf_op jit(solution)/shard_map/all_to_all | solution.py:928
  17.0 18.3 %attend.1 = (f32[256,768]{1,0:T(8,128)}, f32[256,128]{1,0:T(8,128)}, bf16[256,768]{1,0:T(8,128)(2,1)S(1)}, bf16[128,768]{1,0:T(8,128)(2,1)S(1)}, bf16[128,768]{1...) custom-call(s32[1,4]{1,0:T(1,128)S(1)} %copy-done.4, ...), custom_call_target="tpu_custom_call" | custom-call | tf_op jit(solution)/shard_map/attend/pallas_call | solution.py:151
  35.4 1.2 collective-permute-start
  37.2 2.1 collective-permute-start.3
  39.3 13.1 %collective-permute-done.2.got_a = bf16[128,768]{1,0:T(8,128)(2,1)S(1)} collective-permute-done((bf16[128,768]{1,0:T(8,128)(2,1)S(1)}, bf16[128,768]{1,0:T(8,128)(2,1)S(1)}, u32[]{:S(2)}, u32[]{:S(2)}) %collective-permute-start.2) | collective-permute-done | bytes 196640 | tf_op jit(solution)/shard_map/ppermute | solution.py:922
  52.9 5.9 %ffn_near.1 = (bf16[512,768]{1,0:T(8,128)(2,1)S(1)}, bf16[512,768]{1,0:T(8,128)(2,1)S(1)}, f32[256,768]{1,0:T(8,128)S(1)}, bf16[256,768]{1,0:T(8,128)(2,1)S(1)},...) custom-call(bf16[256,768]{1,0:T(8,128)(2,1)S(1)} %get-tuple-element.94.refs_0_, ...), custom_call_target="tpu_custom_call" | custom-call | tf_op jit(solution)/shard_map/ffn_near/pallas_call | solution.py:151
  58.9 3.8 %ffn_far.1 = (bf16[512,768]{1,0:T(8,128)(2,1)S(1)}, bf16[512,768]{1,0:T(8,128)(2,1)S(1)}, f32[256,768]{1,0:T(8,128)S(1)}, bf16[256,768]{1,0:T(8,128)(2,1)S(1)}, bf16[512,768]{1,0:T(8,128)(2,1)S(1)}) custom-call(bf16[128,768]{1,0:T(8,128)(2,1)S(1)} %collective-permute-done.2.got_a, bf16[128,768]{1,0:T(8,128)(2,1)S(1)} %collective-permute-done.3.got_b, ...), custom_call_target="tpu_custom_call" | custom-call | tf_op jit(solution)/shard_map/ffn_far/pallas_call | solution.py:119
  63.3 1.2 collective-permute-done.6.got
  65.2 1.1 collective-permute-start.8
  66.4 4.6 %collective-permute-done.7.refs_3_ = bf16[128,768]{1,0:T(8,128)(2,1)S(1)} collective-permute-done((bf16[128,768]{1,0:T(8,128)(2,1)S(1)}, bf16[128,768]{1,0:T(8,128)(2,1)S(1)}, u32[]{:S(2)}, u32[]{:S(2)}) %collective-permute-start.7) | collective-permute-done | bytes 196640 | tf_op jit(solution)/shard_map/ppermute | solution.py:925
  71.0 1.2 collective-permute-done.8.refs_4_
  72.2 1.8 middle.1
  74.0 1.6 collective-permute-start.9
  75.6 2.7 %collective-permute-start.11 = (bf16[128,768]{1,0:T(8,128)(2,1)S(1)}, bf16[128,768]{1,0:T(8,128)(2,1)S(1)}, u32[]{:S(2)}, u32[]{:S(2)}) collective-permute-start(bf16[128,768]{1,0:T(8,128)(2,1)S(1)} %get-tuple-element.110), channel_id=1, source_target_pairs={{0,48},{8,56},{16,0},{24,8},{32,16},{40,24},{48,32},{56,40},{64,11... | collective-permute-start | bytes 589832 | tf_op jit(solution)/shard_map/ppermute | solution.py:925
  78.3 4.1 %back_near.1 = (f32[256,768]{1,0:T(8,128)}, bf16[256,768]{1,0:T(8,128)(2,1)S(1)}, bf16[512,768]{1,0:T(8,128)(2,1)S(1)}, bf16[512,768]{1,0:T(8,128)(2,1)S(1)}, f32[8,768]{1,0:T(8,128)}) custom-call(bf16[256,768]{1,0:T(8,128)(2,1)S(1)} %get-tuple-element.106.refs_0_, bf16[256,768]{1,0:T(8,128)(2,1)S(1)} %collective-permute-done.9.refs_1_, ...), custom_call_target="tpu_custom_call" | custom-call | tf_op jit(solution)/shard_map/back_near/pallas_call | solution.py:151
  82.4 0.9 collective-permute-done.10.refs_0_
  83.3 0.9 collective-permute-start.13
  84.2 0.8 fusion
  85.6 3.4 %back_far.1 = (f32[256,768]{1,0:T(8,128)S(1)}, bf16[256,768]{1,0:T(8,128)(2,1)S(1)}, bf16[512,768]{1,0:T(8,128)(2,1)S(1)}, bf16[512,768]{1,0:T(8,128)(2,1)S(1)}, f32[8,768]{1,0:T(8,128)}) custom-call(bf16[128,768]{1,0:T(8,128)(2,1)S(1)} %collective-permute-done.10.refs_0_, bf16[128,768]{1,0:T(8,128)(2,1)S(1)} %collective-permute-done.11.refs_1_, ...), custom_call_target="tpu_custom_call" | custom-call | tf_op jit(solution)/shard_map/back_far/pallas_call | solution.py:151
  89.3 0.8 fusion.1
  90.1 0.8 add_convert_fusion.1.refs_1_
  91.1 2.7 %collective-permute-start.16 = (bf16[128,768]{1,0:T(8,128)(2,1)S(1)}, bf16[128,768]{1,0:T(8,128)(2,1)S(1)}, u32[]{:S(2)}, u32[]{:S(2)}) collective-permute-start(bf16[128,768]{1,0:T(8,128)(2,1)S(1)} %get-tuple-element.129), channel_id=1, source_target_pairs={{0,48},{8,56},{16,0},{24,8},{32,16},{40,24},{48,32},{56,40},{64,11... | collective-permute-start | bytes 589832 | tf_op jit(solution)/shard_map/ppermute | solution.py:925
  93.8 0.8 add_convert_fusion.2.refs_0_
  94.7 1.8 pack.1
  96.5 1.4 collective-permute-done.16.refs_3_
  97.9 3.1 %collective-permute-done.17.refs_4_ = bf16[128,768]{1,0:T(8,128)(2,1)S(1)} collective-permute-done((bf16[128,768]{1,0:T(8,128)(2,1)S(1)}, bf16[128,768]{1,0:T(8,128)(2,1)S(1)}, u32[]{:S(2)}, u32[]{:S(2)}) %collective-permute-start.17) | collective-permute-done | bytes 196640 | tf_op jit(solution)/shard_map/ppermute | solution.py:922
  101.0 8.0 %all-to-all-start.1 = ((bf16[128,9,8,128]{3,2,1,0:T(8,128)(2,1)}), bf16[128,9,8,128]{3,2,1,0:T(8,128)(2,1)S(1)}, u32[]{:S(2)}, u32[]{:S(2)}) async-start(bf16[128,9,8,128]{3,2,1,0:T(8,128)(2,1)} %bitcast.28), calls=%async_computation.1 | async-start | bytes 4718592 | tf_op jit(solution)/shard_map/all_to_all | solution.py:928
  109.0 1.4 collective-permute-start.12
  110.3 1.3 collective-permute-done.12.refs_2_
  111.7 13.3 %attend_back.1 = (f32[256,768]{1,0:T(8,128)}, bf16[640,8,128]{2,1,0:T(8,128)(2,1)S(1)}, bf16[640,8,128]{2,1,0:T(8,128)(2,1)S(1)}) custom-call(s32[2]{0:T(128)S(1)} %pad_add_fusion.place.refs_0_, f32[256,768]{1,0:T(8,128)} %get-tuple-element.108.refs_1_, bf16[256,768]{1,0:T(8,128)(2,1)S(1)} %collective-permute-done.12.refs_2_, ...), custom_call_target="tpu_custom_call" | custom-call | tf_op jit(solution)/shard_map/attend_back/pallas_call | solution.py:151
  125.4 2.7 %collective-permute-done.18 = bf16[640,8,128]{2,1,0:T(8,128)(2,1)S(1)} collective-permute-done((bf16[640,8,128]{2,1,0:T(8,128)(2,1)S(1)}, bf16[640,8,128]{2,1,0:T(8,128)(2,1)S(1)}, u32[]{:S(2)}, u32[]{:S(2)}) %collective-permute-start.18) | collective-permute-done | bytes 1310752 | tf_op jit(solution)/shard_map/ppermute | solution.py:919
  128.1 1.4 add_convert_fusion
  129.5 10.7 %all-to-all-done.1.got = bf16[128,9,8,128]{3,2,1,0:T(8,128)(2,1)S(1)} async-done(((bf16[128,9,8,128]{3,2,1,0:T(8,128)(2,1)}), bf16[128,9,8,128]{3,2,1,0:T(8,128)(2,1)S(1)}, u32[]{:S(2)}, u32[]{:S(2)}) %all-to-all-start.1) | async-done | bytes 2359328 | tf_op jit(solution)/shard_map/all_to_all | solution.py:928
  140.6 5.9 %all-to-all-start.2 = ((bf16[128,5,8,128]{3,2,1,0:T(8,128)(2,1)}), bf16[128,5,8,128]{3,2,1,0:T(8,128)(2,1)S(1)}, u32[]{:S(2)}, u32[]{:S(2)}) async-start(bf16[128,5,8,128]{3,2,1,0:T(8,128)(2,1)} %bitcast.29), calls=%async_computation.2 | async-start | bytes 2621440 | tf_op jit(solution)/shard_map/all_to_all | solution.py:928
  146.5 1.5 collective-permute-start.19
  148.0 15.6 %collective-permute-done.19 = bf16[4,9,8,128]{3,2,1,0:T(8,128)(2,1)S(1)} collective-permute-done((bf16[4,9,8,128]{3,2,1,0:T(8,128)(2,1)S(1)}, bf16[4,9,8,128]{3,2,1,0:T(8,128)(2,1)S(1)}, u32[]{:S(2)}, u32[]{:S(2)}) %collective-permute-start.19) | collective-permute-done | bytes 73760 | tf_op jit(solution)/shard_map/ppermute | solution.py:975
  163.6 3.3 %all-to-all-done.2.got = bf16[128,5,8,128]{3,2,1,0:T(8,128)(2,1)S(1)} async-done(((bf16[128,5,8,128]{3,2,1,0:T(8,128)(2,1)}), bf16[128,5,8,128]{3,2,1,0:T(8,128)(2,1)S(1)}, u32[]{:S(2)}, u32[]{:S(2)}) %all-to-all-start.2) | async-done | bytes 1310752 | tf_op jit(solution)/shard_map/all_to_all | solution.py:928
  166.9 1.3 sum_rest.1
  168.3 6.5 %all-to-all-start.3 = ((bf16[128,5,8,128]{3,2,1,0:T(8,128)(2,1)}), bf16[128,5,8,128]{3,2,1,0:T(8,128)(2,1)S(1)}, u32[]{:S(2)}, u32[]{:S(2)}) async-start(bf16[128,5,8,128]{3,2,1,0:T(8,128)(2,1)} %sum_rest.1), calls=%async_computation.3 | async-start | bytes 2621440 | tf_op jit(solution)/shard_map/all_to_all | solution.py:928
  174.8 2.7 %collective-permute-start.22 = (bf16[2,4,9,8,128]{4,3,2,1,0:T(8,128)(2,1)S(1)}, bf16[2,4,9,8,128]{4,3,2,1,0:T(8,128)(2,1)S(1)}, u32[]{:S(2)}, u32[]{:S(2)}) collective-permute-start(bf16[2,4,9,8,128]{4,3,2,1,0:T(8,128)(2,1)S(1)} %pad_maximum_fusion.1), channel_id=1, source_target_pairs={{0,48},{8,56},{16,0},{24,8},{32,16},{40,24},{48,32},{56,40},{64,11... | collective-permute-start | bytes 442376 | tf_op jit(solution)/shard_map/ppermute | solution.py:925
  178.6 14.9 %collective-permute-done.22 = bf16[2,4,9,8,128]{4,3,2,1,0:T(8,128)(2,1)S(1)} collective-permute-done((bf16[2,4,9,8,128]{4,3,2,1,0:T(8,128)(2,1)S(1)}, bf16[2,4,9,8,128]{4,3,2,1,0:T(8,128)(2,1)S(1)}, u32[]{:S(2)}, u32[]{:S(2)}) %collective-permute-start.22) | collective-permute-done | bytes 147488 | tf_op jit(solution)/shard_map/ppermute | solution.py:925
  193.5 1.5 collective-permute-done.21
  195.0 3.0 %collective-permute-done.20 = bf16[2,4,9,8,128]{4,3,2,1,0:T(8,128)(2,1)S(1)} collective-permute-done((bf16[2,4,9,8,128]{4,3,2,1,0:T(8,128)(2,1)S(1)}, bf16[2,4,9,8,128]{4,3,2,1,0:T(8,128)(2,1)S(1)}, u32[]{:S(2)}, u32[]{:S(2)}) %collective-permute-start.20) | collective-permute-done | bytes 147488 | tf_op jit(solution)/shard_map/ppermute | solution.py:922
  198.1 0.8 collective-permute-start.23
  199.0 3.4 %collective-permute-done.24.ffn_oth = bf16[8,4,9,8,128]{4,3,2,1,0:T(8,128)(2,1)S(1)} collective-permute-done((bf16[8,4,9,8,128]{4,3,2,1,0:T(8,128)(2,1)S(1)}, bf16[8,4,9,8,128]{4,3,2,1,0:T(8,128)(2,1)S(1)}, u32[]{:S(2)}, u32[]{:S(2)}) %collective-permute-start.24) | collective-permute-done | bytes 589856 | tf_op jit(solution)/shard_map/ppermute | solution.py:919
  202.4 3.6 %final_ffn.1 = (f32[768,384]{1,0:T(8,128)}, f32[384,768]{1,0:T(8,128)}) custom-call(s32[2]{0:T(128)S(1)} %pad_add_fusion.place.refs_0_, bf16[8,4,9,8,128]{4,3,2,1,0:T(8,128)(2,1)S(1)} %bitcast.25, bf16[8,4,9,8,128]{4,3,2,1,0:T(8,128)(2,1)S(1)} %collective-permute-done.24.ffn_oth), custom_call_target="tpu_custom_call" | custom-call | tf_op jit(solution)/shard_map/final_ffn/pallas_call | solution.py:810
  206.0 4.1 %final.1 = (f32[768,768]{1,0:T(8,128)}, f32[768]{0:T(1024)}, f32[65,768]{1,0:T(8,128)}, f32[768,768]{1,0:T(8,128)}, f32[768]{0:T(1024)}, /*index=5*/f32[768]{0:T...) custom-call(s32[2]{0:T(128)S(1)} %pad_add_fusion.place.refs_0_, ...), custom_call_target="tpu_custom_call" | custom-call | tf_op jit(solution)/shard_map/final/pallas_call | solution.py:868
  (65 shorter events, 6.5 us)
Async XLA Ops:
  4.9 12.0 %copy-start.5 = (bf16[768]{0:T(1024)(128)(2,1)S(1)}, bf16[768]{0:T(1024)(128)(2,1)}, u32[]{:S(2)}) copy-start(bf16[768]{0:T(1024)(128)(2,1)} %param.25) | copy-start | bytes 4612
  4.9 12.0 %copy-start.6 = (bf16[768]{0:T(1024)(128)(2,1)S(1)}, bf16[768]{0:T(1024)(128)(2,1)}, u32[]{:S(2)}) copy-start(bf16[768]{0:T(1024)(128)(2,1)} %param.26) | copy-start | bytes 4612
  4.9 12.0 %copy-start.7 = (bf16[768]{0:T(1024)(128)(2,1)S(1)}, bf16[768]{0:T(1024)(128)(2,1)}, u32[]{:S(2)}) copy-start(bf16[768]{0:T(1024)(128)(2,1)} %param.21) | copy-start | bytes 4612
  4.9 12.0 %copy-start.8 = (bf16[768]{0:T(1024)(128)(2,1)S(1)}, bf16[768]{0:T(1024)(128)(2,1)}, u32[]{:S(2)}) copy-start(bf16[768]{0:T(1024)(128)(2,1)} %param.24) | copy-start | bytes 4612
  5.0 12.0 %copy-start.2 = (bf16[65,768]{1,0:T(8,128)(2,1)S(1)}, bf16[65,768]{1,0:T(8,128)(2,1)}, u32[]{:S(2)}) copy-start(bf16[65,768]{1,0:T(8,128)(2,1)} %refs_4_.1) | copy-start | bytes 299524
  5.0 12.0 %copy-start.3 = (s32[256]{0:T(256)S(1)}, s32[256]{0:T(256)}, u32[]{:S(2)}) copy-start(s32[256]{0:T(256)} %param.35) | copy-start | bytes 3076
  5.0 12.0 %copy-start.4 = (s32[1,4]{1,0:T(1,128)S(1)}, s32[1,4]{1,0:T(1,128)}, u32[]{:S(2)}) copy-start(s32[1,4]{1,0:T(1,128)} %refs_0_.1) | copy-start | bytes 52
  5.0 47.9 %all-to-all-start = ((bf16[128,10,8,128]{3,2,1,0:T(8,128)(2,1)}), bf16[128,10,8,128]{3,2,1,0:T(8,128)(2,1)}, u32[]{:S(2)}, u32[]{:S(2)}) async-start(bf16[128,10,8,128]{3,2,1,0:T(8,128)(2,1)} %prep.1), calls=%async_computation | async-start | bytes 5242880 | tf_op jit(solution)/shard_map/all_to_all | solution.py:928
  35.4 17.5 %collective-permute-start = (bf16[256,768]{1,0:T(8,128)(2,1)S(1)}, bf16[256,768]{1,0:T(8,128)(2,1)S(1)}, u32[]{:S(2)}, u32[]{:S(2)}) collective-permute-start(bf16[256,768]{1,0:T(8,128)(2,1)S(1)} %get-tuple-element.94.refs_0_), channel_id=1, source_target_pairs={{0,8},{8,0},{16,24},{24,16},{32,40},{40,32},{48,56},{56,48},{64,72... | collective-permute-start | bytes 1179656 | tf_op jit(solution)/shard_map/ppermute | solution.py:919
  36.6 15.8 %collective-permute-start.2 = (bf16[128,768]{1,0:T(8,128)(2,1)S(1)}, bf16[128,768]{1,0:T(8,128)(2,1)S(1)}, u32[]{:S(2)}, u32[]{:S(2)}) collective-permute-start(bf16[128,768]{1,0:T(8,128)(2,1)S(1)} %get-tuple-element.97), channel_id=1, source_target_pairs={{0,16},{8,24},{16,32},{24,40},{32,48},{40,56},{48,0},{56,8},{64,80... | collective-permute-start | bytes 589832 | tf_op jit(solution)/shard_map/ppermute | solution.py:922
  37.2 15.6 %collective-permute-start.3 = (bf16[128,768]{1,0:T(8,128)(2,1)S(1)}, bf16[128,768]{1,0:T(8,128)(2,1)S(1)}, u32[]{:S(2)}, u32[]{:S(2)}) collective-permute-start(bf16[128,768]{1,0:T(8,128)(2,1)S(1)} %get-tuple-element.98), channel_id=1, source_target_pairs={{0,48},{8,56},{16,0},{24,8},{32,16},{40,24},{48,32},{56,40},{64,11... | collective-permute-start | bytes 589832 | tf_op jit(solution)/shard_map/ppermute | solution.py:925
  52.4 6.4 %collective-permute-start.4 = (bf16[128,768]{1,0:T(8,128)(2,1)S(1)}, bf16[128,768]{1,0:T(8,128)(2,1)S(1)}, u32[]{:S(2)}, u32[]{:S(2)}) collective-permute-start(bf16[128,768]{1,0:T(8,128)(2,1)S(1)} %collective-permute-done.2.got_a), channel_id=1, source_target_pairs={{0,8},{8,0},{16,24},{24,16},{32,40},{40,32},{48,56},{56,48},{64,72... | collective-permute-start | bytes 589832 | tf_op jit(solution)/shard_map/ppermute | solution.py:919
  52.8 6.0 %collective-permute-start.5 = (bf16[128,768]{1,0:T(8,128)(2,1)S(1)}, bf16[128,768]{1,0:T(8,128)(2,1)S(1)}, u32[]{:S(2)}, u32[]{:S(2)}) collective-permute-start(bf16[128,768]{1,0:T(8,128)(2,1)S(1)} %collective-permute-done.3.got_b), channel_id=1, source_target_pairs={{0,8},{8,0},{16,24},{24,16},{32,40},{40,32},{48,56},{56,48},{64,72... | collective-permute-start | bytes 589832 | tf_op jit(solution)/shard_map/ppermute | solution.py:919
  58.9 7.5 %copy-start.9 = (bf16[768]{0:T(1024)(128)(2,1)S(1)}, bf16[768]{0:T(1024)(128)(2,1)}, u32[]{:S(2)}) copy-start(bf16[768]{0:T(1024)(128)(2,1)} %param.30) | copy-start | bytes 4612
  58.9 7.5 %copy-start.10 = (bf16[768]{0:T(1024)(128)(2,1)S(1)}, bf16[768]{0:T(1024)(128)(2,1)}, u32[]{:S(2)}) copy-start(bf16[768]{0:T(1024)(128)(2,1)} %param.31) | copy-start | bytes 4612
  58.9 7.5 %copy-start.11 = (bf16[768]{0:T(1024)(128)(2,1)S(1)}, bf16[768]{0:T(1024)(128)(2,1)}, u32[]{:S(2)}) copy-start(bf16[768]{0:T(1024)(128)(2,1)} %param.32) | copy-start | bytes 4612
  58.9 13.3 %copy-start = (f32[256,768]{1,0:T(8,128)S(1)}, f32[256,768]{1,0:T(8,128)}, u32[]{:S(2)}) copy-start(f32[256,768]{1,0:T(8,128)} %get-tuple-element.93.refs_0_.refs_6_) | copy-start | bytes 2359300
  58.9 13.3 %copy-start.1 = (bf16[256,768]{1,0:T(8,128)(2,1)S(1)}, bf16[256,768]{1,0:T(8,128)(2,1)}, u32[]{:S(2)}) copy-start(bf16[256,768]{1,0:T(8,128)(2,1)} %refs_10_.4) | copy-start | bytes 1179652
  62.7 1.8 collective-permute-start.6
  63.2 3.2 %collective-permute-start.1 = (bf16[256,768]{1,0:T(8,128)(2,1)S(1)}, bf16[256,768]{1,0:T(8,128)(2,1)S(1)}, u32[]{:S(2)}, u32[]{:S(2)}) collective-permute-start(bf16[256,768]{1,0:T(8,128)(2,1)S(1)} %get-tuple-element.96), channel_id=1, source_target_pairs={{0,8},{8,0},{16,24},{24,16},{32,40},{40,32},{48,56},{56,48},{64,72... | collective-permute-start | bytes 1179656 | tf_op jit(solution)/shard_map/ppermute | solution.py:919
  64.6 6.4 %collective-permute-start.7 = (bf16[128,768]{1,0:T(8,128)(2,1)S(1)}, bf16[128,768]{1,0:T(8,128)(2,1)S(1)}, u32[]{:S(2)}, u32[]{:S(2)}) collective-permute-start(bf16[128,768]{1,0:T(8,128)(2,1)S(1)} %get-tuple-element.103), channel_id=1, source_target_pairs={{0,48},{8,56},{16,0},{24,8},{32,16},{40,24},{48,32},{56,40},{64,11... | collective-permute-start | bytes 589832 | tf_op jit(solution)/shard_map/ppermute | solution.py:925
  65.2 7.0 %collective-permute-start.8 = (bf16[128,768]{1,0:T(8,128)(2,1)S(1)}, bf16[128,768]{1,0:T(8,128)(2,1)S(1)}, u32[]{:S(2)}, u32[]{:S(2)}) collective-permute-start(bf16[128,768]{1,0:T(8,128)(2,1)S(1)} %get-tuple-element.104), channel_id=1, source_target_pairs={{0,16},{8,24},{16,32},{24,40},{32,48},{40,56},{48,0},{56,8},{64,80... | collective-permute-start | bytes 589832 | tf_op jit(solution)/shard_map/ppermute | solution.py:922
  74.0 4.3 %collective-permute-start.9 = (bf16[256,768]{1,0:T(8,128)(2,1)S(1)}, bf16[256,768]{1,0:T(8,128)(2,1)S(1)}, u32[]{:S(2)}, u32[]{:S(2)}) collective-permute-start(bf16[256,768]{1,0:T(8,128)(2,1)S(1)} %get-tuple-element.106.refs_0_), channel_id=1, source_target_pairs={{0,8},{8,0},{16,24},{24,16},{32,40},{40,32},{48,56},{56,48},{64,72... | collective-permute-start | bytes 1179656 | tf_op jit(solution)/shard_map/ppermute | solution.py:919
  75.6 7.7 %collective-permute-start.10 = (bf16[128,768]{1,0:T(8,128)(2,1)S(1)}, bf16[128,768]{1,0:T(8,128)(2,1)S(1)}, u32[]{:S(2)}, u32[]{:S(2)}) collective-permute-start(bf16[128,768]{1,0:T(8,128)(2,1)S(1)} %get-tuple-element.109), channel_id=1, source_target_pairs={{0,16},{8,24},{16,32},{24,40},{32,48},{40,56},{48,0},{56,8},{64,80... | collective-permute-start | bytes 589832 | tf_op jit(solution)/shard_map/ppermute | solution.py:922
  75.6 7.7 %collective-permute-start.11 = (bf16[128,768]{1,0:T(8,128)(2,1)S(1)}, bf16[128,768]{1,0:T(8,128)(2,1)S(1)}, u32[]{:S(2)}, u32[]{:S(2)}) collective-permute-start(bf16[128,768]{1,0:T(8,128)(2,1)S(1)} %get-tuple-element.110), channel_id=1, source_target_pairs={{0,48},{8,56},{16,0},{24,8},{32,16},{40,24},{48,32},{56,40},{64,11... | collective-permute-start | bytes 589832 | tf_op jit(solution)/shard_map/ppermute | solution.py:925
  83.3 1.9 collective-permute-start.13
  84.2 1.4 collective-permute-start.14
  89.0 2.0 collective-permute-start.15
  91.1 6.8 %collective-permute-start.16 = (bf16[128,768]{1,0:T(8,128)(2,1)S(1)}, bf16[128,768]{1,0:T(8,128)(2,1)S(1)}, u32[]{:S(2)}, u32[]{:S(2)}) collective-permute-start(bf16[128,768]{1,0:T(8,128)(2,1)S(1)} %get-tuple-element.129), channel_id=1, source_target_pairs={{0,48},{8,56},{16,0},{24,8},{32,16},{40,24},{48,32},{56,40},{64,11... | collective-permute-start | bytes 589832 | tf_op jit(solution)/shard_map/ppermute | solution.py:925
  93.8 7.2 %collective-permute-start.17 = (bf16[128,768]{1,0:T(8,128)(2,1)S(1)}, bf16[128,768]{1,0:T(8,128)(2,1)S(1)}, u32[]{:S(2)}, u32[]{:S(2)}) collective-permute-start(bf16[128,768]{1,0:T(8,128)(2,1)S(1)} %get-tuple-element.130), channel_id=1, source_target_pairs={{0,16},{8,24},{16,32},{24,40},{32,48},{40,56},{48,0},{56,8},{64,80... | collective-permute-start | bytes 589832 | tf_op jit(solution)/shard_map/ppermute | solution.py:922
  101.0 39.2 %all-to-all-start.1 = ((bf16[128,9,8,128]{3,2,1,0:T(8,128)(2,1)}), bf16[128,9,8,128]{3,2,1,0:T(8,128)(2,1)S(1)}, u32[]{:S(2)}, u32[]{:S(2)}) async-start(bf16[128,9,8,128]{3,2,1,0:T(8,128)(2,1)} %bitcast.28), calls=%async_computation.1 | async-start | bytes 4718592 | tf_op jit(solution)/shard_map/all_to_all | solution.py:928
  109.0 2.7 %collective-permute-start.12 = (bf16[256,768]{1,0:T(8,128)(2,1)S(1)}, bf16[256,768]{1,0:T(8,128)(2,1)S(1)}, u32[]{:S(2)}, u32[]{:S(2)}) collective-permute-start(bf16[256,768]{1,0:T(8,128)(2,1)S(1)} %get-tuple-element.112), channel_id=1, source_target_pairs={{0,8},{8,0},{16,24},{24,16},{32,40},{40,32},{48,56},{56,48},{64,72... | collective-permute-start | bytes 1179656 | tf_op jit(solution)/shard_map/ppermute | solution.py:919
  124.9 3.1 %collective-permute-start.18 = (bf16[640,8,128]{2,1,0:T(8,128)(2,1)S(1)}, bf16[640,8,128]{2,1,0:T(8,128)(2,1)S(1)}, u32[]{:S(2)}, u32[]{:S(2)}) collective-permute-start(bf16[640,8,128]{2,1,0:T(8,128)(2,1)S(1)} %get-tuple-element.150), channel_id=1, source_target_pairs={{0,8},{8,0},{16,24},{24,16},{32,40},{40,32},{48,56},{56,48},{64,72... | collective-permute-start | bytes 3932168 | tf_op jit(solution)/shard_map/ppermute | solution.py:919
  140.6 26.4 %all-to-all-start.2 = ((bf16[128,5,8,128]{3,2,1,0:T(8,128)(2,1)}), bf16[128,5,8,128]{3,2,1,0:T(8,128)(2,1)S(1)}, u32[]{:S(2)}, u32[]{:S(2)}) async-start(bf16[128,5,8,128]{3,2,1,0:T(8,128)(2,1)} %bitcast.29), calls=%async_computation.2 | async-start | bytes 2621440 | tf_op jit(solution)/shard_map/all_to_all | solution.py:928
  146.5 17.1 %collective-permute-start.19 = (bf16[4,9,8,128]{3,2,1,0:T(8,128)(2,1)S(1)}, bf16[4,9,8,128]{3,2,1,0:T(8,128)(2,1)S(1)}, u32[]{:S(2)}, u32[]{:S(2)}) collective-permute-start(bf16[4,9,8,128]{3,2,1,0:T(8,128)(2,1)S(1)} %sum_ffn.1), channel_id=1, source_target_pairs={{0,64},{8,72},{16,80},{24,88},{32,96},{40,104},{48,112},{56,120},{... | collective-permute-start | bytes 221192 | tf_op jit(solution)/shard_map/ppermute | solution.py:975
  168.3 29.8 %all-to-all-start.3 = ((bf16[128,5,8,128]{3,2,1,0:T(8,128)(2,1)}), bf16[128,5,8,128]{3,2,1,0:T(8,128)(2,1)S(1)}, u32[]{:S(2)}, u32[]{:S(2)}) async-start(bf16[128,5,8,128]{3,2,1,0:T(8,128)(2,1)} %sum_rest.1), calls=%async_computation.3 | async-start | bytes 2621440 | tf_op jit(solution)/shard_map/all_to_all | solution.py:928
  174.8 18.7 %collective-permute-start.22 = (bf16[2,4,9,8,128]{4,3,2,1,0:T(8,128)(2,1)S(1)}, bf16[2,4,9,8,128]{4,3,2,1,0:T(8,128)(2,1)S(1)}, u32[]{:S(2)}, u32[]{:S(2)}) collective-permute-start(bf16[2,4,9,8,128]{4,3,2,1,0:T(8,128)(2,1)S(1)} %pad_maximum_fusion.1), channel_id=1, source_target_pairs={{0,48},{8,56},{16,0},{24,8},{32,16},{40,24},{48,32},{56,40},{64,11... | collective-permute-start | bytes 442376 | tf_op jit(solution)/shard_map/ppermute | solution.py:925
  177.5 17.5 %collective-permute-start.21 = (bf16[2,4,9,8,128]{4,3,2,1,0:T(8,128)(2,1)S(1)}, bf16[2,4,9,8,128]{4,3,2,1,0:T(8,128)(2,1)S(1)}, u32[]{:S(2)}, u32[]{:S(2)}) collective-permute-start(bf16[2,4,9,8,128]{4,3,2,1,0:T(8,128)(2,1)S(1)} %pad_maximum_fusion.1), channel_id=1, source_target_pairs={{0,32},{8,40},{16,48},{24,56},{32,0},{40,8},{48,16},{56,24},{64,96... | collective-permute-start | bytes 442376 | tf_op jit(solution)/shard_map/ppermute | solution.py:978
  178.0 20.0 %collective-permute-start.20 = (bf16[2,4,9,8,128]{4,3,2,1,0:T(8,128)(2,1)S(1)}, bf16[2,4,9,8,128]{4,3,2,1,0:T(8,128)(2,1)S(1)}, u32[]{:S(2)}, u32[]{:S(2)}) collective-permute-start(bf16[2,4,9,8,128]{4,3,2,1,0:T(8,128)(2,1)S(1)} %pad_maximum_fusion.1), channel_id=1, source_target_pairs={{0,16},{8,24},{16,32},{24,40},{32,48},{40,56},{48,0},{56,8},{64,80... | collective-permute-start | bytes 442376 | tf_op jit(solution)/shard_map/ppermute | solution.py:922
  198.1 7.9 %collective-permute-start.23 = (bf16[640,8,128]{2,1,0:T(8,128)(2,1)S(1)}, bf16[640,8,128]{2,1,0:T(8,128)(2,1)S(1)}, u32[]{:S(2)}, u32[]{:S(2)}) collective-permute-start(bf16[640,8,128]{2,1,0:T(8,128)(2,1)S(1)} %bitcast.22), channel_id=1, source_target_pairs={{0,8},{8,0},{16,24},{24,16},{32,40},{40,32},{48,56},{56,48},{64,72... | collective-permute-start | bytes 3932168 | tf_op jit(solution)/shard_map/ppermute | solution.py:919
  198.9 3.5 %collective-permute-start.24 = (bf16[8,4,9,8,128]{4,3,2,1,0:T(8,128)(2,1)S(1)}, bf16[8,4,9,8,128]{4,3,2,1,0:T(8,128)(2,1)S(1)}, u32[]{:S(2)}, u32[]{:S(2)}) collective-permute-start(bf16[8,4,9,8,128]{4,3,2,1,0:T(8,128)(2,1)S(1)} %bitcast.24), channel_id=1, source_target_pairs={{0,8},{8,0},{16,24},{24,16},{32,40},{40,32},{48,56},{56,48},{64,72... | collective-permute-start | bytes 1769480 | tf_op jit(solution)/shard_map/ppermute | solution.py:919

commit v4 on v3

--- a/solution.py
+++ b/solution.py
@@ -107,12 +107,34 @@
         self.buf[index] = value
 
 
+class StagedPair:
+    def __init__(self, ref, buf, sems):
+        self.buf = buf
+        self.copies = [pltpu.make_async_copy(ref.at[i], buf.at[i], sems.at[i]) for i in range(2)]
+        self.pending = [True, True]
+        for copy in self.copies:
+            copy.start()
+
+    def ready(self):
+        for i in range(2):
+            if self.pending[i]:
+                self.copies[i].wait()
+                self.pending[i] = False
+
+    def __getitem__(self, index):
+        i = index[0]
+        if self.pending[i]:
+            self.copies[i].wait()
+            self.pending[i] = False
+        return self.buf[index]
+
+
 def staged_call(kernel, name, mib, ins, outs, scratch=()):
-    spec = {"smem": SMEM, "vmem": VMEM, "hbm": HBM}
+    spec = {"smem": SMEM, "vmem": VMEM, "hbm": HBM, "pair": HBM}
     arrays = [a for _, a in ins]
     kinds = [k for k, _ in ins] + [k for k, _ in outs]
     avals = arrays + [o for _, o in outs]
-    staged = [i for i, k in enumerate(kinds) if k == "hbm"]
+    staged = [i for i, k in enumerate(kinds) if k in ("hbm", "pair")]
     n_in = len(ins)
 
     if not staged:
@@ -133,7 +155,10 @@
         bufs = refs[split:]
         refs = refs[:split]
         for n, i in enumerate(staged):
-            refs[i] = Staged(refs[i], bufs[n], sems.at[n], i < n_in)
+            if kinds[i] == "pair":
+                refs[i] = StagedPair(refs[i], bufs[n], sems.at[n])
+            else:
+                refs[i] = Staged(refs[i], bufs[n], sems.at[n, 0], i < n_in)
         kernel(*refs)
         for i in staged:
             if i < n_in:
@@ -146,59 +171,71 @@
 
     buffers = [pltpu.VMEM(avals[i].shape, avals[i].dtype) for i in staged]
     arrays = [
-        pltpu.with_memory_space_constraint(a, pltpu.HBM) if k == "hbm" else a for k, a in ins
+        a if k in ("smem", "vmem") else pltpu.with_memory_space_constraint(a, pltpu.HBM)
+        for k, a in ins
     ]
     return pl.pallas_call(
         run,
         out_shape=tuple(pltpu.HBM(o.shape, o.dtype) if k == "hbm" else o for k, o in outs),
         in_specs=[spec[k] for k, _ in ins],
         out_specs=tuple(spec[k] for k, _ in outs),
-        scratch_shapes=[*scratch, *buffers, pltpu.SemaphoreType.DMA((len(staged),))],
+        scratch_shapes=[*scratch, *buffers, pltpu.SemaphoreType.DMA((len(staged), 2))],
         compiler_params=params(mib),
         name=name,
     )(*arrays)
 
 
-def prep_kernel(place, up_ref, down_ref, bias_ref, out_ref, up, down, tall, cols, block, sems):
+def prep_kernel(place, up_ref, down_ref, bias_hbm, out_ref, half, piece, bias_ref, sems):
     rep = place[0] % 8
-    side = rep % 2
-
-    @pl.when(place[0] < 8)
-    def _():
-        copy = pltpu.make_async_copy(up_ref, up, sems.at[0])
-        copy.start()
-        cols[...] = jnp.broadcast_to(bias_ref[...].astype(f32), (8, 384)).T
-        copy.wait()
-        tall[...] = up[...].astype(f32).T
-
-    @pl.when(place[0] >= 8)
-    def _():
-        copy = pltpu.make_async_copy(down_ref, down, sems.at[0])
-        copy.start()
-        cols[...] = jnp.zeros(cols.shape, f32)
-        copy.wait()
-        tall[...] = down[...].astype(f32)
-
-    for q in range(CLASSES):
-        start = pl.multiple_of(SUB * q + PIECE * (rep // 2), 8)
-        rows = tall[pl.ds(start, PIECE), :]
-        piece = []
-        for j in range(3):
-            left = rows[:, j * 128 : j * 128 + 128]
-            right = rows[:, 384 + j * 128 : 512 + j * 128]
-            piece.append(jnp.where(side == 0, left, right).reshape(3, 8, 128).astype(bf16))
-        bias = jnp.zeros((8, 128), f32)
-        for rt in range(3):
-            col = cols[pl.ds(pl.multiple_of(start + 8 * rt, 8), 8), :][:, 0:1]
-            bias = jnp.where(lanes((8, 128)) == rt, jnp.broadcast_to(col, (8, 128)), bias)
-        bias = jnp.where(side == 0, bias, 0.0).astype(bf16)
-        for n in range(8):
+    is_up = place[0] < 8
+    at = pl.ds(pl.multiple_of(rep % 2 * 384, 128), 384)
+    up = pltpu.make_async_copy(up_ref.at[at, :], half, sems.at[0])
+    down = pltpu.make_async_copy(down_ref.at[:, at], half, sems.at[0])
+    bias_copy = pltpu.make_async_copy(bias_hbm, bias_ref, sems.at[33])
+    bias_copy.start()
+
+    @pl.when(is_up)
+    def _():
+        up.start()
+
+    @pl.when(jnp.logical_not(is_up))
+    def _():
+        down.start()
+
+    n = lax.broadcasted_iota(i32, (SUB, 384), 0)
+    q = sum((n >= PIECE * k).astype(i32) for k in range(1, CLASSES))
+    unit = (SUB - PIECE) * q + n + PIECE * (rep // 2)
+    pick = jnp.where(unit == lanes((SUB, 384)), 1.0, 0.0).astype(bf16)
+    scale = jnp.where(is_up & (rep % 2 == 0), 1.0, 0.0)
+    bias_copy.wait()
+    bias = jnp.broadcast_to(bias_ref[...].astype(f32) * scale, (16, 384)).astype(bf16)
+    column = dot_last(pick, bias)[:, 0:1]
+
+    def fill(rows):
+        for k in range(CLASSES):
+            rs = slice(PIECE * k, PIECE * k + PIECE)
             for j in range(3):
-                block[q * 8 + n, 3 * j : 3 * j + 3] = piece[j]
-            block[q * 8 + n, UNITS - 1] = bias
+                part = rows[rs, j * 128 : j * 128 + 128].reshape(3, 8, 128)
+                piece[k, 3 * j : 3 * j + 3] = part.astype(bf16)
+            col = jnp.broadcast_to(column[rs], (PIECE, 128)).reshape(3, 8, 128)
+            lane = lanes((8, 128))
+            tile = jnp.where(lane == 0, col[0], jnp.where(lane == 1, col[1], col[2]))
+            piece[k, UNITS - 1] = tile.astype(bf16)
+
+    @pl.when(is_up)
+    def _():
+        up.wait()
+        fill(dot_last(pick, half[...]))
+
+    @pl.when(jnp.logical_not(is_up))
+    def _():
+        down.wait()
+        fill(dot(pick, half[...]))
+
     copies = [
-        pltpu.make_async_copy(block, out_ref.at[32 * i : 32 * i + 32], sems.at[1 + i])
-        for i in range(4)
+        pltpu.make_async_copy(piece, out_ref.at[g, :, t], sems.at[1 + 8 * g + t])
+        for g in range(4)
+        for t in range(8)
     ]
     for copy in copies:
         copy.start()
@@ -207,18 +244,16 @@
 
 
 def prep(place, w_up, w_down, b_up):
-    return pl.pallas_call(
+    out = pl.pallas_call(
         prep_kernel,
-        out_shape=pltpu.HBM((128, UNITS, 8, 128), bf16),
-        in_specs=[SMEM, HBM, HBM, VMEM],
+        out_shape=pltpu.HBM((4, CLASSES, 8, UNITS, 8, 128), bf16),
+        in_specs=[SMEM, HBM, HBM, HBM],
         out_specs=HBM,
         scratch_shapes=[
-            pltpu.VMEM((768, 384), bf16),
-            pltpu.VMEM((384, 768), bf16),
-            pltpu.VMEM((384, 768), f32),
-            pltpu.VMEM((384, 8), f32),
-            pltpu.VMEM((32, UNITS, 8, 128), bf16),
-            pltpu.SemaphoreType.DMA((5,)),
+            pltpu.VMEM((384, 384), bf16),
+            pltpu.VMEM((CLASSES, UNITS, 8, 128), bf16),
+            pltpu.VMEM((384,), bf16),
+            pltpu.SemaphoreType.DMA((34,)),
         ],
         compiler_params=params(16),
         name="prep",
@@ -226,8 +261,9 @@
         place,
         pltpu.with_memory_space_constraint(w_up, pltpu.HBM),
         pltpu.with_memory_space_constraint(w_down, pltpu.HBM),
-        b_up,
-    )
+        pltpu.with_memory_space_constraint(b_up, pltpu.HBM),
+    )
+    return out.reshape(128, UNITS, 8, 128)
 
 
 def segment_ends(len_ref):
@@ -455,26 +491,24 @@
     lax.fori_loop(0, HIDDEN // 256, block, 0)
 
 
-def ffn_near_kernel(
-    own, sib, w, act, slope, part_own, part_sib, rows_out, wu, wd, rows, acc,
+def ffn_far_kernel(
+    got_a, got_b, sib_a, sib_b, w, act, slope, part_own, part_sib, rows_out, wu, wd, rows, acc,
 ):
-    rows[0:ROWS, 0:WIDTH] = own[...]
-    rows[ROWS:, 0:WIDTH] = sib[...]
+    for i, ref in enumerate((got_a, got_b, sib_a, sib_b)):
+        rows[i * HALF : i * HALF + HALF, 0:WIDTH] = ref[...]
     rows[:, WIDTH:] = jnp.where(lanes((2 * ROWS, 128)) < 3, 1.0, 0.0).astype(bf16)
+    rows_out[...] = rows[:, 0:WIDTH]
     unpack(w, 0, wu)
     unpack_bias(w, wu)
     unpack(w, 1, wd)
-    rows_out[...] = rows[:, 0:WIDTH]
     ffn_blocks(rows, wu, wd, act, slope, acc)
     part_own[...] = acc[0:ROWS]
     part_sib[...] = acc[ROWS:].astype(bf16)
 
 
-def ffn_far_kernel(
-    got_a, got_b, sib_a, sib_b, wu, wd, act, slope, part_own, part_sib, rows_out, rows, acc,
-):
-    for i, ref in enumerate((got_a, got_b, sib_a, sib_b)):
-        rows[i * HALF : i * HALF + HALF, 0:WIDTH] = ref[...]
+def ffn_near_kernel(own, sib, wu, wd, act, slope, part_own, part_sib, rows_out, rows, acc):
+    rows[0:ROWS, 0:WIDTH] = own[...]
+    rows[ROWS:, 0:WIDTH] = sib[...]
     rows[:, WIDTH:] = jnp.where(lanes((2 * ROWS, 128)) < 3, 1.0, 0.0).astype(bf16)
     rows_out[...] = rows[:, 0:WIDTH]
     ffn_blocks(rows, wu, wd, act, slope, acc)
@@ -492,15 +526,16 @@
     )
 
 
-def ffn_near(own, sib, weights):
+def ffn_far(got_a, got_b, sib_a, sib_b, weights):
+    rows = [("vmem", a) for a in (got_a, got_b, sib_a, sib_b)]
     return ffn_call(
-        ffn_near_kernel, "ffn_near", [("vmem", own), ("vmem", sib), ("hbm", weights)],
+        ffn_far_kernel, "ffn_far", [*rows, ("pair", weights)],
         [shape((HIDDEN, WIDTH + 128), bf16), shape((HIDDEN, WIDTH), bf16)],
     )
 
 
-def ffn_far(*args):
-    return ffn_call(ffn_far_kernel, "ffn_far", [("vmem", a) for a in args], [])
+def ffn_near(*args):
+    return ffn_call(ffn_near_kernel, "ffn_near", [("vmem", a) for a in args], [])
 
 
 def combine_kernel(own, got, out_a, out_b):
@@ -783,7 +818,7 @@
     core = place[0] % 2
 
     def index(m, a):
-        return (place[0] // 2 % 4 + 4 - a) % 4 * 2 + (m + place[0] // 8) % 2
+        return (m + place[0] // 8) % 2 * 4 + (place[0] // 2 % 4 + 4 - a) % 4
 
     def spread(ref):
         for a in range(PIECES):
@@ -930,7 +965,7 @@
     def row(v):
         return v.reshape(1, -1)
 
-    weights = exchange(prep(place, w_up, w_down, row(b_up)))
+    weights = exchange(prep(place, w_up, w_down, b_up))
     weights = weights.reshape(2, PIECES, 2, 8, UNITS, 8, 128)
     (n1, inv1, low, low_a, low_b, ctx, collide, nrm, scl, wave, wavet, ks, vs, tapt, live) = attend(
         seq_lengths, block_input, w_value, row(b_value), conv_kernel, w_out, row(b_out),
@@ -938,13 +973,16 @@
     )
     low_sib = swap(low)
     row_a, row_b = ahead(low_a), behind(low_b)
-    act_n, slope_n, near_own, near_sib, rows_n, wu, wd = ffn_near(low, low_sib, weights)
-    act_f, slope_f, far_own, far_sib, rows_f = ffn_far(
-        row_a, row_b, swap(row_a), swap(row_b), wu, wd
+    act_f, slope_f, far_own, far_sib, rows_f, wu, wd = ffn_far(
+        row_a, row_b, swap(row_a), swap(row_b), weights
     )
     sent_a, sent_b = combine(far_own, swap(far_sib))
+    wu, sent_a, sent_b = lax.optimization_barrier((wu, sent_a, sent_b))
+    act_n, slope_n, near_own, near_sib, rows_n = ffn_near(low, low_sib, wu, wd)
+    back_a, back_b = behind(sent_a), ahead(sent_b)
+    near_sib, back_a, back_b = lax.optimization_barrier((near_sib, back_a, back_b))
     block_output, second, grad, grad_a, grad_b, sums = middle(
-        n1, near_own, swap(near_sib), behind(sent_a), ahead(sent_b), row(b_down), row(gain_attn),
+        n1, near_own, swap(near_sib), back_a, back_b, row(b_down), row(gain_attn),
         row(shift_attn), row(gain_ffn), row(shift_ffn), out_grad,
     )
     got_a, got_b = ahead(grad_a), behind(grad_b)
@@ -972,15 +1010,18 @@
     pair = pair.reshape(128, PACK // 128, 8, 128)
     owned = sum_ffn(owned)
     pair, owned = lax.optimization_barrier((pair, owned))
-    two = jnp.stack([owned, lax.ppermute(owned, "dp", [(i, (i + 8) % 16) for i in range(n_dp)])])
+    around = []
+    for side in range(2):
+        for by in range(4):
+            if side or by:
+                pairs = [(i, (i // 8 + side) % 2 * 8 + shift(i % 8, by)) for i in range(n_dp)]
+                around.append(lax.ppermute(owned, "dp", pairs))
     summed = sum_rest(exchange(pair))
-    summed, two = lax.optimization_barrier((summed, two))
-    opposite = lax.ppermute(two, "dp", [(i, shift(i, 2)) for i in range(n_dp)])
-    ffn_own = jnp.stack([two, ahead(two), opposite, behind(two)])
+    summed, *around = lax.optimization_barrier((summed, *around))
     back = exchange(summed).reshape(PACK, 8, 128)
-    back, ffn_own = lax.optimization_barrier((back, ffn_own))
-    ffn_own = ffn_own.reshape(8, CLASSES, GRAD_UNITS, 8, 128)
+    ffn_own = jnp.stack([owned, *around])
     g_up, g_down = final_ffn(place, ffn_own, swap(ffn_own))
+    back, g_up, g_down = lax.optimization_barrier((back, g_up, g_down))
     g_wv, g_bv, g_conv, g_wo, g_bo, g_ga, g_sa, g_bup, g_bd, g_gf, g_sf = final(
         place, back, swap(back)
     )

time: 211 us -> 208 us (0.986)
  waiting for transfers between devices: 82.7 us -> 71.2 us
  starting transfers between devices: 55.3 us -> 65 us
    ppermute x5 -> x4, waiting for transfers between devices: 20.9 us -> 2.3 us  [behind(): return lax.ppermute(x, 'dp', [(i, shift(i, -1)) for i in range(n_dp)])]
    all_to_all x4, waiting for transfers between devices: 14 us -> 24.5 us  [exchange(): return lax.all_to_all(x, ALL, 0, 0, tiled=True)]
    ppermute x2 -> x7, starting transfers between devices: 1.99 us -> 11.7 us  [body(): around.append(lax.ppermute(owned, 'dp', pairs))]
    ppermute x2 -> x7, waiting for transfers between devices: 17.2 us -> 12.9 us  [body(): around.append(lax.ppermute(owned, 'dp', pairs))]
    ppermute x13, waiting for transfers between devices: 9.32 us -> 12.9 us  [swap(): return lax.ppermute(x, 'dp', [(i, i ^ 1) for i in range(n_dp)])]
    ppermute x5 -> x4, starting transfers between devices: 10.8 us -> 7.37 us  [behind(): return lax.ppermute(x, 'dp', [(i, shift(i, -1)) for i in range(n_dp)])]
    ppermute x5 -> x4, waiting for transfers between devices: 21.4 us -> 18.6 us  [ahead(): return lax.ppermute(x, 'dp', [(i, shift(i, 1)) for i in range(n_dp)])]
    all_to_all x4, starting transfers between devices: 32.3 us -> 34.8 us  [exchange(): return lax.all_to_all(x, ALL, 0, 0, tiled=True)]
  transfers between devices with their start and end apart: 29 -> 32, of which waited for: 18 -> 22; matrix products, arithmetic and copies ran while one was open for 2% -> 2% of each run, Pallas kernels for 22% -> 22%
where the time goes in v4:
time: 208 us
  waiting for transfers between devices  71.2 us (34%)
  Pallas kernels  65.4 us (31%)
  starting transfers between devices  65 us (31%)
  matrix products  3.26 us (2%)
    pallas_call x7, Pallas kernels, staged_call(): pl.pallas_call(run, out_shape=tuple((pltpu.HBM(o.shape, o.dtype) if k ==...  48.6 us
    all_to_all x4, starting transfers between devices, exchange(): return lax.all_to_all(x, ALL, 0, 0, tiled=True)  34.8 us
    all_to_all x4, waiting for transfers between devices, exchange(): return lax.all_to_all(x, ALL, 0, 0, tiled=True)  24.5 us
    ppermute x4, waiting for transfers between devices, ahead(): return lax.ppermute(x, 'dp', [(i, shift(i, 1)) for i in range(n_dp)])  18.6 us
    ppermute x7, waiting for transfers between devices, body(): around.append(lax.ppermute(owned, 'dp', pairs))  12.9 us
    ppermute x13, waiting for transfers between devices, swap(): return lax.ppermute(x, 'dp', [(i, i ^ 1) for i in range(n_dp)])  12.9 us
    ppermute x7, starting transfers between devices, body(): around.append(lax.ppermute(owned, 'dp', pairs))  11.7 us
    ppermute x13, starting transfers between devices, swap(): return lax.ppermute(x, 'dp', [(i, i ^ 1) for i in range(n_dp)])  8.74 us
  transfers between devices with their start and end apart: 32, of which 22 were waited for; matrix products, arithmetic and copies ran while one was open for 2% of the time, Pallas kernels for 22%

profile of v4, /device:TPU:1, one launch (start us, length us, event | category | flops | bytes accessed | tf_op | source)
XLA Modules:
  0.0 207.7 jit_solution(12674250271311690828)
XLA Ops:
  0.7 3.6 %prep.1 = bf16[4,4,8,10,8,128]{5,4,3,2,1,0:T(8,128)(2,1)} custom-call(s32[2]{0:T(128)S(1)} %pad_add_fusion.place.refs_0_, bf16[768,384]{1,0:T(8,128)(2,1)} %up_ref.1, bf16[384,768]{1,0:T(8,128)(2,1)} %down_ref.1, bf16[384]{0:T(512)(128)(2,1)} %bias_hbm.1), custom_call_target="tpu_custom_call" | custom-call | tf_op jit(solution)/shard_map/prep/pallas_call | solution.py:247
  4.4 11.9 %all-to-all-start = ((bf16[128,10,8,128]{3,2,1,0:T(8,128)(2,1)}), bf16[128,10,8,128]{3,2,1,0:T(8,128)(2,1)}, u32[]{:S(2)}, u32[]{:S(2)}) async-start(bf16[128,10,8,128]{3,2,1,0:T(8,128)(2,1)} %bitcast.35), calls=%async_computation | async-start | bytes 5242880 | tf_op jit(solution)/shard_map/all_to_all | solution.py:963
  16.4 18.5 %attend.1 = (f32[256,768]{1,0:T(8,128)}, f32[256,128]{1,0:T(8,128)}, bf16[256,768]{1,0:T(8,128)(2,1)S(1)}, bf16[128,768]{1,0:T(8,128)(2,1)S(1)}, bf16[128,768]{1...) custom-call(s32[1,4]{1,0:T(1,128)S(1)} %copy-done.4, ...), custom_call_target="tpu_custom_call" | custom-call | tf_op jit(solution)/shard_map/attend/pallas_call | solution.py:177
  34.9 1.5 collective-permute-start.1
  36.4 1.4 collective-permute-start.2
  37.7 13.3 %collective-permute-done.1.refs_0_ = bf16[128,768]{1,0:T(8,128)(2,1)S(1)} collective-permute-done((bf16[128,768]{1,0:T(8,128)(2,1)S(1)}, bf16[128,768]{1,0:T(8,128)(2,1)S(1)}, u32[]{:S(2)}, u32[]{:S(2)}) %collective-permute-start.1) | collective-permute-done | bytes 196640 | tf_op jit(solution)/shard_map/ppermute | solution.py:957
  51.8 1.1 collective-permute-done.3.refs_2_
  53.3 5.6 %ffn_far.1 = (bf16[512,768]{1,0:T(8,128)(2,1)S(1)}, bf16[512,768]{1,0:T(8,128)(2,1)S(1)}, f32[256,768]{1,0:T(8,128)S(1)}, bf16[256,768]{1,0:T(8,128)(2,1)S(1)}, ...) custom-call(bf16[128,768]{1,0:T(8,128)(2,1)S(1)} %collective-permute-done.1.refs_0_, ...), custom_call_target="tpu_custom_call" | custom-call | tf_op jit(solution)/shard_map/ffn_far/pallas_call | solution.py:177
  59.5 1.2 collective-permute-done.5.got
  61.4 0.9 collective-permute-start.7
  62.3 3.8 %ffn_near.1 = (bf16[512,768]{1,0:T(8,128)(2,1)S(1)}, bf16[512,768]{1,0:T(8,128)(2,1)S(1)}, f32[256,768]{1,0:T(8,128)S(1)}, bf16[256,768]{1,0:T(8,128)(2,1)S(1)}, bf16[512,768]{1,0:T(8,128)(2,1)S(1)}) custom-call(bf16[256,768]{1,0:T(8,128)(2,1)S(1)} %get-tuple-element.107.own, bf16[256,768]{1,0:T(8,128)(2,1)S(1)} %collective-permute-done.sib, ...), custom_call_target="tpu_custom_call" | custom-call | tf_op jit(solution)/shard_map/ffn_near/pallas_call | solution.py:141
  66.1 0.9 collective-permute-done.6.refs_3_
  67.1 1.4 collective-permute-done.7.refs_4_
  68.5 1.4 collective-permute-start.8
  69.9 1.3 collective-permute-done.8.refs_2_
  71.2 1.9 middle.1
  73.6 2.7 %collective-permute-start.11 = (bf16[128,768]{1,0:T(8,128)(2,1)S(1)}, bf16[128,768]{1,0:T(8,128)(2,1)S(1)}, u32[]{:S(2)}, u32[]{:S(2)}) collective-permute-start(bf16[128,768]{1,0:T(8,128)(2,1)S(1)} %get-tuple-element.129), channel_id=1, source_target_pairs={{0,48},{8,56},{16,0},{24,8},{32,16},{40,24},{48,32},{56,40},{64,11... | collective-permute-start | bytes 589832 | tf_op jit(solution)/shard_map/ppermute | solution.py:960
  76.2 4.1 %back_near.1 = (f32[256,768]{1,0:T(8,128)}, bf16[256,768]{1,0:T(8,128)(2,1)S(1)}, bf16[512,768]{1,0:T(8,128)(2,1)S(1)}, bf16[512,768]{1,0:T(8,128)(2,1)S(1)}, f32[8,768]{1,0:T(8,128)}) custom-call(bf16[256,768]{1,0:T(8,128)(2,1)S(1)} %get-tuple-element.125.refs_0_, bf16[256,768]{1,0:T(8,128)(2,1)S(1)} %collective-permute-done.9.refs_1_, ...), custom_call_target="tpu_custom_call" | custom-call | tf_op jit(solution)/shard_map/back_near/pallas_call | solution.py:177
  81.1 1.0 collective-permute-start.13
  83.5 3.4 %back_far.1 = (f32[256,768]{1,0:T(8,128)S(1)}, bf16[256,768]{1,0:T(8,128)(2,1)S(1)}, bf16[512,768]{1,0:T(8,128)(2,1)S(1)}, bf16[512,768]{1,0:T(8,128)(2,1)S(1)}, f32[8,768]{1,0:T(8,128)}) custom-call(bf16[128,768]{1,0:T(8,128)(2,1)S(1)} %collective-permute-done.10.refs_0_, bf16[128,768]{1,0:T(8,128)(2,1)S(1)} %collective-permute-done.11.refs_1_, ...), custom_call_target="tpu_custom_call" | custom-call | tf_op jit(solution)/shard_map/back_far/pallas_call | solution.py:177
  89.0 2.7 %collective-permute-start.16 = (bf16[128,768]{1,0:T(8,128)(2,1)S(1)}, bf16[128,768]{1,0:T(8,128)(2,1)S(1)}, u32[]{:S(2)}, u32[]{:S(2)}) collective-permute-start(bf16[128,768]{1,0:T(8,128)(2,1)S(1)} %get-tuple-element.148), channel_id=1, source_target_pairs={{0,48},{8,56},{16,0},{24,8},{32,16},{40,24},{48,32},{56,40},{64,11... | collective-permute-start | bytes 589832 | tf_op jit(solution)/shard_map/ppermute | solution.py:960
  92.6 1.8 pack.1
  94.4 1.4 collective-permute-done.16.refs_3_
  95.8 3.1 %collective-permute-done.17.refs_4_ = bf16[128,768]{1,0:T(8,128)(2,1)S(1)} collective-permute-done((bf16[128,768]{1,0:T(8,128)(2,1)S(1)}, bf16[128,768]{1,0:T(8,128)(2,1)S(1)}, u32[]{:S(2)}, u32[]{:S(2)}) %collective-permute-start.17) | collective-permute-done | bytes 196640 | tf_op jit(solution)/shard_map/ppermute | solution.py:957
  98.9 8.1 %all-to-all-start.1 = ((bf16[128,9,8,128]{3,2,1,0:T(8,128)(2,1)}), bf16[128,9,8,128]{3,2,1,0:T(8,128)(2,1)S(1)}, u32[]{:S(2)}, u32[]{:S(2)}) async-start(bf16[128,9,8,128]{3,2,1,0:T(8,128)(2,1)} %bitcast.36), calls=%async_computation.1 | async-start | bytes 4718592 | tf_op jit(solution)/shard_map/all_to_all | solution.py:963
  107.0 1.4 collective-permute-start.12
  108.4 1.3 collective-permute-done.12.refs_2_
  109.7 13.4 %attend_back.1 = (f32[256,768]{1,0:T(8,128)}, bf16[640,8,128]{2,1,0:T(8,128)(2,1)S(1)}, bf16[640,8,128]{2,1,0:T(8,128)(2,1)S(1)}) custom-call(s32[2]{0:T(128)S(1)} %pad_add_fusion.place.refs_0_, f32[256,768]{1,0:T(8,128)} %get-tuple-element.127.refs_1_, bf16[256,768]{1,0:T(8,128)(2,1)S(1)} %collective-permute-done.12.refs_2_, ...), custom_call_target="tpu_custom_call" | custom-call | tf_op jit(solution)/shard_map/attend_back/pallas_call | solution.py:177
  123.6 2.7 %collective-permute-done.18 = bf16[640,8,128]{2,1,0:T(8,128)(2,1)S(1)} collective-permute-done((bf16[640,8,128]{2,1,0:T(8,128)(2,1)S(1)}, bf16[640,8,128]{2,1,0:T(8,128)(2,1)S(1)}, u32[]{:S(2)}, u32[]{:S(2)}) %collective-permute-start.18) | collective-permute-done | bytes 1310752 | tf_op jit(solution)/shard_map/ppermute | solution.py:954
  126.2 1.4 add_convert_fusion
  127.6 10.6 %all-to-all-done.1.got = bf16[128,9,8,128]{3,2,1,0:T(8,128)(2,1)S(1)} async-done(((bf16[128,9,8,128]{3,2,1,0:T(8,128)(2,1)}), bf16[128,9,8,128]{3,2,1,0:T(8,128)(2,1)S(1)}, u32[]{:S(2)}, u32[]{:S(2)}) %all-to-all-start.1) | async-done | bytes 2359328 | tf_op jit(solution)/shard_map/all_to_all | solution.py:963
  138.6 5.9 %all-to-all-start.2 = ((bf16[128,5,8,128]{3,2,1,0:T(8,128)(2,1)}), bf16[128,5,8,128]{3,2,1,0:T(8,128)(2,1)S(1)}, u32[]{:S(2)}, u32[]{:S(2)}) async-start(bf16[128,5,8,128]{3,2,1,0:T(8,128)(2,1)} %bitcast.37), calls=%async_computation.2 | async-start | bytes 2621440 | tf_op jit(solution)/shard_map/all_to_all | solution.py:963
  144.6 3.6 %collective-permute-start.25 = (bf16[4,9,8,128]{3,2,1,0:T(8,128)(2,1)S(1)}, bf16[4,9,8,128]{3,2,1,0:T(8,128)(2,1)S(1)}, u32[]{:S(2)}, u32[]{:S(2)}) collective-permute-start(bf16[4,9,8,128]{3,2,1,0:T(8,128)(2,1)S(1)} %sum_ffn.1), channel_id=1, source_target_pairs={{0,112},{8,120},{16,64},{24,72},{32,80},{40,88},{48,96},{56,104},{... | collective-permute-start | bytes 221192 | tf_op jit(solution)/shard_map/ppermute | solution.py:1018
  148.7 1.5 collective-permute-start.23
  150.5 2.1 %collective-permute-start.21 = (bf16[4,9,8,128]{3,2,1,0:T(8,128)(2,1)S(1)}, bf16[4,9,8,128]{3,2,1,0:T(8,128)(2,1)S(1)}, u32[]{:S(2)}, u32[]{:S(2)}) collective-permute-start(bf16[4,9,8,128]{3,2,1,0:T(8,128)(2,1)S(1)} %sum_ffn.1), channel_id=1, source_target_pairs={{0,48},{8,56},{16,0},{24,8},{32,16},{40,24},{48,32},{56,40},{64,11... | collective-permute-start | bytes 221192 | tf_op jit(solution)/shard_map/ppermute | solution.py:1018
  152.6 10.1 %collective-permute-done.25 = bf16[4,9,8,128]{3,2,1,0:T(8,128)(2,1)S(1)} collective-permute-done((bf16[4,9,8,128]{3,2,1,0:T(8,128)(2,1)S(1)}, bf16[4,9,8,128]{3,2,1,0:T(8,128)(2,1)S(1)}, u32[]{:S(2)}, u32[]{:S(2)}) %collective-permute-start.25) | collective-permute-done | bytes 73760 | tf_op jit(solution)/shard_map/ppermute | solution.py:1018
  162.7 2.7 %collective-permute-start.20 = (bf16[4,9,8,128]{3,2,1,0:T(8,128)(2,1)S(1)}, bf16[4,9,8,128]{3,2,1,0:T(8,128)(2,1)S(1)}, u32[]{:S(2)}, u32[]{:S(2)}) collective-permute-start(bf16[4,9,8,128]{3,2,1,0:T(8,128)(2,1)S(1)} %sum_ffn.1), channel_id=1, source_target_pairs={{0,32},{8,40},{16,48},{24,56},{32,0},{40,8},{48,16},{56,24},{64,96... | collective-permute-start | bytes 221192 | tf_op jit(solution)/shard_map/ppermute | solution.py:1018
  165.7 1.0 collective-permute-start.19
  166.7 1.3 sum_rest.1
  168.6 1.9 collective-permute-done.19
  170.5 8.8 %all-to-all-start.3 = ((bf16[128,5,8,128]{3,2,1,0:T(8,128)(2,1)}), bf16[128,5,8,128]{3,2,1,0:T(8,128)(2,1)S(1)}, u32[]{:S(2)}, u32[]{:S(2)}) async-start(bf16[128,5,8,128]{3,2,1,0:T(8,128)(2,1)} %sum_rest.1), calls=%async_computation.3 | async-start | bytes 2621440 | tf_op jit(solution)/shard_map/all_to_all | solution.py:963
  179.5 1.1 collective-permute-start.26
  180.6 1.6 collective-permute-done.26.ffn_oth
  182.3 3.6 %final_ffn.1 = (f32[768,384]{1,0:T(8,128)}, f32[384,768]{1,0:T(8,128)}) custom-call(s32[2]{0:T(128)S(1)} %pad_add_fusion.place.refs_0_, bf16[8,4,9,8,128]{4,3,2,1,0:T(8,128)(2,1)S(1)} %bitcast_dynamic-update-slice_fusion.ffn_own, bf16[8,4,9,8,128]{4,3,2,1,0:T(8,128)(2,1)S(1)} %collective-permute-done.26.ffn_oth), custom_call_target="tpu_custom_call" | custom-call | tf_op jit(solution)/shard_map/final_ffn/pallas_call | solution.py:845
  185.8 13.9 %all-to-all-done.3 = bf16[128,5,8,128]{3,2,1,0:T(8,128)(2,1)S(1)} async-done(((bf16[128,5,8,128]{3,2,1,0:T(8,128)(2,1)}), bf16[128,5,8,128]{3,2,1,0:T(8,128)(2,1)S(1)}, u32[]{:S(2)}, u32[]{:S(2)}) %all-to-all-start.3) | async-done | bytes 1310752 | tf_op jit(solution)/shard_map/all_to_all | solution.py:963
  199.8 1.2 collective-permute-start.27
  200.9 2.7 %collective-permute-done.27.other = bf16[640,8,128]{2,1,0:T(8,128)(2,1)S(1)} collective-permute-done((bf16[640,8,128]{2,1,0:T(8,128)(2,1)S(1)}, bf16[640,8,128]{2,1,0:T(8,128)(2,1)S(1)}, u32[]{:S(2)}, u32[]{:S(2)}) %collective-permute-start.27) | collective-permute-done | bytes 1310752 | tf_op jit(solution)/shard_map/ppermute | solution.py:954
  203.6 4.0 %final.1 = (f32[768,768]{1,0:T(8,128)}, f32[768]{0:T(1024)}, f32[65,768]{1,0:T(8,128)}, f32[768,768]{1,0:T(8,128)}, f32[768]{0:T(1024)}, /*index=5*/f32[768]{0:T...) custom-call(s32[2]{0:T(128)S(1)} %pad_add_fusion.place.refs_0_, ...), custom_call_target="tpu_custom_call" | custom-call | tf_op jit(solution)/shard_map/final/pallas_call | solution.py:903
  (76 shorter events, 10.9 us)
Async XLA Ops:
  4.3 12.0 %copy-start.5 = (bf16[768]{0:T(1024)(128)(2,1)S(1)}, bf16[768]{0:T(1024)(128)(2,1)}, u32[]{:S(2)}) copy-start(bf16[768]{0:T(1024)(128)(2,1)} %param.25) | copy-start | bytes 4612
  4.3 12.0 %copy-start.6 = (bf16[768]{0:T(1024)(128)(2,1)S(1)}, bf16[768]{0:T(1024)(128)(2,1)}, u32[]{:S(2)}) copy-start(bf16[768]{0:T(1024)(128)(2,1)} %param.26) | copy-start | bytes 4612
  4.3 12.0 %copy-start.7 = (bf16[768]{0:T(1024)(128)(2,1)S(1)}, bf16[768]{0:T(1024)(128)(2,1)}, u32[]{:S(2)}) copy-start(bf16[768]{0:T(1024)(128)(2,1)} %param.21) | copy-start | bytes 4612
  4.3 12.0 %copy-start.8 = (bf16[768]{0:T(1024)(128)(2,1)S(1)}, bf16[768]{0:T(1024)(128)(2,1)}, u32[]{:S(2)}) copy-start(bf16[768]{0:T(1024)(128)(2,1)} %param.24) | copy-start | bytes 4612
  4.3 12.0 %copy-start.2 = (bf16[65,768]{1,0:T(8,128)(2,1)S(1)}, bf16[65,768]{1,0:T(8,128)(2,1)}, u32[]{:S(2)}) copy-start(bf16[65,768]{1,0:T(8,128)(2,1)} %refs_4_.1) | copy-start | bytes 299524
  4.4 12.0 %copy-start.3 = (s32[256]{0:T(256)S(1)}, s32[256]{0:T(256)}, u32[]{:S(2)}) copy-start(s32[256]{0:T(256)} %param.35) | copy-start | bytes 3076
  4.4 12.0 %copy-start.4 = (s32[1,4]{1,0:T(1,128)S(1)}, s32[1,4]{1,0:T(1,128)}, u32[]{:S(2)}) copy-start(s32[1,4]{1,0:T(1,128)} %refs_0_.1) | copy-start | bytes 52
  4.4 48.9 %all-to-all-start = ((bf16[128,10,8,128]{3,2,1,0:T(8,128)(2,1)}), bf16[128,10,8,128]{3,2,1,0:T(8,128)(2,1)}, u32[]{:S(2)}, u32[]{:S(2)}) async-start(bf16[128,10,8,128]{3,2,1,0:T(8,128)(2,1)} %bitcast.35), calls=%async_computation | async-start | bytes 5242880 | tf_op jit(solution)/shard_map/all_to_all | solution.py:963
  34.9 16.1 %collective-permute-start.1 = (bf16[128,768]{1,0:T(8,128)(2,1)S(1)}, bf16[128,768]{1,0:T(8,128)(2,1)S(1)}, u32[]{:S(2)}, u32[]{:S(2)}) collective-permute-start(bf16[128,768]{1,0:T(8,128)(2,1)S(1)} %get-tuple-element.108), channel_id=1, source_target_pairs={{0,16},{8,24},{16,32},{24,40},{32,48},{40,56},{48,0},{56,8},{64,80... | collective-permute-start | bytes 589832 | tf_op jit(solution)/shard_map/ppermute | solution.py:957
  36.4 15.5 %collective-permute-start.2 = (bf16[128,768]{1,0:T(8,128)(2,1)S(1)}, bf16[128,768]{1,0:T(8,128)(2,1)S(1)}, u32[]{:S(2)}, u32[]{:S(2)}) collective-permute-start(bf16[128,768]{1,0:T(8,128)(2,1)S(1)} %get-tuple-element.109), channel_id=1, source_target_pairs={{0,48},{8,56},{16,0},{24,8},{32,16},{40,24},{48,32},{56,40},{64,11... | collective-permute-start | bytes 589832 | tf_op jit(solution)/shard_map/ppermute | solution.py:960
  51.0 1.9 collective-permute-start.3
  51.8 1.4 collective-permute-start.4
  58.9 1.8 collective-permute-start.5
  59.2 3.1 %collective-permute-start = (bf16[256,768]{1,0:T(8,128)(2,1)S(1)}, bf16[256,768]{1,0:T(8,128)(2,1)S(1)}, u32[]{:S(2)}, u32[]{:S(2)}) collective-permute-start(bf16[256,768]{1,0:T(8,128)(2,1)S(1)} %get-tuple-element.107.own), channel_id=1, source_target_pairs={{0,8},{8,0},{16,24},{24,16},{32,40},{40,32},{48,56},{56,48},{64,72... | collective-permute-start | bytes 1179656 | tf_op jit(solution)/shard_map/ppermute | solution.py:954
  60.8 6.3 %collective-permute-start.6 = (bf16[128,768]{1,0:T(8,128)(2,1)S(1)}, bf16[128,768]{1,0:T(8,128)(2,1)S(1)}, u32[]{:S(2)}, u32[]{:S(2)}) collective-permute-start(bf16[128,768]{1,0:T(8,128)(2,1)S(1)} %get-tuple-element.119), channel_id=1, source_target_pairs={{0,48},{8,56},{16,0},{24,8},{32,16},{40,24},{48,32},{56,40},{64,11... | collective-permute-start | bytes 589832 | tf_op jit(solution)/shard_map/ppermute | solution.py:960
  61.4 7.1 %collective-permute-start.7 = (bf16[128,768]{1,0:T(8,128)(2,1)S(1)}, bf16[128,768]{1,0:T(8,128)(2,1)S(1)}, u32[]{:S(2)}, u32[]{:S(2)}) collective-permute-start(bf16[128,768]{1,0:T(8,128)(2,1)S(1)} %get-tuple-element.120), channel_id=1, source_target_pairs={{0,16},{8,24},{16,32},{24,40},{32,48},{40,56},{48,0},{56,8},{64,80... | collective-permute-start | bytes 589832 | tf_op jit(solution)/shard_map/ppermute | solution.py:957
  62.3 7.6 %copy-start.9 = (bf16[768]{0:T(1024)(128)(2,1)S(1)}, bf16[768]{0:T(1024)(128)(2,1)}, u32[]{:S(2)}) copy-start(bf16[768]{0:T(1024)(128)(2,1)} %param.30) | copy-start | bytes 4612
  62.3 7.6 %copy-start.10 = (bf16[768]{0:T(1024)(128)(2,1)S(1)}, bf16[768]{0:T(1024)(128)(2,1)}, u32[]{:S(2)}) copy-start(bf16[768]{0:T(1024)(128)(2,1)} %param.31) | copy-start | bytes 4612
  62.3 7.6 %copy-start.11 = (bf16[768]{0:T(1024)(128)(2,1)S(1)}, bf16[768]{0:T(1024)(128)(2,1)}, u32[]{:S(2)}) copy-start(bf16[768]{0:T(1024)(128)(2,1)} %param.32) | copy-start | bytes 4612
  62.3 8.9 %copy-start = (f32[256,768]{1,0:T(8,128)S(1)}, f32[256,768]{1,0:T(8,128)}, u32[]{:S(2)}) copy-start(f32[256,768]{1,0:T(8,128)} %get-tuple-element.106.refs_0_.refs_6_) | copy-start | bytes 2359300
  62.3 8.9 %copy-start.1 = (bf16[256,768]{1,0:T(8,128)(2,1)S(1)}, bf16[256,768]{1,0:T(8,128)(2,1)}, u32[]{:S(2)}) copy-start(bf16[256,768]{1,0:T(8,128)(2,1)} %refs_10_.4) | copy-start | bytes 1179652
  68.5 2.8 %collective-permute-start.8 = (bf16[256,768]{1,0:T(8,128)(2,1)S(1)}, bf16[256,768]{1,0:T(8,128)(2,1)S(1)}, u32[]{:S(2)}, u32[]{:S(2)}) collective-permute-start(bf16[256,768]{1,0:T(8,128)(2,1)S(1)} %get-tuple-element.121), channel_id=1, source_target_pairs={{0,8},{8,0},{16,24},{24,16},{32,40},{40,32},{48,56},{56,48},{64,72... | collective-permute-start | bytes 1179656 | tf_op jit(solution)/shard_map/ppermute | solution.py:954
  73.1 3.1 %collective-permute-start.9 = (bf16[256,768]{1,0:T(8,128)(2,1)S(1)}, bf16[256,768]{1,0:T(8,128)(2,1)S(1)}, u32[]{:S(2)}, u32[]{:S(2)}) collective-permute-start(bf16[256,768]{1,0:T(8,128)(2,1)S(1)} %get-tuple-element.125.refs_0_), channel_id=1, source_target_pairs={{0,8},{8,0},{16,24},{24,16},{32,40},{40,32},{48,56},{56,48},{64,72... | collective-permute-start | bytes 1179656 | tf_op jit(solution)/shard_map/ppermute | solution.py:954
  73.6 7.6 %collective-permute-start.10 = (bf16[128,768]{1,0:T(8,128)(2,1)S(1)}, bf16[128,768]{1,0:T(8,128)(2,1)S(1)}, u32[]{:S(2)}, u32[]{:S(2)}) collective-permute-start(bf16[128,768]{1,0:T(8,128)(2,1)S(1)} %get-tuple-element.128), channel_id=1, source_target_pairs={{0,16},{8,24},{16,32},{24,40},{32,48},{40,56},{48,0},{56,8},{64,80... | collective-permute-start | bytes 589832 | tf_op jit(solution)/shard_map/ppermute | solution.py:957
  73.6 7.6 %collective-permute-start.11 = (bf16[128,768]{1,0:T(8,128)(2,1)S(1)}, bf16[128,768]{1,0:T(8,128)(2,1)S(1)}, u32[]{:S(2)}, u32[]{:S(2)}) collective-permute-start(bf16[128,768]{1,0:T(8,128)(2,1)S(1)} %get-tuple-element.129), channel_id=1, source_target_pairs={{0,48},{8,56},{16,0},{24,8},{32,16},{40,24},{48,32},{56,40},{64,11... | collective-permute-start | bytes 589832 | tf_op jit(solution)/shard_map/ppermute | solution.py:960
  81.1 2.0 collective-permute-start.13
  82.1 1.4 collective-permute-start.14
  86.9 2.0 collective-permute-start.15
  89.0 6.8 %collective-permute-start.16 = (bf16[128,768]{1,0:T(8,128)(2,1)S(1)}, bf16[128,768]{1,0:T(8,128)(2,1)S(1)}, u32[]{:S(2)}, u32[]{:S(2)}) collective-permute-start(bf16[128,768]{1,0:T(8,128)(2,1)S(1)} %get-tuple-element.148), channel_id=1, source_target_pairs={{0,48},{8,56},{16,0},{24,8},{32,16},{40,24},{48,32},{56,40},{64,11... | collective-permute-start | bytes 589832 | tf_op jit(solution)/shard_map/ppermute | solution.py:960
  91.7 7.2 %collective-permute-start.17 = (bf16[128,768]{1,0:T(8,128)(2,1)S(1)}, bf16[128,768]{1,0:T(8,128)(2,1)S(1)}, u32[]{:S(2)}, u32[]{:S(2)}) collective-permute-start(bf16[128,768]{1,0:T(8,128)(2,1)S(1)} %get-tuple-element.149), channel_id=1, source_target_pairs={{0,16},{8,24},{16,32},{24,40},{32,48},{40,56},{48,0},{56,8},{64,80... | collective-permute-start | bytes 589832 | tf_op jit(solution)/shard_map/ppermute | solution.py:957
  98.9 39.3 %all-to-all-start.1 = ((bf16[128,9,8,128]{3,2,1,0:T(8,128)(2,1)}), bf16[128,9,8,128]{3,2,1,0:T(8,128)(2,1)S(1)}, u32[]{:S(2)}, u32[]{:S(2)}) async-start(bf16[128,9,8,128]{3,2,1,0:T(8,128)(2,1)} %bitcast.36), calls=%async_computation.1 | async-start | bytes 4718592 | tf_op jit(solution)/shard_map/all_to_all | solution.py:963
  107.0 2.7 %collective-permute-start.12 = (bf16[256,768]{1,0:T(8,128)(2,1)S(1)}, bf16[256,768]{1,0:T(8,128)(2,1)S(1)}, u32[]{:S(2)}, u32[]{:S(2)}) collective-permute-start(bf16[256,768]{1,0:T(8,128)(2,1)S(1)} %get-tuple-element.131), channel_id=1, source_target_pairs={{0,8},{8,0},{16,24},{24,16},{32,40},{40,32},{48,56},{56,48},{64,72... | collective-permute-start | bytes 1179656 | tf_op jit(solution)/shard_map/ppermute | solution.py:954
  123.1 3.1 %collective-permute-start.18 = (bf16[640,8,128]{2,1,0:T(8,128)(2,1)S(1)}, bf16[640,8,128]{2,1,0:T(8,128)(2,1)S(1)}, u32[]{:S(2)}, u32[]{:S(2)}) collective-permute-start(bf16[640,8,128]{2,1,0:T(8,128)(2,1)S(1)} %get-tuple-element.169), channel_id=1, source_target_pairs={{0,8},{8,0},{16,24},{24,16},{32,40},{40,32},{48,56},{56,48},{64,72... | collective-permute-start | bytes 3932168 | tf_op jit(solution)/shard_map/ppermute | solution.py:954
  138.6 28.1 %all-to-all-start.2 = ((bf16[128,5,8,128]{3,2,1,0:T(8,128)(2,1)}), bf16[128,5,8,128]{3,2,1,0:T(8,128)(2,1)S(1)}, u32[]{:S(2)}, u32[]{:S(2)}) async-start(bf16[128,5,8,128]{3,2,1,0:T(8,128)(2,1)} %bitcast.37), calls=%async_computation.2 | async-start | bytes 2621440 | tf_op jit(solution)/shard_map/all_to_all | solution.py:963
  144.6 18.1 %collective-permute-start.25 = (bf16[4,9,8,128]{3,2,1,0:T(8,128)(2,1)S(1)}, bf16[4,9,8,128]{3,2,1,0:T(8,128)(2,1)S(1)}, u32[]{:S(2)}, u32[]{:S(2)}) collective-permute-start(bf16[4,9,8,128]{3,2,1,0:T(8,128)(2,1)S(1)} %sum_ffn.1), channel_id=1, source_target_pairs={{0,112},{8,120},{16,64},{24,72},{32,80},{40,88},{48,96},{56,104},{... | collective-permute-start | bytes 221192 | tf_op jit(solution)/shard_map/ppermute | solution.py:1018
  148.2 17.5 %collective-permute-start.24 = (bf16[4,9,8,128]{3,2,1,0:T(8,128)(2,1)S(1)}, bf16[4,9,8,128]{3,2,1,0:T(8,128)(2,1)S(1)}, u32[]{:S(2)}, u32[]{:S(2)}) collective-permute-start(bf16[4,9,8,128]{3,2,1,0:T(8,128)(2,1)S(1)} %sum_ffn.1), channel_id=1, source_target_pairs={{0,96},{8,104},{16,112},{24,120},{32,64},{40,72},{48,80},{56,88},{... | collective-permute-start | bytes 221192 | tf_op jit(solution)/shard_map/ppermute | solution.py:1018
  148.7 19.3 %collective-permute-start.23 = (bf16[4,9,8,128]{3,2,1,0:T(8,128)(2,1)S(1)}, bf16[4,9,8,128]{3,2,1,0:T(8,128)(2,1)S(1)}, u32[]{:S(2)}, u32[]{:S(2)}) collective-permute-start(bf16[4,9,8,128]{3,2,1,0:T(8,128)(2,1)S(1)} %sum_ffn.1), channel_id=1, source_target_pairs={{0,80},{8,88},{16,96},{24,104},{32,112},{40,120},{48,64},{56,72},{... | collective-permute-start | bytes 221192 | tf_op jit(solution)/shard_map/ppermute | solution.py:1018
  150.2 17.8 %collective-permute-start.22 = (bf16[4,9,8,128]{3,2,1,0:T(8,128)(2,1)S(1)}, bf16[4,9,8,128]{3,2,1,0:T(8,128)(2,1)S(1)}, u32[]{:S(2)}, u32[]{:S(2)}) collective-permute-start(bf16[4,9,8,128]{3,2,1,0:T(8,128)(2,1)S(1)} %sum_ffn.1), channel_id=1, source_target_pairs={{0,64},{8,72},{16,80},{24,88},{32,96},{40,104},{48,112},{56,120},{... | collective-permute-start | bytes 221192 | tf_op jit(solution)/shard_map/ppermute | solution.py:1018
  150.5 17.5 %collective-permute-start.21 = (bf16[4,9,8,128]{3,2,1,0:T(8,128)(2,1)S(1)}, bf16[4,9,8,128]{3,2,1,0:T(8,128)(2,1)S(1)}, u32[]{:S(2)}, u32[]{:S(2)}) collective-permute-start(bf16[4,9,8,128]{3,2,1,0:T(8,128)(2,1)S(1)} %sum_ffn.1), channel_id=1, source_target_pairs={{0,48},{8,56},{16,0},{24,8},{32,16},{40,24},{48,32},{56,40},{64,11... | collective-permute-start | bytes 221192 | tf_op jit(solution)/shard_map/ppermute | solution.py:1018
  162.7 5.9 %collective-permute-start.20 = (bf16[4,9,8,128]{3,2,1,0:T(8,128)(2,1)S(1)}, bf16[4,9,8,128]{3,2,1,0:T(8,128)(2,1)S(1)}, u32[]{:S(2)}, u32[]{:S(2)}) collective-permute-start(bf16[4,9,8,128]{3,2,1,0:T(8,128)(2,1)S(1)} %sum_ffn.1), channel_id=1, source_target_pairs={{0,32},{8,40},{16,48},{24,56},{32,0},{40,8},{48,16},{56,24},{64,96... | collective-permute-start | bytes 221192 | tf_op jit(solution)/shard_map/ppermute | solution.py:1018
  165.7 4.8 %collective-permute-start.19 = (bf16[4,9,8,128]{3,2,1,0:T(8,128)(2,1)S(1)}, bf16[4,9,8,128]{3,2,1,0:T(8,128)(2,1)S(1)}, u32[]{:S(2)}, u32[]{:S(2)}) collective-permute-start(bf16[4,9,8,128]{3,2,1,0:T(8,128)(2,1)S(1)} %sum_ffn.1), channel_id=1, source_target_pairs={{0,16},{8,24},{16,32},{24,40},{32,48},{40,56},{48,0},{56,8},{64,80... | collective-permute-start | bytes 221192 | tf_op jit(solution)/shard_map/ppermute | solution.py:1018
  170.5 29.2 %all-to-all-start.3 = ((bf16[128,5,8,128]{3,2,1,0:T(8,128)(2,1)}), bf16[128,5,8,128]{3,2,1,0:T(8,128)(2,1)S(1)}, u32[]{:S(2)}, u32[]{:S(2)}) async-start(bf16[128,5,8,128]{3,2,1,0:T(8,128)(2,1)} %sum_rest.1), calls=%async_computation.3 | async-start | bytes 2621440 | tf_op jit(solution)/shard_map/all_to_all | solution.py:963
  179.5 2.8 %collective-permute-start.26 = (bf16[8,4,9,8,128]{4,3,2,1,0:T(8,128)(2,1)S(1)}, bf16[8,4,9,8,128]{4,3,2,1,0:T(8,128)(2,1)S(1)}, u32[]{:S(2)}, u32[]{:S(2)}) collective-permute-start(bf16[8,4,9,8,128]{4,3,2,1,0:T(8,128)(2,1)S(1)} %bitcast_dynamic-update-slice_fusion.ffn_own), channel_id=1, source_target_pairs={{0,8},{8,0},{16,24},{24,16},{32,40},{40,32},{48,56},{56,48},{64,72... | collective-permute-start | bytes 1769480 | tf_op jit(solution)/shard_map/ppermute | solution.py:954
  199.8 3.8 %collective-permute-start.27 = (bf16[640,8,128]{2,1,0:T(8,128)(2,1)S(1)}, bf16[640,8,128]{2,1,0:T(8,128)(2,1)S(1)}, u32[]{:S(2)}, u32[]{:S(2)}) collective-permute-start(bf16[640,8,128]{2,1,0:T(8,128)(2,1)S(1)} %bitcast.32), channel_id=1, source_target_pairs={{0,8},{8,0},{16,24},{24,16},{32,40},{40,32},{48,56},{56,48},{64,72... | collective-permute-start | bytes 3932168 | tf_op jit(solution)/shard_map/ppermute | solution.py:954

commit v5 on v4

--- a/solution.py
+++ b/solution.py
@@ -491,16 +491,26 @@
     lax.fori_loop(0, HIDDEN // 256, block, 0)
 
 
+def unpack_kernel(w, wu, wd):
+    unpack(w, 0, wu)
+    unpack_bias(w, wu)
+    unpack(w, 1, wd)
+
+
+def unpack_weights(weights):
+    return staged_call(
+        unpack_kernel, "unpack", 12, [("pair", weights)],
+        [("vmem", shape((HIDDEN, WIDTH + 128), bf16)), ("vmem", shape((HIDDEN, WIDTH), bf16))],
+    )
+
+
 def ffn_far_kernel(
-    got_a, got_b, sib_a, sib_b, w, act, slope, part_own, part_sib, rows_out, wu, wd, rows, acc,
+    got_a, got_b, sib_a, sib_b, wu, wd, act, slope, part_own, part_sib, rows_out, rows, acc,
 ):
     for i, ref in enumerate((got_a, got_b, sib_a, sib_b)):
         rows[i * HALF : i * HALF + HALF, 0:WIDTH] = ref[...]
     rows[:, WIDTH:] = jnp.where(lanes((2 * ROWS, 128)) < 3, 1.0, 0.0).astype(bf16)
     rows_out[...] = rows[:, 0:WIDTH]
-    unpack(w, 0, wu)
-    unpack_bias(w, wu)
-    unpack(w, 1, wd)
     ffn_blocks(rows, wu, wd, act, slope, acc)
     part_own[...] = acc[0:ROWS]
     part_sib[...] = acc[ROWS:].astype(bf16)
@@ -516,26 +526,14 @@
     part_sib[...] = acc[ROWS:].astype(bf16)
 
 
-def ffn_call(kernel, name, ins, outs):
+def ffn_call(kernel, name, *args):
     wide = (ROWS, WIDTH)
     tall = shape((2 * ROWS, WIDTH), bf16)
+    outs = (tall, tall, shape(wide, f32), shape(wide, bf16), tall)
     return staged_call(
-        kernel, name, 24, ins,
-        [("vmem", o) for o in (tall, tall, shape(wide, f32), shape(wide, bf16), tall, *outs)],
+        kernel, name, 20, [("vmem", a) for a in args], [("vmem", o) for o in outs],
         [pltpu.VMEM((2 * ROWS, WIDTH + 128), bf16), pltpu.VMEM((2 * ROWS, WIDTH), f32)],
     )
-
-
-def ffn_far(got_a, got_b, sib_a, sib_b, weights):
-    rows = [("vmem", a) for a in (got_a, got_b, sib_a, sib_b)]
-    return ffn_call(
-        ffn_far_kernel, "ffn_far", [*rows, ("pair", weights)],
-        [shape((HIDDEN, WIDTH + 128), bf16), shape((HIDDEN, WIDTH), bf16)],
-    )
-
-
-def ffn_near(*args):
-    return ffn_call(ffn_near_kernel, "ffn_near", [("vmem", a) for a in args], [])
 
 
 def combine_kernel(own, got, out_a, out_b):
@@ -561,35 +559,50 @@
     return own[...] + near[...].astype(f32) + far.astype(f32)
 
 
-def middle_kernel(
-    n1, own, near, far_a, far_b, bd, ga, sa, gf, sf, og, out, second, low, low_a, low_b, sums,
-):
+def second_norm(n1, own, near, far_a, far_b, bd, ga, sa, gf, og):
     first = n1[...] * ga[...].astype(f32) + sa[...].astype(f32)
     n, inv = norm_rows(first + gather_rows(own, near, far_a, far_b) + bd[...].astype(f32))
-    gain = gf[...].astype(f32)
-    out[...] = (n * gain + sf[...].astype(f32)).astype(bf16)
     g = og[...].astype(f32)
-    grad = norm_back(g, n, inv, gain)
+    return n, g, norm_back(g, n, inv, gf[...].astype(f32))
+
+
+def middle_kernel(n1, own, near, far_a, far_b, bd, ga, sa, gf, og, low, low_a, low_b):
+    grad = second_norm(n1, own, near, far_a, far_b, bd, ga, sa, gf, og)[2].astype(bf16)
+    low[...] = grad
+    low_a[...] = grad[0:HALF]
+    low_b[...] = grad[HALF:]
+
+
+def middle(*args):
+    wide = shape((ROWS, WIDTH), bf16)
+    half = shape((HALF, WIDTH), bf16)
+    return pl.pallas_call(
+        middle_kernel,
+        out_shape=(wide, half, half),
+        in_specs=[VMEM] * len(args),
+        out_specs=(VMEM,) * 3,
+        compiler_params=params(16),
+        name="middle",
+    )(*args)
+
+
+def outputs_kernel(
+    n1, own, near, far_a, far_b, bd, ga, sa, gf, og, sf, out, second, sums,
+):
+    n, g, grad = second_norm(n1, own, near, far_a, far_b, bd, ga, sa, gf, og)
+    out[...] = (n * gf[...].astype(f32) + sf[...].astype(f32)).astype(bf16)
     second[...] = grad
-    grad_low = grad.astype(bf16)
-    low[...] = grad_low
-    low_a[...] = grad_low[0:HALF]
-    low_b[...] = grad_low[HALF:]
-    sums[0:1] = jnp.sum(grad_low.astype(f32), axis=0, keepdims=True)
+    sums[0:1] = jnp.sum(grad.astype(bf16).astype(f32), axis=0, keepdims=True)
     sums[1:2] = jnp.sum(g * n, axis=0, keepdims=True)
     sums[2:3] = jnp.sum(g, axis=0, keepdims=True)
     sums[3:8] = jnp.zeros((5, WIDTH), f32)
 
 
-def middle(*args):
+def outputs(*args):
     wide = (ROWS, WIDTH)
-    half = (HALF, WIDTH)
     return staged_call(
-        middle_kernel, "middle", 16, [("vmem", a) for a in args],
-        [
-            ("hbm", shape(wide, bf16)), ("hbm", shape(wide, f32)), ("vmem", shape(wide, bf16)),
-            ("vmem", shape(half, bf16)), ("vmem", shape(half, bf16)), ("hbm", shape((8, WIDTH), f32)),
-        ],
+        outputs_kernel, "outputs", 16, [("vmem", a) for a in args],
+        [("hbm", shape(wide, bf16)), ("hbm", shape(wide, f32)), ("hbm", shape((8, WIDTH), f32))],
     )
 
 
@@ -640,15 +653,16 @@
 
 
 def pack_kernel(gu, gd, grads):
-    for a in range(PIECES):
-        rs = slice(a * 192, a * 192 + 192)
-        for ct in range(COLS):
-            cs = slice(ct * 128, ct * 128 + 128)
-            us = slice(3 * (ct % 3), 3 * (ct % 3) + 3)
-            up = gu[rs, cs].astype(f32).reshape(8, 3, 8, 128)
-            down = gd[rs, cs].astype(f32).reshape(8, 3, 8, 128)
-            grads[0, a, ct // 3, :, us] = up.astype(bf16)
-            grads[1, a, ct // 3, :, us] = down.astype(bf16)
+    def piece(a, carry):
+        rs = pl.ds(pl.multiple_of(a * 192, 192), 192)
+        for m, ref in enumerate((gu, gd)):
+            for ct in range(COLS):
+                us = slice(3 * (ct % 3), 3 * (ct % 3) + 3)
+                part = ref[rs, ct * 128 : ct * 128 + 128].astype(f32).reshape(8, 3, 8, 128)
+                grads[m, a, ct // 3, :, us] = part.astype(bf16)
+        return carry
+
+    lax.fori_loop(0, PIECES, piece, 0)
 
 
 def pack(*args):
@@ -973,23 +987,28 @@
     )
     low_sib = swap(low)
     row_a, row_b = ahead(low_a), behind(low_b)
-    act_f, slope_f, far_own, far_sib, rows_f, wu, wd = ffn_far(
-        row_a, row_b, swap(row_a), swap(row_b), weights
+    wu, wd = unpack_weights(weights)
+    act_f, slope_f, far_own, far_sib, rows_f = ffn_call(
+        ffn_far_kernel, "ffn_far", row_a, row_b, swap(row_a), swap(row_b), wu, wd
     )
     sent_a, sent_b = combine(far_own, swap(far_sib))
     wu, sent_a, sent_b = lax.optimization_barrier((wu, sent_a, sent_b))
-    act_n, slope_n, near_own, near_sib, rows_n = ffn_near(low, low_sib, wu, wd)
+    act_n, slope_n, near_own, near_sib, rows_n = ffn_call(
+        ffn_near_kernel, "ffn_near", low, low_sib, wu, wd
+    )
     back_a, back_b = behind(sent_a), ahead(sent_b)
     near_sib, back_a, back_b = lax.optimization_barrier((near_sib, back_a, back_b))
-    block_output, second, grad, grad_a, grad_b, sums = middle(
-        n1, near_own, swap(near_sib), back_a, back_b, row(b_down), row(gain_attn),
-        row(shift_attn), row(gain_ffn), row(shift_ffn), out_grad,
-    )
+    second_args = (
+        n1, near_own, swap(near_sib), back_a, back_b, row(b_down), row(gain_attn), row(shift_attn),
+        row(gain_ffn), out_grad,
+    )
+    grad, grad_a, grad_b = middle(*second_args)
     got_a, got_b = ahead(grad_a), behind(grad_b)
     near_own, near_sib, g_n, u_n, bias_n = back_call(
         back_near_kernel, "back_near", grad, swap(grad), wu, wd, slope_n
     )
-    got_a, got_b, near_sib = lax.optimization_barrier((got_a, got_b, near_sib))
+    block_output, second, sums = outputs(*second_args, row(shift_ffn))
+    got_a, got_b, near_sib, second = lax.optimization_barrier((got_a, got_b, near_sib, second))
     far_own, far_sib, g_f, u_f, bias_f = back_call(
         back_far_kernel, "back_far", got_a, got_b, swap(got_a), swap(got_b), wu, wd, slope_f
     )

time: 208 us -> 206 us (level)
  waiting for transfers between devices: 71.2 us -> 69 us
    pallas_call x1 -> x2, Pallas kernels: 3.8 us -> 7.6 us  [staged_call(): pl.pallas_call(kernel, out_shape=tuple((o for _, o in outs)), in_specs=[s...]
    pallas_call x7, Pallas kernels: 48.6 us -> 44.9 us  [staged_call(): pl.pallas_call(run, out_shape=tuple((pltpu.HBM(o.shape, o.dtype) if k ==...]
  transfers between devices with their start and end apart: 32 -> 32, of which waited for: 22 -> 19; matrix products, arithmetic and copies ran while one was open for 2% -> 2% of each run, Pallas kernels for 22% -> 24%
where the time goes in v5:
time: 206 us; the launch traced here: 205 us
  waiting for transfers between devices  69 us (33%)
  Pallas kernels  66.2 us (32%)
  starting transfers between devices  64 us (31%)
  matrix products  3.26 us (2%)
    pallas_call x7, Pallas kernels, staged_call(): pl.pallas_call(run, out_shape=tuple((pltpu.HBM(o.shape, o.dtype) if k ==...  44.9 us
    all_to_all x4, starting transfers between devices, exchange(): return lax.all_to_all(x, ALL, 0, 0, tiled=True)  34.6 us
    all_to_all x4, waiting for transfers between devices, exchange(): return lax.all_to_all(x, ALL, 0, 0, tiled=True)  24.5 us
    ppermute x4, waiting for transfers between devices, ahead(): return lax.ppermute(x, 'dp', [(i, shift(i, 1)) for i in range(n_dp)])  17.5 us
    ppermute x7, waiting for transfers between devices, body(): around.append(lax.ppermute(owned, 'dp', pairs))  12.9 us
    ppermute x7, starting transfers between devices, body(): around.append(lax.ppermute(owned, 'dp', pairs))  11.7 us
    ppermute x13, waiting for transfers between devices, swap(): return lax.ppermute(x, 'dp', [(i, i ^ 1) for i in range(n_dp)])  11.4 us
    ppermute x13, starting transfers between devices, swap(): return lax.ppermute(x, 'dp', [(i, i ^ 1) for i in range(n_dp)])  8.87 us
  transfers between devices with their start and end apart: 32, of which 19 were waited for; matrix products, arithmetic and copies ran while one was open for 2% of the time, Pallas kernels for 24%

profile of v5, /device:TPU:1, one launch (start us, length us, event | category | flops | bytes accessed | tf_op | source)
XLA Modules:
  0.0 205.4 jit_solution(16067272256686097017)
XLA Ops:
  0.7 3.6 %prep.1 = bf16[4,4,8,10,8,128]{5,4,3,2,1,0:T(8,128)(2,1)} custom-call(s32[2]{0:T(128)S(1)} %pad_add_fusion.place.refs_0_, bf16[768,384]{1,0:T(8,128)(2,1)} %up_ref.1, bf16[384,768]{1,0:T(8,128)(2,1)} %down_ref.1, bf16[384]{0:T(512)(128)(2,1)} %bias_hbm.1), custom_call_target="tpu_custom_call" | custom-call | tf_op jit(solution)/shard_map/prep/pallas_call | solution.py:247
  4.4 11.9 %all-to-all-start = ((bf16[128,10,8,128]{3,2,1,0:T(8,128)(2,1)}), bf16[128,10,8,128]{3,2,1,0:T(8,128)(2,1)}, u32[]{:S(2)}, u32[]{:S(2)}) async-start(bf16[128,10,8,128]{3,2,1,0:T(8,128)(2,1)} %bitcast.35), calls=%async_computation | async-start | bytes 5242880 | tf_op jit(solution)/shard_map/all_to_all | solution.py:977
  16.4 18.5 %attend.1 = (f32[256,768]{1,0:T(8,128)}, f32[256,128]{1,0:T(8,128)}, bf16[256,768]{1,0:T(8,128)(2,1)S(1)}, bf16[128,768]{1,0:T(8,128)(2,1)S(1)}, bf16[128,768]{1...) custom-call(s32[1,4]{1,0:T(1,128)S(1)} %copy-done.4, ...), custom_call_target="tpu_custom_call" | custom-call | tf_op jit(solution)/shard_map/attend/pallas_call | solution.py:177
  34.9 1.5 collective-permute-start.1
  36.4 1.3 collective-permute-start.2
  37.7 13.3 %collective-permute-done.1.got_a = bf16[128,768]{1,0:T(8,128)(2,1)S(1)} collective-permute-done((bf16[128,768]{1,0:T(8,128)(2,1)S(1)}, bf16[128,768]{1,0:T(8,128)(2,1)S(1)}, u32[]{:S(2)}, u32[]{:S(2)}) %collective-permute-start.1) | collective-permute-done | bytes 196640 | tf_op jit(solution)/shard_map/ppermute | solution.py:971
  51.0 0.8 collective-permute-start.3
  51.8 1.9 unpack.1
  53.8 3.8 %ffn_far.1 = (bf16[512,768]{1,0:T(8,128)(2,1)S(1)}, bf16[512,768]{1,0:T(8,128)(2,1)S(1)}, f32[256,768]{1,0:T(8,128)S(1)}, bf16[256,768]{1,0:T(8,128)(2,1)S(1)}, bf16[512,768]{1,0:T(8,128)(2,1)S(1)}) custom-call(bf16[128,768]{1,0:T(8,128)(2,1)S(1)} %collective-permute-done.1.got_a, bf16[128,768]{1,0:T(8,128)(2,1)S(1)} %collective-permute-done.2.got_b, ...), custom_call_target="tpu_custom_call" | custom-call | tf_op jit(solution)/shard_map/ffn_far/pallas_call | solution.py:141
  58.3 1.3 collective-permute-done.5.got
  61.2 3.8 %ffn_near.1 = (bf16[512,768]{1,0:T(8,128)(2,1)S(1)}, bf16[512,768]{1,0:T(8,128)(2,1)S(1)}, f32[256,768]{1,0:T(8,128)S(1)}, bf16[256,768]{1,0:T(8,128)(2,1)S(1)}, bf16[512,768]{1,0:T(8,128)(2,1)S(1)}) custom-call(bf16[256,768]{1,0:T(8,128)(2,1)S(1)} %get-tuple-element.108.own, bf16[256,768]{1,0:T(8,128)(2,1)S(1)} %collective-permute-done.sib, ...), custom_call_target="tpu_custom_call" | custom-call | tf_op jit(solution)/shard_map/ffn_near/pallas_call | solution.py:141
  65.0 0.8 collective-permute-done.6.refs_3_.far_a
  65.8 1.6 collective-permute-done.7.refs_4_.far_b
  67.4 1.5 collective-permute-start.8
  69.0 1.3 collective-permute-done.8.refs_2_.near
  71.4 2.7 %collective-permute-start.11 = (bf16[128,768]{1,0:T(8,128)(2,1)S(1)}, bf16[128,768]{1,0:T(8,128)(2,1)S(1)}, u32[]{:S(2)}, u32[]{:S(2)}) collective-permute-start(bf16[128,768]{1,0:T(8,128)(2,1)S(1)} %get-tuple-element.130), channel_id=1, source_target_pairs={{0,48},{8,56},{16,0},{24,8},{32,16},{40,24},{48,32},{56,40},{64,11... | collective-permute-start | bytes 589832 | tf_op jit(solution)/shard_map/ppermute | solution.py:974
  74.1 1.8 outputs.1
  75.9 4.1 %back_near.1 = (f32[256,768]{1,0:T(8,128)}, bf16[256,768]{1,0:T(8,128)(2,1)S(1)}, bf16[512,768]{1,0:T(8,128)(2,1)S(1)}, bf16[512,768]{1,0:T(8,128)(2,1)S(1)}, f32[8,768]{1,0:T(8,128)}) custom-call(bf16[256,768]{1,0:T(8,128)(2,1)S(1)} %get-tuple-element.126.refs_0_, bf16[256,768]{1,0:T(8,128)(2,1)S(1)} %collective-permute-done.9.refs_1_, ...), custom_call_target="tpu_custom_call" | custom-call | tf_op jit(solution)/shard_map/back_near/pallas_call | solution.py:177
  82.3 3.4 %back_far.1 = (f32[256,768]{1,0:T(8,128)S(1)}, bf16[256,768]{1,0:T(8,128)(2,1)S(1)}, bf16[512,768]{1,0:T(8,128)(2,1)S(1)}, bf16[512,768]{1,0:T(8,128)(2,1)S(1)}, f32[8,768]{1,0:T(8,128)}) custom-call(bf16[128,768]{1,0:T(8,128)(2,1)S(1)} %collective-permute-done.10.refs_0_, bf16[128,768]{1,0:T(8,128)(2,1)S(1)} %collective-permute-done.11.refs_1_, ...), custom_call_target="tpu_custom_call" | custom-call | tf_op jit(solution)/shard_map/back_far/pallas_call | solution.py:177
  87.7 1.8 collective-permute-start.16
  89.6 0.8 add_convert_fusion.2.refs_0_
  90.4 1.9 pack.1
  92.3 1.8 collective-permute-done.16.refs_3_
  94.1 2.6 %collective-permute-done.17.refs_4_ = bf16[128,768]{1,0:T(8,128)(2,1)S(1)} collective-permute-done((bf16[128,768]{1,0:T(8,128)(2,1)S(1)}, bf16[128,768]{1,0:T(8,128)(2,1)S(1)}, u32[]{:S(2)}, u32[]{:S(2)}) %collective-permute-start.17) | collective-permute-done | bytes 196640 | tf_op jit(solution)/shard_map/ppermute | solution.py:971
  96.7 8.0 %all-to-all-start.1 = ((bf16[128,9,8,128]{3,2,1,0:T(8,128)(2,1)}), bf16[128,9,8,128]{3,2,1,0:T(8,128)(2,1)S(1)}, u32[]{:S(2)}, u32[]{:S(2)}) async-start(bf16[128,9,8,128]{3,2,1,0:T(8,128)(2,1)} %bitcast.36), calls=%async_computation.1 | async-start | bytes 4718592 | tf_op jit(solution)/shard_map/all_to_all | solution.py:977
  104.7 1.4 collective-permute-start.12
  106.1 1.3 collective-permute-done.12.refs_2_
  107.4 13.4 %attend_back.1 = (f32[256,768]{1,0:T(8,128)}, bf16[640,8,128]{2,1,0:T(8,128)(2,1)S(1)}, bf16[640,8,128]{2,1,0:T(8,128)(2,1)S(1)}) custom-call(s32[2]{0:T(128)S(1)} %pad_add_fusion.place.refs_0_, f32[256,768]{1,0:T(8,128)} %get-tuple-element.128.refs_1_, bf16[256,768]{1,0:T(8,128)(2,1)S(1)} %collective-permute-done.12.refs_2_, ...), custom_call_target="tpu_custom_call" | custom-call | tf_op jit(solution)/shard_map/attend_back/pallas_call | solution.py:177
  121.3 2.7 %collective-permute-done.18 = bf16[640,8,128]{2,1,0:T(8,128)(2,1)S(1)} collective-permute-done((bf16[640,8,128]{2,1,0:T(8,128)(2,1)S(1)}, bf16[640,8,128]{2,1,0:T(8,128)(2,1)S(1)}, u32[]{:S(2)}, u32[]{:S(2)}) %collective-permute-start.18) | collective-permute-done | bytes 1310752 | tf_op jit(solution)/shard_map/ppermute | solution.py:968
  123.9 1.4 add_convert_fusion
  125.3 10.6 %all-to-all-done.1.got = bf16[128,9,8,128]{3,2,1,0:T(8,128)(2,1)S(1)} async-done(((bf16[128,9,8,128]{3,2,1,0:T(8,128)(2,1)}), bf16[128,9,8,128]{3,2,1,0:T(8,128)(2,1)S(1)}, u32[]{:S(2)}, u32[]{:S(2)}) %all-to-all-start.1) | async-done | bytes 2359328 | tf_op jit(solution)/shard_map/all_to_all | solution.py:977
  136.3 5.9 %all-to-all-start.2 = ((bf16[128,5,8,128]{3,2,1,0:T(8,128)(2,1)}), bf16[128,5,8,128]{3,2,1,0:T(8,128)(2,1)S(1)}, u32[]{:S(2)}, u32[]{:S(2)}) async-start(bf16[128,5,8,128]{3,2,1,0:T(8,128)(2,1)} %bitcast.37), calls=%async_computation.2 | async-start | bytes 2621440 | tf_op jit(solution)/shard_map/all_to_all | solution.py:977
  142.3 3.6 %collective-permute-start.25 = (bf16[4,9,8,128]{3,2,1,0:T(8,128)(2,1)S(1)}, bf16[4,9,8,128]{3,2,1,0:T(8,128)(2,1)S(1)}, u32[]{:S(2)}, u32[]{:S(2)}) collective-permute-start(bf16[4,9,8,128]{3,2,1,0:T(8,128)(2,1)S(1)} %sum_ffn.1), channel_id=1, source_target_pairs={{0,112},{8,120},{16,64},{24,72},{32,80},{40,88},{48,96},{56,104},{... | collective-permute-start | bytes 221192 | tf_op jit(solution)/shard_map/ppermute | solution.py:1037
  146.4 1.5 collective-permute-start.23
  148.2 2.1 %collective-permute-start.21 = (bf16[4,9,8,128]{3,2,1,0:T(8,128)(2,1)S(1)}, bf16[4,9,8,128]{3,2,1,0:T(8,128)(2,1)S(1)}, u32[]{:S(2)}, u32[]{:S(2)}) collective-permute-start(bf16[4,9,8,128]{3,2,1,0:T(8,128)(2,1)S(1)} %sum_ffn.1), channel_id=1, source_target_pairs={{0,48},{8,56},{16,0},{24,8},{32,16},{40,24},{48,32},{56,40},{64,11... | collective-permute-start | bytes 221192 | tf_op jit(solution)/shard_map/ppermute | solution.py:1037
  150.3 10.1 %collective-permute-done.25 = bf16[4,9,8,128]{3,2,1,0:T(8,128)(2,1)S(1)} collective-permute-done((bf16[4,9,8,128]{3,2,1,0:T(8,128)(2,1)S(1)}, bf16[4,9,8,128]{3,2,1,0:T(8,128)(2,1)S(1)}, u32[]{:S(2)}, u32[]{:S(2)}) %collective-permute-start.25) | collective-permute-done | bytes 73760 | tf_op jit(solution)/shard_map/ppermute | solution.py:1037
  160.4 2.7 %collective-permute-start.20 = (bf16[4,9,8,128]{3,2,1,0:T(8,128)(2,1)S(1)}, bf16[4,9,8,128]{3,2,1,0:T(8,128)(2,1)S(1)}, u32[]{:S(2)}, u32[]{:S(2)}) collective-permute-start(bf16[4,9,8,128]{3,2,1,0:T(8,128)(2,1)S(1)} %sum_ffn.1), channel_id=1, source_target_pairs={{0,32},{8,40},{16,48},{24,56},{32,0},{40,8},{48,16},{56,24},{64,96... | collective-permute-start | bytes 221192 | tf_op jit(solution)/shard_map/ppermute | solution.py:1037
  163.4 1.0 collective-permute-start.19
  164.4 1.3 sum_rest.1
  166.3 1.9 collective-permute-done.19
  168.2 8.8 %all-to-all-start.3 = ((bf16[128,5,8,128]{3,2,1,0:T(8,128)(2,1)}), bf16[128,5,8,128]{3,2,1,0:T(8,128)(2,1)S(1)}, u32[]{:S(2)}, u32[]{:S(2)}) async-start(bf16[128,5,8,128]{3,2,1,0:T(8,128)(2,1)} %sum_rest.1), calls=%async_computation.3 | async-start | bytes 2621440 | tf_op jit(solution)/shard_map/all_to_all | solution.py:977
  177.2 1.1 collective-permute-start.26
  178.3 1.6 collective-permute-done.26.ffn_oth
  179.9 3.6 %final_ffn.1 = (f32[768,384]{1,0:T(8,128)}, f32[384,768]{1,0:T(8,128)}) custom-call(s32[2]{0:T(128)S(1)} %pad_add_fusion.place.refs_0_, bf16[8,4,9,8,128]{4,3,2,1,0:T(8,128)(2,1)S(1)} %bitcast_dynamic-update-slice_fusion.ffn_own, bf16[8,4,9,8,128]{4,3,2,1,0:T(8,128)(2,1)S(1)} %collective-permute-done.26.ffn_oth), custom_call_target="tpu_custom_call" | custom-call | tf_op jit(solution)/shard_map/final_ffn/pallas_call | solution.py:859
  183.5 13.9 %all-to-all-done.3 = bf16[128,5,8,128]{3,2,1,0:T(8,128)(2,1)S(1)} async-done(((bf16[128,5,8,128]{3,2,1,0:T(8,128)(2,1)}), bf16[128,5,8,128]{3,2,1,0:T(8,128)(2,1)S(1)}, u32[]{:S(2)}, u32[]{:S(2)}) %all-to-all-start.3) | async-done | bytes 1310752 | tf_op jit(solution)/shard_map/all_to_all | solution.py:977
  197.4 1.2 collective-permute-start.27
  198.6 2.7 %collective-permute-done.27.other = bf16[640,8,128]{2,1,0:T(8,128)(2,1)S(1)} collective-permute-done((bf16[640,8,128]{2,1,0:T(8,128)(2,1)S(1)}, bf16[640,8,128]{2,1,0:T(8,128)(2,1)S(1)}, u32[]{:S(2)}, u32[]{:S(2)}) %collective-permute-start.27) | collective-permute-done | bytes 1310752 | tf_op jit(solution)/shard_map/ppermute | solution.py:968
  201.3 4.0 %final.1 = (f32[768,768]{1,0:T(8,128)}, f32[768]{0:T(1024)}, f32[65,768]{1,0:T(8,128)}, f32[768,768]{1,0:T(8,128)}, f32[768]{0:T(1024)}, /*index=5*/f32[768]{0:T...) custom-call(s32[2]{0:T(128)S(1)} %pad_add_fusion.place.refs_0_, ...), custom_call_target="tpu_custom_call" | custom-call | tf_op jit(solution)/shard_map/final/pallas_call | solution.py:917
  (78 shorter events, 10.5 us)
Async XLA Ops:
  4.3 12.0 %copy-start.5 = (bf16[768]{0:T(1024)(128)(2,1)S(1)}, bf16[768]{0:T(1024)(128)(2,1)}, u32[]{:S(2)}) copy-start(bf16[768]{0:T(1024)(128)(2,1)} %param.25) | copy-start | bytes 4612
  4.3 12.0 %copy-start.6 = (bf16[768]{0:T(1024)(128)(2,1)S(1)}, bf16[768]{0:T(1024)(128)(2,1)}, u32[]{:S(2)}) copy-start(bf16[768]{0:T(1024)(128)(2,1)} %param.26) | copy-start | bytes 4612
  4.3 12.0 %copy-start.7 = (bf16[768]{0:T(1024)(128)(2,1)S(1)}, bf16[768]{0:T(1024)(128)(2,1)}, u32[]{:S(2)}) copy-start(bf16[768]{0:T(1024)(128)(2,1)} %param.21) | copy-start | bytes 4612
  4.3 12.0 %copy-start.8 = (bf16[768]{0:T(1024)(128)(2,1)S(1)}, bf16[768]{0:T(1024)(128)(2,1)}, u32[]{:S(2)}) copy-start(bf16[768]{0:T(1024)(128)(2,1)} %param.24) | copy-start | bytes 4612
  4.4 12.0 %copy-start.2 = (bf16[65,768]{1,0:T(8,128)(2,1)S(1)}, bf16[65,768]{1,0:T(8,128)(2,1)}, u32[]{:S(2)}) copy-start(bf16[65,768]{1,0:T(8,128)(2,1)} %refs_4_.1) | copy-start | bytes 299524
  4.4 12.0 %copy-start.3 = (s32[256]{0:T(256)S(1)}, s32[256]{0:T(256)}, u32[]{:S(2)}) copy-start(s32[256]{0:T(256)} %param.35) | copy-start | bytes 3076
  4.4 12.0 %copy-start.4 = (s32[1,4]{1,0:T(1,128)S(1)}, s32[1,4]{1,0:T(1,128)}, u32[]{:S(2)}) copy-start(s32[1,4]{1,0:T(1,128)} %refs_0_.1) | copy-start | bytes 52
  4.4 47.5 %all-to-all-start = ((bf16[128,10,8,128]{3,2,1,0:T(8,128)(2,1)}), bf16[128,10,8,128]{3,2,1,0:T(8,128)(2,1)}, u32[]{:S(2)}, u32[]{:S(2)}) async-start(bf16[128,10,8,128]{3,2,1,0:T(8,128)(2,1)} %bitcast.35), calls=%async_computation | async-start | bytes 5242880 | tf_op jit(solution)/shard_map/all_to_all | solution.py:977
  34.9 16.1 %collective-permute-start.1 = (bf16[128,768]{1,0:T(8,128)(2,1)S(1)}, bf16[128,768]{1,0:T(8,128)(2,1)S(1)}, u32[]{:S(2)}, u32[]{:S(2)}) collective-permute-start(bf16[128,768]{1,0:T(8,128)(2,1)S(1)} %get-tuple-element.110), channel_id=1, source_target_pairs={{0,16},{8,24},{16,32},{24,40},{32,48},{40,56},{48,0},{56,8},{64,80... | collective-permute-start | bytes 589832 | tf_op jit(solution)/shard_map/ppermute | solution.py:971
  36.4 15.5 %collective-permute-start.2 = (bf16[128,768]{1,0:T(8,128)(2,1)S(1)}, bf16[128,768]{1,0:T(8,128)(2,1)S(1)}, u32[]{:S(2)}, u32[]{:S(2)}) collective-permute-start(bf16[128,768]{1,0:T(8,128)(2,1)S(1)} %get-tuple-element.111), channel_id=1, source_target_pairs={{0,48},{8,56},{16,0},{24,8},{32,16},{40,24},{48,32},{56,40},{64,11... | collective-permute-start | bytes 589832 | tf_op jit(solution)/shard_map/ppermute | solution.py:974
  51.0 2.8 %collective-permute-start.3 = (bf16[128,768]{1,0:T(8,128)(2,1)S(1)}, bf16[128,768]{1,0:T(8,128)(2,1)S(1)}, u32[]{:S(2)}, u32[]{:S(2)}) collective-permute-start(bf16[128,768]{1,0:T(8,128)(2,1)S(1)} %collective-permute-done.1.got_a), channel_id=1, source_target_pairs={{0,8},{8,0},{16,24},{24,16},{32,40},{40,32},{48,56},{56,48},{64,72... | collective-permute-start | bytes 589832 | tf_op jit(solution)/shard_map/ppermute | solution.py:968
  51.8 2.0 collective-permute-start.4
  57.6 1.9 collective-permute-start.5
  58.2 3.0 %collective-permute-start = (bf16[256,768]{1,0:T(8,128)(2,1)S(1)}, bf16[256,768]{1,0:T(8,128)(2,1)S(1)}, u32[]{:S(2)}, u32[]{:S(2)}) collective-permute-start(bf16[256,768]{1,0:T(8,128)(2,1)S(1)} %get-tuple-element.108.own), channel_id=1, source_target_pairs={{0,8},{8,0},{16,24},{24,16},{32,40},{40,32},{48,56},{56,48},{64,72... | collective-permute-start | bytes 1179656 | tf_op jit(solution)/shard_map/ppermute | solution.py:968
  59.6 9.3 %copy-start.9 = (bf16[768]{0:T(1024)(128)(2,1)S(1)}, bf16[768]{0:T(1024)(128)(2,1)}, u32[]{:S(2)}) copy-start(bf16[768]{0:T(1024)(128)(2,1)} %param.30) | copy-start | bytes 4612
  59.6 9.3 %copy-start.10 = (bf16[768]{0:T(1024)(128)(2,1)S(1)}, bf16[768]{0:T(1024)(128)(2,1)}, u32[]{:S(2)}) copy-start(bf16[768]{0:T(1024)(128)(2,1)} %param.31) | copy-start | bytes 4612
  59.6 10.7 %copy-start = (f32[256,768]{1,0:T(8,128)S(1)}, f32[256,768]{1,0:T(8,128)}, u32[]{:S(2)}) copy-start(f32[256,768]{1,0:T(8,128)} %get-tuple-element.107.refs_0_.n1.refs_6_) | copy-start | bytes 2359300
  59.7 10.6 %copy-start.1 = (bf16[256,768]{1,0:T(8,128)(2,1)S(1)}, bf16[256,768]{1,0:T(8,128)(2,1)}, u32[]{:S(2)}) copy-start(bf16[256,768]{1,0:T(8,128)(2,1)} %og.1) | copy-start | bytes 1179652
  59.7 6.2 %collective-permute-start.6 = (bf16[128,768]{1,0:T(8,128)(2,1)S(1)}, bf16[128,768]{1,0:T(8,128)(2,1)S(1)}, u32[]{:S(2)}, u32[]{:S(2)}) collective-permute-start(bf16[128,768]{1,0:T(8,128)(2,1)S(1)} %get-tuple-element.120), channel_id=1, source_target_pairs={{0,48},{8,56},{16,0},{24,8},{32,16},{40,24},{48,32},{56,40},{64,11... | collective-permute-start | bytes 589832 | tf_op jit(solution)/shard_map/ppermute | solution.py:974
  60.4 7.0 %collective-permute-start.7 = (bf16[128,768]{1,0:T(8,128)(2,1)S(1)}, bf16[128,768]{1,0:T(8,128)(2,1)S(1)}, u32[]{:S(2)}, u32[]{:S(2)}) collective-permute-start(bf16[128,768]{1,0:T(8,128)(2,1)S(1)} %get-tuple-element.121), channel_id=1, source_target_pairs={{0,16},{8,24},{16,32},{24,40},{32,48},{40,56},{48,0},{56,8},{64,80... | collective-permute-start | bytes 589832 | tf_op jit(solution)/shard_map/ppermute | solution.py:971
  65.0 9.1 %copy-start.11 = (bf16[768]{0:T(1024)(128)(2,1)S(1)}, bf16[768]{0:T(1024)(128)(2,1)}, u32[]{:S(2)}) copy-start(bf16[768]{0:T(1024)(128)(2,1)} %param.32) | copy-start | bytes 4612
  67.4 2.9 %collective-permute-start.8 = (bf16[256,768]{1,0:T(8,128)(2,1)S(1)}, bf16[256,768]{1,0:T(8,128)(2,1)S(1)}, u32[]{:S(2)}, u32[]{:S(2)}) collective-permute-start(bf16[256,768]{1,0:T(8,128)(2,1)S(1)} %get-tuple-element.122), channel_id=1, source_target_pairs={{0,8},{8,0},{16,24},{24,16},{32,40},{40,32},{48,56},{56,48},{64,72... | collective-permute-start | bytes 1179656 | tf_op jit(solution)/shard_map/ppermute | solution.py:968
  71.0 5.0 %collective-permute-start.9 = (bf16[256,768]{1,0:T(8,128)(2,1)S(1)}, bf16[256,768]{1,0:T(8,128)(2,1)S(1)}, u32[]{:S(2)}, u32[]{:S(2)}) collective-permute-start(bf16[256,768]{1,0:T(8,128)(2,1)S(1)} %get-tuple-element.126.refs_0_), channel_id=1, source_target_pairs={{0,8},{8,0},{16,24},{24,16},{32,40},{40,32},{48,56},{56,48},{64,72... | collective-permute-start | bytes 1179656 | tf_op jit(solution)/shard_map/ppermute | solution.py:968
  71.4 8.6 %collective-permute-start.10 = (bf16[128,768]{1,0:T(8,128)(2,1)S(1)}, bf16[128,768]{1,0:T(8,128)(2,1)S(1)}, u32[]{:S(2)}, u32[]{:S(2)}) collective-permute-start(bf16[128,768]{1,0:T(8,128)(2,1)S(1)} %get-tuple-element.129), channel_id=1, source_target_pairs={{0,16},{8,24},{16,32},{24,40},{32,48},{40,56},{48,0},{56,8},{64,80... | collective-permute-start | bytes 589832 | tf_op jit(solution)/shard_map/ppermute | solution.py:971
  71.4 8.6 %collective-permute-start.11 = (bf16[128,768]{1,0:T(8,128)(2,1)S(1)}, bf16[128,768]{1,0:T(8,128)(2,1)S(1)}, u32[]{:S(2)}, u32[]{:S(2)}) collective-permute-start(bf16[128,768]{1,0:T(8,128)(2,1)S(1)} %get-tuple-element.130), channel_id=1, source_target_pairs={{0,48},{8,56},{16,0},{24,8},{32,16},{40,24},{48,32},{56,40},{64,11... | collective-permute-start | bytes 589832 | tf_op jit(solution)/shard_map/ppermute | solution.py:974
  80.1 1.9 collective-permute-start.13
  80.9 1.4 collective-permute-start.14
  85.7 2.0 collective-permute-start.15
  87.7 6.3 %collective-permute-start.16 = (bf16[128,768]{1,0:T(8,128)(2,1)S(1)}, bf16[128,768]{1,0:T(8,128)(2,1)S(1)}, u32[]{:S(2)}, u32[]{:S(2)}) collective-permute-start(bf16[128,768]{1,0:T(8,128)(2,1)S(1)} %get-tuple-element.150), channel_id=1, source_target_pairs={{0,48},{8,56},{16,0},{24,8},{32,16},{40,24},{48,32},{56,40},{64,11... | collective-permute-start | bytes 589832 | tf_op jit(solution)/shard_map/ppermute | solution.py:974
  89.6 7.2 %collective-permute-start.17 = (bf16[128,768]{1,0:T(8,128)(2,1)S(1)}, bf16[128,768]{1,0:T(8,128)(2,1)S(1)}, u32[]{:S(2)}, u32[]{:S(2)}) collective-permute-start(bf16[128,768]{1,0:T(8,128)(2,1)S(1)} %get-tuple-element.151), channel_id=1, source_target_pairs={{0,16},{8,24},{16,32},{24,40},{32,48},{40,56},{48,0},{56,8},{64,80... | collective-permute-start | bytes 589832 | tf_op jit(solution)/shard_map/ppermute | solution.py:971
  96.7 39.2 %all-to-all-start.1 = ((bf16[128,9,8,128]{3,2,1,0:T(8,128)(2,1)}), bf16[128,9,8,128]{3,2,1,0:T(8,128)(2,1)S(1)}, u32[]{:S(2)}, u32[]{:S(2)}) async-start(bf16[128,9,8,128]{3,2,1,0:T(8,128)(2,1)} %bitcast.36), calls=%async_computation.1 | async-start | bytes 4718592 | tf_op jit(solution)/shard_map/all_to_all | solution.py:977
  104.7 2.7 %collective-permute-start.12 = (bf16[256,768]{1,0:T(8,128)(2,1)S(1)}, bf16[256,768]{1,0:T(8,128)(2,1)S(1)}, u32[]{:S(2)}, u32[]{:S(2)}) collective-permute-start(bf16[256,768]{1,0:T(8,128)(2,1)S(1)} %get-tuple-element.133), channel_id=1, source_target_pairs={{0,8},{8,0},{16,24},{24,16},{32,40},{40,32},{48,56},{56,48},{64,72... | collective-permute-start | bytes 1179656 | tf_op jit(solution)/shard_map/ppermute | solution.py:968
  120.8 3.1 %collective-permute-start.18 = (bf16[640,8,128]{2,1,0:T(8,128)(2,1)S(1)}, bf16[640,8,128]{2,1,0:T(8,128)(2,1)S(1)}, u32[]{:S(2)}, u32[]{:S(2)}) collective-permute-start(bf16[640,8,128]{2,1,0:T(8,128)(2,1)S(1)} %get-tuple-element.171), channel_id=1, source_target_pairs={{0,8},{8,0},{16,24},{24,16},{32,40},{40,32},{48,56},{56,48},{64,72... | collective-permute-start | bytes 3932168 | tf_op jit(solution)/shard_map/ppermute | solution.py:968
  136.3 28.1 %all-to-all-start.2 = ((bf16[128,5,8,128]{3,2,1,0:T(8,128)(2,1)}), bf16[128,5,8,128]{3,2,1,0:T(8,128)(2,1)S(1)}, u32[]{:S(2)}, u32[]{:S(2)}) async-start(bf16[128,5,8,128]{3,2,1,0:T(8,128)(2,1)} %bitcast.37), calls=%async_computation.2 | async-start | bytes 2621440 | tf_op jit(solution)/shard_map/all_to_all | solution.py:977
  142.3 18.1 %collective-permute-start.25 = (bf16[4,9,8,128]{3,2,1,0:T(8,128)(2,1)S(1)}, bf16[4,9,8,128]{3,2,1,0:T(8,128)(2,1)S(1)}, u32[]{:S(2)}, u32[]{:S(2)}) collective-permute-start(bf16[4,9,8,128]{3,2,1,0:T(8,128)(2,1)S(1)} %sum_ffn.1), channel_id=1, source_target_pairs={{0,112},{8,120},{16,64},{24,72},{32,80},{40,88},{48,96},{56,104},{... | collective-permute-start | bytes 221192 | tf_op jit(solution)/shard_map/ppermute | solution.py:1037
  145.9 17.5 %collective-permute-start.24 = (bf16[4,9,8,128]{3,2,1,0:T(8,128)(2,1)S(1)}, bf16[4,9,8,128]{3,2,1,0:T(8,128)(2,1)S(1)}, u32[]{:S(2)}, u32[]{:S(2)}) collective-permute-start(bf16[4,9,8,128]{3,2,1,0:T(8,128)(2,1)S(1)} %sum_ffn.1), channel_id=1, source_target_pairs={{0,96},{8,104},{16,112},{24,120},{32,64},{40,72},{48,80},{56,88},{... | collective-permute-start | bytes 221192 | tf_op jit(solution)/shard_map/ppermute | solution.py:1037
  146.4 19.3 %collective-permute-start.23 = (bf16[4,9,8,128]{3,2,1,0:T(8,128)(2,1)S(1)}, bf16[4,9,8,128]{3,2,1,0:T(8,128)(2,1)S(1)}, u32[]{:S(2)}, u32[]{:S(2)}) collective-permute-start(bf16[4,9,8,128]{3,2,1,0:T(8,128)(2,1)S(1)} %sum_ffn.1), channel_id=1, source_target_pairs={{0,80},{8,88},{16,96},{24,104},{32,112},{40,120},{48,64},{56,72},{... | collective-permute-start | bytes 221192 | tf_op jit(solution)/shard_map/ppermute | solution.py:1037
  147.9 17.8 %collective-permute-start.22 = (bf16[4,9,8,128]{3,2,1,0:T(8,128)(2,1)S(1)}, bf16[4,9,8,128]{3,2,1,0:T(8,128)(2,1)S(1)}, u32[]{:S(2)}, u32[]{:S(2)}) collective-permute-start(bf16[4,9,8,128]{3,2,1,0:T(8,128)(2,1)S(1)} %sum_ffn.1), channel_id=1, source_target_pairs={{0,64},{8,72},{16,80},{24,88},{32,96},{40,104},{48,112},{56,120},{... | collective-permute-start | bytes 221192 | tf_op jit(solution)/shard_map/ppermute | solution.py:1037
  148.2 17.5 %collective-permute-start.21 = (bf16[4,9,8,128]{3,2,1,0:T(8,128)(2,1)S(1)}, bf16[4,9,8,128]{3,2,1,0:T(8,128)(2,1)S(1)}, u32[]{:S(2)}, u32[]{:S(2)}) collective-permute-start(bf16[4,9,8,128]{3,2,1,0:T(8,128)(2,1)S(1)} %sum_ffn.1), channel_id=1, source_target_pairs={{0,48},{8,56},{16,0},{24,8},{32,16},{40,24},{48,32},{56,40},{64,11... | collective-permute-start | bytes 221192 | tf_op jit(solution)/shard_map/ppermute | solution.py:1037
  160.4 5.9 %collective-permute-start.20 = (bf16[4,9,8,128]{3,2,1,0:T(8,128)(2,1)S(1)}, bf16[4,9,8,128]{3,2,1,0:T(8,128)(2,1)S(1)}, u32[]{:S(2)}, u32[]{:S(2)}) collective-permute-start(bf16[4,9,8,128]{3,2,1,0:T(8,128)(2,1)S(1)} %sum_ffn.1), channel_id=1, source_target_pairs={{0,32},{8,40},{16,48},{24,56},{32,0},{40,8},{48,16},{56,24},{64,96... | collective-permute-start | bytes 221192 | tf_op jit(solution)/shard_map/ppermute | solution.py:1037
  163.4 4.8 %collective-permute-start.19 = (bf16[4,9,8,128]{3,2,1,0:T(8,128)(2,1)S(1)}, bf16[4,9,8,128]{3,2,1,0:T(8,128)(2,1)S(1)}, u32[]{:S(2)}, u32[]{:S(2)}) collective-permute-start(bf16[4,9,8,128]{3,2,1,0:T(8,128)(2,1)S(1)} %sum_ffn.1), channel_id=1, source_target_pairs={{0,16},{8,24},{16,32},{24,40},{32,48},{40,56},{48,0},{56,8},{64,80... | collective-permute-start | bytes 221192 | tf_op jit(solution)/shard_map/ppermute | solution.py:1037
  168.2 29.2 %all-to-all-start.3 = ((bf16[128,5,8,128]{3,2,1,0:T(8,128)(2,1)}), bf16[128,5,8,128]{3,2,1,0:T(8,128)(2,1)S(1)}, u32[]{:S(2)}, u32[]{:S(2)}) async-start(bf16[128,5,8,128]{3,2,1,0:T(8,128)(2,1)} %sum_rest.1), calls=%async_computation.3 | async-start | bytes 2621440 | tf_op jit(solution)/shard_map/all_to_all | solution.py:977
  177.2 2.8 %collective-permute-start.26 = (bf16[8,4,9,8,128]{4,3,2,1,0:T(8,128)(2,1)S(1)}, bf16[8,4,9,8,128]{4,3,2,1,0:T(8,128)(2,1)S(1)}, u32[]{:S(2)}, u32[]{:S(2)}) collective-permute-start(bf16[8,4,9,8,128]{4,3,2,1,0:T(8,128)(2,1)S(1)} %bitcast_dynamic-update-slice_fusion.ffn_own), channel_id=1, source_target_pairs={{0,8},{8,0},{16,24},{24,16},{32,40},{40,32},{48,56},{56,48},{64,72... | collective-permute-start | bytes 1769480 | tf_op jit(solution)/shard_map/ppermute | solution.py:968
  197.4 3.8 %collective-permute-start.27 = (bf16[640,8,128]{2,1,0:T(8,128)(2,1)S(1)}, bf16[640,8,128]{2,1,0:T(8,128)(2,1)S(1)}, u32[]{:S(2)}, u32[]{:S(2)}) collective-permute-start(bf16[640,8,128]{2,1,0:T(8,128)(2,1)S(1)} %bitcast.32), channel_id=1, source_target_pairs={{0,8},{8,0},{16,24},{24,16},{32,40},{40,32},{48,56},{56,48},{64,72... | collective-permute-start | bytes 3932168 | tf_op jit(solution)/shard_map/ppermute | solution.py:968

commit v6 on v5

--- a/solution.py
+++ b/solution.py
@@ -25,7 +25,6 @@
 UNITS = 10
 GRAD_UNITS = 9
 HIDDEN = 768
-HALF = ROWS // 2
 TALL = 848
 TALL_TILES = TALL // 8
 PACK = 640
@@ -291,7 +290,7 @@
 
 def attend_kernel(
     len_ref, x_ref, wv_ref, bv_ref, taps_ref, wo_ref, bo_ref, ga_ref, sa_ref, q_ref, k_ref, live_ref,
-    n_ref, inv_ref, low_ref, low_a, low_b, ctx_ref, col_ref, nrm_ref, scl_ref, wave_ref, wavet_ref, ks_ref, vs_ref,
+    n_ref, inv_ref, low_ref, ctx_ref, col_ref, nrm_ref, scl_ref, wave_ref, wavet_ref, ks_ref, vs_ref,
     tapt_ref, live_out, qw, kb, jn, tapbuf, mix, mskd,
 ):
     ends = segment_ends(len_ref)
@@ -420,15 +419,11 @@
     n, inv = norm_rows(x_ref[...].astype(f32) + attended)
     n_ref[...] = n
     inv_ref[...] = jnp.broadcast_to(inv, (ROWS, 128))
-    low = (n * ga_ref[...].astype(f32) + sa_ref[...].astype(f32)).astype(bf16)
-    low_ref[...] = low
-    low_a[...] = low[0:HALF]
-    low_b[...] = low[HALF:]
+    low_ref[...] = (n * ga_ref[...].astype(f32) + sa_ref[...].astype(f32)).astype(bf16)
 
 
 def attend(seq_lengths, x, wv, bv, taps, wo, bo, ga, sa, q, k, live):
     wide = (ROWS, WIDTH)
-    half = (HALF, WIDTH)
     h = "hbm"
     v = "vmem"
     return staged_call(
@@ -439,7 +434,7 @@
         ],
         [
             (h, shape(wide, f32)), (h, shape((ROWS, 128), f32)), (v, shape(wide, bf16)),
-            (v, shape(half, bf16)), (v, shape(half, bf16)), (h, shape(wide, bf16)),
+            (h, shape(wide, bf16)),
             (h, shape((HEADS, ROWS, ROWS), bf16)), (h, shape(wide, bf16)), (h, shape(wide, f32)),
             (h, shape((2 * FREQ, ROWS), bf16)), (h, shape((ROWS, 2 * FREQ), bf16)),
             (h, shape((2 * FREQ, WIDTH), f32)), (h, shape((2 * FREQ, WIDTH), bf16)),
@@ -504,19 +499,7 @@
     )
 
 
-def ffn_far_kernel(
-    got_a, got_b, sib_a, sib_b, wu, wd, act, slope, part_own, part_sib, rows_out, rows, acc,
-):
-    for i, ref in enumerate((got_a, got_b, sib_a, sib_b)):
-        rows[i * HALF : i * HALF + HALF, 0:WIDTH] = ref[...]
-    rows[:, WIDTH:] = jnp.where(lanes((2 * ROWS, 128)) < 3, 1.0, 0.0).astype(bf16)
-    rows_out[...] = rows[:, 0:WIDTH]
-    ffn_blocks(rows, wu, wd, act, slope, acc)
-    part_own[...] = acc[0:ROWS]
-    part_sib[...] = acc[ROWS:].astype(bf16)
-
-
-def ffn_near_kernel(own, sib, wu, wd, act, slope, part_own, part_sib, rows_out, rows, acc):
+def ffn_kernel(own, sib, wu, wd, act, slope, part_own, part_sib, rows_out, rows, acc):
     rows[0:ROWS, 0:WIDTH] = own[...]
     rows[ROWS:, 0:WIDTH] = sib[...]
     rows[:, WIDTH:] = jnp.where(lanes((2 * ROWS, 128)) < 3, 1.0, 0.0).astype(bf16)
@@ -526,70 +509,61 @@
     part_sib[...] = acc[ROWS:].astype(bf16)
 
 
-def ffn_call(kernel, name, *args):
+def ffn(*args):
     wide = (ROWS, WIDTH)
     tall = shape((2 * ROWS, WIDTH), bf16)
     outs = (tall, tall, shape(wide, f32), shape(wide, bf16), tall)
     return staged_call(
-        kernel, name, 20, [("vmem", a) for a in args], [("vmem", o) for o in outs],
+        ffn_kernel, "ffn", 20, [("vmem", a) for a in args], [("vmem", o) for o in outs],
         [pltpu.VMEM((2 * ROWS, WIDTH + 128), bf16), pltpu.VMEM((2 * ROWS, WIDTH), f32)],
     )
 
 
-def combine_kernel(own, got, out_a, out_b):
-    total = (own[...] + got[...].astype(f32)).astype(bf16)
-    out_a[...] = total[0:HALF]
-    out_b[...] = total[HALF:]
+def combine_kernel(own, got, out):
+    out[...] = (own[...] + got[...].astype(f32)).astype(bf16)
 
 
 def combine(own, got):
-    half = shape((HALF, WIDTH), bf16)
     return pl.pallas_call(
         combine_kernel,
-        out_shape=(half, half),
+        out_shape=shape((ROWS, WIDTH), bf16),
         in_specs=[VMEM] * 2,
-        out_specs=(VMEM,) * 2,
-        compiler_params=params(32),
+        out_specs=VMEM,
+        compiler_params=params(16),
         name="combine",
     )(own, got)
 
 
-def gather_rows(own, near, far_a, far_b):
-    far = jnp.concatenate([far_a[...], far_b[...]], axis=0)
-    return own[...] + near[...].astype(f32) + far.astype(f32)
-
-
-def second_norm(n1, own, near, far_a, far_b, bd, ga, sa, gf, og):
+def gather_rows(own, near, far):
+    return own[...] + near[...].astype(f32) + far[...].astype(f32)
+
+
+def second_norm(n1, own, near, far, bd, ga, sa, gf, og):
     first = n1[...] * ga[...].astype(f32) + sa[...].astype(f32)
-    n, inv = norm_rows(first + gather_rows(own, near, far_a, far_b) + bd[...].astype(f32))
+    n, inv = norm_rows(first + gather_rows(own, near, far) + bd[...].astype(f32))
     g = og[...].astype(f32)
     return n, g, norm_back(g, n, inv, gf[...].astype(f32))
 
 
-def middle_kernel(n1, own, near, far_a, far_b, bd, ga, sa, gf, og, low, low_a, low_b):
-    grad = second_norm(n1, own, near, far_a, far_b, bd, ga, sa, gf, og)[2].astype(bf16)
-    low[...] = grad
-    low_a[...] = grad[0:HALF]
-    low_b[...] = grad[HALF:]
+def middle_kernel(n1, own, near, far, bd, ga, sa, gf, og, low):
+    low[...] = second_norm(n1, own, near, far, bd, ga, sa, gf, og)[2].astype(bf16)
 
 
 def middle(*args):
-    wide = shape((ROWS, WIDTH), bf16)
-    half = shape((HALF, WIDTH), bf16)
     return pl.pallas_call(
         middle_kernel,
-        out_shape=(wide, half, half),
+        out_shape=shape((ROWS, WIDTH), bf16),
         in_specs=[VMEM] * len(args),
-        out_specs=(VMEM,) * 3,
+        out_specs=VMEM,
         compiler_params=params(16),
         name="middle",
     )(*args)
 
 
 def outputs_kernel(
-    n1, own, near, far_a, far_b, bd, ga, sa, gf, og, sf, out, second, sums,
+    n1, own, near, far, bd, ga, sa, gf, og, sf, out, second, sums,
 ):
-    n, g, grad = second_norm(n1, own, near, far_a, far_b, bd, ga, sa, gf, og)
+    n, g, grad = second_norm(n1, own, near, far, bd, ga, sa, gf, og)
     out[...] = (n * gf[...].astype(f32) + sf[...].astype(f32)).astype(bf16)
     second[...] = grad
     sums[0:1] = jnp.sum(grad.astype(bf16).astype(f32), axis=0, keepdims=True)
@@ -621,7 +595,7 @@
     lax.fori_loop(0, HIDDEN // 256, block, 0)
 
 
-def back_near_kernel(own, sib, wu, wd, slope, first_own, first_sib, g, u, bias, acc):
+def back_ffn_kernel(own, sib, wu, wd, slope, first_own, first_sib, g, u, bias, acc):
     g[0:ROWS] = own[...]
     g[ROWS:] = sib[...]
     back_blocks(g, wu, wd, slope, u, bias, acc)
@@ -629,21 +603,11 @@
     first_sib[...] = acc[ROWS:].astype(bf16)
 
 
-def back_far_kernel(
-    got_a, got_b, sib_a, sib_b, wu, wd, slope, first_own, first_sib, g, u, bias, acc,
-):
-    for i, ref in enumerate((got_a, got_b, sib_a, sib_b)):
-        g[i * HALF : i * HALF + HALF] = ref[...]
-    back_blocks(g, wu, wd, slope, u, bias, acc)
-    first_own[...] = acc[0:ROWS]
-    first_sib[...] = acc[ROWS:].astype(bf16)
-
-
-def back_call(kernel, name, *args):
+def back_ffn(name, *args):
     wide = (ROWS, WIDTH)
     tall = shape((2 * ROWS, WIDTH), bf16)
     return staged_call(
-        kernel, name, 20, [("vmem", a) for a in args],
+        back_ffn_kernel, name, 20, [("vmem", a) for a in args],
         [
             ("hbm" if name == "back_near" else "vmem", shape(wide, f32)), ("vmem", shape(wide, bf16)),
             ("vmem", tall), ("vmem", tall), ("hbm", shape((8, HIDDEN), f32)),
@@ -673,10 +637,10 @@
 
 
 def back_kernel(
-    place, own, near, far_a, far_b, second, n1, inv1, ga, ctx, wo, nrm, scl, wave, wavet, ks, vs, tapt, col, live, x,
+    place, own, near, far, second, n1, inv1, ga, ctx, wo, nrm, scl, wave, wavet, ks, vs, tapt, col, live, x,
     wv, sums, bias_n, bias_f, in_grad, keep, give, buf_a, buf_b, mb,
 ):
-    first_grad = second[...] + gather_rows(own, near, far_a, far_b)
+    first_grad = second[...] + gather_rows(own, near, far)
     n = n1[...]
     buf_a[768 + 2 : 768 + 3] = jnp.sum(first_grad * n, axis=0, keepdims=True)
     buf_a[768 + 3 : 768 + 4] = jnp.sum(first_grad, axis=0, keepdims=True)
@@ -758,7 +722,7 @@
     wide = (ROWS, WIDTH)
     packed = shape((PACK, 8, 128), bf16)
     kinds = ["smem"] + ["hbm"] * (len(args) - 1)
-    for i in (2, 3, 4, 8):
+    for i in (2, 3, 7):
         kinds[i] = "vmem"
     return staged_call(
         back_kernel, "attend_back", 40, list(zip(kinds, args, strict=True)),
@@ -830,26 +794,26 @@
 def final_ffn_kernel(place, ffn_own, ffn_oth, g_up, g_down, tall):
     ct = pl.program_id(0)
     core = place[0] % 2
-
-    def index(m, a):
-        return (m + place[0] // 8) % 2 * 4 + (place[0] // 2 % 4 + 4 - a) % 4
-
-    def spread(ref):
+    x_lo = place[0] // 8
+    half = ct // 3
+
+    def spread(up_ref, down_ref):
         for a in range(PIECES):
-            up = ref[index(0, a)].astype(f32)
-            down = ref[index(1, a)].astype(f32)
+            at = (place[0] // 2 % 4 + 4 - a) % 4 * 2
+            up = up_ref[at + (half + x_lo) % 2].astype(f32)
+            down = down_ref[at + (half + x_lo + 1) % 2].astype(f32)
             for q in range(CLASSES):
                 rs = slice(SUB * q + PIECE * a, SUB * q + PIECE * a + PIECE)
                 tall[rs, :] = up[q].reshape(PIECE, 128)
                 g_down[rs, :] = down[q].reshape(PIECE, 128)
 
-    @pl.when(ct // 3 == core)
-    def _():
-        spread(ffn_own)
-
-    @pl.when(ct // 3 != core)
-    def _():
-        spread(ffn_oth)
+    @pl.when(x_lo == core)
+    def _():
+        spread(ffn_own, ffn_oth)
+
+    @pl.when(x_lo != core)
+    def _():
+        spread(ffn_oth, ffn_own)
 
     g_up[...] = tall[...].T
 
@@ -967,11 +931,13 @@
     def swap(x):
         return lax.ppermute(x, "dp", [(i, i ^ 1) for i in range(n_dp)])
 
-    def ahead(x):
-        return lax.ppermute(x, "dp", [(i, shift(i, 1)) for i in range(n_dp)])
-
-    def behind(x):
-        return lax.ppermute(x, "dp", [(i, shift(i, -1)) for i in range(n_dp)])
+    def away(x):
+        pairs = [(i, shift(i, 1 - i % 2 * 2)) for i in range(n_dp)]
+        return lax.ppermute(x, "dp", pairs)
+
+    def home(x):
+        pairs = [(shift(i, 1 - i % 2 * 2), i) for i in range(n_dp)]
+        return lax.ppermute(x, "dp", pairs)
 
     def exchange(x):
         return lax.all_to_all(x, ALL, 0, 0, tiled=True)
@@ -981,47 +947,36 @@
 
     weights = exchange(prep(place, w_up, w_down, b_up))
     weights = weights.reshape(2, PIECES, 2, 8, UNITS, 8, 128)
-    (n1, inv1, low, low_a, low_b, ctx, collide, nrm, scl, wave, wavet, ks, vs, tapt, live) = attend(
+    (n1, inv1, low, ctx, collide, nrm, scl, wave, wavet, ks, vs, tapt, live) = attend(
         seq_lengths, block_input, w_value, row(b_value), conv_kernel, w_out, row(b_out),
         row(gain_attn), row(shift_attn), query_codes, key_codes, row(key_live),
     )
     low_sib = swap(low)
-    row_a, row_b = ahead(low_a), behind(low_b)
+    got = away(low)
     wu, wd = unpack_weights(weights)
-    act_f, slope_f, far_own, far_sib, rows_f = ffn_call(
-        ffn_far_kernel, "ffn_far", row_a, row_b, swap(row_a), swap(row_b), wu, wd
-    )
-    sent_a, sent_b = combine(far_own, swap(far_sib))
-    wu, sent_a, sent_b = lax.optimization_barrier((wu, sent_a, sent_b))
-    act_n, slope_n, near_own, near_sib, rows_n = ffn_call(
-        ffn_near_kernel, "ffn_near", low, low_sib, wu, wd
-    )
-    back_a, back_b = behind(sent_a), ahead(sent_b)
-    near_sib, back_a, back_b = lax.optimization_barrier((near_sib, back_a, back_b))
+    act_f, slope_f, far_own, far_sib, rows_f = ffn(got, swap(got), wu, wd)
+    sent = combine(far_own, swap(far_sib))
+    wu, sent = lax.optimization_barrier((wu, sent))
+    act_n, slope_n, near_own, near_sib, rows_n = ffn(low, low_sib, wu, wd)
+    near_sib, far = lax.optimization_barrier((near_sib, home(sent)))
     second_args = (
-        n1, near_own, swap(near_sib), back_a, back_b, row(b_down), row(gain_attn), row(shift_attn),
+        n1, near_own, swap(near_sib), far, row(b_down), row(gain_attn), row(shift_attn),
         row(gain_ffn), out_grad,
     )
-    grad, grad_a, grad_b = middle(*second_args)
-    got_a, got_b = ahead(grad_a), behind(grad_b)
-    near_own, near_sib, g_n, u_n, bias_n = back_call(
-        back_near_kernel, "back_near", grad, swap(grad), wu, wd, slope_n
-    )
+    grad = middle(*second_args)
+    got = away(grad)
+    near_own, near_sib, g_n, u_n, bias_n = back_ffn("back_near", grad, swap(grad), wu, wd, slope_n)
     block_output, second, sums = outputs(*second_args, row(shift_ffn))
-    got_a, got_b, near_sib, second = lax.optimization_barrier((got_a, got_b, near_sib, second))
-    far_own, far_sib, g_f, u_f, bias_f = back_call(
-        back_far_kernel, "back_far", got_a, got_b, swap(got_a), swap(got_b), wu, wd, slope_f
-    )
-    sent_a, sent_b = combine(far_own, swap(far_sib))
-    u_f, sent_a, sent_b = lax.optimization_barrier((u_f, sent_a, sent_b))
+    got, near_sib, second = lax.optimization_barrier((got, near_sib, second))
+    far_own, far_sib, g_f, u_f, bias_f = back_ffn("back_far", got, swap(got), wu, wd, slope_f)
+    sent = combine(far_own, swap(far_sib))
+    u_f, sent = lax.optimization_barrier((u_f, sent))
     grad_down = (dot_first(act_n, g_n) + dot_first(act_f, g_f)).astype(bf16)
     grad_up = (dot_first(u_n, rows_n) + dot_first(u_f, rows_f)).astype(bf16)
-    grads = pack(grad_up, grad_down)
-    back_a, back_b = behind(sent_a), ahead(sent_b)
-    grads, back_a, back_b = lax.optimization_barrier((grads, back_a, back_b))
+    grads, far = lax.optimization_barrier((pack(grad_up, grad_down), home(sent)))
     owned = exchange(grads.reshape(128, GRAD_UNITS, 8, 128))
     input_grad, keep, give = attend_back(
-        place, near_own, swap(near_sib), back_a, back_b, second, n1, inv1,
+        place, near_own, swap(near_sib), far, second, n1, inv1,
         row(gain_attn), ctx, w_out, nrm, scl, wave, wavet, ks, vs, tapt, collide, live, block_input,
         w_value, sums, bias_n, bias_f,
     )
@@ -1029,16 +984,15 @@
     pair = pair.reshape(128, PACK // 128, 8, 128)
     owned = sum_ffn(owned)
     pair, owned = lax.optimization_barrier((pair, owned))
+    both = jnp.stack([owned, swap(owned)])
     around = []
-    for side in range(2):
-        for by in range(4):
-            if side or by:
-                pairs = [(i, (i // 8 + side) % 2 * 8 + shift(i % 8, by)) for i in range(n_dp)]
-                around.append(lax.ppermute(owned, "dp", pairs))
+    for by in range(4):
+        pairs = [(i, (i // 8 ^ i % 2) * 8 + shift(i % 8, by)) for i in range(n_dp)]
+        around.append(lax.ppermute(both, "dp", pairs))
     summed = sum_rest(exchange(pair))
     summed, *around = lax.optimization_barrier((summed, *around))
     back = exchange(summed).reshape(PACK, 8, 128)
-    ffn_own = jnp.stack([owned, *around])
+    ffn_own = jnp.stack(around).reshape(8, CLASSES, GRAD_UNITS, 8, 128)
     g_up, g_down = final_ffn(place, ffn_own, swap(ffn_own))
     back, g_up, g_down = lax.optimization_barrier((back, g_up, g_down))
     g_wv, g_bv, g_conv, g_wo, g_bo, g_ga, g_sa, g_bup, g_bd, g_gf, g_sf = final(

time: 206 us -> 200 us (0.971)
  starting transfers between devices: 64 us -> 56 us
  waiting for transfers between devices: 69 us -> 71.7 us
    all_to_all x4, waiting for transfers between devices: 24.5 us -> 35.9 us  [exchange(): return lax.all_to_all(x, ALL, 0, 0, tiled=True)]
    ppermute x15 -> x8, waiting for transfers between devices: 33 us -> 22.1 us  [the longest x2 12.6 us: away(): return lax.ppermute(x, 'dp', pairs)]
    ppermute x15 -> x8, starting transfers between devices: 20.5 us -> 11.9 us  [the longest x4 7.1 us: body(): around.append(lax.ppermute(both, 'dp', pairs))]
    ppermute x13 -> x12, waiting for transfers between devices: 11.4 us -> 13.7 us  [swap(): return lax.ppermute(x, 'dp', [(i, i ^ 1) for i in range(n_dp)])]
    ppermute x13 -> x12, starting transfers between devices: 8.87 us -> 10.1 us  [swap(): return lax.ppermute(x, 'dp', [(i, i ^ 1) for i in range(n_dp)])]
  transfers between devices with their start and end apart: 32 -> 24, of which waited for: 19 -> 16; matrix products, arithmetic and copies ran while one was open for 2% -> 2% of each run, Pallas kernels for 24% -> 25%
where the time goes in v6:
time: 200 us
  waiting for transfers between devices  71.7 us (36%)
  Pallas kernels  66.1 us (33%)
  starting transfers between devices  56 us (28%)
  matrix products  3.28 us (2%)
    pallas_call x7, Pallas kernels, staged_call(): pl.pallas_call(run, out_shape=tuple((pltpu.HBM(o.shape, o.dtype) if k ==...  44.8 us
    all_to_all x4, waiting for transfers between devices, exchange(): return lax.all_to_all(x, ALL, 0, 0, tiled=True)  35.9 us
    all_to_all x4, starting transfers between devices, exchange(): return lax.all_to_all(x, ALL, 0, 0, tiled=True)  34 us
    ppermute x12, waiting for transfers between devices, swap(): return lax.ppermute(x, 'dp', [(i, i ^ 1) for i in range(n_dp)])  13.7 us
    ppermute x2, waiting for transfers between devices, away(): return lax.ppermute(x, 'dp', pairs)  12.6 us
    ppermute x12, starting transfers between devices, swap(): return lax.ppermute(x, 'dp', [(i, i ^ 1) for i in range(n_dp)])  10.1 us
    ppermute x2, waiting for transfers between devices, home(): return lax.ppermute(x, 'dp', pairs)  7.94 us
    pallas_call x2, Pallas kernels, staged_call(): pl.pallas_call(kernel, out_shape=tuple((o for _, o in outs)), in_specs=[s...  7.6 us
  transfers between devices with their start and end apart: 24, of which 16 were waited for; matrix products, arithmetic and copies ran while one was open for 2% of the time, Pallas kernels for 25%

profile of v6, /device:TPU:1, one launch (start us, length us, event | category | flops | bytes accessed | tf_op | source)
XLA Modules:
  0.0 200.0 jit_solution(80594084703085057)
XLA Ops:
  0.7 3.6 %prep.1 = bf16[4,4,8,10,8,128]{5,4,3,2,1,0:T(8,128)(2,1)} custom-call(s32[2]{0:T(128)S(1)} %pad_add_fusion.place.refs_0_, bf16[768,384]{1,0:T(8,128)(2,1)} %up_ref.1, bf16[384,768]{1,0:T(8,128)(2,1)} %down_ref.1, bf16[384]{0:T(512)(128)(2,1)} %bias_hbm.1), custom_call_target="tpu_custom_call" | custom-call | tf_op jit(solution)/shard_map/prep/pallas_call | solution.py:246
  4.4 11.9 %all-to-all-start = ((bf16[128,10,8,128]{3,2,1,0:T(8,128)(2,1)}), bf16[128,10,8,128]{3,2,1,0:T(8,128)(2,1)}, u32[]{:S(2)}, u32[]{:S(2)}) async-start(bf16[128,10,8,128]{3,2,1,0:T(8,128)(2,1)} %bitcast.29), calls=%async_computation | async-start | bytes 5242880 | tf_op jit(solution)/shard_map/all_to_all | solution.py:943
  16.5 18.5 %attend.1 = (f32[256,768]{1,0:T(8,128)}, f32[256,128]{1,0:T(8,128)}, bf16[256,768]{1,0:T(8,128)(2,1)S(1)}, bf16[256,768]{1,0:T(8,128)(2,1)}, bf16[12,256,256]{2,...) custom-call(s32[1,4]{1,0:T(1,128)S(1)} %copy-done.4, ...), custom_call_target="tpu_custom_call" | custom-call | tf_op jit(solution)/shard_map/attend/pallas_call | solution.py:176
  34.9 2.7 %collective-permute-start.1 = (bf16[256,768]{1,0:T(8,128)(2,1)S(1)}, bf16[256,768]{1,0:T(8,128)(2,1)S(1)}, u32[]{:S(2)}, u32[]{:S(2)}) collective-permute-start(bf16[256,768]{1,0:T(8,128)(2,1)S(1)} %get-tuple-element.91.own), channel_id=1, source_target_pairs={{0,16},{8,56},{16,32},{24,8},{32,48},{40,24},{48,0},{56,40},{64,80... | collective-permute-start | bytes 1179656 | tf_op jit(solution)/shard_map/ppermute | solution.py:936
  37.7 12.6 %collective-permute-done.1.own = bf16[256,768]{1,0:T(8,128)(2,1)S(1)} collective-permute-done((bf16[256,768]{1,0:T(8,128)(2,1)S(1)}, bf16[256,768]{1,0:T(8,128)(2,1)S(1)}, u32[]{:S(2)}, u32[]{:S(2)}) %collective-permute-start.1) | collective-permute-done | bytes 393248 | tf_op jit(solution)/shard_map/ppermute | solution.py:936
  50.3 1.9 collective-permute-start.2
  52.2 1.9 unpack.1
  54.2 3.8 %ffn.2 = (bf16[512,768]{1,0:T(8,128)(2,1)S(1)}, bf16[512,768]{1,0:T(8,128)(2,1)S(1)}, f32[256,768]{1,0:T(8,128)S(1)}, bf16[256,768]{1,0:T(8,128)(2,1)S(1)}, bf16[512,768]{1,0:T(8,128)(2,1)S(1)}) custom-call(bf16[256,768]{1,0:T(8,128)(2,1)S(1)} %collective-permute-done.1.own, bf16[256,768]{1,0:T(8,128)(2,1)S(1)} %collective-permute-done.2.sib, ...), custom_call_target="tpu_custom_call" | custom-call | tf_op jit(solution)/shard_map/ffn/pallas_call | solution.py:140
  58.6 1.2 collective-permute-done.3.got
  60.4 3.8 %ffn.3 = (bf16[512,768]{1,0:T(8,128)(2,1)S(1)}, bf16[512,768]{1,0:T(8,128)(2,1)S(1)}, f32[256,768]{1,0:T(8,128)S(1)}, bf16[256,768]{1,0:T(8,128)(2,1)S(1)}, bf16[512,768]{1,0:T(8,128)(2,1)S(1)}) custom-call(bf16[256,768]{1,0:T(8,128)(2,1)S(1)} %get-tuple-element.91.own, bf16[256,768]{1,0:T(8,128)(2,1)S(1)} %collective-permute-done.sib, ...), custom_call_target="tpu_custom_call" | custom-call | tf_op jit(solution)/shard_map/ffn/pallas_call | solution.py:140
  64.2 3.7 %collective-permute-done.4.refs_3_.far = bf16[256,768]{1,0:T(8,128)(2,1)S(1)} collective-permute-done((bf16[256,768]{1,0:T(8,128)(2,1)S(1)}, bf16[256,768]{1,0:T(8,128)(2,1)S(1)}, u32[]{:S(2)}, u32[]{:S(2)}) %collective-permute-start.4) | collective-permute-done | bytes 393248 | tf_op jit(solution)/shard_map/ppermute | solution.py:940
  67.9 1.6 collective-permute-done.5.refs_2_.near
  70.4 1.8 collective-permute-start.7
  72.3 1.8 outputs.1
  74.1 4.1 %back_near.1 = (f32[256,768]{1,0:T(8,128)}, bf16[256,768]{1,0:T(8,128)(2,1)S(1)}, bf16[512,768]{1,0:T(8,128)(2,1)S(1)}, bf16[512,768]{1,0:T(8,128)(2,1)S(1)}, f32[8,768]{1,0:T(8,128)}) custom-call(bf16[256,768]{1,0:T(8,128)(2,1)S(1)} %middle.1.refs_0_, bf16[256,768]{1,0:T(8,128)(2,1)S(1)} %collective-permute-done.6.refs_1_, ...), custom_call_target="tpu_custom_call" | custom-call | tf_op jit(solution)/shard_map/back_near/pallas_call | solution.py:176
  78.2 1.6 collective-permute-start.9
  79.8 1.3 collective-permute-done.9.refs_1_
  81.1 3.4 %back_far.1 = (f32[256,768]{1,0:T(8,128)S(1)}, bf16[256,768]{1,0:T(8,128)(2,1)S(1)}, bf16[512,768]{1,0:T(8,128)(2,1)S(1)}, bf16[512,768]{1,0:T(8,128)(2,1)S(1)}, f32[8,768]{1,0:T(8,128)}) custom-call(bf16[256,768]{1,0:T(8,128)(2,1)S(1)} %collective-permute-done.7.refs_0_, bf16[256,768]{1,0:T(8,128)(2,1)S(1)} %collective-permute-done.9.refs_1_, ...), custom_call_target="tpu_custom_call" | custom-call | tf_op jit(solution)/shard_map/back_far/pallas_call | solution.py:176
  85.0 0.8 fusion
  85.8 0.8 fusion.1
  86.7 0.8 add_convert_fusion.1.refs_1_
  87.6 0.8 add_convert_fusion.2.refs_0_
  88.4 1.9 pack.1
  90.3 4.3 %collective-permute-done.11.refs_3_ = bf16[256,768]{1,0:T(8,128)(2,1)S(1)} collective-permute-done((bf16[256,768]{1,0:T(8,128)(2,1)S(1)}, bf16[256,768]{1,0:T(8,128)(2,1)S(1)}, u32[]{:S(2)}, u32[]{:S(2)}) %collective-permute-start.11) | collective-permute-done | bytes 393248 | tf_op jit(solution)/shard_map/ppermute | solution.py:940
  94.6 7.9 %all-to-all-start.1 = ((bf16[128,9,8,128]{3,2,1,0:T(8,128)(2,1)}), bf16[128,9,8,128]{3,2,1,0:T(8,128)(2,1)S(1)}, u32[]{:S(2)}, u32[]{:S(2)}) async-start(bf16[128,9,8,128]{3,2,1,0:T(8,128)(2,1)} %bitcast.30), calls=%async_computation.1 | async-start | bytes 4718592 | tf_op jit(solution)/shard_map/all_to_all | solution.py:943
  102.5 1.4 collective-permute-start.8
  103.9 1.3 collective-permute-done.8.refs_2_
  105.2 13.3 %attend_back.1 = (f32[256,768]{1,0:T(8,128)}, bf16[640,8,128]{2,1,0:T(8,128)(2,1)S(1)}, bf16[640,8,128]{2,1,0:T(8,128)(2,1)S(1)}) custom-call(s32[2]{0:T(128)S(1)} %pad_add_fusion.place.refs_0_, f32[256,768]{1,0:T(8,128)} %get-tuple-element.104.refs_1_, bf16[256,768]{1,0:T(8,128)(2,1)S(1)} %collective-permute-done.8.refs_2_, ...), custom_call_target="tpu_custom_call" | custom-call | tf_op jit(solution)/shard_map/attend_back/pallas_call | solution.py:176
  119.0 2.7 %collective-permute-done.12 = bf16[640,8,128]{2,1,0:T(8,128)(2,1)S(1)} collective-permute-done((bf16[640,8,128]{2,1,0:T(8,128)(2,1)S(1)}, bf16[640,8,128]{2,1,0:T(8,128)(2,1)S(1)}, u32[]{:S(2)}, u32[]{:S(2)}) %collective-permute-start.12) | collective-permute-done | bytes 1310752 | tf_op jit(solution)/shard_map/ppermute | solution.py:932
  121.7 1.4 add_convert_fusion
  123.1 10.6 %all-to-all-done.1.got = bf16[128,9,8,128]{3,2,1,0:T(8,128)(2,1)S(1)} async-done(((bf16[128,9,8,128]{3,2,1,0:T(8,128)(2,1)}), bf16[128,9,8,128]{3,2,1,0:T(8,128)(2,1)S(1)}, u32[]{:S(2)}, u32[]{:S(2)}) %all-to-all-start.1) | async-done | bytes 2359328 | tf_op jit(solution)/shard_map/all_to_all | solution.py:943
  134.1 5.9 %all-to-all-start.2 = ((bf16[128,5,8,128]{3,2,1,0:T(8,128)(2,1)}), bf16[128,5,8,128]{3,2,1,0:T(8,128)(2,1)S(1)}, u32[]{:S(2)}, u32[]{:S(2)}) async-start(bf16[128,5,8,128]{3,2,1,0:T(8,128)(2,1)} %bitcast.31), calls=%async_computation.2 | async-start | bytes 2621440 | tf_op jit(solution)/shard_map/all_to_all | solution.py:943
  140.1 1.1 collective-permute-start.13
  141.2 0.9 collective-permute-done.13
  142.1 2.9 %collective-permute-start.17 = (bf16[2,4,9,8,128]{4,3,2,1,0:T(8,128)(2,1)S(1)}, bf16[2,4,9,8,128]{4,3,2,1,0:T(8,128)(2,1)S(1)}, u32[]{:S(2)}, u32[]{:S(2)}) collective-permute-start(bf16[2,4,9,8,128]{4,3,2,1,0:T(8,128)(2,1)S(1)} %pad_maximum_fusion.1), channel_id=1, source_target_pairs={{0,48},{8,120},{16,0},{24,72},{32,16},{40,88},{48,32},{56,104},{64... | collective-permute-start | bytes 442376 | tf_op jit(solution)/shard_map/ppermute | solution.py:991
  145.6 1.5 collective-permute-start.15
  147.1 2.2 %collective-permute-start.14 = (bf16[2,4,9,8,128]{4,3,2,1,0:T(8,128)(2,1)S(1)}, bf16[2,4,9,8,128]{4,3,2,1,0:T(8,128)(2,1)S(1)}, u32[]{:S(2)}, u32[]{:S(2)}) collective-permute-start(bf16[2,4,9,8,128]{4,3,2,1,0:T(8,128)(2,1)S(1)} %pad_maximum_fusion.1), channel_id=1, source_target_pairs={{0,0},{8,72},{16,16},{24,88},{32,32},{40,104},{48,48},{56,120},{64... | collective-permute-start | bytes 442376 | tf_op jit(solution)/shard_map/ppermute | solution.py:991
  149.2 11.3 %all-to-all-done.2.got = bf16[128,5,8,128]{3,2,1,0:T(8,128)(2,1)S(1)} async-done(((bf16[128,5,8,128]{3,2,1,0:T(8,128)(2,1)}), bf16[128,5,8,128]{3,2,1,0:T(8,128)(2,1)S(1)}, u32[]{:S(2)}, u32[]{:S(2)}) %all-to-all-start.2) | async-done | bytes 1310752 | tf_op jit(solution)/shard_map/all_to_all | solution.py:943
  160.5 1.3 sum_rest.1
  161.9 1.5 collective-permute-done.15
  163.4 8.2 %all-to-all-start.3 = ((bf16[128,5,8,128]{3,2,1,0:T(8,128)(2,1)}), bf16[128,5,8,128]{3,2,1,0:T(8,128)(2,1)S(1)}, u32[]{:S(2)}, u32[]{:S(2)}) async-start(bf16[128,5,8,128]{3,2,1,0:T(8,128)(2,1)} %sum_rest.1), calls=%async_computation.3 | async-start | bytes 2621440 | tf_op jit(solution)/shard_map/all_to_all | solution.py:943
  171.7 1.1 collective-permute-start.18
  172.8 1.6 collective-permute-done.18.ffn_oth
  174.5 3.6 %final_ffn.1 = (f32[768,384]{1,0:T(8,128)}, f32[384,768]{1,0:T(8,128)}) custom-call(s32[2]{0:T(128)S(1)} %pad_add_fusion.place.refs_0_, bf16[8,4,9,8,128]{4,3,2,1,0:T(8,128)(2,1)S(1)} %bitcast.26, bf16[8,4,9,8,128]{4,3,2,1,0:T(8,128)(2,1)S(1)} %collective-permute-done.18.ffn_oth), custom_call_target="tpu_custom_call" | custom-call | tf_op jit(solution)/shard_map/final_ffn/pallas_call | solution.py:823
  178.0 14.0 %all-to-all-done.3 = bf16[128,5,8,128]{3,2,1,0:T(8,128)(2,1)S(1)} async-done(((bf16[128,5,8,128]{3,2,1,0:T(8,128)(2,1)}), bf16[128,5,8,128]{3,2,1,0:T(8,128)(2,1)S(1)}, u32[]{:S(2)}, u32[]{:S(2)}) %all-to-all-start.3) | async-done | bytes 1310752 | tf_op jit(solution)/shard_map/all_to_all | solution.py:943
  192.0 1.2 collective-permute-start.19
  193.2 2.7 %collective-permute-done.19.other = bf16[640,8,128]{2,1,0:T(8,128)(2,1)S(1)} collective-permute-done((bf16[640,8,128]{2,1,0:T(8,128)(2,1)S(1)}, bf16[640,8,128]{2,1,0:T(8,128)(2,1)S(1)}, u32[]{:S(2)}, u32[]{:S(2)}) %collective-permute-start.19) | collective-permute-done | bytes 1310752 | tf_op jit(solution)/shard_map/ppermute | solution.py:932
  195.9 4.0 %final.1 = (f32[768,768]{1,0:T(8,128)}, f32[768]{0:T(1024)}, f32[65,768]{1,0:T(8,128)}, f32[768,768]{1,0:T(8,128)}, f32[768]{0:T(1024)}, /*index=5*/f32[768]{0:T...) custom-call(s32[2]{0:T(128)S(1)} %pad_add_fusion.place.refs_0_, ...), custom_call_target="tpu_custom_call" | custom-call | tf_op jit(solution)/shard_map/final/pallas_call | solution.py:881
  (56 shorter events, 4.3 us)
Async XLA Ops:
  4.3 12.0 %copy-start.5 = (bf16[768]{0:T(1024)(128)(2,1)S(1)}, bf16[768]{0:T(1024)(128)(2,1)}, u32[]{:S(2)}) copy-start(bf16[768]{0:T(1024)(128)(2,1)} %param.25) | copy-start | bytes 4612
  4.3 12.0 %copy-start.6 = (bf16[768]{0:T(1024)(128)(2,1)S(1)}, bf16[768]{0:T(1024)(128)(2,1)}, u32[]{:S(2)}) copy-start(bf16[768]{0:T(1024)(128)(2,1)} %param.26) | copy-start | bytes 4612
  4.4 12.0 %copy-start.7 = (bf16[768]{0:T(1024)(128)(2,1)S(1)}, bf16[768]{0:T(1024)(128)(2,1)}, u32[]{:S(2)}) copy-start(bf16[768]{0:T(1024)(128)(2,1)} %param.21) | copy-start | bytes 4612
  4.4 12.0 %copy-start.8 = (bf16[768]{0:T(1024)(128)(2,1)S(1)}, bf16[768]{0:T(1024)(128)(2,1)}, u32[]{:S(2)}) copy-start(bf16[768]{0:T(1024)(128)(2,1)} %param.24) | copy-start | bytes 4612
  4.4 12.0 %copy-start.2 = (bf16[65,768]{1,0:T(8,128)(2,1)S(1)}, bf16[65,768]{1,0:T(8,128)(2,1)}, u32[]{:S(2)}) copy-start(bf16[65,768]{1,0:T(8,128)(2,1)} %refs_4_.1) | copy-start | bytes 299524
  4.4 12.0 %copy-start.3 = (s32[256]{0:T(256)S(1)}, s32[256]{0:T(256)}, u32[]{:S(2)}) copy-start(s32[256]{0:T(256)} %param.35) | copy-start | bytes 3076
  4.4 12.0 %copy-start.4 = (s32[1,4]{1,0:T(1,128)S(1)}, s32[1,4]{1,0:T(1,128)}, u32[]{:S(2)}) copy-start(s32[1,4]{1,0:T(1,128)} %refs_0_.1) | copy-start | bytes 52
  4.4 47.8 %all-to-all-start = ((bf16[128,10,8,128]{3,2,1,0:T(8,128)(2,1)}), bf16[128,10,8,128]{3,2,1,0:T(8,128)(2,1)}, u32[]{:S(2)}, u32[]{:S(2)}) async-start(bf16[128,10,8,128]{3,2,1,0:T(8,128)(2,1)} %bitcast.29), calls=%async_computation | async-start | bytes 5242880 | tf_op jit(solution)/shard_map/all_to_all | solution.py:943
  34.9 15.4 %collective-permute-start.1 = (bf16[256,768]{1,0:T(8,128)(2,1)S(1)}, bf16[256,768]{1,0:T(8,128)(2,1)S(1)}, u32[]{:S(2)}, u32[]{:S(2)}) collective-permute-start(bf16[256,768]{1,0:T(8,128)(2,1)S(1)} %get-tuple-element.91.own), channel_id=1, source_target_pairs={{0,16},{8,56},{16,32},{24,8},{32,48},{40,24},{48,0},{56,40},{64,80... | collective-permute-start | bytes 1179656 | tf_op jit(solution)/shard_map/ppermute | solution.py:936
  50.3 3.9 %collective-permute-start.2 = (bf16[256,768]{1,0:T(8,128)(2,1)S(1)}, bf16[256,768]{1,0:T(8,128)(2,1)S(1)}, u32[]{:S(2)}, u32[]{:S(2)}) collective-permute-start(bf16[256,768]{1,0:T(8,128)(2,1)S(1)} %collective-permute-done.1.own), channel_id=1, source_target_pairs={{0,8},{8,0},{16,24},{24,16},{32,40},{40,32},{48,56},{56,48},{64,72... | collective-permute-start | bytes 1179656 | tf_op jit(solution)/shard_map/ppermute | solution.py:932
  58.0 1.8 collective-permute-start.3
  58.1 2.3 %collective-permute-start = (bf16[256,768]{1,0:T(8,128)(2,1)S(1)}, bf16[256,768]{1,0:T(8,128)(2,1)S(1)}, u32[]{:S(2)}, u32[]{:S(2)}) collective-permute-start(bf16[256,768]{1,0:T(8,128)(2,1)S(1)} %get-tuple-element.91.own), channel_id=1, source_target_pairs={{0,8},{8,0},{16,24},{24,16},{32,40},{40,32},{48,56},{56,48},{64,72... | collective-permute-start | bytes 1179656 | tf_op jit(solution)/shard_map/ppermute | solution.py:932
  59.9 8.0 %copy-start.9 = (bf16[768]{0:T(1024)(128)(2,1)S(1)}, bf16[768]{0:T(1024)(128)(2,1)}, u32[]{:S(2)}) copy-start(bf16[768]{0:T(1024)(128)(2,1)} %param.30) | copy-start | bytes 4612
  59.9 8.0 %copy-start.10 = (bf16[768]{0:T(1024)(128)(2,1)S(1)}, bf16[768]{0:T(1024)(128)(2,1)}, u32[]{:S(2)}) copy-start(bf16[768]{0:T(1024)(128)(2,1)} %param.31) | copy-start | bytes 4612
  59.9 9.7 %copy-start = (f32[256,768]{1,0:T(8,128)S(1)}, f32[256,768]{1,0:T(8,128)}, u32[]{:S(2)}) copy-start(f32[256,768]{1,0:T(8,128)} %get-tuple-element.90.refs_0_.n1.refs_5_) | copy-start | bytes 2359300
  59.9 9.6 %copy-start.1 = (bf16[256,768]{1,0:T(8,128)(2,1)S(1)}, bf16[256,768]{1,0:T(8,128)(2,1)}, u32[]{:S(2)}) copy-start(bf16[256,768]{1,0:T(8,128)(2,1)} %og.1) | copy-start | bytes 1179652
  59.9 7.9 %collective-permute-start.4 = (bf16[256,768]{1,0:T(8,128)(2,1)S(1)}, bf16[256,768]{1,0:T(8,128)(2,1)S(1)}, u32[]{:S(2)}, u32[]{:S(2)}) collective-permute-start(bf16[256,768]{1,0:T(8,128)(2,1)S(1)} %combine.2), channel_id=1, source_target_pairs={{16,0},{56,8},{32,16},{8,24},{48,32},{24,40},{0,48},{40,56},{80,64... | collective-permute-start | bytes 1179656 | tf_op jit(solution)/shard_map/ppermute | solution.py:940
  67.8 1.7 collective-permute-start.5
  69.5 2.7 %copy-start.11 = (bf16[768]{0:T(1024)(128)(2,1)S(1)}, bf16[768]{0:T(1024)(128)(2,1)}, u32[]{:S(2)}) copy-start(bf16[768]{0:T(1024)(128)(2,1)} %param.32) | copy-start | bytes 4612
  70.2 3.9 %collective-permute-start.6 = (bf16[256,768]{1,0:T(8,128)(2,1)S(1)}, bf16[256,768]{1,0:T(8,128)(2,1)S(1)}, u32[]{:S(2)}, u32[]{:S(2)}) collective-permute-start(bf16[256,768]{1,0:T(8,128)(2,1)S(1)} %middle.1.refs_0_), channel_id=1, source_target_pairs={{0,8},{8,0},{16,24},{24,16},{32,40},{40,32},{48,56},{56,48},{64,72... | collective-permute-start | bytes 1179656 | tf_op jit(solution)/shard_map/ppermute | solution.py:932
  70.4 7.8 %collective-permute-start.7 = (bf16[256,768]{1,0:T(8,128)(2,1)S(1)}, bf16[256,768]{1,0:T(8,128)(2,1)S(1)}, u32[]{:S(2)}, u32[]{:S(2)}) collective-permute-start(bf16[256,768]{1,0:T(8,128)(2,1)S(1)} %middle.1.refs_0_), channel_id=1, source_target_pairs={{0,16},{8,56},{16,32},{24,8},{32,48},{40,24},{48,0},{56,40},{64,80... | collective-permute-start | bytes 1179656 | tf_op jit(solution)/shard_map/ppermute | solution.py:936
  78.2 2.9 %collective-permute-start.9 = (bf16[256,768]{1,0:T(8,128)(2,1)S(1)}, bf16[256,768]{1,0:T(8,128)(2,1)S(1)}, u32[]{:S(2)}, u32[]{:S(2)}) collective-permute-start(bf16[256,768]{1,0:T(8,128)(2,1)S(1)} %collective-permute-done.7.refs_0_), channel_id=1, source_target_pairs={{0,8},{8,0},{16,24},{24,16},{32,40},{40,32},{48,56},{56,48},{64,72... | collective-permute-start | bytes 1179656 | tf_op jit(solution)/shard_map/ppermute | solution.py:932
  84.5 2.1 %collective-permute-start.10 = (bf16[256,768]{1,0:T(8,128)(2,1)S(1)}, bf16[256,768]{1,0:T(8,128)(2,1)S(1)}, u32[]{:S(2)}, u32[]{:S(2)}) collective-permute-start(bf16[256,768]{1,0:T(8,128)(2,1)S(1)} %get-tuple-element.114), channel_id=1, source_target_pairs={{0,8},{8,0},{16,24},{24,16},{32,40},{40,32},{48,56},{56,48},{64,72... | collective-permute-start | bytes 1179656 | tf_op jit(solution)/shard_map/ppermute | solution.py:932
  86.7 7.9 %collective-permute-start.11 = (bf16[256,768]{1,0:T(8,128)(2,1)S(1)}, bf16[256,768]{1,0:T(8,128)(2,1)S(1)}, u32[]{:S(2)}, u32[]{:S(2)}) collective-permute-start(bf16[256,768]{1,0:T(8,128)(2,1)S(1)} %combine.3), channel_id=1, source_target_pairs={{16,0},{56,8},{32,16},{8,24},{48,32},{24,40},{0,48},{40,56},{80,64... | collective-permute-start | bytes 1179656 | tf_op jit(solution)/shard_map/ppermute | solution.py:940
  94.6 39.1 %all-to-all-start.1 = ((bf16[128,9,8,128]{3,2,1,0:T(8,128)(2,1)}), bf16[128,9,8,128]{3,2,1,0:T(8,128)(2,1)S(1)}, u32[]{:S(2)}, u32[]{:S(2)}) async-start(bf16[128,9,8,128]{3,2,1,0:T(8,128)(2,1)} %bitcast.30), calls=%async_computation.1 | async-start | bytes 4718592 | tf_op jit(solution)/shard_map/all_to_all | solution.py:943
  102.5 2.7 %collective-permute-start.8 = (bf16[256,768]{1,0:T(8,128)(2,1)S(1)}, bf16[256,768]{1,0:T(8,128)(2,1)S(1)}, u32[]{:S(2)}, u32[]{:S(2)}) collective-permute-start(bf16[256,768]{1,0:T(8,128)(2,1)S(1)} %get-tuple-element.107), channel_id=1, source_target_pairs={{0,8},{8,0},{16,24},{24,16},{32,40},{40,32},{48,56},{56,48},{64,72... | collective-permute-start | bytes 1179656 | tf_op jit(solution)/shard_map/ppermute | solution.py:932
  118.5 3.1 %collective-permute-start.12 = (bf16[640,8,128]{2,1,0:T(8,128)(2,1)S(1)}, bf16[640,8,128]{2,1,0:T(8,128)(2,1)S(1)}, u32[]{:S(2)}, u32[]{:S(2)}) collective-permute-start(bf16[640,8,128]{2,1,0:T(8,128)(2,1)S(1)} %get-tuple-element.140), channel_id=1, source_target_pairs={{0,8},{8,0},{16,24},{24,16},{32,40},{40,32},{48,56},{56,48},{64,72... | collective-permute-start | bytes 3932168 | tf_op jit(solution)/shard_map/ppermute | solution.py:932
  134.1 26.4 %all-to-all-start.2 = ((bf16[128,5,8,128]{3,2,1,0:T(8,128)(2,1)}), bf16[128,5,8,128]{3,2,1,0:T(8,128)(2,1)S(1)}, u32[]{:S(2)}, u32[]{:S(2)}) async-start(bf16[128,5,8,128]{3,2,1,0:T(8,128)(2,1)} %bitcast.31), calls=%async_computation.2 | async-start | bytes 2621440 | tf_op jit(solution)/shard_map/all_to_all | solution.py:943
  140.1 2.1 %collective-permute-start.13 = (bf16[4,9,8,128]{3,2,1,0:T(8,128)(2,1)S(1)}, bf16[4,9,8,128]{3,2,1,0:T(8,128)(2,1)S(1)}, u32[]{:S(2)}, u32[]{:S(2)}) collective-permute-start(bf16[4,9,8,128]{3,2,1,0:T(8,128)(2,1)S(1)} %sum_ffn.1), channel_id=1, source_target_pairs={{0,8},{8,0},{16,24},{24,16},{32,40},{40,32},{48,56},{56,48},{64,72... | collective-permute-start | bytes 221192 | tf_op jit(solution)/shard_map/ppermute | solution.py:932
  142.1 19.7 %collective-permute-start.17 = (bf16[2,4,9,8,128]{4,3,2,1,0:T(8,128)(2,1)S(1)}, bf16[2,4,9,8,128]{4,3,2,1,0:T(8,128)(2,1)S(1)}, u32[]{:S(2)}, u32[]{:S(2)}) collective-permute-start(bf16[2,4,9,8,128]{4,3,2,1,0:T(8,128)(2,1)S(1)} %pad_maximum_fusion.1), channel_id=1, source_target_pairs={{0,48},{8,120},{16,0},{24,72},{32,16},{40,88},{48,32},{56,104},{64... | collective-permute-start | bytes 442376 | tf_op jit(solution)/shard_map/ppermute | solution.py:991
  145.1 16.8 %collective-permute-start.16 = (bf16[2,4,9,8,128]{4,3,2,1,0:T(8,128)(2,1)S(1)}, bf16[2,4,9,8,128]{4,3,2,1,0:T(8,128)(2,1)S(1)}, u32[]{:S(2)}, u32[]{:S(2)}) collective-permute-start(bf16[2,4,9,8,128]{4,3,2,1,0:T(8,128)(2,1)S(1)} %pad_maximum_fusion.1), channel_id=1, source_target_pairs={{0,32},{8,104},{16,48},{24,120},{32,0},{40,72},{48,16},{56,88},{64... | collective-permute-start | bytes 442376 | tf_op jit(solution)/shard_map/ppermute | solution.py:991
  145.6 17.8 %collective-permute-start.15 = (bf16[2,4,9,8,128]{4,3,2,1,0:T(8,128)(2,1)S(1)}, bf16[2,4,9,8,128]{4,3,2,1,0:T(8,128)(2,1)S(1)}, u32[]{:S(2)}, u32[]{:S(2)}) collective-permute-start(bf16[2,4,9,8,128]{4,3,2,1,0:T(8,128)(2,1)S(1)} %pad_maximum_fusion.1), channel_id=1, source_target_pairs={{0,16},{8,88},{16,32},{24,104},{32,48},{40,120},{48,0},{56,72},{64... | collective-permute-start | bytes 442376 | tf_op jit(solution)/shard_map/ppermute | solution.py:991
  147.1 16.3 %collective-permute-start.14 = (bf16[2,4,9,8,128]{4,3,2,1,0:T(8,128)(2,1)S(1)}, bf16[2,4,9,8,128]{4,3,2,1,0:T(8,128)(2,1)S(1)}, u32[]{:S(2)}, u32[]{:S(2)}) collective-permute-start(bf16[2,4,9,8,128]{4,3,2,1,0:T(8,128)(2,1)S(1)} %pad_maximum_fusion.1), channel_id=1, source_target_pairs={{0,0},{8,72},{16,16},{24,88},{32,32},{40,104},{48,48},{56,120},{64... | collective-permute-start | bytes 442376 | tf_op jit(solution)/shard_map/ppermute | solution.py:991
  163.4 28.7 %all-to-all-start.3 = ((bf16[128,5,8,128]{3,2,1,0:T(8,128)(2,1)}), bf16[128,5,8,128]{3,2,1,0:T(8,128)(2,1)S(1)}, u32[]{:S(2)}, u32[]{:S(2)}) async-start(bf16[128,5,8,128]{3,2,1,0:T(8,128)(2,1)} %sum_rest.1), calls=%async_computation.3 | async-start | bytes 2621440 | tf_op jit(solution)/shard_map/all_to_all | solution.py:943
  171.7 2.8 %collective-permute-start.18 = (bf16[8,4,9,8,128]{4,3,2,1,0:T(8,128)(2,1)S(1)}, bf16[8,4,9,8,128]{4,3,2,1,0:T(8,128)(2,1)S(1)}, u32[]{:S(2)}, u32[]{:S(2)}) collective-permute-start(bf16[8,4,9,8,128]{4,3,2,1,0:T(8,128)(2,1)S(1)} %bitcast.25), channel_id=1, source_target_pairs={{0,8},{8,0},{16,24},{24,16},{32,40},{40,32},{48,56},{56,48},{64,72... | collective-permute-start | bytes 1769480 | tf_op jit(solution)/shard_map/ppermute | solution.py:932
  192.0 3.8 %collective-permute-start.19 = (bf16[640,8,128]{2,1,0:T(8,128)(2,1)S(1)}, bf16[640,8,128]{2,1,0:T(8,128)(2,1)S(1)}, u32[]{:S(2)}, u32[]{:S(2)}) collective-permute-start(bf16[640,8,128]{2,1,0:T(8,128)(2,1)S(1)} %bitcast.23), channel_id=1, source_target_pairs={{0,8},{8,0},{16,24},{24,16},{32,40},{40,32},{48,56},{56,48},{64,72... | collective-permute-start | bytes 3932168 | tf_op jit(solution)/shard_map/ppermute | solution.py:932

commit v7 on v6

--- a/solution.py
+++ b/solution.py
@@ -839,14 +839,17 @@
     place, own, other, g_wv, g_bv, g_conv, g_wo, g_bo, g_ga, g_sa, g_bup, g_bd, g_gf, g_sf, vecs,
     bias, line,
 ):
-    ct = pl.program_id(0)
+    step = pl.program_id(0)
 
     def write(a, b):
-        g_wv[...] = a[0:96].astype(f32).reshape(768, 128)
-        vecs[ct] = a[96].astype(f32)
-        bias[ct] = a[97].astype(f32)
-        g_wo[...] = b[0:96].astype(f32).reshape(768, 128)
-        g_conv[...] = b[96:105].astype(f32).reshape(72, 128)[0:TAPS]
+        for j in range(3):
+            cs = slice(j * 128, j * 128 + 128)
+            at = j * TALL_TILES
+            g_wv[:, cs] = a[at : at + 96].astype(f32).reshape(768, 128)
+            vecs[step * 3 + j] = a[at + 96].astype(f32)
+            bias[step * 3 + j] = a[at + 97].astype(f32)
+            g_wo[:, cs] = b[at : at + 96].astype(f32).reshape(768, 128)
+            g_conv[:, cs] = b[at + 96 : at + 105].astype(f32).reshape(72, 128)[0:TAPS]
 
     @pl.when(place[0] % 2 == 0)
     def _():
@@ -856,7 +859,7 @@
     def _():
         write(other, own)
 
-    @pl.when(ct == COLS - 1)
+    @pl.when(step == COLS // 3 - 1)
     def _():
         for j, ref in enumerate((g_bv, g_bo, g_ga, g_sa, g_bd, g_gf, g_sf)):
             for i in range(COLS):
@@ -874,20 +877,20 @@
 
 
 def final(place, own, other):
-    tile = pl.BlockSpec((TALL_TILES, 8, 128), lambda i: (i, 0, 0))
-    tall = pl.BlockSpec((768, 128), lambda i: (0, i))
+    tile = pl.BlockSpec((3 * TALL_TILES, 8, 128), lambda i: (i, 0, 0))
+    tall = pl.BlockSpec((768, 384), lambda i: (0, i))
     vec = pl.BlockSpec((WIDTH,), lambda i: (0,))
     v = shape((WIDTH,), f32)
     return pl.pallas_call(
         final_kernel,
-        grid=(COLS,),
+        grid=(COLS // 3,),
         out_shape=(
             shape((768, 768), f32), v, shape((TAPS, 768), f32), shape((768, 768), f32), v, v, v,
             shape((384,), f32), v, v, v,
         ),
         in_specs=[SMEM, tile, tile],
         out_specs=(
-            tall, vec, pl.BlockSpec((TAPS, 128), lambda i: (0, i)), tall, vec, vec, vec,
+            tall, vec, pl.BlockSpec((TAPS, 384), lambda i: (0, i)), tall, vec, vec, vec,
             pl.BlockSpec((384,), lambda i: (0,)), vec, vec, vec,
         ),
         scratch_shapes=[

time: 200 us -> 199 us (level)
  no operation moved by 1% of the time
where the time goes in v7:
time: 199 us
  waiting for transfers between devices  71.7 us (36%)
  Pallas kernels  65.1 us (33%)
  starting transfers between devices  56 us (28%)
  matrix products  3.28 us (2%)
    pallas_call x7, Pallas kernels, staged_call(): pl.pallas_call(run, out_shape=tuple((pltpu.HBM(o.shape, o.dtype) if k ==...  44.8 us
    all_to_all x4, waiting for transfers between devices, exchange(): return lax.all_to_all(x, ALL, 0, 0, tiled=True)  35.9 us
    all_to_all x4, starting transfers between devices, exchange(): return lax.all_to_all(x, ALL, 0, 0, tiled=True)  34 us
    ppermute x12, waiting for transfers between devices, swap(): return lax.ppermute(x, 'dp', [(i, i ^ 1) for i in range(n_dp)])  13.7 us
    ppermute x2, waiting for transfers between devices, away(): return lax.ppermute(x, 'dp', pairs)  12.6 us
    ppermute x12, starting transfers between devices, swap(): return lax.ppermute(x, 'dp', [(i, i ^ 1) for i in range(n_dp)])  10.1 us
    ppermute x2, waiting for transfers between devices, home(): return lax.ppermute(x, 'dp', pairs)  7.94 us
    pallas_call x2, Pallas kernels, staged_call(): pl.pallas_call(kernel, out_shape=tuple((o for _, o in outs)), in_specs=[s...  7.6 us
  transfers between devices with their start and end apart: 24, of which 16 were waited for; matrix products, arithmetic and copies ran while one was open for 2% of the time, Pallas kernels for 25%

profile of v7, /device:TPU:1, one launch (start us, length us, event | category | flops | bytes accessed | tf_op | source)
XLA Modules:
  0.0 199.0 jit_solution(5926398266546765868)
XLA Ops:
  0.7 3.6 %prep.1 = bf16[4,4,8,10,8,128]{5,4,3,2,1,0:T(8,128)(2,1)} custom-call(s32[2]{0:T(128)S(1)} %pad_add_fusion.place.refs_0_, bf16[768,384]{1,0:T(8,128)(2,1)} %up_ref.1, bf16[384,768]{1,0:T(8,128)(2,1)} %down_ref.1, bf16[384]{0:T(512)(128)(2,1)} %bias_hbm.1), custom_call_target="tpu_custom_call" | custom-call | tf_op jit(solution)/shard_map/prep/pallas_call | solution.py:246
  4.4 11.9 %all-to-all-start = ((bf16[128,10,8,128]{3,2,1,0:T(8,128)(2,1)}), bf16[128,10,8,128]{3,2,1,0:T(8,128)(2,1)}, u32[]{:S(2)}, u32[]{:S(2)}) async-start(bf16[128,10,8,128]{3,2,1,0:T(8,128)(2,1)} %bitcast.29), calls=%async_computation | async-start | bytes 5242880 | tf_op jit(solution)/shard_map/all_to_all | solution.py:946
  16.5 18.5 %attend.1 = (f32[256,768]{1,0:T(8,128)}, f32[256,128]{1,0:T(8,128)}, bf16[256,768]{1,0:T(8,128)(2,1)S(1)}, bf16[256,768]{1,0:T(8,128)(2,1)}, bf16[12,256,256]{2,...) custom-call(s32[1,4]{1,0:T(1,128)S(1)} %copy-done.4, ...), custom_call_target="tpu_custom_call" | custom-call | tf_op jit(solution)/shard_map/attend/pallas_call | solution.py:176
  34.9 2.7 %collective-permute-start.1 = (bf16[256,768]{1,0:T(8,128)(2,1)S(1)}, bf16[256,768]{1,0:T(8,128)(2,1)S(1)}, u32[]{:S(2)}, u32[]{:S(2)}) collective-permute-start(bf16[256,768]{1,0:T(8,128)(2,1)S(1)} %get-tuple-element.91.own), channel_id=1, source_target_pairs={{0,16},{8,56},{16,32},{24,8},{32,48},{40,24},{48,0},{56,40},{64,80... | collective-permute-start | bytes 1179656 | tf_op jit(solution)/shard_map/ppermute | solution.py:939
  37.7 12.6 %collective-permute-done.1.own = bf16[256,768]{1,0:T(8,128)(2,1)S(1)} collective-permute-done((bf16[256,768]{1,0:T(8,128)(2,1)S(1)}, bf16[256,768]{1,0:T(8,128)(2,1)S(1)}, u32[]{:S(2)}, u32[]{:S(2)}) %collective-permute-start.1) | collective-permute-done | bytes 393248 | tf_op jit(solution)/shard_map/ppermute | solution.py:939
  50.3 1.9 collective-permute-start.2
  52.2 1.9 unpack.1
  54.2 3.8 %ffn.2 = (bf16[512,768]{1,0:T(8,128)(2,1)S(1)}, bf16[512,768]{1,0:T(8,128)(2,1)S(1)}, f32[256,768]{1,0:T(8,128)S(1)}, bf16[256,768]{1,0:T(8,128)(2,1)S(1)}, bf16[512,768]{1,0:T(8,128)(2,1)S(1)}) custom-call(bf16[256,768]{1,0:T(8,128)(2,1)S(1)} %collective-permute-done.1.own, bf16[256,768]{1,0:T(8,128)(2,1)S(1)} %collective-permute-done.2.sib, ...), custom_call_target="tpu_custom_call" | custom-call | tf_op jit(solution)/shard_map/ffn/pallas_call | solution.py:140
  58.6 1.2 collective-permute-done.3.got
  60.4 3.8 %ffn.3 = (bf16[512,768]{1,0:T(8,128)(2,1)S(1)}, bf16[512,768]{1,0:T(8,128)(2,1)S(1)}, f32[256,768]{1,0:T(8,128)S(1)}, bf16[256,768]{1,0:T(8,128)(2,1)S(1)}, bf16[512,768]{1,0:T(8,128)(2,1)S(1)}) custom-call(bf16[256,768]{1,0:T(8,128)(2,1)S(1)} %get-tuple-element.91.own, bf16[256,768]{1,0:T(8,128)(2,1)S(1)} %collective-permute-done.sib, ...), custom_call_target="tpu_custom_call" | custom-call | tf_op jit(solution)/shard_map/ffn/pallas_call | solution.py:140
  64.2 3.7 %collective-permute-done.4.refs_3_.far = bf16[256,768]{1,0:T(8,128)(2,1)S(1)} collective-permute-done((bf16[256,768]{1,0:T(8,128)(2,1)S(1)}, bf16[256,768]{1,0:T(8,128)(2,1)S(1)}, u32[]{:S(2)}, u32[]{:S(2)}) %collective-permute-start.4) | collective-permute-done | bytes 393248 | tf_op jit(solution)/shard_map/ppermute | solution.py:943
  67.9 1.6 collective-permute-done.5.refs_2_.near
  70.4 1.8 collective-permute-start.7
  72.3 1.8 outputs.1
  74.1 4.1 %back_near.1 = (f32[256,768]{1,0:T(8,128)}, bf16[256,768]{1,0:T(8,128)(2,1)S(1)}, bf16[512,768]{1,0:T(8,128)(2,1)S(1)}, bf16[512,768]{1,0:T(8,128)(2,1)S(1)}, f32[8,768]{1,0:T(8,128)}) custom-call(bf16[256,768]{1,0:T(8,128)(2,1)S(1)} %middle.1.refs_0_, bf16[256,768]{1,0:T(8,128)(2,1)S(1)} %collective-permute-done.6.refs_1_, ...), custom_call_target="tpu_custom_call" | custom-call | tf_op jit(solution)/shard_map/back_near/pallas_call | solution.py:176
  78.2 1.6 collective-permute-start.9
  79.8 1.3 collective-permute-done.9.refs_1_
  81.1 3.4 %back_far.1 = (f32[256,768]{1,0:T(8,128)S(1)}, bf16[256,768]{1,0:T(8,128)(2,1)S(1)}, bf16[512,768]{1,0:T(8,128)(2,1)S(1)}, bf16[512,768]{1,0:T(8,128)(2,1)S(1)}, f32[8,768]{1,0:T(8,128)}) custom-call(bf16[256,768]{1,0:T(8,128)(2,1)S(1)} %collective-permute-done.7.refs_0_, bf16[256,768]{1,0:T(8,128)(2,1)S(1)} %collective-permute-done.9.refs_1_, ...), custom_call_target="tpu_custom_call" | custom-call | tf_op jit(solution)/shard_map/back_far/pallas_call | solution.py:176
  85.0 0.8 fusion
  85.8 0.8 fusion.1
  86.7 0.8 add_convert_fusion.1.refs_1_
  87.6 0.8 add_convert_fusion.2.refs_0_
  88.4 1.9 pack.1
  90.3 4.3 %collective-permute-done.11.refs_3_ = bf16[256,768]{1,0:T(8,128)(2,1)S(1)} collective-permute-done((bf16[256,768]{1,0:T(8,128)(2,1)S(1)}, bf16[256,768]{1,0:T(8,128)(2,1)S(1)}, u32[]{:S(2)}, u32[]{:S(2)}) %collective-permute-start.11) | collective-permute-done | bytes 393248 | tf_op jit(solution)/shard_map/ppermute | solution.py:943
  94.6 7.9 %all-to-all-start.1 = ((bf16[128,9,8,128]{3,2,1,0:T(8,128)(2,1)}), bf16[128,9,8,128]{3,2,1,0:T(8,128)(2,1)S(1)}, u32[]{:S(2)}, u32[]{:S(2)}) async-start(bf16[128,9,8,128]{3,2,1,0:T(8,128)(2,1)} %bitcast.30), calls=%async_computation.1 | async-start | bytes 4718592 | tf_op jit(solution)/shard_map/all_to_all | solution.py:946
  102.5 1.4 collective-permute-start.8
  103.9 1.3 collective-permute-done.8.refs_2_
  105.2 13.3 %attend_back.1 = (f32[256,768]{1,0:T(8,128)}, bf16[640,8,128]{2,1,0:T(8,128)(2,1)S(1)}, bf16[640,8,128]{2,1,0:T(8,128)(2,1)S(1)}) custom-call(s32[2]{0:T(128)S(1)} %pad_add_fusion.place.refs_0_, f32[256,768]{1,0:T(8,128)} %get-tuple-element.104.refs_1_, bf16[256,768]{1,0:T(8,128)(2,1)S(1)} %collective-permute-done.8.refs_2_, ...), custom_call_target="tpu_custom_call" | custom-call | tf_op jit(solution)/shard_map/attend_back/pallas_call | solution.py:176
  119.0 2.7 %collective-permute-done.12 = bf16[640,8,128]{2,1,0:T(8,128)(2,1)S(1)} collective-permute-done((bf16[640,8,128]{2,1,0:T(8,128)(2,1)S(1)}, bf16[640,8,128]{2,1,0:T(8,128)(2,1)S(1)}, u32[]{:S(2)}, u32[]{:S(2)}) %collective-permute-start.12) | collective-permute-done | bytes 1310752 | tf_op jit(solution)/shard_map/ppermute | solution.py:935
  121.7 1.4 add_convert_fusion
  123.1 10.6 %all-to-all-done.1.got = bf16[128,9,8,128]{3,2,1,0:T(8,128)(2,1)S(1)} async-done(((bf16[128,9,8,128]{3,2,1,0:T(8,128)(2,1)}), bf16[128,9,8,128]{3,2,1,0:T(8,128)(2,1)S(1)}, u32[]{:S(2)}, u32[]{:S(2)}) %all-to-all-start.1) | async-done | bytes 2359328 | tf_op jit(solution)/shard_map/all_to_all | solution.py:946
  134.1 5.9 %all-to-all-start.2 = ((bf16[128,5,8,128]{3,2,1,0:T(8,128)(2,1)}), bf16[128,5,8,128]{3,2,1,0:T(8,128)(2,1)S(1)}, u32[]{:S(2)}, u32[]{:S(2)}) async-start(bf16[128,5,8,128]{3,2,1,0:T(8,128)(2,1)} %bitcast.31), calls=%async_computation.2 | async-start | bytes 2621440 | tf_op jit(solution)/shard_map/all_to_all | solution.py:946
  140.1 1.1 collective-permute-start.13
  141.2 0.9 collective-permute-done.13
  142.1 2.9 %collective-permute-start.17 = (bf16[2,4,9,8,128]{4,3,2,1,0:T(8,128)(2,1)S(1)}, bf16[2,4,9,8,128]{4,3,2,1,0:T(8,128)(2,1)S(1)}, u32[]{:S(2)}, u32[]{:S(2)}) collective-permute-start(bf16[2,4,9,8,128]{4,3,2,1,0:T(8,128)(2,1)S(1)} %pad_maximum_fusion.1), channel_id=1, source_target_pairs={{0,48},{8,120},{16,0},{24,72},{32,16},{40,88},{48,32},{56,104},{64... | collective-permute-start | bytes 442376 | tf_op jit(solution)/shard_map/ppermute | solution.py:994
  145.6 1.5 collective-permute-start.15
  147.1 2.2 %collective-permute-start.14 = (bf16[2,4,9,8,128]{4,3,2,1,0:T(8,128)(2,1)S(1)}, bf16[2,4,9,8,128]{4,3,2,1,0:T(8,128)(2,1)S(1)}, u32[]{:S(2)}, u32[]{:S(2)}) collective-permute-start(bf16[2,4,9,8,128]{4,3,2,1,0:T(8,128)(2,1)S(1)} %pad_maximum_fusion.1), channel_id=1, source_target_pairs={{0,0},{8,72},{16,16},{24,88},{32,32},{40,104},{48,48},{56,120},{64... | collective-permute-start | bytes 442376 | tf_op jit(solution)/shard_map/ppermute | solution.py:994
  149.2 11.3 %all-to-all-done.2.got = bf16[128,5,8,128]{3,2,1,0:T(8,128)(2,1)S(1)} async-done(((bf16[128,5,8,128]{3,2,1,0:T(8,128)(2,1)}), bf16[128,5,8,128]{3,2,1,0:T(8,128)(2,1)S(1)}, u32[]{:S(2)}, u32[]{:S(2)}) %all-to-all-start.2) | async-done | bytes 1310752 | tf_op jit(solution)/shard_map/all_to_all | solution.py:946
  160.5 1.3 sum_rest.1
  161.9 1.5 collective-permute-done.15
  163.4 8.2 %all-to-all-start.3 = ((bf16[128,5,8,128]{3,2,1,0:T(8,128)(2,1)}), bf16[128,5,8,128]{3,2,1,0:T(8,128)(2,1)S(1)}, u32[]{:S(2)}, u32[]{:S(2)}) async-start(bf16[128,5,8,128]{3,2,1,0:T(8,128)(2,1)} %sum_rest.1), calls=%async_computation.3 | async-start | bytes 2621440 | tf_op jit(solution)/shard_map/all_to_all | solution.py:946
  171.7 1.1 collective-permute-start.18
  172.8 1.6 collective-permute-done.18.ffn_oth
  174.5 3.6 %final_ffn.1 = (f32[768,384]{1,0:T(8,128)}, f32[384,768]{1,0:T(8,128)}) custom-call(s32[2]{0:T(128)S(1)} %pad_add_fusion.place.refs_0_, bf16[8,4,9,8,128]{4,3,2,1,0:T(8,128)(2,1)S(1)} %bitcast.26, bf16[8,4,9,8,128]{4,3,2,1,0:T(8,128)(2,1)S(1)} %collective-permute-done.18.ffn_oth), custom_call_target="tpu_custom_call" | custom-call | tf_op jit(solution)/shard_map/final_ffn/pallas_call | solution.py:823
  178.0 14.0 %all-to-all-done.3 = bf16[128,5,8,128]{3,2,1,0:T(8,128)(2,1)S(1)} async-done(((bf16[128,5,8,128]{3,2,1,0:T(8,128)(2,1)}), bf16[128,5,8,128]{3,2,1,0:T(8,128)(2,1)S(1)}, u32[]{:S(2)}, u32[]{:S(2)}) %all-to-all-start.3) | async-done | bytes 1310752 | tf_op jit(solution)/shard_map/all_to_all | solution.py:946
  192.0 1.2 collective-permute-start.19
  193.2 2.7 %collective-permute-done.19.other = bf16[640,8,128]{2,1,0:T(8,128)(2,1)S(1)} collective-permute-done((bf16[640,8,128]{2,1,0:T(8,128)(2,1)S(1)}, bf16[640,8,128]{2,1,0:T(8,128)(2,1)S(1)}, u32[]{:S(2)}, u32[]{:S(2)}) %collective-permute-start.19) | collective-permute-done | bytes 1310752 | tf_op jit(solution)/shard_map/ppermute | solution.py:935
  195.9 3.0 %final.1 = (f32[768,768]{1,0:T(8,128)}, f32[768]{0:T(1024)}, f32[65,768]{1,0:T(8,128)}, f32[768,768]{1,0:T(8,128)}, f32[768]{0:T(1024)}, /*index=5*/f32[768]{0:T...) custom-call(s32[2]{0:T(128)S(1)} %pad_add_fusion.place.refs_0_, ...), custom_call_target="tpu_custom_call" | custom-call | tf_op jit(solution)/shard_map/final/pallas_call | solution.py:884
  (56 shorter events, 4.3 us)
Async XLA Ops:
  4.3 12.0 %copy-start.5 = (bf16[768]{0:T(1024)(128)(2,1)S(1)}, bf16[768]{0:T(1024)(128)(2,1)}, u32[]{:S(2)}) copy-start(bf16[768]{0:T(1024)(128)(2,1)} %param.25) | copy-start | bytes 4612
  4.3 12.0 %copy-start.6 = (bf16[768]{0:T(1024)(128)(2,1)S(1)}, bf16[768]{0:T(1024)(128)(2,1)}, u32[]{:S(2)}) copy-start(bf16[768]{0:T(1024)(128)(2,1)} %param.26) | copy-start | bytes 4612
  4.4 12.0 %copy-start.7 = (bf16[768]{0:T(1024)(128)(2,1)S(1)}, bf16[768]{0:T(1024)(128)(2,1)}, u32[]{:S(2)}) copy-start(bf16[768]{0:T(1024)(128)(2,1)} %param.21) | copy-start | bytes 4612
  4.4 12.0 %copy-start.8 = (bf16[768]{0:T(1024)(128)(2,1)S(1)}, bf16[768]{0:T(1024)(128)(2,1)}, u32[]{:S(2)}) copy-start(bf16[768]{0:T(1024)(128)(2,1)} %param.24) | copy-start | bytes 4612
  4.4 12.0 %copy-start.2 = (bf16[65,768]{1,0:T(8,128)(2,1)S(1)}, bf16[65,768]{1,0:T(8,128)(2,1)}, u32[]{:S(2)}) copy-start(bf16[65,768]{1,0:T(8,128)(2,1)} %refs_4_.1) | copy-start | bytes 299524
  4.4 12.0 %copy-start.3 = (s32[256]{0:T(256)S(1)}, s32[256]{0:T(256)}, u32[]{:S(2)}) copy-start(s32[256]{0:T(256)} %param.35) | copy-start | bytes 3076
  4.4 12.0 %copy-start.4 = (s32[1,4]{1,0:T(1,128)S(1)}, s32[1,4]{1,0:T(1,128)}, u32[]{:S(2)}) copy-start(s32[1,4]{1,0:T(1,128)} %refs_0_.1) | copy-start | bytes 52
  4.4 47.8 %all-to-all-start = ((bf16[128,10,8,128]{3,2,1,0:T(8,128)(2,1)}), bf16[128,10,8,128]{3,2,1,0:T(8,128)(2,1)}, u32[]{:S(2)}, u32[]{:S(2)}) async-start(bf16[128,10,8,128]{3,2,1,0:T(8,128)(2,1)} %bitcast.29), calls=%async_computation | async-start | bytes 5242880 | tf_op jit(solution)/shard_map/all_to_all | solution.py:946
  34.9 15.4 %collective-permute-start.1 = (bf16[256,768]{1,0:T(8,128)(2,1)S(1)}, bf16[256,768]{1,0:T(8,128)(2,1)S(1)}, u32[]{:S(2)}, u32[]{:S(2)}) collective-permute-start(bf16[256,768]{1,0:T(8,128)(2,1)S(1)} %get-tuple-element.91.own), channel_id=1, source_target_pairs={{0,16},{8,56},{16,32},{24,8},{32,48},{40,24},{48,0},{56,40},{64,80... | collective-permute-start | bytes 1179656 | tf_op jit(solution)/shard_map/ppermute | solution.py:939
  50.3 3.9 %collective-permute-start.2 = (bf16[256,768]{1,0:T(8,128)(2,1)S(1)}, bf16[256,768]{1,0:T(8,128)(2,1)S(1)}, u32[]{:S(2)}, u32[]{:S(2)}) collective-permute-start(bf16[256,768]{1,0:T(8,128)(2,1)S(1)} %collective-permute-done.1.own), channel_id=1, source_target_pairs={{0,8},{8,0},{16,24},{24,16},{32,40},{40,32},{48,56},{56,48},{64,72... | collective-permute-start | bytes 1179656 | tf_op jit(solution)/shard_map/ppermute | solution.py:935
  58.0 1.8 collective-permute-start.3
  58.1 2.3 %collective-permute-start = (bf16[256,768]{1,0:T(8,128)(2,1)S(1)}, bf16[256,768]{1,0:T(8,128)(2,1)S(1)}, u32[]{:S(2)}, u32[]{:S(2)}) collective-permute-start(bf16[256,768]{1,0:T(8,128)(2,1)S(1)} %get-tuple-element.91.own), channel_id=1, source_target_pairs={{0,8},{8,0},{16,24},{24,16},{32,40},{40,32},{48,56},{56,48},{64,72... | collective-permute-start | bytes 1179656 | tf_op jit(solution)/shard_map/ppermute | solution.py:935
  59.9 8.0 %copy-start.9 = (bf16[768]{0:T(1024)(128)(2,1)S(1)}, bf16[768]{0:T(1024)(128)(2,1)}, u32[]{:S(2)}) copy-start(bf16[768]{0:T(1024)(128)(2,1)} %param.30) | copy-start | bytes 4612
  59.9 8.0 %copy-start.10 = (bf16[768]{0:T(1024)(128)(2,1)S(1)}, bf16[768]{0:T(1024)(128)(2,1)}, u32[]{:S(2)}) copy-start(bf16[768]{0:T(1024)(128)(2,1)} %param.31) | copy-start | bytes 4612
  59.9 9.7 %copy-start = (f32[256,768]{1,0:T(8,128)S(1)}, f32[256,768]{1,0:T(8,128)}, u32[]{:S(2)}) copy-start(f32[256,768]{1,0:T(8,128)} %get-tuple-element.90.refs_0_.n1.refs_5_) | copy-start | bytes 2359300
  59.9 9.6 %copy-start.1 = (bf16[256,768]{1,0:T(8,128)(2,1)S(1)}, bf16[256,768]{1,0:T(8,128)(2,1)}, u32[]{:S(2)}) copy-start(bf16[256,768]{1,0:T(8,128)(2,1)} %og.1) | copy-start | bytes 1179652
  59.9 7.9 %collective-permute-start.4 = (bf16[256,768]{1,0:T(8,128)(2,1)S(1)}, bf16[256,768]{1,0:T(8,128)(2,1)S(1)}, u32[]{:S(2)}, u32[]{:S(2)}) collective-permute-start(bf16[256,768]{1,0:T(8,128)(2,1)S(1)} %combine.2), channel_id=1, source_target_pairs={{16,0},{56,8},{32,16},{8,24},{48,32},{24,40},{0,48},{40,56},{80,64... | collective-permute-start | bytes 1179656 | tf_op jit(solution)/shard_map/ppermute | solution.py:943
  67.8 1.7 collective-permute-start.5
  69.5 2.7 %copy-start.11 = (bf16[768]{0:T(1024)(128)(2,1)S(1)}, bf16[768]{0:T(1024)(128)(2,1)}, u32[]{:S(2)}) copy-start(bf16[768]{0:T(1024)(128)(2,1)} %param.32) | copy-start | bytes 4612
  70.2 3.9 %collective-permute-start.6 = (bf16[256,768]{1,0:T(8,128)(2,1)S(1)}, bf16[256,768]{1,0:T(8,128)(2,1)S(1)}, u32[]{:S(2)}, u32[]{:S(2)}) collective-permute-start(bf16[256,768]{1,0:T(8,128)(2,1)S(1)} %middle.1.refs_0_), channel_id=1, source_target_pairs={{0,8},{8,0},{16,24},{24,16},{32,40},{40,32},{48,56},{56,48},{64,72... | collective-permute-start | bytes 1179656 | tf_op jit(solution)/shard_map/ppermute | solution.py:935
  70.4 7.8 %collective-permute-start.7 = (bf16[256,768]{1,0:T(8,128)(2,1)S(1)}, bf16[256,768]{1,0:T(8,128)(2,1)S(1)}, u32[]{:S(2)}, u32[]{:S(2)}) collective-permute-start(bf16[256,768]{1,0:T(8,128)(2,1)S(1)} %middle.1.refs_0_), channel_id=1, source_target_pairs={{0,16},{8,56},{16,32},{24,8},{32,48},{40,24},{48,0},{56,40},{64,80... | collective-permute-start | bytes 1179656 | tf_op jit(solution)/shard_map/ppermute | solution.py:939
  78.2 2.9 %collective-permute-start.9 = (bf16[256,768]{1,0:T(8,128)(2,1)S(1)}, bf16[256,768]{1,0:T(8,128)(2,1)S(1)}, u32[]{:S(2)}, u32[]{:S(2)}) collective-permute-start(bf16[256,768]{1,0:T(8,128)(2,1)S(1)} %collective-permute-done.7.refs_0_), channel_id=1, source_target_pairs={{0,8},{8,0},{16,24},{24,16},{32,40},{40,32},{48,56},{56,48},{64,72... | collective-permute-start | bytes 1179656 | tf_op jit(solution)/shard_map/ppermute | solution.py:935
  84.5 2.1 %collective-permute-start.10 = (bf16[256,768]{1,0:T(8,128)(2,1)S(1)}, bf16[256,768]{1,0:T(8,128)(2,1)S(1)}, u32[]{:S(2)}, u32[]{:S(2)}) collective-permute-start(bf16[256,768]{1,0:T(8,128)(2,1)S(1)} %get-tuple-element.114), channel_id=1, source_target_pairs={{0,8},{8,0},{16,24},{24,16},{32,40},{40,32},{48,56},{56,48},{64,72... | collective-permute-start | bytes 1179656 | tf_op jit(solution)/shard_map/ppermute | solution.py:935
  86.7 7.9 %collective-permute-start.11 = (bf16[256,768]{1,0:T(8,128)(2,1)S(1)}, bf16[256,768]{1,0:T(8,128)(2,1)S(1)}, u32[]{:S(2)}, u32[]{:S(2)}) collective-permute-start(bf16[256,768]{1,0:T(8,128)(2,1)S(1)} %combine.3), channel_id=1, source_target_pairs={{16,0},{56,8},{32,16},{8,24},{48,32},{24,40},{0,48},{40,56},{80,64... | collective-permute-start | bytes 1179656 | tf_op jit(solution)/shard_map/ppermute | solution.py:943
  94.6 39.1 %all-to-all-start.1 = ((bf16[128,9,8,128]{3,2,1,0:T(8,128)(2,1)}), bf16[128,9,8,128]{3,2,1,0:T(8,128)(2,1)S(1)}, u32[]{:S(2)}, u32[]{:S(2)}) async-start(bf16[128,9,8,128]{3,2,1,0:T(8,128)(2,1)} %bitcast.30), calls=%async_computation.1 | async-start | bytes 4718592 | tf_op jit(solution)/shard_map/all_to_all | solution.py:946
  102.5 2.7 %collective-permute-start.8 = (bf16[256,768]{1,0:T(8,128)(2,1)S(1)}, bf16[256,768]{1,0:T(8,128)(2,1)S(1)}, u32[]{:S(2)}, u32[]{:S(2)}) collective-permute-start(bf16[256,768]{1,0:T(8,128)(2,1)S(1)} %get-tuple-element.107), channel_id=1, source_target_pairs={{0,8},{8,0},{16,24},{24,16},{32,40},{40,32},{48,56},{56,48},{64,72... | collective-permute-start | bytes 1179656 | tf_op jit(solution)/shard_map/ppermute | solution.py:935
  118.5 3.1 %collective-permute-start.12 = (bf16[640,8,128]{2,1,0:T(8,128)(2,1)S(1)}, bf16[640,8,128]{2,1,0:T(8,128)(2,1)S(1)}, u32[]{:S(2)}, u32[]{:S(2)}) collective-permute-start(bf16[640,8,128]{2,1,0:T(8,128)(2,1)S(1)} %get-tuple-element.140), channel_id=1, source_target_pairs={{0,8},{8,0},{16,24},{24,16},{32,40},{40,32},{48,56},{56,48},{64,72... | collective-permute-start | bytes 3932168 | tf_op jit(solution)/shard_map/ppermute | solution.py:935
  134.1 26.4 %all-to-all-start.2 = ((bf16[128,5,8,128]{3,2,1,0:T(8,128)(2,1)}), bf16[128,5,8,128]{3,2,1,0:T(8,128)(2,1)S(1)}, u32[]{:S(2)}, u32[]{:S(2)}) async-start(bf16[128,5,8,128]{3,2,1,0:T(8,128)(2,1)} %bitcast.31), calls=%async_computation.2 | async-start | bytes 2621440 | tf_op jit(solution)/shard_map/all_to_all | solution.py:946
  140.1 2.1 %collective-permute-start.13 = (bf16[4,9,8,128]{3,2,1,0:T(8,128)(2,1)S(1)}, bf16[4,9,8,128]{3,2,1,0:T(8,128)(2,1)S(1)}, u32[]{:S(2)}, u32[]{:S(2)}) collective-permute-start(bf16[4,9,8,128]{3,2,1,0:T(8,128)(2,1)S(1)} %sum_ffn.1), channel_id=1, source_target_pairs={{0,8},{8,0},{16,24},{24,16},{32,40},{40,32},{48,56},{56,48},{64,72... | collective-permute-start | bytes 221192 | tf_op jit(solution)/shard_map/ppermute | solution.py:935
  142.1 19.7 %collective-permute-start.17 = (bf16[2,4,9,8,128]{4,3,2,1,0:T(8,128)(2,1)S(1)}, bf16[2,4,9,8,128]{4,3,2,1,0:T(8,128)(2,1)S(1)}, u32[]{:S(2)}, u32[]{:S(2)}) collective-permute-start(bf16[2,4,9,8,128]{4,3,2,1,0:T(8,128)(2,1)S(1)} %pad_maximum_fusion.1), channel_id=1, source_target_pairs={{0,48},{8,120},{16,0},{24,72},{32,16},{40,88},{48,32},{56,104},{64... | collective-permute-start | bytes 442376 | tf_op jit(solution)/shard_map/ppermute | solution.py:994
  145.1 16.8 %collective-permute-start.16 = (bf16[2,4,9,8,128]{4,3,2,1,0:T(8,128)(2,1)S(1)}, bf16[2,4,9,8,128]{4,3,2,1,0:T(8,128)(2,1)S(1)}, u32[]{:S(2)}, u32[]{:S(2)}) collective-permute-start(bf16[2,4,9,8,128]{4,3,2,1,0:T(8,128)(2,1)S(1)} %pad_maximum_fusion.1), channel_id=1, source_target_pairs={{0,32},{8,104},{16,48},{24,120},{32,0},{40,72},{48,16},{56,88},{64... | collective-permute-start | bytes 442376 | tf_op jit(solution)/shard_map/ppermute | solution.py:994
  145.6 17.8 %collective-permute-start.15 = (bf16[2,4,9,8,128]{4,3,2,1,0:T(8,128)(2,1)S(1)}, bf16[2,4,9,8,128]{4,3,2,1,0:T(8,128)(2,1)S(1)}, u32[]{:S(2)}, u32[]{:S(2)}) collective-permute-start(bf16[2,4,9,8,128]{4,3,2,1,0:T(8,128)(2,1)S(1)} %pad_maximum_fusion.1), channel_id=1, source_target_pairs={{0,16},{8,88},{16,32},{24,104},{32,48},{40,120},{48,0},{56,72},{64... | collective-permute-start | bytes 442376 | tf_op jit(solution)/shard_map/ppermute | solution.py:994
  147.1 16.3 %collective-permute-start.14 = (bf16[2,4,9,8,128]{4,3,2,1,0:T(8,128)(2,1)S(1)}, bf16[2,4,9,8,128]{4,3,2,1,0:T(8,128)(2,1)S(1)}, u32[]{:S(2)}, u32[]{:S(2)}) collective-permute-start(bf16[2,4,9,8,128]{4,3,2,1,0:T(8,128)(2,1)S(1)} %pad_maximum_fusion.1), channel_id=1, source_target_pairs={{0,0},{8,72},{16,16},{24,88},{32,32},{40,104},{48,48},{56,120},{64... | collective-permute-start | bytes 442376 | tf_op jit(solution)/shard_map/ppermute | solution.py:994
  163.4 28.7 %all-to-all-start.3 = ((bf16[128,5,8,128]{3,2,1,0:T(8,128)(2,1)}), bf16[128,5,8,128]{3,2,1,0:T(8,128)(2,1)S(1)}, u32[]{:S(2)}, u32[]{:S(2)}) async-start(bf16[128,5,8,128]{3,2,1,0:T(8,128)(2,1)} %sum_rest.1), calls=%async_computation.3 | async-start | bytes 2621440 | tf_op jit(solution)/shard_map/all_to_all | solution.py:946
  171.7 2.8 %collective-permute-start.18 = (bf16[8,4,9,8,128]{4,3,2,1,0:T(8,128)(2,1)S(1)}, bf16[8,4,9,8,128]{4,3,2,1,0:T(8,128)(2,1)S(1)}, u32[]{:S(2)}, u32[]{:S(2)}) collective-permute-start(bf16[8,4,9,8,128]{4,3,2,1,0:T(8,128)(2,1)S(1)} %bitcast.25), channel_id=1, source_target_pairs={{0,8},{8,0},{16,24},{24,16},{32,40},{40,32},{48,56},{56,48},{64,72... | collective-permute-start | bytes 1769480 | tf_op jit(solution)/shard_map/ppermute | solution.py:935
  192.0 3.8 %collective-permute-start.19 = (bf16[640,8,128]{2,1,0:T(8,128)(2,1)S(1)}, bf16[640,8,128]{2,1,0:T(8,128)(2,1)S(1)}, u32[]{:S(2)}, u32[]{:S(2)}) collective-permute-start(bf16[640,8,128]{2,1,0:T(8,128)(2,1)S(1)} %bitcast.23), channel_id=1, source_target_pairs={{0,8},{8,0},{16,24},{24,16},{32,40},{40,32},{48,56},{56,48},{64,72... | collective-permute-start | bytes 3932168 | tf_op jit(solution)/shard_map/ppermute | solution.py:935

commit v8 on v7

--- a/solution.py
+++ b/solution.py
@@ -483,7 +483,7 @@
         acc[...] += dot(a, wd[hs, :])
         return carry
 
-    lax.fori_loop(0, HIDDEN // 256, block, 0)
+    lax.fori_loop(0, HIDDEN // 256, block, 0, unroll=True)
 
 
 def unpack_kernel(w, wu, wd):
@@ -592,7 +592,7 @@
         acc[...] += dot(u, wu[hs, 0:WIDTH])
         return carry
 
-    lax.fori_loop(0, HIDDEN // 256, block, 0)
+    lax.fori_loop(0, HIDDEN // 256, block, 0, unroll=True)
 
 
 def back_ffn_kernel(own, sib, wu, wd, slope, first_own, first_sib, g, u, bias, acc):

time: 199 us -> 197 us (0.990)
  Pallas kernels: 65.1 us -> 59.8 us
  waiting for transfers between devices: 71.7 us -> 73.9 us
    pallas_call x2, Pallas kernels: 7.6 us -> 4.81 us  [staged_call(): pl.pallas_call(kernel, out_shape=tuple((o for _, o in outs)), in_specs=[s...]
    pallas_call x7, Pallas kernels: 44.8 us -> 42.3 us  [staged_call(): pl.pallas_call(run, out_shape=tuple((pltpu.HBM(o.shape, o.dtype) if k ==...]
  transfers between devices with their start and end apart: 24 -> 24, of which waited for: 16 -> 17; matrix products, arithmetic and copies ran while one was open for 2% -> 2% of each run, Pallas kernels for 25% -> 24%
where the time goes in v8:
time: 197 us
  waiting for transfers between devices  73.9 us (38%)
  Pallas kernels  59.8 us (30%)
  starting transfers between devices  56.8 us (29%)
  matrix products  3.28 us (2%)
    pallas_call x7, Pallas kernels, staged_call(): pl.pallas_call(run, out_shape=tuple((pltpu.HBM(o.shape, o.dtype) if k ==...  42.3 us
    all_to_all x4, waiting for transfers between devices, exchange(): return lax.all_to_all(x, ALL, 0, 0, tiled=True)  36.1 us
    all_to_all x4, starting transfers between devices, exchange(): return lax.all_to_all(x, ALL, 0, 0, tiled=True)  34 us
    ppermute x12, waiting for transfers between devices, swap(): return lax.ppermute(x, 'dp', [(i, i ^ 1) for i in range(n_dp)])  13.5 us
    ppermute x2, waiting for transfers between devices, away(): return lax.ppermute(x, 'dp', pairs)  13.2 us
    ppermute x12, starting transfers between devices, swap(): return lax.ppermute(x, 'dp', [(i, i ^ 1) for i in range(n_dp)])  10.7 us
    ppermute x2, waiting for transfers between devices, home(): return lax.ppermute(x, 'dp', pairs)  9.52 us
    ppermute x4, starting transfers between devices, body(): around.append(lax.ppermute(both, 'dp', pairs))  7.1 us
  transfers between devices with their start and end apart: 24, of which 17 were waited for; matrix products, arithmetic and copies ran while one was open for 2% of the time, Pallas kernels for 24%

profile of v8, /device:TPU:1, one launch (start us, length us, event | category | flops | bytes accessed | tf_op | source)
XLA Modules:
  0.0 196.6 jit_solution(8761931578979098997)
XLA Ops:
  0.7 3.6 %prep.1 = bf16[4,4,8,10,8,128]{5,4,3,2,1,0:T(8,128)(2,1)} custom-call(s32[2]{0:T(128)S(1)} %pad_add_fusion.place.refs_0_, bf16[768,384]{1,0:T(8,128)(2,1)} %up_ref.1, bf16[384,768]{1,0:T(8,128)(2,1)} %down_ref.1, bf16[384]{0:T(512)(128)(2,1)} %bias_hbm.1), custom_call_target="tpu_custom_call" | custom-call | tf_op jit(solution)/shard_map/prep/pallas_call | solution.py:246
  4.4 11.9 %all-to-all-start = ((bf16[128,10,8,128]{3,2,1,0:T(8,128)(2,1)}), bf16[128,10,8,128]{3,2,1,0:T(8,128)(2,1)}, u32[]{:S(2)}, u32[]{:S(2)}) async-start(bf16[128,10,8,128]{3,2,1,0:T(8,128)(2,1)} %bitcast.29), calls=%async_computation | async-start | bytes 5242880 | tf_op jit(solution)/shard_map/all_to_all | solution.py:946
  16.5 18.5 %attend.1 = (f32[256,768]{1,0:T(8,128)}, f32[256,128]{1,0:T(8,128)}, bf16[256,768]{1,0:T(8,128)(2,1)S(1)}, bf16[256,768]{1,0:T(8,128)(2,1)}, bf16[12,256,256]{2,...) custom-call(s32[1,4]{1,0:T(1,128)S(1)} %copy-done.4, ...), custom_call_target="tpu_custom_call" | custom-call | tf_op jit(solution)/shard_map/attend/pallas_call | solution.py:176
  34.9 2.7 %collective-permute-start.1 = (bf16[256,768]{1,0:T(8,128)(2,1)S(1)}, bf16[256,768]{1,0:T(8,128)(2,1)S(1)}, u32[]{:S(2)}, u32[]{:S(2)}) collective-permute-start(bf16[256,768]{1,0:T(8,128)(2,1)S(1)} %get-tuple-element.91.own), channel_id=1, source_target_pairs={{0,16},{8,56},{16,32},{24,8},{32,48},{40,24},{48,0},{56,40},{64,80... | collective-permute-start | bytes 1179656 | tf_op jit(solution)/shard_map/ppermute | solution.py:939
  37.7 12.6 %collective-permute-done.1.own = bf16[256,768]{1,0:T(8,128)(2,1)S(1)} collective-permute-done((bf16[256,768]{1,0:T(8,128)(2,1)S(1)}, bf16[256,768]{1,0:T(8,128)(2,1)S(1)}, u32[]{:S(2)}, u32[]{:S(2)}) %collective-permute-start.1) | collective-permute-done | bytes 393248 | tf_op jit(solution)/shard_map/ppermute | solution.py:939
  50.3 1.9 collective-permute-start.2
  52.2 1.9 unpack.1
  54.2 2.4 %ffn.2 = (bf16[512,768]{1,0:T(8,128)(2,1)S(1)}, bf16[512,768]{1,0:T(8,128)(2,1)S(1)}, f32[256,768]{1,0:T(8,128)S(1)}, bf16[256,768]{1,0:T(8,128)(2,1)S(1)}, bf16[512,768]{1,0:T(8,128)(2,1)S(1)}) custom-call(bf16[256,768]{1,0:T(8,128)(2,1)S(1)} %collective-permute-done.1.own, bf16[256,768]{1,0:T(8,128)(2,1)S(1)} %collective-permute-done.2.sib, ...), custom_call_target="tpu_custom_call" | custom-call | tf_op jit(solution)/shard_map/ffn/pallas_call | solution.py:140
  57.2 1.2 collective-permute-done.3.got
  59.0 2.4 %ffn.3 = (bf16[512,768]{1,0:T(8,128)(2,1)S(1)}, bf16[512,768]{1,0:T(8,128)(2,1)S(1)}, f32[256,768]{1,0:T(8,128)S(1)}, bf16[256,768]{1,0:T(8,128)(2,1)S(1)}, bf16[512,768]{1,0:T(8,128)(2,1)S(1)}) custom-call(bf16[256,768]{1,0:T(8,128)(2,1)S(1)} %get-tuple-element.91.own, bf16[256,768]{1,0:T(8,128)(2,1)S(1)} %collective-permute-done.sib, ...), custom_call_target="tpu_custom_call" | custom-call | tf_op jit(solution)/shard_map/ffn/pallas_call | solution.py:140
  61.4 5.2 %collective-permute-done.4.refs_3_.far = bf16[256,768]{1,0:T(8,128)(2,1)S(1)} collective-permute-done((bf16[256,768]{1,0:T(8,128)(2,1)S(1)}, bf16[256,768]{1,0:T(8,128)(2,1)S(1)}, u32[]{:S(2)}, u32[]{:S(2)}) %collective-permute-start.4) | collective-permute-done | bytes 393248 | tf_op jit(solution)/shard_map/ppermute | solution.py:943
  66.7 1.6 collective-permute-done.5.refs_2_.near
  69.2 1.8 collective-permute-start.7
  71.1 1.8 outputs.1
  72.9 2.7 %back_near.1 = (f32[256,768]{1,0:T(8,128)}, bf16[256,768]{1,0:T(8,128)(2,1)S(1)}, bf16[512,768]{1,0:T(8,128)(2,1)S(1)}, bf16[512,768]{1,0:T(8,128)(2,1)S(1)}, f32[8,768]{1,0:T(8,128)}) custom-call(bf16[256,768]{1,0:T(8,128)(2,1)S(1)} %middle.1.refs_0_, bf16[256,768]{1,0:T(8,128)(2,1)S(1)} %collective-permute-done.6.refs_1_, ...), custom_call_target="tpu_custom_call" | custom-call | tf_op jit(solution)/shard_map/back_near/pallas_call | solution.py:176
  76.1 2.4 %collective-permute-start.9 = (bf16[256,768]{1,0:T(8,128)(2,1)S(1)}, bf16[256,768]{1,0:T(8,128)(2,1)S(1)}, u32[]{:S(2)}, u32[]{:S(2)}) collective-permute-start(bf16[256,768]{1,0:T(8,128)(2,1)S(1)} %collective-permute-done.7.refs_0_), channel_id=1, source_target_pairs={{0,8},{8,0},{16,24},{24,16},{32,40},{40,32},{48,56},{56,48},{64,72... | collective-permute-start | bytes 1179656 | tf_op jit(solution)/shard_map/ppermute | solution.py:935
  78.6 1.3 collective-permute-done.9.refs_1_
  79.9 2.2 %back_far.1 = (f32[256,768]{1,0:T(8,128)S(1)}, bf16[256,768]{1,0:T(8,128)(2,1)S(1)}, bf16[512,768]{1,0:T(8,128)(2,1)S(1)}, bf16[512,768]{1,0:T(8,128)(2,1)S(1)}, f32[8,768]{1,0:T(8,128)}) custom-call(bf16[256,768]{1,0:T(8,128)(2,1)S(1)} %collective-permute-done.7.refs_0_, bf16[256,768]{1,0:T(8,128)(2,1)S(1)} %collective-permute-done.9.refs_1_, ...), custom_call_target="tpu_custom_call" | custom-call | tf_op jit(solution)/shard_map/back_far/pallas_call | solution.py:176
  82.6 0.8 fusion
  83.4 0.8 fusion.1
  84.4 0.8 add_convert_fusion.1.refs_1_
  85.2 0.8 add_convert_fusion.2.refs_0_
  86.1 1.9 pack.1
  87.9 4.3 %collective-permute-done.11.refs_3_ = bf16[256,768]{1,0:T(8,128)(2,1)S(1)} collective-permute-done((bf16[256,768]{1,0:T(8,128)(2,1)S(1)}, bf16[256,768]{1,0:T(8,128)(2,1)S(1)}, u32[]{:S(2)}, u32[]{:S(2)}) %collective-permute-start.11) | collective-permute-done | bytes 393248 | tf_op jit(solution)/shard_map/ppermute | solution.py:943
  92.2 7.9 %all-to-all-start.1 = ((bf16[128,9,8,128]{3,2,1,0:T(8,128)(2,1)}), bf16[128,9,8,128]{3,2,1,0:T(8,128)(2,1)S(1)}, u32[]{:S(2)}, u32[]{:S(2)}) async-start(bf16[128,9,8,128]{3,2,1,0:T(8,128)(2,1)} %bitcast.30), calls=%async_computation.1 | async-start | bytes 4718592 | tf_op jit(solution)/shard_map/all_to_all | solution.py:946
  100.1 1.1 collective-permute-start.8
  101.3 1.3 collective-permute-done.8.refs_2_
  102.6 13.3 %attend_back.1 = (f32[256,768]{1,0:T(8,128)}, bf16[640,8,128]{2,1,0:T(8,128)(2,1)S(1)}, bf16[640,8,128]{2,1,0:T(8,128)(2,1)S(1)}) custom-call(s32[2]{0:T(128)S(1)} %pad_add_fusion.place.refs_0_, f32[256,768]{1,0:T(8,128)} %get-tuple-element.104.refs_1_, bf16[256,768]{1,0:T(8,128)(2,1)S(1)} %collective-permute-done.8.refs_2_, ...), custom_call_target="tpu_custom_call" | custom-call | tf_op jit(solution)/shard_map/attend_back/pallas_call | solution.py:176
  116.4 2.7 %collective-permute-done.12 = bf16[640,8,128]{2,1,0:T(8,128)(2,1)S(1)} collective-permute-done((bf16[640,8,128]{2,1,0:T(8,128)(2,1)S(1)}, bf16[640,8,128]{2,1,0:T(8,128)(2,1)S(1)}, u32[]{:S(2)}, u32[]{:S(2)}) %collective-permute-start.12) | collective-permute-done | bytes 1310752 | tf_op jit(solution)/shard_map/ppermute | solution.py:935
  119.1 1.4 add_convert_fusion
  120.5 10.9 %all-to-all-done.1.got = bf16[128,9,8,128]{3,2,1,0:T(8,128)(2,1)S(1)} async-done(((bf16[128,9,8,128]{3,2,1,0:T(8,128)(2,1)}), bf16[128,9,8,128]{3,2,1,0:T(8,128)(2,1)S(1)}, u32[]{:S(2)}, u32[]{:S(2)}) %all-to-all-start.1) | async-done | bytes 2359328 | tf_op jit(solution)/shard_map/all_to_all | solution.py:946
  131.7 5.9 %all-to-all-start.2 = ((bf16[128,5,8,128]{3,2,1,0:T(8,128)(2,1)}), bf16[128,5,8,128]{3,2,1,0:T(8,128)(2,1)S(1)}, u32[]{:S(2)}, u32[]{:S(2)}) async-start(bf16[128,5,8,128]{3,2,1,0:T(8,128)(2,1)} %bitcast.31), calls=%async_computation.2 | async-start | bytes 2621440 | tf_op jit(solution)/shard_map/all_to_all | solution.py:946
  137.7 1.1 collective-permute-start.13
  138.8 0.9 collective-permute-done.13
  139.8 2.9 %collective-permute-start.17 = (bf16[2,4,9,8,128]{4,3,2,1,0:T(8,128)(2,1)S(1)}, bf16[2,4,9,8,128]{4,3,2,1,0:T(8,128)(2,1)S(1)}, u32[]{:S(2)}, u32[]{:S(2)}) collective-permute-start(bf16[2,4,9,8,128]{4,3,2,1,0:T(8,128)(2,1)S(1)} %pad_maximum_fusion.1), channel_id=1, source_target_pairs={{0,48},{8,120},{16,0},{24,72},{32,16},{40,88},{48,32},{56,104},{64... | collective-permute-start | bytes 442376 | tf_op jit(solution)/shard_map/ppermute | solution.py:994
  143.2 1.5 collective-permute-start.15
  144.7 2.2 %collective-permute-start.14 = (bf16[2,4,9,8,128]{4,3,2,1,0:T(8,128)(2,1)S(1)}, bf16[2,4,9,8,128]{4,3,2,1,0:T(8,128)(2,1)S(1)}, u32[]{:S(2)}, u32[]{:S(2)}) collective-permute-start(bf16[2,4,9,8,128]{4,3,2,1,0:T(8,128)(2,1)S(1)} %pad_maximum_fusion.1), channel_id=1, source_target_pairs={{0,0},{8,72},{16,16},{24,88},{32,32},{40,104},{48,48},{56,120},{64... | collective-permute-start | bytes 442376 | tf_op jit(solution)/shard_map/ppermute | solution.py:994
  146.9 11.3 %all-to-all-done.2.got = bf16[128,5,8,128]{3,2,1,0:T(8,128)(2,1)S(1)} async-done(((bf16[128,5,8,128]{3,2,1,0:T(8,128)(2,1)}), bf16[128,5,8,128]{3,2,1,0:T(8,128)(2,1)S(1)}, u32[]{:S(2)}, u32[]{:S(2)}) %all-to-all-start.2) | async-done | bytes 1310752 | tf_op jit(solution)/shard_map/all_to_all | solution.py:946
  158.2 1.3 sum_rest.1
  159.5 1.5 collective-permute-done.15
  161.0 8.2 %all-to-all-start.3 = ((bf16[128,5,8,128]{3,2,1,0:T(8,128)(2,1)}), bf16[128,5,8,128]{3,2,1,0:T(8,128)(2,1)S(1)}, u32[]{:S(2)}, u32[]{:S(2)}) async-start(bf16[128,5,8,128]{3,2,1,0:T(8,128)(2,1)} %sum_rest.1), calls=%async_computation.3 | async-start | bytes 2621440 | tf_op jit(solution)/shard_map/all_to_all | solution.py:946
  169.3 1.1 collective-permute-start.18
  170.5 1.6 collective-permute-done.18.ffn_oth
  172.1 3.6 %final_ffn.1 = (f32[768,384]{1,0:T(8,128)}, f32[384,768]{1,0:T(8,128)}) custom-call(s32[2]{0:T(128)S(1)} %pad_add_fusion.place.refs_0_, bf16[8,4,9,8,128]{4,3,2,1,0:T(8,128)(2,1)S(1)} %bitcast.26, bf16[8,4,9,8,128]{4,3,2,1,0:T(8,128)(2,1)S(1)} %collective-permute-done.18.ffn_oth), custom_call_target="tpu_custom_call" | custom-call | tf_op jit(solution)/shard_map/final_ffn/pallas_call | solution.py:823
  175.7 14.0 %all-to-all-done.3 = bf16[128,5,8,128]{3,2,1,0:T(8,128)(2,1)S(1)} async-done(((bf16[128,5,8,128]{3,2,1,0:T(8,128)(2,1)}), bf16[128,5,8,128]{3,2,1,0:T(8,128)(2,1)S(1)}, u32[]{:S(2)}, u32[]{:S(2)}) %all-to-all-start.3) | async-done | bytes 1310752 | tf_op jit(solution)/shard_map/all_to_all | solution.py:946
  189.7 1.2 collective-permute-start.19
  190.8 2.7 %collective-permute-done.19.other = bf16[640,8,128]{2,1,0:T(8,128)(2,1)S(1)} collective-permute-done((bf16[640,8,128]{2,1,0:T(8,128)(2,1)S(1)}, bf16[640,8,128]{2,1,0:T(8,128)(2,1)S(1)}, u32[]{:S(2)}, u32[]{:S(2)}) %collective-permute-start.19) | collective-permute-done | bytes 1310752 | tf_op jit(solution)/shard_map/ppermute | solution.py:935
  193.5 3.0 %final.1 = (f32[768,768]{1,0:T(8,128)}, f32[768]{0:T(1024)}, f32[65,768]{1,0:T(8,128)}, f32[768,768]{1,0:T(8,128)}, f32[768]{0:T(1024)}, /*index=5*/f32[768]{0:T...) custom-call(s32[2]{0:T(128)S(1)} %pad_add_fusion.place.refs_0_, ...), custom_call_target="tpu_custom_call" | custom-call | tf_op jit(solution)/shard_map/final/pallas_call | solution.py:884
  (56 shorter events, 4.8 us)
Async XLA Ops:
  4.3 12.0 %copy-start.5 = (bf16[768]{0:T(1024)(128)(2,1)S(1)}, bf16[768]{0:T(1024)(128)(2,1)}, u32[]{:S(2)}) copy-start(bf16[768]{0:T(1024)(128)(2,1)} %param.25) | copy-start | bytes 4612
  4.3 12.0 %copy-start.6 = (bf16[768]{0:T(1024)(128)(2,1)S(1)}, bf16[768]{0:T(1024)(128)(2,1)}, u32[]{:S(2)}) copy-start(bf16[768]{0:T(1024)(128)(2,1)} %param.26) | copy-start | bytes 4612
  4.4 12.0 %copy-start.7 = (bf16[768]{0:T(1024)(128)(2,1)S(1)}, bf16[768]{0:T(1024)(128)(2,1)}, u32[]{:S(2)}) copy-start(bf16[768]{0:T(1024)(128)(2,1)} %param.21) | copy-start | bytes 4612
  4.4 12.0 %copy-start.8 = (bf16[768]{0:T(1024)(128)(2,1)S(1)}, bf16[768]{0:T(1024)(128)(2,1)}, u32[]{:S(2)}) copy-start(bf16[768]{0:T(1024)(128)(2,1)} %param.24) | copy-start | bytes 4612
  4.4 12.0 %copy-start.2 = (bf16[65,768]{1,0:T(8,128)(2,1)S(1)}, bf16[65,768]{1,0:T(8,128)(2,1)}, u32[]{:S(2)}) copy-start(bf16[65,768]{1,0:T(8,128)(2,1)} %refs_4_.1) | copy-start | bytes 299524
  4.4 12.0 %copy-start.3 = (s32[256]{0:T(256)S(1)}, s32[256]{0:T(256)}, u32[]{:S(2)}) copy-start(s32[256]{0:T(256)} %param.35) | copy-start | bytes 3076
  4.4 12.0 %copy-start.4 = (s32[1,4]{1,0:T(1,128)S(1)}, s32[1,4]{1,0:T(1,128)}, u32[]{:S(2)}) copy-start(s32[1,4]{1,0:T(1,128)} %refs_0_.1) | copy-start | bytes 52
  4.4 47.8 %all-to-all-start = ((bf16[128,10,8,128]{3,2,1,0:T(8,128)(2,1)}), bf16[128,10,8,128]{3,2,1,0:T(8,128)(2,1)}, u32[]{:S(2)}, u32[]{:S(2)}) async-start(bf16[128,10,8,128]{3,2,1,0:T(8,128)(2,1)} %bitcast.29), calls=%async_computation | async-start | bytes 5242880 | tf_op jit(solution)/shard_map/all_to_all | solution.py:946
  34.9 15.4 %collective-permute-start.1 = (bf16[256,768]{1,0:T(8,128)(2,1)S(1)}, bf16[256,768]{1,0:T(8,128)(2,1)S(1)}, u32[]{:S(2)}, u32[]{:S(2)}) collective-permute-start(bf16[256,768]{1,0:T(8,128)(2,1)S(1)} %get-tuple-element.91.own), channel_id=1, source_target_pairs={{0,16},{8,56},{16,32},{24,8},{32,48},{40,24},{48,0},{56,40},{64,80... | collective-permute-start | bytes 1179656 | tf_op jit(solution)/shard_map/ppermute | solution.py:939
  50.3 3.9 %collective-permute-start.2 = (bf16[256,768]{1,0:T(8,128)(2,1)S(1)}, bf16[256,768]{1,0:T(8,128)(2,1)S(1)}, u32[]{:S(2)}, u32[]{:S(2)}) collective-permute-start(bf16[256,768]{1,0:T(8,128)(2,1)S(1)} %collective-permute-done.1.own), channel_id=1, source_target_pairs={{0,8},{8,0},{16,24},{24,16},{32,40},{40,32},{48,56},{56,48},{64,72... | collective-permute-start | bytes 1179656 | tf_op jit(solution)/shard_map/ppermute | solution.py:935
  56.6 1.8 collective-permute-start.3
  56.7 2.3 %collective-permute-start = (bf16[256,768]{1,0:T(8,128)(2,1)S(1)}, bf16[256,768]{1,0:T(8,128)(2,1)S(1)}, u32[]{:S(2)}, u32[]{:S(2)}) collective-permute-start(bf16[256,768]{1,0:T(8,128)(2,1)S(1)} %get-tuple-element.91.own), channel_id=1, source_target_pairs={{0,8},{8,0},{16,24},{24,16},{32,40},{40,32},{48,56},{56,48},{64,72... | collective-permute-start | bytes 1179656 | tf_op jit(solution)/shard_map/ppermute | solution.py:935
  58.5 8.2 %copy-start.9 = (bf16[768]{0:T(1024)(128)(2,1)S(1)}, bf16[768]{0:T(1024)(128)(2,1)}, u32[]{:S(2)}) copy-start(bf16[768]{0:T(1024)(128)(2,1)} %param.30) | copy-start | bytes 4612
  58.5 8.2 %copy-start.10 = (bf16[768]{0:T(1024)(128)(2,1)S(1)}, bf16[768]{0:T(1024)(128)(2,1)}, u32[]{:S(2)}) copy-start(bf16[768]{0:T(1024)(128)(2,1)} %param.31) | copy-start | bytes 4612
  58.5 9.8 %copy-start = (f32[256,768]{1,0:T(8,128)S(1)}, f32[256,768]{1,0:T(8,128)}, u32[]{:S(2)}) copy-start(f32[256,768]{1,0:T(8,128)} %get-tuple-element.90.refs_0_.n1.refs_5_) | copy-start | bytes 2359300
  58.5 9.8 %copy-start.1 = (bf16[256,768]{1,0:T(8,128)(2,1)S(1)}, bf16[256,768]{1,0:T(8,128)(2,1)}, u32[]{:S(2)}) copy-start(bf16[256,768]{1,0:T(8,128)(2,1)} %og.1) | copy-start | bytes 1179652
  58.5 8.1 %collective-permute-start.4 = (bf16[256,768]{1,0:T(8,128)(2,1)S(1)}, bf16[256,768]{1,0:T(8,128)(2,1)S(1)}, u32[]{:S(2)}, u32[]{:S(2)}) collective-permute-start(bf16[256,768]{1,0:T(8,128)(2,1)S(1)} %combine.2), channel_id=1, source_target_pairs={{16,0},{56,8},{32,16},{8,24},{48,32},{24,40},{0,48},{40,56},{80,64... | collective-permute-start | bytes 1179656 | tf_op jit(solution)/shard_map/ppermute | solution.py:943
  66.6 1.7 collective-permute-start.5
  68.3 2.7 %copy-start.11 = (bf16[768]{0:T(1024)(128)(2,1)S(1)}, bf16[768]{0:T(1024)(128)(2,1)}, u32[]{:S(2)}) copy-start(bf16[768]{0:T(1024)(128)(2,1)} %param.32) | copy-start | bytes 4612
  69.0 3.9 %collective-permute-start.6 = (bf16[256,768]{1,0:T(8,128)(2,1)S(1)}, bf16[256,768]{1,0:T(8,128)(2,1)S(1)}, u32[]{:S(2)}, u32[]{:S(2)}) collective-permute-start(bf16[256,768]{1,0:T(8,128)(2,1)S(1)} %middle.1.refs_0_), channel_id=1, source_target_pairs={{0,8},{8,0},{16,24},{24,16},{32,40},{40,32},{48,56},{56,48},{64,72... | collective-permute-start | bytes 1179656 | tf_op jit(solution)/shard_map/ppermute | solution.py:935
  69.2 6.9 %collective-permute-start.7 = (bf16[256,768]{1,0:T(8,128)(2,1)S(1)}, bf16[256,768]{1,0:T(8,128)(2,1)S(1)}, u32[]{:S(2)}, u32[]{:S(2)}) collective-permute-start(bf16[256,768]{1,0:T(8,128)(2,1)S(1)} %middle.1.refs_0_), channel_id=1, source_target_pairs={{0,16},{8,56},{16,32},{24,8},{32,48},{40,24},{48,0},{56,40},{64,80... | collective-permute-start | bytes 1179656 | tf_op jit(solution)/shard_map/ppermute | solution.py:939
  76.1 3.8 %collective-permute-start.9 = (bf16[256,768]{1,0:T(8,128)(2,1)S(1)}, bf16[256,768]{1,0:T(8,128)(2,1)S(1)}, u32[]{:S(2)}, u32[]{:S(2)}) collective-permute-start(bf16[256,768]{1,0:T(8,128)(2,1)S(1)} %collective-permute-done.7.refs_0_), channel_id=1, source_target_pairs={{0,8},{8,0},{16,24},{24,16},{32,40},{40,32},{48,56},{56,48},{64,72... | collective-permute-start | bytes 1179656 | tf_op jit(solution)/shard_map/ppermute | solution.py:935
  82.1 2.1 %collective-permute-start.10 = (bf16[256,768]{1,0:T(8,128)(2,1)S(1)}, bf16[256,768]{1,0:T(8,128)(2,1)S(1)}, u32[]{:S(2)}, u32[]{:S(2)}) collective-permute-start(bf16[256,768]{1,0:T(8,128)(2,1)S(1)} %get-tuple-element.114), channel_id=1, source_target_pairs={{0,8},{8,0},{16,24},{24,16},{32,40},{40,32},{48,56},{56,48},{64,72... | collective-permute-start | bytes 1179656 | tf_op jit(solution)/shard_map/ppermute | solution.py:935
  84.3 7.9 %collective-permute-start.11 = (bf16[256,768]{1,0:T(8,128)(2,1)S(1)}, bf16[256,768]{1,0:T(8,128)(2,1)S(1)}, u32[]{:S(2)}, u32[]{:S(2)}) collective-permute-start(bf16[256,768]{1,0:T(8,128)(2,1)S(1)} %combine.3), channel_id=1, source_target_pairs={{16,0},{56,8},{32,16},{8,24},{48,32},{24,40},{0,48},{40,56},{80,64... | collective-permute-start | bytes 1179656 | tf_op jit(solution)/shard_map/ppermute | solution.py:943
  92.2 39.1 %all-to-all-start.1 = ((bf16[128,9,8,128]{3,2,1,0:T(8,128)(2,1)}), bf16[128,9,8,128]{3,2,1,0:T(8,128)(2,1)S(1)}, u32[]{:S(2)}, u32[]{:S(2)}) async-start(bf16[128,9,8,128]{3,2,1,0:T(8,128)(2,1)} %bitcast.30), calls=%async_computation.1 | async-start | bytes 4718592 | tf_op jit(solution)/shard_map/all_to_all | solution.py:946
  100.1 2.5 %collective-permute-start.8 = (bf16[256,768]{1,0:T(8,128)(2,1)S(1)}, bf16[256,768]{1,0:T(8,128)(2,1)S(1)}, u32[]{:S(2)}, u32[]{:S(2)}) collective-permute-start(bf16[256,768]{1,0:T(8,128)(2,1)S(1)} %get-tuple-element.107), channel_id=1, source_target_pairs={{0,8},{8,0},{16,24},{24,16},{32,40},{40,32},{48,56},{56,48},{64,72... | collective-permute-start | bytes 1179656 | tf_op jit(solution)/shard_map/ppermute | solution.py:935
  116.0 3.1 %collective-permute-start.12 = (bf16[640,8,128]{2,1,0:T(8,128)(2,1)S(1)}, bf16[640,8,128]{2,1,0:T(8,128)(2,1)S(1)}, u32[]{:S(2)}, u32[]{:S(2)}) collective-permute-start(bf16[640,8,128]{2,1,0:T(8,128)(2,1)S(1)} %get-tuple-element.140), channel_id=1, source_target_pairs={{0,8},{8,0},{16,24},{24,16},{32,40},{40,32},{48,56},{56,48},{64,72... | collective-permute-start | bytes 3932168 | tf_op jit(solution)/shard_map/ppermute | solution.py:935
  131.7 26.4 %all-to-all-start.2 = ((bf16[128,5,8,128]{3,2,1,0:T(8,128)(2,1)}), bf16[128,5,8,128]{3,2,1,0:T(8,128)(2,1)S(1)}, u32[]{:S(2)}, u32[]{:S(2)}) async-start(bf16[128,5,8,128]{3,2,1,0:T(8,128)(2,1)} %bitcast.31), calls=%async_computation.2 | async-start | bytes 2621440 | tf_op jit(solution)/shard_map/all_to_all | solution.py:946
  137.7 2.1 %collective-permute-start.13 = (bf16[4,9,8,128]{3,2,1,0:T(8,128)(2,1)S(1)}, bf16[4,9,8,128]{3,2,1,0:T(8,128)(2,1)S(1)}, u32[]{:S(2)}, u32[]{:S(2)}) collective-permute-start(bf16[4,9,8,128]{3,2,1,0:T(8,128)(2,1)S(1)} %sum_ffn.1), channel_id=1, source_target_pairs={{0,8},{8,0},{16,24},{24,16},{32,40},{40,32},{48,56},{56,48},{64,72... | collective-permute-start | bytes 221192 | tf_op jit(solution)/shard_map/ppermute | solution.py:935
  139.8 19.7 %collective-permute-start.17 = (bf16[2,4,9,8,128]{4,3,2,1,0:T(8,128)(2,1)S(1)}, bf16[2,4,9,8,128]{4,3,2,1,0:T(8,128)(2,1)S(1)}, u32[]{:S(2)}, u32[]{:S(2)}) collective-permute-start(bf16[2,4,9,8,128]{4,3,2,1,0:T(8,128)(2,1)S(1)} %pad_maximum_fusion.1), channel_id=1, source_target_pairs={{0,48},{8,120},{16,0},{24,72},{32,16},{40,88},{48,32},{56,104},{64... | collective-permute-start | bytes 442376 | tf_op jit(solution)/shard_map/ppermute | solution.py:994
  142.7 16.8 %collective-permute-start.16 = (bf16[2,4,9,8,128]{4,3,2,1,0:T(8,128)(2,1)S(1)}, bf16[2,4,9,8,128]{4,3,2,1,0:T(8,128)(2,1)S(1)}, u32[]{:S(2)}, u32[]{:S(2)}) collective-permute-start(bf16[2,4,9,8,128]{4,3,2,1,0:T(8,128)(2,1)S(1)} %pad_maximum_fusion.1), channel_id=1, source_target_pairs={{0,32},{8,104},{16,48},{24,120},{32,0},{40,72},{48,16},{56,88},{64... | collective-permute-start | bytes 442376 | tf_op jit(solution)/shard_map/ppermute | solution.py:994
  143.2 17.8 %collective-permute-start.15 = (bf16[2,4,9,8,128]{4,3,2,1,0:T(8,128)(2,1)S(1)}, bf16[2,4,9,8,128]{4,3,2,1,0:T(8,128)(2,1)S(1)}, u32[]{:S(2)}, u32[]{:S(2)}) collective-permute-start(bf16[2,4,9,8,128]{4,3,2,1,0:T(8,128)(2,1)S(1)} %pad_maximum_fusion.1), channel_id=1, source_target_pairs={{0,16},{8,88},{16,32},{24,104},{32,48},{40,120},{48,0},{56,72},{64... | collective-permute-start | bytes 442376 | tf_op jit(solution)/shard_map/ppermute | solution.py:994
  144.7 16.3 %collective-permute-start.14 = (bf16[2,4,9,8,128]{4,3,2,1,0:T(8,128)(2,1)S(1)}, bf16[2,4,9,8,128]{4,3,2,1,0:T(8,128)(2,1)S(1)}, u32[]{:S(2)}, u32[]{:S(2)}) collective-permute-start(bf16[2,4,9,8,128]{4,3,2,1,0:T(8,128)(2,1)S(1)} %pad_maximum_fusion.1), channel_id=1, source_target_pairs={{0,0},{8,72},{16,16},{24,88},{32,32},{40,104},{48,48},{56,120},{64... | collective-permute-start | bytes 442376 | tf_op jit(solution)/shard_map/ppermute | solution.py:994
  161.0 28.7 %all-to-all-start.3 = ((bf16[128,5,8,128]{3,2,1,0:T(8,128)(2,1)}), bf16[128,5,8,128]{3,2,1,0:T(8,128)(2,1)S(1)}, u32[]{:S(2)}, u32[]{:S(2)}) async-start(bf16[128,5,8,128]{3,2,1,0:T(8,128)(2,1)} %sum_rest.1), calls=%async_computation.3 | async-start | bytes 2621440 | tf_op jit(solution)/shard_map/all_to_all | solution.py:946
  169.3 2.8 %collective-permute-start.18 = (bf16[8,4,9,8,128]{4,3,2,1,0:T(8,128)(2,1)S(1)}, bf16[8,4,9,8,128]{4,3,2,1,0:T(8,128)(2,1)S(1)}, u32[]{:S(2)}, u32[]{:S(2)}) collective-permute-start(bf16[8,4,9,8,128]{4,3,2,1,0:T(8,128)(2,1)S(1)} %bitcast.25), channel_id=1, source_target_pairs={{0,8},{8,0},{16,24},{24,16},{32,40},{40,32},{48,56},{56,48},{64,72... | collective-permute-start | bytes 1769480 | tf_op jit(solution)/shard_map/ppermute | solution.py:935
  189.7 3.8 %collective-permute-start.19 = (bf16[640,8,128]{2,1,0:T(8,128)(2,1)S(1)}, bf16[640,8,128]{2,1,0:T(8,128)(2,1)S(1)}, u32[]{:S(2)}, u32[]{:S(2)}) collective-permute-start(bf16[640,8,128]{2,1,0:T(8,128)(2,1)S(1)} %bitcast.23), channel_id=1, source_target_pairs={{0,8},{8,0},{16,24},{24,16},{32,40},{40,32},{48,56},{56,48},{64,72... | collective-permute-start | bytes 3932168 | tf_op jit(solution)/shard_map/ppermute | solution.py:935
